TPU v7x, 32 devices: a whole 2x2x4 slice. The times are simulated.
32 devices in a mesh: fsdp: 4 (over z), ctx: 4 (over x, core), tp: 2 (over y).
Axes of the slice: x: 2, y: 2, z: 4, core: 2. Of those that a mesh axis runs over, the one named last changes fastest.
Arguments:
- x_in: bfloat16 [8, 1024, 2048], P(None, ('fsdp', 'ctx')), may hold values from -6 to 6
- cotangent: bfloat16 [8, 1024, 2048], P(None, ('fsdp', 'ctx')), may hold values from -6 to 6
- lengths: int32 [8], replicated, may hold values from 128 to 1024, as said below
- adapter_ids: int32 [8], replicated, may hold values from 0 to 7
- w_qkv: bfloat16 [3, 2048, 2048], P(None, 'fsdp', 'tp'), may hold values from -0.125 to 0.125
- w_out: bfloat16 [2048, 2048], P('tp', 'fsdp'), may hold values from -2 to 2
- w_up: bfloat16 [2048, 8192], P('fsdp', 'tp'), may hold values from -0.125 to 0.125
- w_down: bfloat16 [8192, 2048], P('tp', 'fsdp'), may hold values from -0.0625 to 0.0625
- ln_gain: float32 [2, 2048], replicated, may hold values from 0.1 to 1.9
- ln_bias: float32 [2, 2048], replicated, may hold values from -1.5 to 1.5
- a_qkv: bfloat16 [3, 2048, 128], replicated, may hold values from -0.125 to 0.125
- b_qkv: bfloat16 [3, 128, 2048], P(None, None, 'tp'), may hold values from -0.5 to 0.5
- a_out: bfloat16 [2048, 128], P('tp'), may hold values from -2 to 2
- b_out: bfloat16 [128, 2048], replicated, may hold values from -0.5 to 0.5
- a_up: bfloat16 [2048, 128], replicated, may hold values from -0.125 to 0.125
- b_up: bfloat16 [128, 8192], P(None, 'tp'), may hold values from -0.5 to 0.5
- a_down: bfloat16 [8192, 128], P('tp'), may hold values from -0.0625 to 0.0625
- b_down: bfloat16 [128, 2048], replicated, may hold values from -0.5 to 0.5
Outputs:
- activations: bfloat16 [8, 1024, 2048], P(None, ('fsdp', 'ctx'))
- input_grad: bfloat16 [8, 1024, 2048], P(None, ('fsdp', 'ctx'))
- grad_a_qkv: float32 [3, 2048, 128], replicated
- grad_b_qkv: float32 [3, 128, 2048], P(None, None, 'tp')
- grad_a_out: float32 [2048, 128], P('tp')
- grad_b_out: float32 [128, 2048], replicated
- grad_a_up: float32 [2048, 128], replicated
- grad_b_up: float32 [128, 8192], P(None, 'tp')
- grad_a_down: float32 [8192, 128], P('tp')
- grad_b_down: float32 [128, 2048], replicated
Inputs may be any that keep to these rules, and one draw needn't show every extreme that they name: `lengths`: each aligned block of 2 sequences holds at least one sequence of length 1024.
All inputs are finite; a program needn't handle non-finite values.
Results may differ from a plain program's by a relative error of at most 0.019.
Values may be sent and summed in bfloat16 or wider, within the bound.
A program may use at most 256 MiB of HBM per device.

v0:
```python
from functools import partial
import math

import jax
import jax.numpy as jnp
from jax import lax
from jax.sharding import PartitionSpec as P

HEAD_DIM = 128
RANK = 16
ADAPTERS = 8


NORM_EPS = 1e-06
GELU_COEF = 0.7978845608028654


def norm_rows(values, gain_row, shift_row):
    center = values - jnp.mean(values, axis=-1, keepdims=True)
    spread = jnp.mean(center * center, axis=-1, keepdims=True)
    return center * lax.rsqrt(spread + NORM_EPS) * gain_row + shift_row


def gelu_tanh(values):
    return (
        0.5 * values * (1.0 + jnp.tanh(GELU_COEF * (values + 0.044715 * values * values * values)))
    )


def product(left_side, right_side):
    return jnp.dot(left_side, right_side, preferred_element_type=jnp.float32)


def against(left_side, right_side):
    return lax.dot_general(
        left_side, right_side, (((1,), (1,)), ((), ())), preferred_element_type=jnp.float32
    )


def across(left_side, right_side):
    return lax.dot_general(
        left_side, right_side, (((0,), (0,)), ((), ())), preferred_element_type=jnp.float32
    )


def local(
    x_in,
    cotangent,
    lengths,
    adapter_ids,
    w_qkv,
    w_out,
    w_up,
    w_down,
    ln_gain,
    ln_bias,
    a_qkv,
    b_qkv,
    a_out,
    b_out,
    a_up,
    b_up,
    a_down,
    b_down,
):
    n_ctx = lax.axis_size("ctx")
    n_fsdp = lax.axis_size("fsdp")
    owner_index = lax.axis_index("fsdp")
    seq_total, piece_rows, model_width = x_in.shape
    per_dev = seq_total // n_fsdp
    local_len = n_fsdp * piece_rows
    dev_rows = per_dev * local_len
    key_count = n_ctx * local_len
    heads_width = w_qkv.shape[2]
    heads_here = heads_width // HEAD_DIM
    score_scale = 1.0 / math.sqrt(HEAD_DIM)
    dealt_x, dealt_cot = (
        lax.all_to_all(x_in, "fsdp", split_axis=0, concat_axis=1, tiled=True),
        lax.all_to_all(cotangent, "fsdp", split_axis=0, concat_axis=1, tiled=True),
    )
    x_rows = dealt_x.reshape(dev_rows, model_width)
    my_lengths = lax.dynamic_slice_in_dim(lengths, owner_index * per_dev, per_dev)
    my_ids = lax.dynamic_slice_in_dim(adapter_ids, owner_index * per_dev, per_dev)
    picked = (my_ids[:, None] == jnp.arange(ADAPTERS)[None, :]).astype(jnp.float32)
    pick_rows = jnp.repeat(jnp.repeat(picked, RANK, axis=1), local_len, axis=0)
    key_index = jnp.arange(key_count)
    ctx_block = key_index // local_len
    remain = key_index % local_len
    key_pos = (remain // piece_rows * n_ctx + ctx_block) * piece_rows + remain % piece_rows
    usable = key_pos[None, :] < my_lengths[:, None]
    qkv_full, out_full = (
        lax.all_gather(w_qkv, "fsdp", axis=1, tiled=True),
        lax.all_gather(w_out, "fsdp", axis=1, tiled=True),
    )
    adapt_qkv = [
        (product(x_rows, a_qkv[proj_index]) * pick_rows).astype(jnp.bfloat16)
        for proj_index in range(3)
    ]
    projected = [
        (product(x_rows, qkv_full[proj_index]) + product(adapt_qkv[proj_index], b_qkv[proj_index]))
        .astype(jnp.bfloat16)
        .reshape(per_dev, local_len, heads_width)
        for proj_index in range(3)
    ]
    queries_all = projected[0]
    keys_all, values_all = (
        lax.all_gather(projected[1], "ctx", axis=1, tiled=True),
        lax.all_gather(projected[2], "ctx", axis=1, tiled=True),
    )

    def score_block(query_heads, key_heads, usable_row):
        scores = (
            jnp.einsum("qhd,khd->hqk", query_heads, key_heads, preferred_element_type=jnp.float32)
            * score_scale
        )
        return jnp.where(usable_row[None, None, :], scores, -1e30)

    def attend(packed):
        queries, keys_seq, values_seq, usable_row = packed
        query_heads = queries.reshape(local_len, heads_here, HEAD_DIM)
        key_heads = keys_seq.reshape(key_count, heads_here, HEAD_DIM)
        value_heads = values_seq.reshape(key_count, heads_here, HEAD_DIM)
        scores = score_block(query_heads, key_heads, usable_row)
        row_max = jnp.max(scores, axis=-1, keepdims=True)
        row_total = jnp.sum(jnp.exp(scores - row_max), axis=-1, keepdims=True)
        log_total = row_max + jnp.log(row_total)
        attn_probs = jnp.exp(scores - log_total).astype(jnp.bfloat16)
        mixed_heads = jnp.einsum(
            "hqk,khd->qhd", attn_probs, value_heads, preferred_element_type=jnp.float32
        )
        return (mixed_heads.reshape(local_len, heads_width).astype(jnp.bfloat16), log_total[..., 0])

    context, log_totals = lax.map(attend, (queries_all, keys_all, values_all, usable))
    ctx_rows = context.reshape(dev_rows, heads_width)
    part_out = product(ctx_rows, out_full)
    part_adapt = product(ctx_rows, a_out) * pick_rows
    attn_sum, adapt_out_sum = lax.psum((part_out, part_adapt), "tp")
    adapt_out = adapt_out_sum.astype(jnp.bfloat16)
    attn_branch = attn_sum + product(adapt_out, b_out)
    hidden_one, norm_one_back = jax.vjp(
        partial(norm_rows, gain_row=ln_gain[0], shift_row=ln_bias[0]),
        x_rows.astype(jnp.float32) + attn_branch,
    )
    hidden_low = hidden_one.astype(jnp.bfloat16)
    up_full, down_full = (
        lax.all_gather(w_up, "fsdp", axis=0, tiled=True),
        lax.all_gather(w_down, "fsdp", axis=1, tiled=True),
    )
    adapt_up = (product(hidden_low, a_up) * pick_rows).astype(jnp.bfloat16)
    pre_act = product(hidden_low, up_full) + product(adapt_up, b_up)
    activated, gelu_back = jax.vjp(gelu_tanh, pre_act)
    gelu_out = activated.astype(jnp.bfloat16)
    part_down = product(gelu_out, down_full)
    part_adapt_down = product(gelu_out, a_down) * pick_rows
    down_sum, adapt_down_sum = lax.psum((part_down, part_adapt_down), "tp")
    adapt_down = adapt_down_sum.astype(jnp.bfloat16)
    second_in = hidden_one + down_sum + product(adapt_down, b_down)
    layer_out, norm_two_back = jax.vjp(
        partial(norm_rows, gain_row=ln_gain[1], shift_row=ln_bias[1]), second_in
    )
    grad_out = dealt_cot.reshape(dev_rows, model_width).astype(jnp.float32)
    (grad_second,) = norm_two_back(grad_out)
    grad_down_low = grad_second.astype(jnp.bfloat16)
    up_back, down_back = (
        lax.all_gather(w_up, "fsdp", axis=0, tiled=True),
        lax.all_gather(w_down, "fsdp", axis=1, tiled=True),
    )
    grad_adapt_down = (against(grad_down_low, b_down) * pick_rows).astype(jnp.bfloat16)
    grad_b_down = across(adapt_down, grad_down_low)
    grad_a_down = across(gelu_out, grad_adapt_down)
    grad_gelu = against(grad_down_low, down_back) + against(grad_adapt_down, a_down)
    (grad_pre,) = gelu_back(grad_gelu)
    grad_pre_low = grad_pre.astype(jnp.bfloat16)
    grad_b_up = across(adapt_up, grad_pre_low)
    part_hidden = against(grad_pre_low, up_back)
    part_adapt_up = against(grad_pre_low, b_up)
    grad_hidden_sum, grad_adapt_up_sum = lax.psum((part_hidden, part_adapt_up), "tp")
    grad_adapt_up = (grad_adapt_up_sum * pick_rows).astype(jnp.bfloat16)
    grad_a_up = across(hidden_low, grad_adapt_up)
    grad_hidden = grad_second + grad_hidden_sum + against(grad_adapt_up, a_up)
    (grad_first,) = norm_one_back(grad_hidden)
    grad_attn_low = grad_first.astype(jnp.bfloat16)
    qkv_back, out_back = (
        lax.all_gather(w_qkv, "fsdp", axis=1, tiled=True),
        lax.all_gather(w_out, "fsdp", axis=1, tiled=True),
    )
    grad_adapt_out = (against(grad_attn_low, b_out) * pick_rows).astype(jnp.bfloat16)
    grad_b_out = across(adapt_out, grad_attn_low)
    grad_a_out = across(ctx_rows, grad_adapt_out)
    grad_context = (against(grad_attn_low, out_back) + against(grad_adapt_out, a_out)).astype(
        jnp.bfloat16
    )

    def attend_back(packed):
        queries, keys_seq, values_seq, usable_row, log_total, grad_ctx_seq = packed
        query_heads = queries.reshape(local_len, heads_here, HEAD_DIM)
        key_heads = keys_seq.reshape(key_count, heads_here, HEAD_DIM)
        value_heads = values_seq.reshape(key_count, heads_here, HEAD_DIM)
        scores = score_block(query_heads, key_heads, usable_row)
        attn_probs = jnp.exp(scores - log_total[..., None])
        probs_low = attn_probs.astype(jnp.bfloat16)
        grad_heads = grad_ctx_seq.reshape(local_len, heads_here, HEAD_DIM)
        grad_values = jnp.einsum(
            "hqk,qhd->khd", probs_low, grad_heads, preferred_element_type=jnp.float32
        )
        grad_probs = jnp.einsum(
            "qhd,khd->hqk", grad_heads, value_heads, preferred_element_type=jnp.float32
        )
        row_dot = jnp.sum(attn_probs * grad_probs, axis=-1, keepdims=True)
        grad_scores = (attn_probs * (grad_probs - row_dot)).astype(jnp.bfloat16)
        grad_query = (
            jnp.einsum("hqk,khd->qhd", grad_scores, key_heads, preferred_element_type=jnp.float32)
            * score_scale
        )
        grad_keys = (
            jnp.einsum("hqk,qhd->khd", grad_scores, query_heads, preferred_element_type=jnp.float32)
            * score_scale
        )
        return (
            grad_query.reshape(local_len, heads_width).astype(jnp.bfloat16),
            grad_keys.reshape(key_count, heads_width),
            grad_values.reshape(key_count, heads_width),
        )

    grad_ctx_seqs = grad_context.reshape(per_dev, local_len, heads_width)
    grad_queries, grad_keys_all, grad_values_all = lax.map(
        attend_back, (queries_all, keys_all, values_all, usable, log_totals, grad_ctx_seqs)
    )
    grad_keys_mine, grad_values_mine = (
        lax.psum_scatter(
            grad_keys_all.astype(jnp.bfloat16), "ctx", scatter_dimension=1, tiled=True
        ).astype(jnp.float32),
        lax.psum_scatter(
            grad_values_all.astype(jnp.bfloat16), "ctx", scatter_dimension=1, tiled=True
        ).astype(jnp.float32),
    )
    grad_proj = [
        grad_queries.reshape(dev_rows, heads_width),
        grad_keys_mine.astype(jnp.bfloat16).reshape(dev_rows, heads_width),
        grad_values_mine.astype(jnp.bfloat16).reshape(dev_rows, heads_width),
    ]
    grad_b_qkv = jnp.stack(
        [across(adapt_qkv[proj_index], grad_proj[proj_index]) for proj_index in range(3)]
    )
    part_input = (
        against(grad_proj[0], qkv_back[0])
        + against(grad_proj[1], qkv_back[1])
        + against(grad_proj[2], qkv_back[2])
    )
    part_adapt_qkv = jnp.stack(
        [against(grad_proj[proj_index], b_qkv[proj_index]) for proj_index in range(3)]
    )
    grad_input_sum, grad_adapt_qkv_sum = (
        lax.psum(part_input.astype(jnp.bfloat16), "tp").astype(jnp.float32),
        lax.psum(part_adapt_qkv.astype(jnp.bfloat16), "tp").astype(jnp.float32),
    )
    grad_adapt_qkv = (grad_adapt_qkv_sum * pick_rows[None]).astype(jnp.bfloat16)
    grad_a_qkv = jnp.stack([across(x_rows, grad_adapt_qkv[proj_index]) for proj_index in range(3)])
    grad_input = (
        grad_first
        + grad_input_sum
        + against(grad_adapt_qkv[0], a_qkv[0])
        + against(grad_adapt_qkv[1], a_qkv[1])
        + against(grad_adapt_qkv[2], a_qkv[2])
    )
    summed_grads = lax.psum(
        (
            grad_a_qkv,
            grad_b_qkv,
            grad_a_out,
            grad_b_out,
            grad_a_up,
            grad_b_up,
            grad_a_down,
            grad_b_down,
        ),
        ("fsdp", "ctx"),
    )
    out_low = layer_out.astype(jnp.bfloat16).reshape(per_dev, local_len, model_width)
    input_low = grad_input.astype(jnp.bfloat16).reshape(per_dev, local_len, model_width)
    back_out, back_input = (
        lax.all_to_all(out_low, "fsdp", split_axis=1, concat_axis=0, tiled=True),
        lax.all_to_all(input_low, "fsdp", split_axis=1, concat_axis=0, tiled=True),
    )
    return (
        back_out,
        back_input,
        summed_grads[0],
        summed_grads[1],
        summed_grads[2],
        summed_grads[3],
        summed_grads[4],
        summed_grads[5],
        summed_grads[6],
        summed_grads[7],
    )


def solution(mesh):
    return jax.shard_map(
        local,
        mesh=mesh,
        in_specs=(
            P(None, ("fsdp", "ctx"), None),
            P(None, ("fsdp", "ctx"), None),
            P(),
            P(),
            P(None, "fsdp", "tp"),
            P("tp", "fsdp"),
            P("fsdp", "tp"),
            P("tp", "fsdp"),
            P(),
            P(),
            P(),
            P(None, None, "tp"),
            P("tp", None),
            P(),
            P(),
            P(None, "tp"),
            P("tp", None),
            P(),
        ),
        out_specs=(
            P(None, ("fsdp", "ctx"), None),
            P(None, ("fsdp", "ctx"), None),
            P(),
            P(None, None, "tp"),
            P("tp", None),
            P(),
            P(),
            P(None, "tp"),
            P("tp", None),
            P(),
        ),
        check_vma=False,
    )
```

profile of v0, /device:TPU:0, one launch (start us, length us, event | category | flops | bytes accessed | tf_op | source)
XLA Modules:
  0.0 2011.9 jit_solution(7236679362293835580)
XLA Ops:
  14.6 104.2 %all-to-all-done = bf16[8,64,2048]{2,1,0:T(8,128)(2,1)S(1)} async-done(((bf16[8,64,2048]{2,1,0:T(8,128)(2,1)}), bf16[8,64,2048]{2,1,0:T(8,128)(2,1)S(1)}, u32[]{:S(2)}, u32[]{:S(2)}) %all-to-all-start) | async-done | bytes 2097184 | tf_op jit(solution)/shard_map/all_to_all | solution.py:78
  124.0 141.4 %all-gather.7.cloned.1.call-done = bf16[3,2048,1024]{2,1,0:T(8,128)(2,1)} async-done(((bf16[3,512,1024]{2,1,0:T(8,128)(2,1)}), bf16[3,2048,1024]{2,1,0:T(8,128)(2,1)}) %all-gather.7.cloned.1.call-update) | async-done | bytes 12582928 | tf_op jit(solution)/shard_map/all_gather | solution.py:92
  297.9 11.0 all-gather.11.cloned.1.call-done
  308.8 37.2 %all-gather.9.cloned.1.call-done = bf16[2,1024,1024]{1,2,0:T(8,128)(2,1)} async-done(((bf16[2,256,1024]{1,2,0:T(8,128)(2,1)}), bf16[2,1024,1024]{1,2,0:T(8,128)(2,1)}) %all-gather.9.cloned.1.call-update) | async-done | bytes 4194320 | tf_op jit(solution)/shard_map/all_gather | solution.py:108
  347.1 26.9 %while.26 = (s32[]{:T(128)}, bf16[2,256,1024]{2,1,0:T(8,128)(2,1)}, f32[2,8,256]{2,1,0:T(8,128)S(1)}, bf16[2,1024,1024]{1,2,0:T(8,128)(2,1)}, pred[2,1024]{1,0:T...) while((s32[]{:T(128)}, bf16[2,256,1024]{2,1,0:T(8,128)(2,1)}, ...), condition=%wide.region_3.4_spmd, body=%wide.region_0.3_spmd.sunk | while | flops 1097070592 | bytes 46208640 | solution.py:133
  374.1 54.2 %all-gather.13.cloned.1.call-done = bf16[1024,2048]{1,0:T(8,128)(2,1)} async-done(((bf16[1024,512]{1,0:T(8,128)(2,1)}), bf16[1024,2048]{1,0:T(8,128)(2,1)}) %all-gather.13.cloned.1.call-update) | async-done | bytes 4194320 | tf_op jit(solution)/shard_map/all_gather | solution.py:93
  439.0 19.6 all-reduce.20
  458.6 88.7 %all-reduce.11.cloned.1.call-done = f32[512,2048]{1,0:T(8,128)} async-done(((f32[512,2048]{1,0:T(8,128)}), f32[512,2048]{1,0:T(8,128)}) %all-reduce.11.cloned.1.call-update) | async-done | bytes 4194320 | tf_op jit(solution)/shard_map/psum | solution.py:137
  559.5 276.1 %all-gather.15.cloned.1.call-done = bf16[2048,4096]{1,0:T(8,128)(2,1)} async-done(((bf16[512,4096]{1,0:T(8,128)(2,1)}), bf16[2048,4096]{1,0:T(8,128)(2,1)}) %all-gather.15.cloned.1.call-update) | async-done | bytes 16777232 | tf_op jit(solution)/shard_map/all_gather | solution.py:146
  835.6 20.4 %multiply_convert_fusion.1 = (bf16[512,4096]{1,0:T(8,128)(2,1)}, f32[512,4096]{1,0:T(8,128)}) fusion(f32[512,4096]{1,0:T(8,128)} %fusion.102, bf16[512,2048]{1,0:T(8,128)(2,1)S(1)} %fusion.31, bf16[2048,4096]{1,0:T(8,128)(2,1)} %all-gather.15.cloned.1.call-done), kind=kOutput, calls=%fused_computation.52 | convolution fusion | flops 8610906112 | bytes 39845888 | tf_op jit(solution)/shard_map/dot_general | solution.py:31
  856.0 266.2 %all-gather.17.cloned.1.call-done = bf16[4096,2048]{1,0:T(8,128)(2,1)} async-done(((bf16[4096,512]{1,0:T(8,128)(2,1)}), bf16[4096,2048]{1,0:T(8,128)(2,1)}) %all-gather.17.cloned.1.call-update) | async-done | bytes 16777232 | tf_op jit(solution)/shard_map/all_gather | solution.py:147
  1122.2 14.9 fusion.103
  1138.7 51.1 %all_to_all.60 = bf16[8,64,2048]{2,1,0:T(8,128)(2,1)S(1)} all-to-all(bf16[8,64,2048]{2,1,0:T(8,128)(2,1)S(1)} %copy-done.39), channel_id=1, replica_groups=mesh['fsdp'=4,'ctx'=4,'tp'=2] {'fsdp'}, dimensions={0} | all-to-all | bytes 4194304 | tf_op jit(solution)/shard_map/all_to_all | solution.py:79
  1194.8 18.4 all-reduce.21
  1213.2 35.7 %all-reduce.13.cloned.1.call-done = f32[512,2048]{1,0:T(8,128)} async-done(((f32[512,2048]{1,0:T(8,128)}), f32[512,2048]{1,0:T(8,128)}) %all-reduce.13.cloned.1.call-update) | async-done | bytes 4194320 | tf_op jit(solution)/shard_map/psum | solution.py:155
  1264.7 22.3 %fusion.22 = bf16[512,4096]{1,0:T(8,128)(2,1)} fusion(f32[512,4096]{1,0:T(8,128)} %get-tuple-element.250, f32[512,4096]{1,0:T(8,128)} %fusion.104, bf16[512,2048]{1,0:T(8,128)(2,1)S(1)} %add_convert_fusion.4, bf16[4096,2048]{1,0:T(8,128)(2,1)} %all-gather.17.cloned.1.call-done), kind=kOutput, calls=%fused_computation.49 | convolution fusion | flops 8642363392 | bytes 39845888 | tf_op jit(solution)/shard_map/dot_general | solution.py:35
  1291.3 14.2 fusion.105
  1305.6 113.3 %all-reduce.17.cloned.1.call-done = (f32[512,2048]{1,0:T(8,128)}, f32[512,128]{1,0:T(8,128)}) async-done(((f32[512,2048]{1,0:T(8,128)}, f32[512,128]{1,0:T(8,128)}), (f32[512,2048]{1,0:T(8,128)}, f32[512,128]{1,0:T(8,128)})) %all-reduce.17.cloned.1.call-update) | async-done | bytes 4456464 | tf_op jit(solution)/shard_map/psum | solution.py:177
  1436.6 91.6 %while.27 = (s32[]{:T(128)}, bf16[2,256,1024]{2,1,0:T(8,128)(2,1)}, bf16[2,1024,1024]{2,1,0:T(8,128)(2,1)}, bf16[2,1024,1024]{2,1,0:T(8,128)(2,1)}, bf16[2,1024,...) while((s32[]{:T(128)}, bf16[2,256,1024]{2,1,0:T(8,128)(2,1)}, ...), condition=%wide.region_20.21_spmd, body=%wide.region_18.20_spmd.sunk | while | flops 2718431232 | bytes 173603120 | solution.py:226
  1545.5 27.4 %reduce-scatter.3.cloned.1.call-done = bf16[2,256,1024]{2,1,0:T(8,128)(2,1)} async-done(((bf16[2,1024,1024]{2,1,0:T(8,128)(2,1)}), bf16[2,256,1024]{2,1,0:T(8,128)(2,1)}) %reduce-scatter.3.cloned.1.call-update) | async-done | bytes 1048592 | tf_op jit(solution)/shard_map/reduce_scatter | solution.py:230
  1574.6 45.4 %reduce-scatter.5.cloned.1.call-done = bf16[2,256,1024]{2,1,0:T(8,128)(2,1)} async-done(((bf16[2,1024,1024]{2,1,0:T(8,128)(2,1)}), bf16[2,256,1024]{2,1,0:T(8,128)(2,1)}) %reduce-scatter.5.cloned.1.call-update) | async-done | bytes 1048592 | tf_op jit(solution)/shard_map/reduce_scatter | solution.py:233
  1649.3 56.2 %all-reduce.19.cloned.1.call-done = (bf16[3,512,128]{2,1,0:T(8,128)(2,1)}, bf16[512,2048]{1,0:T(8,128)(2,1)}) async-done(((bf16[3,512,128]{2,1,0:T(8,128)(2,1)}, bf16[512,2048]{1,0:T(8,128)(2,1)}), (bf16[3,512,128]{2,1,0:T(8,128)(2,1)}, bf16[512,2048]{1,0:T(8,128)(2,1)})) %all-reduce.19.cloned.1.call-update) | async-done | bytes 2490384 | tf_op jit(solution)/shard_map/psum | solution.py:255
  1727.4 67.8 %all-to-all-done.3 = bf16[2,256,2048]{2,0,1:T(2,128)(2,1)S(1)} async-done(((bf16[2,256,2048]{2,0,1:T(2,128)(2,1)}), bf16[2,256,2048]{2,0,1:T(2,128)(2,1)S(1)}, u32[]{:S(2)}, u32[]{:S(2)}) %all-to-all-start.3) | async-done | bytes 2097184 | tf_op jit(solution)/shard_map/all_to_all | solution.py:283
  1797.5 196.2 %all-reduce.15.cloned.1.call-done = (f32[3,2048,128]{1,2,0:T(8,128)}, f32[3,128,1024]{2,1,0:T(8,128)}, f32[1024,128]{1,0:T(8,128)}, f32[128,2048]{1,0:T(8,128)},...) async-done(((f32[3,2048,128]{1,2,0:T(8,128)}, f32[3,128,1024]{2,1,0:T(8,128)}, f32[1024,128]{1,0:T(8,128)}, ...) | async-done | bytes 12582928 | tf_op jit(solution)/shard_map/psum | solution.py:266
  (365 shorter events, 314.1 us)
Async XLA Ops:
  7.2 1185.3 %copy-start = (bf16[4096,128]{1,0:T(8,128)(2,1)S(1)}, bf16[4096,128]{1,0:T(8,128)(2,1)}, u32[]{:S(2)}) copy-start(bf16[4096,128]{1,0:T(8,128)(2,1)} %param.38) | copy-start | bytes 3145732
  7.2 258.2 %all-gather.7.cloned.1.call-start = ((), (), s32[]{:S(2)}) async-start(), calls=%async_computation.6 | async-start | bytes 15728640 | tf_op jit(solution)/shard_map/all_gather | solution.py:92
  7.9 110.8 %all-to-all-start = ((bf16[8,64,2048]{2,1,0:T(8,128)(2,1)}), bf16[8,64,2048]{2,1,0:T(8,128)(2,1)S(1)}, u32[]{:S(2)}, u32[]{:S(2)}) async-start(bf16[8,64,2048]{2,1,0:T(8,128)(2,1)} %param.22), calls=%async_computation | async-start | bytes 4194304 | tf_op jit(solution)/shard_map/all_to_all | solution.py:78
  14.3 294.6 %all-gather.11.cloned.1.call-start = ((), (), s32[]{:S(2)}) async-start(), calls=%async_computation.8 | async-start | bytes 5242880 | tf_op jit(solution)/shard_map/all_gather | solution.py:107
  14.6 1413.4 %copy-start.71 = (f32[2,128]{1,0:T(2,128)}, f32[2,128]{1,0:T(2,128)S(1)}, u32[]{:S(2)}) copy-start(f32[2,128]{1,0:T(2,128)S(1)} %reshape.257) | copy-start | bytes 3076
  121.8 425.5 %copy-start.6 = (bf16[4,2,64,2048]{3,2,0,1:T(8,128)(2,1)}, bf16[4,2,64,2048]{3,2,0,1:T(8,128)(2,1)S(1)}, u32[]{:S(2)}) copy-start(bf16[4,2,64,2048]{3,2,0,1:T(8,128)(2,1)S(1)} %copy.63) | copy-start | bytes 6291460
  124.0 145.9 %copy-start.53 = (bf16[512,128]{1,0:T(8,128)(2,1)}, bf16[512,128]{1,0:T(8,128)(2,1)S(1)}, u32[]{:S(2)}) copy-start(bf16[512,128]{1,0:T(8,128)(2,1)S(1)} %fusion.34) | copy-start | bytes 393220
  274.5 71.5 %all-gather.9.cloned.1.call-start = ((), (), s32[]{:S(2)}) async-start(), calls=%async_computation.7 | async-start | bytes 5242880 | tf_op jit(solution)/shard_map/all_gather | solution.py:108
  285.6 142.6 %all-gather.13.cloned.1.call-start = ((), (), s32[]{:S(2)}) async-start(), calls=%async_computation.9 | async-start | bytes 5242880 | tf_op jit(solution)/shard_map/all_gather | solution.py:93
  286.2 261.1 %all-reduce.11.cloned.1.call-start = ((), (), s32[]{:S(2)}) async-start(), calls=%async_computation.10 | async-start | bytes 8388608 | tf_op jit(solution)/shard_map/psum | solution.py:137
  374.1 61.0 %copy-start.73 = (f32[2,8,256]{2,1,0:T(8,128)}, f32[2,8,256]{2,1,0:T(8,128)S(1)}, u32[]{:S(2)}) copy-start(f32[2,8,256]{2,1,0:T(8,128)S(1)} %get-tuple-element.410) | copy-start | bytes 49156
  435.1 400.5 %all-gather.15.cloned.1.call-start = ((), (), s32[]{:S(2)}) async-start(), calls=%async_computation.11 | async-start | bytes 20971520 | tf_op jit(solution)/shard_map/all_gather | solution.py:146
  435.7 686.5 %all-gather.17.cloned.1.call-start = ((), (), s32[]{:S(2)}) async-start(), calls=%async_computation.12 | async-start | bytes 20971520 | tf_op jit(solution)/shard_map/all_gather | solution.py:147
  436.5 812.5 %all-reduce.13.cloned.1.call-start = ((), (), s32[]{:S(2)}) async-start(), calls=%async_computation.13 | async-start | bytes 8388608 | tf_op jit(solution)/shard_map/psum | solution.py:155
  458.6 91.9 %copy-start.47 = (bf16[512,128]{1,0:T(8,128)(2,1)}, bf16[512,128]{1,0:T(8,128)(2,1)S(1)}, u32[]{:S(2)}) copy-start(bf16[512,128]{1,0:T(8,128)(2,1)S(1)} %all-reduce.20) | copy-start | bytes 393220
  552.5 283.1 %copy-start.14 = (bf16[512,2048]{1,0:T(8,128)(2,1)}, bf16[512,2048]{1,0:T(8,128)(2,1)S(1)}, u32[]{:S(2)}) copy-start(bf16[512,2048]{1,0:T(8,128)(2,1)S(1)} %fusion.31) | copy-start | bytes 6291460
  1137.1 281.8 %all-reduce.17.cloned.1.call-start = ((), (), s32[]{:S(2)}) async-start(), calls=%async_computation.17 | async-start | bytes 8912896 | tf_op jit(solution)/shard_map/psum | solution.py:177
  1305.5 114.4 %copy-start.37 = (bf16[2048,128]{1,0:T(8,128)(2,1)S(1)}, bf16[2048,128]{1,0:T(8,128)(2,1)}, u32[]{:S(2)}) copy-start(bf16[2048,128]{1,0:T(8,128)(2,1)} %param.36) | copy-start | bytes 1572868
  1305.6 267.4 %reduce-scatter.3.cloned.1.call-start = ((), (), s32[]{:S(2)}) async-start(), calls=%async_computation.14 | async-start | bytes 5242880 | tf_op jit(solution)/shard_map/reduce_scatter | solution.py:230
  1528.3 91.8 %reduce-scatter.5.cloned.1.call-start = ((), (), s32[]{:S(2)}) async-start(), calls=%async_computation.15 | async-start | bytes 5242880 | tf_op jit(solution)/shard_map/reduce_scatter | solution.py:233
  1533.3 185.7 %all-to-all-start.1 = ((bf16[2,256,2048]{2,0,1:T(2,128)(2,1)}), bf16[2,256,2048]{2,0,1:T(2,128)(2,1)}, u32[]{:S(2)}, u32[]{:S(2)}) async-start(bf16[2,256,2048]{2,0,1:T(2,128)(2,1)} %copy.68), calls=%async_computation.1 | async-start | bytes 4194304 | tf_op jit(solution)/shard_map/all_to_all | solution.py:282
  1538.0 167.5 %all-reduce.19.cloned.1.call-start = ((), (), s32[]{:S(2)}) async-start(), calls=%async_computation.18 | async-start | bytes 4980736 | tf_op jit(solution)/shard_map/psum | solution.py:255
  1633.7 360.0 %all-reduce.15.cloned.1.call-start = ((), (), s32[]{:S(2)}) async-start(), calls=%async_computation.16 | async-start | bytes 25165824 | tf_op jit(solution)/shard_map/psum | solution.py:266
  1719.0 76.3 %all-to-all-start.3 = ((bf16[2,256,2048]{2,0,1:T(2,128)(2,1)}), bf16[2,256,2048]{2,0,1:T(2,128)(2,1)S(1)}, u32[]{:S(2)}, u32[]{:S(2)}) async-start(bf16[2,256,2048]{2,0,1:T(2,128)(2,1)} %copy.76), calls=%async_computation.5 | async-start | bytes 4194304 | tf_op jit(solution)/shard_map/all_to_all | solution.py:283
  (84 other events, 574.7 us)
Sparse Core Ops, SparseCore 0:
  9.6 255.7 all-gather.6
  274.7 34.1 all-gather.10
  311.0 35.0 all-gather.8
  347.5 80.7 all-gather.12
  435.2 112.0 all-reduce.10
  548.8 286.7 all-gather.14
  837.2 284.9 all-gather.16
  1137.2 111.6 all-reduce.12
  1305.7 113.2 all-reduce.16
  1528.4 44.5 reduce-scatter.2
  1575.5 44.5 reduce-scatter.4
  1633.8 71.6 all-reduce.18
  1712.1 281.6 all-reduce.14
where the time goes:
time: 2020 us; the launch traced here: 2010 us
  waiting for transfers between devices  1520 us (75%)
  matrix products  235 us (12%)
  local copies, waits for them, and re-layouts  108 us (5%)
  blocking collectives  89.1 us (4%)
  other arithmetic  22 us (1%)
    all_gather x1, waiting for transfers between devices, local(): lax.all_gather(w_up, 'fsdp', axis=0, tiled=True)  276 us
    all_gather x1, waiting for transfers between devices, local(): lax.all_gather(w_down, 'fsdp', axis=1, tiled=True)  266 us
    psum x1, waiting for transfers between devices, local(): lax.psum((grad_a_qkv, grad_b_qkv, grad_a_out, grad_b_out, grad_a_up, grad...  196 us
    all_gather x1, waiting for transfers between devices, local(): lax.all_gather(w_qkv, 'fsdp', axis=1, tiled=True)  141 us
    psum x1, waiting for transfers between devices, local(): lax.psum((part_hidden, part_adapt_up), 'tp')  113 us
    all_to_all x1, waiting for transfers between devices, local(): lax.all_to_all(x_in, 'fsdp', split_axis=0, concat_axis=1, tiled=True)  104 us
    psum x1, waiting for transfers between devices, local(): attn_sum, adapt_out_sum = lax.psum((part_out, part_adapt), 'tp')  88.7 us
    dot_general x18, matrix products, product(): return jnp.dot(left_side, right_side, preferred_element_type=jnp.float32)  86.4 us
  transfers between devices with their start and end apart: 16, of which 15 were waited for; matrix products, arithmetic and copies ran while one was open for 7% of the time, Pallas kernels for 0%

commit v1 on v0

v1 whole, which is shorter than its diff:
```python
import math

import jax
import jax.numpy as jnp
from jax import lax
from jax.experimental import pallas as pl
from jax.experimental.pallas import tpu as pltpu
from jax.sharding import PartitionSpec as P

HEAD_DIM = 128
RANK = 16
ADAPTERS = 8
NR = RANK * ADAPTERS
NORM_EPS = 1e-06
GELU_COEF = 0.7978845608028654
SCALE = 1.0 / math.sqrt(HEAD_DIM)
GROUPS = 2
F32 = jnp.float32
BF16 = jnp.bfloat16


def dot(left, right):
    return jnp.dot(left, right, preferred_element_type=F32)


def dot_nt(left, right):
    return lax.dot_general(left, right, (((1,), (1,)), ((), ())), preferred_element_type=F32)


def dot_tn(left, right):
    return lax.dot_general(left, right, (((0,), (0,)), ((), ())), preferred_element_type=F32)


def shift(block, axis, step):
    n = lax.axis_size(axis)
    return lax.ppermute(block, axis, [(i, (i + step) % n) for i in range(n)])


def swap(block, axis, mask):
    n = lax.axis_size(axis)
    return lax.ppermute(block, axis, [(i, i ^ mask) for i in range(n)])


def masks_of(n):
    out = []
    while n > 1:
        n //= 2
        out.append(n)
    return out


def spread(pieces, axis):
    for mask in masks_of(lax.axis_size(axis)):
        pieces = pieces + [swap(piece, axis, mask) for piece in pieces]
    return pieces


def offsets(n):
    out = [0]
    for mask in masks_of(n):
        out = out + [o ^ mask for o in out]
    return out


def fold(pieces, axis):
    for mask in reversed(masks_of(lax.axis_size(axis))):
        half = len(pieces) // 2
        got = [swap(piece, axis, mask) for piece in pieces[half:]]
        pieces = [
            (mine.astype(F32) + other.astype(F32)).astype(BF16)
            for mine, other in zip(pieces[:half], got)
        ]
    return pieces[0]


def both(part):
    low = part.astype(BF16)
    for mask in masks_of(lax.axis_size("tp")):
        total = low.astype(F32) + swap(low, "tp", mask).astype(F32)
        low = total.astype(BF16)
    return total


def attend_kernel(n_piece, q_ref, bias_ref, *refs):
    kv_refs, (out_ref, log_ref) = refs[:n_piece], refs[n_piece:]
    query = q_ref[0]
    loc = query.shape[0]
    scores = []
    for j in range(n_piece):
        bias = bias_ref[0, pl.ds(j * loc, loc), :]
        bias = jnp.concatenate([bias] * (loc // 128), axis=1)
        scores.append(dot_nt(kv_refs[j][0, 0], query) * SCALE + bias)
    top = scores[0].max(axis=0, keepdims=True)
    for s in scores[1:]:
        top = jnp.maximum(top, s.max(axis=0, keepdims=True))
    total = jnp.zeros_like(top)
    mixed = None
    for j in range(n_piece):
        probs = jnp.exp(scores[j] - top)
        total = total + probs.sum(axis=0, keepdims=True)
        term = dot_tn(kv_refs[j][1, 0], probs.astype(BF16))
        mixed = term if mixed is None else mixed + term
    out_ref[0] = (mixed / total).T.astype(BF16)
    log_ref[0, 0] = top + jnp.log(total)


def attend_back_kernel(n_piece, q_ref, bias_ref, g_ref, log_ref, *refs):
    kv_refs, dq_ref, dkv_refs = refs[:n_piece], refs[n_piece], refs[n_piece + 1 :]
    query = q_ref[0]
    grad = g_ref[0]
    log_total = log_ref[0, 0]
    loc = query.shape[0]
    probs, dprobs = [], []
    delta = jnp.zeros_like(log_total)
    for j in range(n_piece):
        bias = bias_ref[0, pl.ds(j * loc, loc), :]
        bias = jnp.concatenate([bias] * (loc // 128), axis=1)
        p = jnp.exp(dot_nt(kv_refs[j][0, 0], query) * SCALE + bias - log_total)
        dp = dot_nt(kv_refs[j][1, 0], grad)
        dkv_refs[j][1, 0] = dot(p.astype(BF16), grad).astype(BF16)
        delta = delta + (p * dp).sum(axis=0, keepdims=True)
        probs.append(p)
        dprobs.append(dp)
    dq = None
    for j in range(n_piece):
        ds = (probs[j] * (dprobs[j] - delta)).astype(BF16)
        dkv_refs[j][0, 0] = (dot(ds, query) * SCALE).astype(BF16)
        term = dot_tn(kv_refs[j][0, 0], ds)
        dq = term if dq is None else dq + term
    dq_ref[0] = (dq * SCALE).T.astype(BF16)


def attend_specs(n_seq, loc, n_piece):
    row = pl.BlockSpec((1, loc, HEAD_DIM), lambda s, h: (s, 0, h))
    bias = pl.BlockSpec((1, n_piece * loc, 128), lambda s, h: (s, 0, 0))
    pair = pl.BlockSpec((2, 1, loc, HEAD_DIM), lambda s, h: (0, s, 0, h))
    log = pl.BlockSpec((1, 1, 1, loc), lambda s, h: (s, h, 0, 0))
    return row, bias, pair, log


def attend(query, kv, bias):
    n_seq, loc, width = query.shape
    n_piece, heads = len(kv), width // HEAD_DIM
    row, bias_spec, pair, log = attend_specs(n_seq, loc, n_piece)
    return pl.pallas_call(
        lambda *refs: attend_kernel(n_piece, *refs),
        grid=(n_seq, heads),
        in_specs=[row, bias_spec] + [pair] * n_piece,
        out_specs=[row, log],
        out_shape=[
            jax.ShapeDtypeStruct(query.shape, BF16),
            jax.ShapeDtypeStruct((n_seq, heads, 1, loc), F32),
        ],
        compiler_params=pltpu.CompilerParams(vmem_limit_bytes=32 << 20),
        cost_estimate=pl.CostEstimate(
            flops=n_seq * heads * 4 * loc * loc * n_piece * HEAD_DIM * 4,
            bytes_accessed=2 * n_seq * loc * width * (2 + 2 * n_piece),
            transcendentals=n_seq * heads * loc * loc * n_piece,
        ),
    )(query, bias, *kv)


def attend_back(query, kv, bias, grad, log_total):
    n_seq, loc, width = query.shape
    n_piece, heads = len(kv), width // HEAD_DIM
    row, bias_spec, pair, log = attend_specs(n_seq, loc, n_piece)
    out = pl.pallas_call(
        lambda *refs: attend_back_kernel(n_piece, *refs),
        grid=(n_seq, heads),
        in_specs=[row, bias_spec, row, log] + [pair] * n_piece,
        out_specs=[row] + [pair] * n_piece,
        out_shape=[jax.ShapeDtypeStruct(query.shape, BF16)]
        + [jax.ShapeDtypeStruct(kv[0].shape, BF16)] * n_piece,
        compiler_params=pltpu.CompilerParams(vmem_limit_bytes=40 << 20),
        cost_estimate=pl.CostEstimate(
            flops=n_seq * heads * 10 * loc * loc * n_piece * HEAD_DIM * 4,
            bytes_accessed=2 * n_seq * loc * width * (3 + 4 * n_piece),
            transcendentals=n_seq * heads * loc * loc * n_piece,
        ),
    )(query, bias, grad, log_total, *kv)
    return out[0], list(out[1:])


def norm_parts(values):
    center = values - jnp.mean(values, axis=-1, keepdims=True)
    rstd = lax.rsqrt(jnp.mean(center * center, axis=-1, keepdims=True) + NORM_EPS)
    return center * rstd, rstd


def norm_back(hat, rstd, dhat):
    first = jnp.mean(dhat, axis=-1, keepdims=True)
    second = jnp.mean(dhat * hat, axis=-1, keepdims=True)
    return rstd * (dhat - first - hat * second)


def gelu_both(pre):
    square = pre * pre
    bent = jnp.tanh(GELU_COEF * (pre + 0.044715 * square * pre))
    out = 0.5 * pre * (1.0 + bent)
    slope = 0.5 * (1.0 + bent) + 0.5 * pre * (1.0 - bent * bent) * GELU_COEF * (
        1.0 + 3.0 * 0.044715 * square
    )
    return out.astype(BF16), slope.astype(BF16)


def local(
    x_in,
    cotangent,
    lengths,
    adapter_ids,
    w_qkv,
    w_out,
    w_up,
    w_down,
    ln_gain,
    ln_bias,
    a_qkv,
    b_qkv,
    a_out,
    b_out,
    a_up,
    b_up,
    a_down,
    b_down,
):
    n_ctx, n_fsdp = lax.axis_size("ctx"), lax.axis_size("fsdp")
    z, ct = lax.axis_index("fsdp"), lax.axis_index("ctx")
    seqs, piece, width = x_in.shape
    per = seqs // n_fsdp
    loc = n_fsdp * piece
    heads_width = w_qkv.shape[2]
    n_group = GROUPS if per % GROUPS == 0 else 1
    g_per = per // n_group
    g_rows = g_per * loc

    def take(array, start, size, axis=0):
        return lax.dynamic_slice_in_dim(array, start, size, axis)

    def put(array, block, *starts):
        return lax.dynamic_update_slice(array, block, starts)

    def deal(array, group):
        out = []
        for step in range(n_fsdp):
            to = lax.rem(z + step, n_fsdp)
            block = take(array, to * per + group * g_per, g_per)
            out.append(block if step == 0 else shift(block, "fsdp", step))
        return jnp.concatenate(out, axis=1)

    def undeal(rows, group_out):
        rows = rows.reshape(g_per, n_fsdp, piece, width)
        out = []
        for step in range(n_fsdp):
            block = rows[:, step]
            out.append(block if step == 0 else shift(block, "fsdp", -step))
        return out

    def gathered(shard, z_axis, full):
        size = shard.shape[0] // n_ctx
        mine = take(shard, ct * size, size)
        got = [shift(mine, "fsdp", step) for step in range(1, n_fsdp)]
        pieces = spread([jnp.stack(got)], "ctx")
        z_size = shard.shape[z_axis]
        full = put(full, shard, *((z * z_size, 0) if z_axis == 0 else (0, z * z_size)))
        for offset, block in zip(offsets(n_ctx), pieces):
            row = (ct ^ offset) * size
            for step in range(1, n_fsdp):
                start = lax.rem(z - step + n_fsdp, n_fsdp) * z_size
                at = (start + row, 0) if z_axis == 0 else (row, start)
                full = put(full, block[step - 1], *at)
        return full

    zero = jnp.zeros((), BF16)
    bands = [jnp.pad(b_qkv[j], ((0, 0), (j * heads_width, (2 - j) * heads_width))) for j in range(3)]
    qkv_base = jnp.pad(jnp.concatenate(bands, axis=0), ((width, 0), (0, 0)))
    qkv_shard = w_qkv.transpose(1, 0, 2).reshape(w_qkv.shape[1], 3 * heads_width)
    qkv_x = gathered(qkv_shard, 0, qkv_base)
    out_x = gathered(w_out, 1, jnp.pad(a_out, ((0, 0), (width, 0))))
    up_x = gathered(w_up, 0, jnp.pad(b_up, ((width, 0), (0, 0))))
    down_x = gathered(w_down, 1, jnp.pad(a_down, ((0, 0), (width, 0))))
    a_in = a_qkv.transpose(1, 0, 2).reshape(width, 3 * NR)

    my_lengths = take(lengths, z * per, per)
    my_ids = take(adapter_ids, z * per, per)
    picked = (my_ids[:, None] == jnp.arange(NR)[None, :] // RANK).astype(F32)
    steps = lax.rem(z - jnp.arange(n_fsdp) + n_fsdp, n_fsdp)
    ctx_of = ct ^ jnp.array(offsets(n_ctx))
    key_pos = (
        (steps[None, :, None] * n_ctx + ctx_of[:, None, None]) * piece
        + jnp.arange(piece)[None, None, :]
    ).reshape(-1)
    bias_all = jnp.where(key_pos[None, :] < my_lengths[:, None], 0.0, -1e30).astype(F32)
    bias_all = jnp.broadcast_to(bias_all[:, :, None], bias_all.shape + (128,))

    acts, ins = [], []
    early, late = [], []
    for group in range(n_group):
        pick = jnp.repeat(take(picked, group * g_per, g_per), loc, axis=0)
        pick3 = jnp.concatenate([pick] * 3, axis=1)
        bias = bias_all[group * g_per : (group + 1) * g_per]
        x_rows = deal(x_in, group).reshape(g_rows, width)
        grad_out = deal(cotangent, group).reshape(g_rows, width)

        def compact(codes, values, j=0):
            out = []
            for n in range(g_per):
                first = my_ids[group * g_per + n] * RANK + j * NR
                rows = slice(n * loc, (n + 1) * loc)
                out.append(dot_tn(take(codes[rows], first, RANK, 1), values[rows]).astype(BF16))
            return jnp.concatenate(out, axis=0)

        adapt_in = (dot(x_rows, a_in) * pick3).astype(BF16)
        proj = dot(jnp.concatenate([x_rows, adapt_in], axis=1), qkv_x).astype(BF16)
        query = proj[:, :heads_width].reshape(g_per, loc, heads_width)
        pair = jnp.stack([proj[:, heads_width : 2 * heads_width], proj[:, 2 * heads_width :]])
        kv = spread([pair.reshape(2, g_per, loc, heads_width)], "ctx")
        context, log_total = attend(query, kv, bias)
        ctx_rows = context.reshape(g_rows, heads_width)
        summed = both(dot(ctx_rows, out_x))
        adapt_out = (summed[:, width:] * pick).astype(BF16)
        hat1, rstd1 = norm_parts(x_rows.astype(F32) + summed[:, :width] + dot(adapt_out, b_out))
        hidden = hat1 * ln_gain[0] + ln_bias[0]
        hidden_low = hidden.astype(BF16)
        adapt_up = (dot(hidden_low, a_up) * pick).astype(BF16)
        gelu_out, slope = gelu_both(dot(jnp.concatenate([hidden_low, adapt_up], axis=1), up_x))
        summed = both(dot(gelu_out, down_x))
        adapt_down = (summed[:, width:] * pick).astype(BF16)
        hat2, rstd2 = norm_parts(hidden + summed[:, :width] + dot(adapt_down, b_down))
        layer_out = (hat2 * ln_gain[1] + ln_bias[1]).astype(BF16)
        acts.append(undeal(layer_out, group))

        dy2 = norm_back(hat2, rstd2, grad_out.astype(F32) * ln_gain[1])
        d_down = dy2.astype(BF16)
        dadapt_down = (dot_nt(d_down, b_down) * pick).astype(BF16)
        d_gelu = dot_nt(jnp.concatenate([d_down, dadapt_down], axis=1), down_x)
        d_pre = (d_gelu * slope.astype(F32)).astype(BF16)
        summed = both(dot_nt(d_pre, up_x))
        dadapt_up = (summed[:, width:] * pick).astype(BF16)
        dh1 = dy2 + summed[:, :width] + dot_nt(dadapt_up, a_up)
        dy1 = norm_back(hat1, rstd1, dh1 * ln_gain[0])
        d_attn = dy1.astype(BF16)
        dadapt_out = (dot_nt(d_attn, b_out) * pick).astype(BF16)
        d_context = dot_nt(jnp.concatenate([d_attn, dadapt_out], axis=1), out_x).astype(BF16)
        early.append(
            jnp.concatenate(
                [
                    compact(adapt_down, d_down),
                    compact(dadapt_down, gelu_out),
                    compact(adapt_up, d_pre),
                    compact(dadapt_up, hidden_low),
                    compact(adapt_out, d_attn),
                    compact(dadapt_out, ctx_rows),
                ],
                axis=1,
            )
        )
        d_query, d_kv = attend_back(
            query, kv, bias, d_context.reshape(g_per, loc, heads_width), log_total
        )
        d_pair = fold(d_kv, "ctx").reshape(2, g_rows, heads_width)
        d_proj = jnp.concatenate([d_query.reshape(g_rows, heads_width), d_pair[0], d_pair[1]], axis=1)
        summed = both(dot_nt(d_proj, qkv_x))
        dadapt_in = (summed[:, width:] * pick3).astype(BF16)
        d_x = (dy1 + summed[:, :width] + dot_nt(dadapt_in, a_in)).astype(BF16)
        ins.append(undeal(d_x, group))
        late.append(
            jnp.concatenate(
                [
                    compact(adapt_in, d_proj[:, j * heads_width : (j + 1) * heads_width], j)
                    for j in range(3)
                ]
                + [compact(dadapt_in, x_rows, j) for j in range(3)],
                axis=1,
            )
        )

    def assemble(parts):
        full = jnp.zeros((seqs, piece, width), BF16)
        for group, blocks in enumerate(parts):
            for step, block in enumerate(blocks):
                owner = lax.rem(z + step, n_fsdp)
                full = put(full, block, owner * per + group * g_per, 0, 0)
        return full

    codes = (adapter_ids[:, None] * RANK + jnp.arange(RANK)[None, :]).reshape(-1)
    chosen = (codes[:, None] == jnp.arange(NR)[None, :]).astype(BF16)

    def everywhere(parts):
        mine = jnp.concatenate(parts, axis=0)
        rows, columns = mine.shape
        size = columns // n_ctx
        blocks = [take(mine, (ct ^ offset) * size, size, 1) for offset in offsets(n_ctx)]
        own = fold(blocks, "ctx")
        got = jnp.stack([own] + [shift(own, "fsdp", step) for step in range(1, n_fsdp)])
        full = jnp.zeros((n_fsdp * rows, columns), BF16)
        for offset, block in zip(offsets(n_ctx), spread([got], "ctx")):
            for step in range(n_fsdp):
                owner = lax.rem(z - step + n_fsdp, n_fsdp)
                full = put(full, block[step], owner * rows, (ct ^ offset) * size)
        return full

    def split(full, sizes):
        out, at = [], 0
        for size in sizes:
            out.append(full[:, at : at + size])
            at += size
        return out

    units = w_up.shape[1]
    e = split(everywhere(early), [width, units, units, width, width, heads_width])
    l = split(everywhere(late), [heads_width] * 3 + [width] * 3)
    return (
        assemble(acts),
        assemble(ins),
        jnp.stack([dot_tn(l[3 + j], chosen) for j in range(3)]),
        jnp.stack([dot_tn(chosen, l[j]) for j in range(3)]),
        dot_tn(e[5], chosen),
        dot_tn(chosen, e[4]),
        dot_tn(e[3], chosen),
        dot_tn(chosen, e[2]),
        dot_tn(e[1], chosen),
        dot_tn(chosen, e[0]),
    )


def solution(mesh):
    rows = P(None, ("fsdp", "ctx"), None)
    return jax.shard_map(
        local,
        mesh=mesh,
        in_specs=(
            rows,
            rows,
            P(),
            P(),
            P(None, "fsdp", "tp"),
            P("tp", "fsdp"),
            P("fsdp", "tp"),
            P("tp", "fsdp"),
            P(),
            P(),
            P(),
            P(None, None, "tp"),
            P("tp", None),
            P(),
            P(),
            P(None, "tp"),
            P("tp", None),
            P(),
        ),
        out_specs=(
            rows,
            rows,
            P(),
            P(None, None, "tp"),
            P("tp", None),
            P(),
            P(),
            P(None, "tp"),
            P("tp", None),
            P(),
        ),
        check_vma=False,
    )
```

time: 2020 us -> 1210 us (0.60)
  waiting for transfers between devices: 1520 us -> 473 us
  local copies, waits for them, and re-layouts: 108 us -> 262 us
  starting transfers between devices: 17 us -> 170 us
  blocking collectives: 89.1 us -> 0 us
  Pallas kernels: 0 us -> 43.3 us
  matrix products: 235 us -> 192 us
  other arithmetic: 22 us -> 49.3 us
    all_gather x6 -> x0, waiting for transfers between devices: 786 us -> none  [the longest x1 276 us: local(): lax.all_gather(w_up, 'fsdp', axis=0, tiled=True)]
    psum x5 -> x0, waiting for transfers between devices: 490 us -> none  [the longest x1 196 us: local(): lax.psum((grad_a_qkv, grad_b_qkv, grad_a_out, grad_b_out, grad_a_up, grad...]
    ppermute x0 -> x86, waiting for transfers between devices: none -> 473 us  [the longest x44 259 us: swap(): return lax.ppermute(block, axis, [(i, i ^ mask) for i in range(n)])]
    all_to_all x3 -> x0, waiting for transfers between devices: 172 us -> none  [the longest x1 104 us: local(): lax.all_to_all(x_in, 'fsdp', split_axis=0, concat_axis=1, tiled=True)]
    ppermute x0 -> x86, starting transfers between devices: none -> 170 us  [the longest x42 150 us: shift(): return lax.ppermute(block, axis, [(i, (i + step) % n) for i in range(n)])]
    dynamic_update_slice x14 -> x98, local copies, waits for them, and re-layouts: 35.4 us -> 161 us  [put(): return lax.dynamic_update_slice(array, block, starts)]
    reduce_scatter x2 -> x0, waiting for transfers between devices: 72.9 us -> none  [the longest x1 45.4 us: local(): lax.psum_scatter(grad_values_all.astype(jnp.bfloat16), 'ctx', scatter_dim...]
    all_to_all x1 -> x0, blocking collectives: 51.1 us -> none  [local(): lax.all_to_all(cotangent, 'fsdp', split_axis=0, concat_axis=1, tiled=True)]
  transfers between devices with their start and end apart: 16 -> 86, of which waited for: 15 -> 29; matrix products, arithmetic and copies ran while one was open for 7% -> 37% of each run, Pallas kernels for 0% -> 4%
where the time goes in v1:
time: 1210 us; the launch traced here: 1200 us
  waiting for transfers between devices  473 us (39%)
  local copies, waits for them, and re-layouts  262 us (22%)
  matrix products  192 us (16%)
  starting transfers between devices  170 us (14%)
  other arithmetic  49.3 us (4%)
  Pallas kernels  43.3 us (4%)
    ppermute x44, waiting for transfers between devices, swap(): return lax.ppermute(block, axis, [(i, i ^ mask) for i in range(n)])  259 us
    ppermute x42, waiting for transfers between devices, shift(): return lax.ppermute(block, axis, [(i, (i + step) % n) for i in range(n)])  214 us
    dynamic_update_slice x98, local copies, waits for them, and re-layouts, put(): return lax.dynamic_update_slice(array, block, starts)  161 us
    ppermute x42, starting transfers between devices, shift(): return lax.ppermute(block, axis, [(i, (i + step) % n) for i in range(n)])  150 us
    dot_general x16, matrix products, dot_nt(): lax.dot_general(left, right, (((1,), (1,)), ((), ())), preferred_element_...  95.1 us
    dot_general x16, matrix products, dot(): return jnp.dot(left, right, preferred_element_type=F32)  62.2 us
    dot_general x36, matrix products, dot_tn(): lax.dot_general(left, right, (((0,), (0,)), ((), ())), preferred_element_...  34.7 us
    pallas_call x2, Pallas kernels, attend_back(): pl.pallas_call(lambda *refs: attend_back_kernel(n_piece, *refs), grid=(n_...  26.2 us
  transfers between devices with their start and end apart: 86, of which 29 were waited for; matrix products, arithmetic and copies ran while one was open for 37% of the time, Pallas kernels for 4%

profile of v1, /device:TPU:0, one launch (start us, length us, event | category | flops | bytes accessed | tf_op | source)
XLA Modules:
  0.0 1195.1 jit_solution(7876476060801333525)
XLA Ops:
  101.2 33.5 %collective-permute-done.35 = bf16[1,64,2048]{2,1,0:T(8,128)(2,1)S(1)} collective-permute-done((bf16[1,64,2048]{2,1,0:T(8,128)(2,1)S(1)}, bf16[1,64,2048]{2,1,0:T(8,128)(2,1)S(1)}, u32[]{:S(2)}, u32[]{:S(2)}) %collective-permute-start.35) | collective-permute-done | bytes 262176 | tf_op jit(solution)/shard_map/ppermute | solution.py:36
  140.5 43.8 %collective-permute-start.25 = (bf16[1024,512]{1,0:T(8,128)(2,1)}, bf16[1024,512]{1,0:T(8,128)(2,1)}, u32[]{:S(2)}, u32[]{:S(2)}) collective-permute-start(bf16[1024,512]{1,0:T(8,128)(2,1)} %constant_dynamic-slice_fusion.12), channel_id=1, source_target_pairs={{0,8},{8,16},{16,24},{24,0},{1,9},{9,17},{17,25},{25,1},{2,10},{10... | collective-permute-start | bytes 3145736 | tf_op jit(solution)/shard_map/ppermute | solution.py:36
  208.8 32.3 %collective-permute-start.20 = (bf16[128,4096]{1,0:T(8,128)(2,1)}, bf16[128,4096]{1,0:T(8,128)(2,1)}, u32[]{:S(2)}, u32[]{:S(2)}) collective-permute-start(bf16[128,4096]{1,0:T(8,128)(2,1)} %constant_dynamic-slice_fusion.13), channel_id=1, source_target_pairs={{0,16},{8,24},{16,0},{24,8},{1,17},{9,25},{17,1},{25,9},{2,18},{10... | collective-permute-start | bytes 3145736 | tf_op jit(solution)/shard_map/ppermute | solution.py:36
  249.4 40.6 %collective-permute-done.19 = bf16[128,4096]{1,0:T(8,128)(2,1)} collective-permute-done((bf16[128,4096]{1,0:T(8,128)(2,1)}, bf16[128,4096]{1,0:T(8,128)(2,1)}, u32[]{:S(2)}, u32[]{:S(2)}) %collective-permute-start.19) | collective-permute-done | bytes 1048608 | tf_op jit(solution)/shard_map/ppermute | solution.py:36
  293.8 60.1 %collective-permute-done.20 = bf16[128,4096]{1,0:T(8,128)(2,1)} collective-permute-done((bf16[128,4096]{1,0:T(8,128)(2,1)}, bf16[128,4096]{1,0:T(8,128)(2,1)}, u32[]{:S(2)}, u32[]{:S(2)}) %collective-permute-start.20) | collective-permute-done | bytes 1048608 | tf_op jit(solution)/shard_map/ppermute | solution.py:36
  361.4 20.4 %collective-permute-done.21 = bf16[128,4096]{1,0:T(8,128)(2,1)S(1)} collective-permute-done((bf16[128,4096]{1,0:T(8,128)(2,1)S(1)}, bf16[128,4096]{1,0:T(8,128)(2,1)S(1)}, u32[]{:S(2)}, u32[]{:S(2)}) %collective-permute-start.21) | collective-permute-done | bytes 1048608 | tf_op jit(solution)/shard_map/ppermute | solution.py:36
  400.8 11.7 dynamic_update_slice.341
  412.5 11.7 dynamic_update_slice.342
  458.2 41.5 %collective-permute-done.28 = bf16[3,1024,512]{2,1,0:T(8,128)(2,1)} collective-permute-done((bf16[3,1024,512]{2,1,0:T(8,128)(2,1)}, bf16[3,1024,512]{2,1,0:T(8,128)(2,1)}, u32[]{:S(2)}, u32[]{:S(2)}) %collective-permute-start.28) | collective-permute-done | bytes 3145760 | tf_op jit(solution)/shard_map/ppermute | solution.py:41
  509.8 56.5 %collective-permute-done.22 = bf16[3,128,4096]{2,1,0:T(8,128)(2,1)} collective-permute-done((bf16[3,128,4096]{2,1,0:T(8,128)(2,1)}, bf16[3,128,4096]{2,1,0:T(8,128)(2,1)}, u32[]{:S(2)}, u32[]{:S(2)}) %collective-permute-start.22) | collective-permute-done | bytes 3145760 | tf_op jit(solution)/shard_map/ppermute | solution.py:41
  615.3 15.1 %collective-permute-done.9.refs_3_.refs_5_ = bf16[2,1,256,1024]{3,2,1,0:T(8,128)(2,1)S(1)} collective-permute-done((bf16[2,1,256,1024]{3,2,1,0:T(8,128)(2,1)S(1)}, bf16[2,1,256,1024]{3,2,1,0:T(8,128)(2,1)S(1)}, u32[]{:S(2)}, u32[]{:S(2)}) %collective-permute-start.9) | collective-permute-done | bytes 1048608 | tf_op jit(solution)/shard_map/ppermute | solution.py:41
  636.0 18.6 %collective-permute-done.38.refs_3_.refs_5_ = bf16[2,1,256,1024]{3,2,1,0:T(8,128)(2,1)S(1)} collective-permute-done((bf16[2,1,256,1024]{3,2,1,0:T(8,128)(2,1)S(1)}, bf16[2,1,256,1024]{3,2,1,0:T(8,128)(2,1)S(1)}, u32[]{:S(2)}, u32[]{:S(2)}) %collective-permute-start.38) | collective-permute-done | bytes 1048608 | tf_op jit(solution)/shard_map/ppermute | solution.py:41
  693.5 22.2 %collective-permute-done.41 = bf16[256,2176]{1,0:T(8,128)(2,1)S(1)} collective-permute-done((bf16[256,2176]{1,0:T(8,128)(2,1)S(1)}, bf16[256,2176]{1,0:T(8,128)(2,1)S(1)}, u32[]{:S(2)}, u32[]{:S(2)}) %collective-permute-start.41) | collective-permute-done | bytes 1114144 | tf_op jit(solution)/shard_map/ppermute | solution.py:41
  738.0 11.6 convolution_convert_fusion.10
  763.7 13.7 %collective-permute-done.31 = bf16[256,2176]{1,0:T(8,128)(2,1)} collective-permute-done((bf16[256,2176]{1,0:T(8,128)(2,1)}, bf16[256,2176]{1,0:T(8,128)(2,1)}, u32[]{:S(2)}, u32[]{:S(2)}) %collective-permute-start.31) | collective-permute-done | bytes 1114144 | tf_op jit(solution)/shard_map/ppermute | solution.py:41
  782.4 17.5 %collective-permute-done.42 = bf16[256,2176]{1,0:T(8,128)(2,1)S(1)} collective-permute-done((bf16[256,2176]{1,0:T(8,128)(2,1)S(1)}, bf16[256,2176]{1,0:T(8,128)(2,1)S(1)}, u32[]{:S(2)}, u32[]{:S(2)}) %collective-permute-start.42) | collective-permute-done | bytes 1114144 | tf_op jit(solution)/shard_map/ppermute | solution.py:41
  831.5 19.0 %convolution_convert_fusion.7 = bf16[256,2176]{1,0:T(8,128)(2,1)} fusion(bf16[256,4096]{1,0:T(8,128)(2,1)} %fusion, bf16[2176,4096]{1,0:T(8,128)(2,1)} %fusion.121), kind=kOutput, calls=%fused_computation.33 | convolution fusion | flops 4563959808 | bytes 21037056 | tf_op jit(solution)/shard_map/dot_general | solution.py:27
  854.1 11.8 fusion.1
  865.9 19.0 %convolution_convert_fusion.5 = bf16[256,2176]{1,0:T(8,128)(2,1)} fusion(bf16[256,4096]{1,0:T(8,128)(2,1)} %fusion.1, bf16[2176,4096]{1,0:T(8,128)(2,1)} %fusion.121), kind=kOutput, calls=%fused_computation.31 | convolution fusion | flops 4563959808 | bytes 21037056 | tf_op jit(solution)/shard_map/dot_general | solution.py:27
  896.2 13.1 %collective-permute-done.60 = bf16[256,2176]{1,0:T(8,128)(2,1)S(1)} collective-permute-done((bf16[256,2176]{1,0:T(8,128)(2,1)}, bf16[256,2176]{1,0:T(8,128)(2,1)S(1)}, u32[]{:S(2)}, u32[]{:S(2)}) %collective-permute-start.60) | collective-permute-done | bytes 1114144 | tf_op jit(solution)/shard_map/ppermute | solution.py:41
  935.0 12.9 %shard_map.260 = (bf16[1,256,1024]{2,1,0:T(8,128)(2,1)S(1)}, bf16[2,1,256,1024]{3,2,1,0:T(8,128)(2,1)S(1)}, bf16[2,1,256,1024]{3,2,1,0:T(8,128)(2,1)S(1)}, bf16[...) custom-call(bf16[1,256,1024]{2,1,0:T(8,128)(2,1)S(1)} %copy-done.14, f32[1,1024,128]{2,1,0:T(8,128)S(1)} %copy-done.6, ...), custom_call_target="tpu_custom_call" | custom-call | flops 10737418240 | bytes 9961472 | tf_op jit(solution)/shard_map/pallas_call | solution.py:167
  947.9 13.3 %shard_map.261 = (bf16[1,256,1024]{2,1,0:T(8,128)(2,1)S(1)}, bf16[2,1,256,1024]{3,2,1,0:T(8,128)(2,1)S(1)}, bf16[2,1,256,1024]{3,2,1,0:T(8,128)(2,1)S(1)}, bf16[...) custom-call(bf16[1,256,1024]{2,1,0:T(8,128)(2,1)S(1)} %copy-done.12, f32[1,1024,128]{2,1,0:T(8,128)S(1)} %copy-done.8, ...), custom_call_target="tpu_custom_call" | custom-call | flops 10737418240 | bytes 9961472 | tf_op jit(solution)/shard_map/pallas_call | solution.py:167
  1029.6 17.9 %collective-permute-done.52 = bf16[2,1,256,1024]{3,2,1,0:T(8,128)(2,1)S(1)} collective-permute-done((bf16[2,1,256,1024]{3,2,1,0:T(8,128)(2,1)S(1)}, bf16[2,1,256,1024]{3,2,1,0:T(8,128)(2,1)S(1)}, u32[]{:S(2)}, u32[]{:S(2)}) %collective-permute-start.52) | collective-permute-done | bytes 1048608 | tf_op jit(solution)/shard_map/ppermute | solution.py:41
  1128.6 20.2 %collective-permute-done.55 = bf16[1,64,2048]{2,1,0:T(8,128)(2,1)S(1)} collective-permute-done((bf16[1,64,2048]{2,1,0:T(8,128)(2,1)S(1)}, bf16[1,64,2048]{2,1,0:T(8,128)(2,1)S(1)}, u32[]{:S(2)}, u32[]{:S(2)}) %collective-permute-start.55) | collective-permute-done | bytes 262176 | tf_op jit(solution)/shard_map/ppermute | solution.py:36
  (795 shorter events, 611.9 us)
Async XLA Ops:
  2.4 83.0 %collective-permute-start.12 = (bf16[256,512]{1,0:T(8,128)(2,1)}, bf16[256,512]{1,0:T(8,128)(2,1)}, u32[]{:S(2)}, u32[]{:S(2)}) collective-permute-start(bf16[256,512]{1,0:T(8,128)(2,1)} %constant_dynamic-slice_fusion.14), channel_id=1, source_target_pairs={{0,8},{8,16},{16,24},{24,0},{1,9},{9,17},{17,25},{25,1},{2,10},{10... | collective-permute-start | bytes 786440 | tf_op jit(solution)/shard_map/ppermute | solution.py:36
  8.2 69.1 %collective-permute-start.2 = (bf16[1,64,2048]{2,1,0:T(8,128)(2,1)}, bf16[1,64,2048]{2,1,0:T(8,128)(2,1)}, u32[]{:S(2)}, u32[]{:S(2)}) collective-permute-start(bf16[1,64,2048]{2,1,0:T(8,128)(2,1)} %get-tuple-element.85), channel_id=1, source_target_pairs={{0,24},{8,0},{16,8},{24,16},{1,25},{9,1},{17,9},{25,17},{2,26},{10... | collective-permute-start | bytes 786440 | tf_op jit(solution)/shard_map/ppermute | solution.py:36
  10.3 71.0 %collective-permute-start.1 = (bf16[1,64,2048]{2,1,0:T(8,128)(2,1)}, bf16[1,64,2048]{2,1,0:T(8,128)(2,1)}, u32[]{:S(2)}, u32[]{:S(2)}) collective-permute-start(bf16[1,64,2048]{2,1,0:T(8,128)(2,1)} %get-tuple-element.86), channel_id=1, source_target_pairs={{0,16},{8,24},{16,0},{24,8},{1,17},{9,25},{17,1},{25,9},{2,18},{10... | collective-permute-start | bytes 786440 | tf_op jit(solution)/shard_map/ppermute | solution.py:36
  11.3 72.9 %collective-permute-start = (bf16[1,64,2048]{2,1,0:T(8,128)(2,1)}, bf16[1,64,2048]{2,1,0:T(8,128)(2,1)}, u32[]{:S(2)}, u32[]{:S(2)}) collective-permute-start(bf16[1,64,2048]{2,1,0:T(8,128)(2,1)} %get-tuple-element.87), channel_id=1, source_target_pairs={{0,8},{8,16},{16,24},{24,0},{1,9},{9,17},{17,25},{25,1},{2,10},{10... | collective-permute-start | bytes 786440 | tf_op jit(solution)/shard_map/ppermute | solution.py:36
  12.9 74.6 %collective-permute-start.37 = (bf16[1,64,2048]{2,1,0:T(8,128)(2,1)}, bf16[1,64,2048]{2,1,0:T(8,128)(2,1)}, u32[]{:S(2)}, u32[]{:S(2)}) collective-permute-start(bf16[1,64,2048]{2,1,0:T(8,128)(2,1)} %get-tuple-element.89), channel_id=1, source_target_pairs={{0,24},{8,0},{16,8},{24,16},{1,25},{9,1},{17,9},{25,17},{2,26},{10... | collective-permute-start | bytes 786440 | tf_op jit(solution)/shard_map/ppermute | solution.py:36
  84.2 104.6 %collective-permute-start.14 = (bf16[256,512]{1,0:T(8,128)(2,1)}, bf16[256,512]{1,0:T(8,128)(2,1)S(1)}, u32[]{:S(2)}, u32[]{:S(2)}) collective-permute-start(bf16[256,512]{1,0:T(8,128)(2,1)} %constant_dynamic-slice_fusion.14), channel_id=1, source_target_pairs={{0,24},{8,0},{16,8},{24,16},{1,25},{9,1},{17,9},{25,17},{2,26},{10... | collective-permute-start | bytes 786440 | tf_op jit(solution)/shard_map/ppermute | solution.py:36
  85.4 114.5 %collective-permute-start.3 = (bf16[128,3072]{0,1:T(8,128)(2,1)}, bf16[128,3072]{0,1:T(8,128)(2,1)}, u32[]{:S(2)}, u32[]{:S(2)}) collective-permute-start(bf16[128,3072]{0,1:T(8,128)(2,1)} %constant_dynamic-slice_fusion.15), channel_id=1, source_target_pairs={{0,8},{8,16},{16,24},{24,0},{1,9},{9,17},{17,25},{25,1},{2,10},{10... | collective-permute-start | bytes 2359304 | tf_op jit(solution)/shard_map/ppermute | solution.py:36
  87.5 115.5 %collective-permute-start.4 = (bf16[128,3072]{0,1:T(8,128)(2,1)}, bf16[128,3072]{0,1:T(8,128)(2,1)}, u32[]{:S(2)}, u32[]{:S(2)}) collective-permute-start(bf16[128,3072]{0,1:T(8,128)(2,1)} %constant_dynamic-slice_fusion.15), channel_id=1, source_target_pairs={{0,16},{8,24},{16,0},{24,8},{1,17},{9,25},{17,1},{25,9},{2,18},{10... | collective-permute-start | bytes 2359304 | tf_op jit(solution)/shard_map/ppermute | solution.py:36
  134.7 74.1 %collective-permute-start.5 = (bf16[128,3072]{0,1:T(8,128)(2,1)}, bf16[128,3072]{0,1:T(8,128)(2,1)}, u32[]{:S(2)}, u32[]{:S(2)}) collective-permute-start(bf16[128,3072]{0,1:T(8,128)(2,1)} %constant_dynamic-slice_fusion.15), channel_id=1, source_target_pairs={{0,24},{8,0},{16,8},{24,16},{1,25},{9,1},{17,9},{25,17},{2,26},{10... | collective-permute-start | bytes 2359304 | tf_op jit(solution)/shard_map/ppermute | solution.py:36
  140.5 244.4 %collective-permute-start.25 = (bf16[1024,512]{1,0:T(8,128)(2,1)}, bf16[1024,512]{1,0:T(8,128)(2,1)}, u32[]{:S(2)}, u32[]{:S(2)}) collective-permute-start(bf16[1024,512]{1,0:T(8,128)(2,1)} %constant_dynamic-slice_fusion.12), channel_id=1, source_target_pairs={{0,8},{8,16},{16,24},{24,0},{1,9},{9,17},{17,25},{25,1},{2,10},{10... | collective-permute-start | bytes 3145736 | tf_op jit(solution)/shard_map/ppermute | solution.py:36
  188.8 196.1 %collective-permute-start.26 = (bf16[1024,512]{1,0:T(8,128)(2,1)}, bf16[1024,512]{1,0:T(8,128)(2,1)}, u32[]{:S(2)}, u32[]{:S(2)}) collective-permute-start(bf16[1024,512]{1,0:T(8,128)(2,1)} %constant_dynamic-slice_fusion.12), channel_id=1, source_target_pairs={{0,16},{8,24},{16,0},{24,8},{1,17},{9,25},{17,1},{25,9},{2,18},{10... | collective-permute-start | bytes 3145736 | tf_op jit(solution)/shard_map/ppermute | solution.py:36
  200.0 185.0 %collective-permute-start.27 = (bf16[1024,512]{1,0:T(8,128)(2,1)}, bf16[1024,512]{1,0:T(8,128)(2,1)}, u32[]{:S(2)}, u32[]{:S(2)}) collective-permute-start(bf16[1024,512]{1,0:T(8,128)(2,1)} %constant_dynamic-slice_fusion.12), channel_id=1, source_target_pairs={{0,24},{8,0},{16,8},{24,16},{1,25},{9,1},{17,9},{25,17},{2,26},{10... | collective-permute-start | bytes 3145736 | tf_op jit(solution)/shard_map/ppermute | solution.py:36
  203.0 87.0 %collective-permute-start.19 = (bf16[128,4096]{1,0:T(8,128)(2,1)}, bf16[128,4096]{1,0:T(8,128)(2,1)}, u32[]{:S(2)}, u32[]{:S(2)}) collective-permute-start(bf16[128,4096]{1,0:T(8,128)(2,1)} %constant_dynamic-slice_fusion.13), channel_id=1, source_target_pairs={{0,8},{8,16},{16,24},{24,0},{1,9},{9,17},{17,25},{25,1},{2,10},{10... | collective-permute-start | bytes 3145736 | tf_op jit(solution)/shard_map/ppermute | solution.py:36
  208.8 145.1 %collective-permute-start.20 = (bf16[128,4096]{1,0:T(8,128)(2,1)}, bf16[128,4096]{1,0:T(8,128)(2,1)}, u32[]{:S(2)}, u32[]{:S(2)}) collective-permute-start(bf16[128,4096]{1,0:T(8,128)(2,1)} %constant_dynamic-slice_fusion.13), channel_id=1, source_target_pairs={{0,16},{8,24},{16,0},{24,8},{1,17},{9,25},{17,1},{25,9},{2,18},{10... | collective-permute-start | bytes 3145736 | tf_op jit(solution)/shard_map/ppermute | solution.py:36
  290.0 66.2 %collective-permute-start.15 = (bf16[3,256,512]{2,1,0:T(8,128)(2,1)S(1)}, bf16[3,256,512]{2,1,0:T(8,128)(2,1)S(1)}, u32[]{:S(2)}, u32[]{:S(2)}) collective-permute-start(bf16[3,256,512]{2,1,0:T(8,128)(2,1)S(1)} %copy-done.97), channel_id=1, source_target_pairs={{0,4},{2,6},{4,0},{6,2},{1,5},{3,7},{5,1},{7,3},{8,12},{10,14},{12... | collective-permute-start | bytes 2359304 | tf_op jit(solution)/shard_map/ppermute | solution.py:41
  358.5 73.6 %collective-permute-start.6 = (bf16[3,128,3072]{1,2,0:T(8,128)(2,1)S(1)}, bf16[3,128,3072]{1,2,0:T(8,128)(2,1)S(1)}, u32[]{:S(2)}, u32[]{:S(2)}) collective-permute-start(bf16[3,128,3072]{1,2,0:T(8,128)(2,1)S(1)} %pad_maximum_fusion.3), channel_id=1, source_target_pairs={{0,4},{2,6},{4,0},{6,2},{1,5},{3,7},{5,1},{7,3},{8,12},{10,14},{12... | collective-permute-start | bytes 7077896 | tf_op jit(solution)/shard_map/ppermute | solution.py:41
  381.8 429.0 %collective-permute-start.48 = (bf16[1,64,2048]{2,1,0:T(8,128)(2,1)}, bf16[1,64,2048]{2,1,0:T(8,128)(2,1)}, u32[]{:S(2)}, u32[]{:S(2)}) collective-permute-start(bf16[1,64,2048]{2,1,0:T(8,128)(2,1)} %get-tuple-element.77), channel_id=1, source_target_pairs={{0,24},{8,0},{16,8},{24,16},{1,25},{9,1},{17,9},{25,17},{2,26},{10... | collective-permute-start | bytes 786440 | tf_op jit(solution)/shard_map/ppermute | solution.py:36
  384.9 425.8 %collective-permute-start.47 = (bf16[1,64,2048]{2,1,0:T(8,128)(2,1)}, bf16[1,64,2048]{2,1,0:T(8,128)(2,1)}, u32[]{:S(2)}, u32[]{:S(2)}) collective-permute-start(bf16[1,64,2048]{2,1,0:T(8,128)(2,1)} %get-tuple-element.78), channel_id=1, source_target_pairs={{0,16},{8,24},{16,0},{24,8},{1,17},{9,25},{17,1},{25,9},{2,18},{10... | collective-permute-start | bytes 786440 | tf_op jit(solution)/shard_map/ppermute | solution.py:36
  428.5 71.3 %collective-permute-start.28 = (bf16[3,1024,512]{2,1,0:T(8,128)(2,1)}, bf16[3,1024,512]{2,1,0:T(8,128)(2,1)}, u32[]{:S(2)}, u32[]{:S(2)}) collective-permute-start(bf16[3,1024,512]{2,1,0:T(8,128)(2,1)} %pad_maximum_fusion.1), channel_id=1, source_target_pairs={{0,4},{2,6},{4,0},{6,2},{1,5},{3,7},{5,1},{7,3},{8,12},{10,14},{12... | collective-permute-start | bytes 9437192 | tf_op jit(solution)/shard_map/ppermute | solution.py:41
  432.1 74.8 %collective-permute-start.29 = (bf16[3,1024,512]{2,1,0:T(8,128)(2,1)}, bf16[3,1024,512]{2,1,0:T(8,128)(2,1)}, u32[]{:S(2)}, u32[]{:S(2)}) collective-permute-start(bf16[3,1024,512]{2,1,0:T(8,128)(2,1)} %pad_maximum_fusion.1), channel_id=1, source_target_pairs={{0,2},{2,0},{4,6},{6,4},{1,3},{3,1},{5,7},{7,5},{8,10},{10,8},{12,... | collective-permute-start | bytes 9437192 | tf_op jit(solution)/shard_map/ppermute | solution.py:41
  434.2 132.1 %collective-permute-start.22 = (bf16[3,128,4096]{2,1,0:T(8,128)(2,1)}, bf16[3,128,4096]{2,1,0:T(8,128)(2,1)}, u32[]{:S(2)}, u32[]{:S(2)}) collective-permute-start(bf16[3,128,4096]{2,1,0:T(8,128)(2,1)} %pad_maximum_fusion), channel_id=1, source_target_pairs={{0,4},{2,6},{4,0},{6,2},{1,5},{3,7},{5,1},{7,3},{8,12},{10,14},{12... | collective-permute-start | bytes 9437192 | tf_op jit(solution)/shard_map/ppermute | solution.py:41
  499.8 73.5 %collective-permute-start.23 = (bf16[3,128,4096]{2,1,0:T(8,128)(2,1)}, bf16[3,128,4096]{2,1,0:T(8,128)(2,1)S(1)}, u32[]{:S(2)}, u32[]{:S(2)}) collective-permute-start(bf16[3,128,4096]{2,1,0:T(8,128)(2,1)} %pad_maximum_fusion), channel_id=1, source_target_pairs={{0,2},{2,0},{4,6},{6,4},{1,3},{3,1},{5,7},{7,5},{8,10},{10,8},{12,... | collective-permute-start | bytes 9437192 | tf_op jit(solution)/shard_map/ppermute | solution.py:41
  506.9 74.6 %collective-permute-start.8 = (bf16[3,128,3072]{1,2,0:T(8,128)(2,1)S(1)}, bf16[3,128,3072]{1,2,0:T(8,128)(2,1)S(1)}, u32[]{:S(2)}, u32[]{:S(2)}) collective-permute-start(bf16[3,128,3072]{1,2,0:T(8,128)(2,1)S(1)} %copy-done.70), channel_id=1, source_target_pairs={{0,2},{2,0},{4,6},{6,4},{1,3},{3,1},{5,7},{7,5},{8,10},{10,8},{12,... | collective-permute-start | bytes 7077896 | tf_op jit(solution)/shard_map/ppermute | solution.py:41
  671.0 134.1 %collective-permute-start.59 = (bf16[1,64,2048]{2,1,0:T(8,128)(2,1)}, bf16[1,64,2048]{2,1,0:T(8,128)(2,1)}, u32[]{:S(2)}, u32[]{:S(2)}) collective-permute-start(bf16[1,64,2048]{2,1,0:T(8,128)(2,1)} %get-tuple-element.81), channel_id=1, source_target_pairs={{0,24},{8,0},{16,8},{24,16},{1,25},{9,1},{17,9},{25,17},{2,26},{10... | collective-permute-start | bytes 786440 | tf_op jit(solution)/shard_map/ppermute | solution.py:36
  (236 other events, 7368.9 us)

commit v2 on v1

--- a/solution.py
+++ b/solution.py
@@ -130,18 +130,19 @@
     dq_ref[0] = (dq * SCALE).T.astype(BF16)
 
 
-def attend_specs(n_seq, loc, n_piece):
+def attend_specs(n_seq, loc, n_piece, first):
     row = pl.BlockSpec((1, loc, HEAD_DIM), lambda s, h: (s, 0, h))
     bias = pl.BlockSpec((1, n_piece * loc, 128), lambda s, h: (s, 0, 0))
-    pair = pl.BlockSpec((2, 1, loc, HEAD_DIM), lambda s, h: (0, s, 0, h))
+    pair = pl.BlockSpec((2, 1, loc, HEAD_DIM), lambda s, h: (0, s + first, 0, h))
+    grads = pl.BlockSpec((2, 1, loc, HEAD_DIM), lambda s, h: (0, s, 0, h))
     log = pl.BlockSpec((1, 1, 1, loc), lambda s, h: (s, h, 0, 0))
-    return row, bias, pair, log
-
-
-def attend(query, kv, bias):
+    return row, bias, pair, log, grads
+
+
+def attend(query, kv, bias, first):
     n_seq, loc, width = query.shape
     n_piece, heads = len(kv), width // HEAD_DIM
-    row, bias_spec, pair, log = attend_specs(n_seq, loc, n_piece)
+    row, bias_spec, pair, log, grads = attend_specs(n_seq, loc, n_piece, first)
     return pl.pallas_call(
         lambda *refs: attend_kernel(n_piece, *refs),
         grid=(n_seq, heads),
@@ -160,17 +161,17 @@
     )(query, bias, *kv)
 
 
-def attend_back(query, kv, bias, grad, log_total):
+def attend_back(query, kv, bias, grad, log_total, first):
     n_seq, loc, width = query.shape
     n_piece, heads = len(kv), width // HEAD_DIM
-    row, bias_spec, pair, log = attend_specs(n_seq, loc, n_piece)
+    row, bias_spec, pair, log, grads = attend_specs(n_seq, loc, n_piece, first)
     out = pl.pallas_call(
         lambda *refs: attend_back_kernel(n_piece, *refs),
         grid=(n_seq, heads),
         in_specs=[row, bias_spec, row, log] + [pair] * n_piece,
-        out_specs=[row] + [pair] * n_piece,
+        out_specs=[row] + [grads] * n_piece,
         out_shape=[jax.ShapeDtypeStruct(query.shape, BF16)]
-        + [jax.ShapeDtypeStruct(kv[0].shape, BF16)] * n_piece,
+        + [jax.ShapeDtypeStruct((2, n_seq, loc, width), BF16)] * n_piece,
         compiler_params=pltpu.CompilerParams(vmem_limit_bytes=40 << 20),
         cost_estimate=pl.CostEstimate(
             flops=n_seq * heads * 10 * loc * loc * n_piece * HEAD_DIM * 4,
@@ -179,6 +180,209 @@
         ),
     )(query, bias, grad, log_total, *kv)
     return out[0], list(out[1:])
+
+
+def flip(ct, offset):
+    mask = 1
+    while mask <= offset:
+        if offset & mask:
+            ct = ct + mask - 2 * mask * lax.rem(ct // mask, 2)
+        mask *= 2
+    return ct
+
+
+class Weight:
+    def __init__(self, shard_at, whole_at):
+        self.shard_at, self.whole_at = shard_at, whole_at
+
+
+class Deal:
+    def __init__(self, source_at, rows_at):
+        self.source_at, self.rows_at = source_at, rows_at
+
+
+class Pair:
+    def __init__(self, slot_at):
+        self.slot_at = slot_at
+
+
+class Mover:
+    def __init__(self, n_fsdp, n_ctx, send, recv):
+        self.n_fsdp, self.n_ctx = n_fsdp, n_ctx
+        self.z, self.ct = lax.axis_index("fsdp"), lax.axis_index("ctx")
+        self.send, self.recv = send, recv
+        self.used = 0
+        self.open = []
+        self.masks = masks_of(n_ctx)
+        self.offsets = offsets(n_ctx)
+        self.came, self.waiting = {}, {}
+
+    def greet(self):
+        barrier = pltpu.get_barrier_semaphore()
+        others = [{"fsdp": lax.rem(self.z + s, self.n_fsdp)} for s in range(1, self.n_fsdp)]
+        others += [{"ctx": flip(self.ct, mask)} for mask in self.masks]
+        for other in others:
+            pl.semaphore_signal(
+                barrier, inc=1, device_id=other, device_id_type=pl.DeviceIdType.MESH
+            )
+        pl.semaphore_wait(barrier, len(others))
+
+    def copy(self, source, target, device, at=None):
+        if at is None:
+            at = self.used
+            self.used += 1
+        return pltpu.make_async_remote_copy(
+            src_ref=source,
+            dst_ref=target,
+            send_sem=self.send.at[at],
+            recv_sem=self.recv.at[at],
+            device_id=device,
+            device_id_type=pl.DeviceIdType.MESH,
+        )
+
+    def go(self, source, target, device):
+        copy = self.copy(source, target, device)
+        copy.start()
+        self.open.append((None, copy))
+        return copy
+
+    def along(self, item, owner, right, ok, source, slot):
+        target = item.whole_at(owner, self.ct)
+        device = {"fsdp": lax.rem(self.z + (1 if right else self.n_fsdp - 1), self.n_fsdp)}
+        copy = self.copy(source, target, device, self.came[item] + slot - 1)
+        pl.when(ok)(copy.start)
+        self.open.append((ok, copy))
+
+    def begin(self, item):
+        if isinstance(item, Pair):
+            self.waiting[item] = [[] for _ in self.masks]
+            self.cast(item, item.slot_at, lambda k, level: item.slot_at(k + 2**level), 0, 0)
+            return
+        if isinstance(item, Weight):
+            self.came[item] = self.used
+            self.used += self.n_fsdp - 1
+            source = item.shard_at(self.ct)
+            self.along(item, self.z, True, self.z < self.n_fsdp - 1, source, 1)
+            self.along(item, self.z, False, self.z > 0, source, self.n_fsdp - 1)
+            return
+        self.came[item] = [
+            self.go(
+                item.source_at(lax.rem(self.z + s, self.n_fsdp)),
+                item.rows_at(s),
+                {"fsdp": lax.rem(self.z + s, self.n_fsdp)},
+            )
+            for s in range(1, self.n_fsdp)
+        ]
+
+    def cast(self, item, source_at, target_at, k, first):
+        for level in range(first, len(self.masks)):
+            device = {"ctx": flip(self.ct, self.masks[level])}
+            copy = self.go(source_at(k), target_at(k, level), device)
+            self.waiting[item][level].append((copy, k + 2**level, source_at, target_at))
+
+    def relay(self, item):
+        if isinstance(item, Pair):
+            return
+        if isinstance(item, Deal):
+            for copy in self.came[item]:
+                copy.wait_recv()
+            return
+        self.waiting[item] = [[] for _ in self.masks]
+        n = self.n_fsdp
+        for i in range(n - 1):
+            s = i // 2 + 1 if i % 2 == 0 else n - 1 - i // 2
+            owner = lax.rem(self.z - s + n, n)
+            here = item.whole_at(owner, self.ct)
+            self.copy(here, here, {"fsdp": owner}, self.came[item] + s - 1).wait_recv()
+            if s < n - 1:
+                ok = (self.z >= s) & (self.z < n - 1)
+                self.along(item, owner, True, ok, here, s + 1)
+            if s > 1:
+                ok = (self.z < s) & (self.z > 0)
+                self.along(item, owner, False, ok, here, s - 1)
+
+            def at(k, owner=owner):
+                return item.whole_at(owner, flip(self.ct, self.offsets[k]))
+
+            self.cast(item, at, lambda k, level, at=at: at(k), 0, 0)
+
+    def finish(self, item, level):
+        if isinstance(item, Deal):
+            return
+        for copy, k, source_at, target_at in self.waiting[item][level]:
+            copy.wait_recv()
+            self.cast(item, source_at, target_at, k, level + 1)
+
+    def close(self):
+        for ok, copy in self.open:
+            if ok is None:
+                copy.wait_send()
+            else:
+                pl.when(ok)(copy.wait_send)
+
+
+def copies_of(items, n_fsdp, n_ctx):
+    total = 0
+    for item in items:
+        total += {Weight: (n_fsdp - 1) * n_ctx, Deal: n_fsdp - 1, Pair: n_ctx - 1}[item]
+    return total
+
+
+def keep(stay, room, sems):
+    out = []
+    for k, (source, target) in enumerate(stay):
+        first = pltpu.make_async_copy(source, room[k], sems.at[2 * k])
+        first.start()
+        out.append((first, pltpu.make_async_copy(room[k], target, sems.at[2 * k + 1])))
+    return out
+
+
+def move(make, kinds, inputs, outputs, n_fsdp, n_ctx, local_shapes, ident, ahead=2):
+    n_in = len(inputs)
+    n_copy = copies_of(kinds, n_fsdp, n_ctx)
+
+    def kernel(*refs):
+        ins, outs = refs[:n_in], refs[n_in : n_in + len(outputs)]
+        send, recv, here = refs[n_in + len(outputs) : n_in + len(outputs) + 3]
+        room = refs[n_in + len(outputs) + 3 :]
+        mover = Mover(n_fsdp, n_ctx, send, recv)
+        items, stay = make(ins, outs, mover.z)
+        mover.greet()
+        for item in items[:ahead]:
+            mover.begin(item)
+        kept = keep(stay, room, here)
+        levels = len(mover.masks)
+        for i in range(len(items) + levels):
+            if i < len(items):
+                mover.relay(items[i])
+                if i + ahead < len(items):
+                    mover.begin(items[i + ahead])
+            if i == 0:
+                for first, second in kept:
+                    first.wait()
+                    second.start()
+            for level in range(levels):
+                if 0 <= i - 1 - level < len(items):
+                    mover.finish(items[i - 1 - level], level)
+        for _, second in kept:
+            second.wait()
+        mover.close()
+
+    return pl.pallas_call(
+        kernel,
+        in_specs=[pl.BlockSpec(memory_space=pl.ANY)] * n_in,
+        out_specs=[pl.BlockSpec(memory_space=pl.ANY)] * len(outputs),
+        out_shape=[jax.ShapeDtypeStruct(shape, BF16) for shape in outputs],
+        scratch_shapes=[
+            pltpu.SemaphoreType.DMA((n_copy,)),
+            pltpu.SemaphoreType.DMA((n_copy,)),
+            pltpu.SemaphoreType.DMA((2 * len(local_shapes),)),
+        ]
+        + [pltpu.VMEM(shape, BF16) for shape in local_shapes],
+        compiler_params=pltpu.CompilerParams(
+            collective_id=ident, has_side_effects=True, vmem_limit_bytes=32 << 20
+        ),
+    )(*inputs)
 
 
 def norm_parts(values):
@@ -239,14 +443,6 @@
     def put(array, block, *starts):
         return lax.dynamic_update_slice(array, block, starts)
 
-    def deal(array, group):
-        out = []
-        for step in range(n_fsdp):
-            to = lax.rem(z + step, n_fsdp)
-            block = take(array, to * per + group * g_per, g_per)
-            out.append(block if step == 0 else shift(block, "fsdp", step))
-        return jnp.concatenate(out, axis=1)
-
     def undeal(rows, group_out):
         rows = rows.reshape(g_per, n_fsdp, piece, width)
         out = []
@@ -255,29 +451,94 @@
             out.append(block if step == 0 else shift(block, "fsdp", -step))
         return out
 
-    def gathered(shard, z_axis, full):
-        size = shard.shape[0] // n_ctx
-        mine = take(shard, ct * size, size)
-        got = [shift(mine, "fsdp", step) for step in range(1, n_fsdp)]
-        pieces = spread([jnp.stack(got)], "ctx")
-        z_size = shard.shape[z_axis]
-        full = put(full, shard, *((z * z_size, 0) if z_axis == 0 else (0, z * z_size)))
-        for offset, block in zip(offsets(n_ctx), pieces):
-            row = (ct ^ offset) * size
-            for step in range(1, n_fsdp):
-                start = lax.rem(z - step + n_fsdp, n_fsdp) * z_size
-                at = (start + row, 0) if z_axis == 0 else (row, start)
-                full = put(full, block[step - 1], *at)
-        return full
-
-    zero = jnp.zeros((), BF16)
+    units = w_up.shape[1]
     bands = [jnp.pad(b_qkv[j], ((0, 0), (j * heads_width, (2 - j) * heads_width))) for j in range(3)]
-    qkv_base = jnp.pad(jnp.concatenate(bands, axis=0), ((width, 0), (0, 0)))
-    qkv_shard = w_qkv.transpose(1, 0, 2).reshape(w_qkv.shape[1], 3 * heads_width)
-    qkv_x = gathered(qkv_shard, 0, qkv_base)
-    out_x = gathered(w_out, 1, jnp.pad(a_out, ((0, 0), (width, 0))))
-    up_x = gathered(w_up, 0, jnp.pad(b_up, ((width, 0), (0, 0))))
-    down_x = gathered(w_down, 1, jnp.pad(a_down, ((0, 0), (width, 0))))
+    qkv_foot = jnp.concatenate(bands, axis=0)
+    rows_shape = (per, n_fsdp, piece, width)
+    zq, zu = w_qkv.shape[1], w_up.shape[0]
+
+    def first_items(ins, outs, z):
+        x_ref, w_ref, foot_ref = ins
+        rows_ref, whole_ref = outs
+
+        def deal(g):
+            return Deal(lambda to: x_ref.at[to * per + g], lambda s: rows_ref.at[g, s])
+
+        def weight(j):
+            size = zq // n_ctx
+            columns = pl.ds(j * heads_width, heads_width)
+            return Weight(
+                lambda c: w_ref.at[j, pl.ds(pl.multiple_of(c * size, size), size)],
+                lambda o, c: whole_ref.at[
+                    pl.ds(pl.multiple_of(o * zq + c * size, size), size), columns
+                ],
+            )
+
+        stay = [(x_ref.at[z * per + g], rows_ref.at[g, 0]) for g in range(per)]
+        for j in range(3):
+            own = whole_ref.at[
+                pl.ds(pl.multiple_of(z * zq, zq), zq), pl.ds(j * heads_width, heads_width)
+            ]
+            stay.append((w_ref.at[j], own))
+        stay.append((foot_ref, whole_ref.at[pl.ds(width, 3 * NR)]))
+        items = [weight(0), deal(0), weight(1), weight(2)] + [deal(g) for g in range(1, per)]
+        return items, stay
+
+    x_all, qkv_x = move(
+        first_items,
+        [Weight] * 3 + [Deal] * per,
+        (x_in, w_qkv, qkv_foot),
+        (rows_shape, (width + 3 * NR, 3 * heads_width)),
+        n_fsdp,
+        n_ctx,
+        ((piece, width),) * per + (w_qkv.shape[1:],) * 3 + (qkv_foot.shape,),
+        0,
+    )
+
+    def second_items(ins, outs, z):
+        kv_ref, cot_ref, wo_ref, wu_ref, wd_ref, ao_ref, bu_ref, ad_ref = ins
+        slots, (rows_ref, out_ref, up_ref, down_ref) = outs[: n_ctx - 1], outs[n_ctx - 1 :]
+
+        def ds(start, size):
+            return pl.ds(pl.multiple_of(start, size), size)
+
+        def deal(g):
+            return Deal(lambda to: cot_ref.at[to * per + g], lambda s: rows_ref.at[g, s])
+
+        zo = wo_ref.shape[1]
+        so, su, sd = wo_ref.shape[0] // n_ctx, zu // n_ctx, wd_ref.shape[0] // n_ctx
+        out_item = Weight(
+            lambda c: wo_ref.at[ds(c * so, so)],
+            lambda o, c: out_ref.at[ds(c * so, so), ds(o * zo, zo)],
+        )
+
+        def up_item(h):
+            columns = pl.ds(h * (units // 2), units // 2)
+            return Weight(
+                lambda c: wu_ref.at[ds(c * su, su), columns],
+                lambda o, c: up_ref.at[ds(o * zu + c * su, su), columns],
+            )
+
+        def down_item(h):
+            half = sd // 2
+            return Weight(
+                lambda c: wd_ref.at[ds(c * sd + h * half, half)],
+                lambda o, c: down_ref.at[ds(c * sd + h * half, half), ds(o * zo, zo)],
+            )
+
+        pair = Pair(lambda k: kv_ref if k == 0 else slots[k - 1])
+        stay = [(cot_ref.at[z * per + g], rows_ref.at[g, 0]) for g in range(per)]
+        stay += [
+            (wo_ref, out_ref.at[:, ds(z * zo, zo)]),
+            (wu_ref, up_ref.at[ds(z * zu, zu)]),
+            (wd_ref, down_ref.at[:, ds(z * zo, zo)]),
+            (ao_ref, out_ref.at[:, pl.ds(width, NR)]),
+            (bu_ref, up_ref.at[pl.ds(width, NR)]),
+            (ad_ref, down_ref.at[:, pl.ds(width, NR)]),
+        ]
+        items = [pair, out_item, up_item(0), up_item(1), down_item(0), down_item(1)]
+        return items + [deal(g) for g in range(per)], stay
+
     a_in = a_qkv.transpose(1, 0, 2).reshape(width, 3 * NR)
 
     my_lengths = take(lengths, z * per, per)
@@ -292,14 +553,45 @@
     bias_all = jnp.where(key_pos[None, :] < my_lengths[:, None], 0.0, -1e30).astype(F32)
     bias_all = jnp.broadcast_to(bias_all[:, :, None], bias_all.shape + (128,))
 
+    pick_all = jnp.repeat(picked, loc, axis=0)
+    x_flat = x_all.reshape(per * loc, width)
+    adapt_all = (dot(x_flat, a_in) * jnp.concatenate([pick_all] * 3, axis=1)).astype(BF16)
+    proj_all = dot(jnp.concatenate([x_flat, adapt_all], axis=1), qkv_x).astype(BF16)
+    kv_own = jnp.stack([proj_all[:, heads_width : 2 * heads_width], proj_all[:, 2 * heads_width :]])
+    kv_own = kv_own.reshape(2, per, loc, heads_width)
+    moved = move(
+        second_items,
+        [Pair] + [Weight] * 5 + [Deal] * per,
+        (kv_own, cotangent, w_out, w_up, w_down, a_out, b_up, a_down),
+        ((2, per, loc, heads_width),) * (n_ctx - 1)
+        + (
+            rows_shape,
+            (heads_width, width + NR),
+            (width + NR, units),
+            (units, width + NR),
+        ),
+        n_fsdp,
+        n_ctx,
+        ((piece, width),) * per
+        + (w_out.shape, w_up.shape, w_down.shape, a_out.shape, b_up.shape, a_down.shape),
+        1,
+    )
+    kv_all = [kv_own] + list(moved[: n_ctx - 1])
+    cot_all, out_x, up_x, down_x = moved[n_ctx - 1 :]
+    cot_flat = cot_all.reshape(per * loc, width)
+
     acts, ins = [], []
     early, late = [], []
     for group in range(n_group):
+        mine = slice(group * g_rows, (group + 1) * g_rows)
         pick = jnp.repeat(take(picked, group * g_per, g_per), loc, axis=0)
         pick3 = jnp.concatenate([pick] * 3, axis=1)
         bias = bias_all[group * g_per : (group + 1) * g_per]
-        x_rows = deal(x_in, group).reshape(g_rows, width)
-        grad_out = deal(cotangent, group).reshape(g_rows, width)
+        x_rows = x_flat[mine]
+        grad_out = cot_flat[mine]
+        adapt_in = adapt_all[mine]
+        query = proj_all[mine, :heads_width].reshape(g_per, loc, heads_width)
+        first = group * g_per
 
         def compact(codes, values, j=0):
             out = []
@@ -309,12 +601,7 @@
                 out.append(dot_tn(take(codes[rows], first, RANK, 1), values[rows]).astype(BF16))
             return jnp.concatenate(out, axis=0)
 
-        adapt_in = (dot(x_rows, a_in) * pick3).astype(BF16)
-        proj = dot(jnp.concatenate([x_rows, adapt_in], axis=1), qkv_x).astype(BF16)
-        query = proj[:, :heads_width].reshape(g_per, loc, heads_width)
-        pair = jnp.stack([proj[:, heads_width : 2 * heads_width], proj[:, 2 * heads_width :]])
-        kv = spread([pair.reshape(2, g_per, loc, heads_width)], "ctx")
-        context, log_total = attend(query, kv, bias)
+        context, log_total = attend(query, kv_all, bias, first)
         ctx_rows = context.reshape(g_rows, heads_width)
         summed = both(dot(ctx_rows, out_x))
         adapt_out = (summed[:, width:] * pick).astype(BF16)
@@ -355,7 +642,7 @@
             )
         )
         d_query, d_kv = attend_back(
-            query, kv, bias, d_context.reshape(g_per, loc, heads_width), log_total
+            query, kv_all, bias, d_context.reshape(g_per, loc, heads_width), log_total, first
         )
         d_pair = fold(d_kv, "ctx").reshape(2, g_rows, heads_width)
         d_proj = jnp.concatenate([d_query.reshape(g_rows, heads_width), d_pair[0], d_pair[1]], axis=1)
@@ -406,7 +693,6 @@
             at += size
         return out
 
-    units = w_up.shape[1]
     e = split(everywhere(early), [width, units, units, width, width, heads_width])
     l = split(everywhere(late), [heads_width] * 3 + [width] * 3)
     return (

time: 1210 us -> 916 us (0.76)
  Pallas kernels: 43.3 us -> 384 us
  waiting for transfers between devices: 473 us -> 162 us
  local copies, waits for them, and re-layouts: 262 us -> 61.5 us
  starting transfers between devices: 170 us -> 65.6 us
    pallas_call x0 -> x2, Pallas kernels: none -> 340 us  [move(): pl.pallas_call(kernel, in_specs=[pl.BlockSpec(memory_space=pl.ANY)] * n_i...]
    ppermute x42 -> x18, waiting for transfers between devices: 214 us -> 47.7 us  [shift(): return lax.ppermute(block, axis, [(i, (i + step) % n) for i in range(n)])]
    ppermute x44 -> x26, waiting for transfers between devices: 259 us -> 114 us  [swap(): return lax.ppermute(block, axis, [(i, i ^ mask) for i in range(n)])]
    dynamic_update_slice x98 -> x46, local copies, waits for them, and re-layouts: 161 us -> 31.2 us  [put(): return lax.dynamic_update_slice(array, block, starts)]
    ppermute x42 -> x18, starting transfers between devices: 150 us -> 52.1 us  [shift(): return lax.ppermute(block, axis, [(i, (i + step) % n) for i in range(n)])]
    pad x4 -> x0, local copies, waits for them, and re-layouts: 26 us -> none  [the longest x1 8.96 us: local(): up_x = gathered(w_up, 0, jnp.pad(b_up, ((width, 0), (0, 0))))]
    squeeze x12 -> x0, local copies, waits for them, and re-layouts: 25 us -> none  [gathered(): full = put(full, block[step - 1], *at)]
    dot_general x16 -> x14, matrix products: 62.2 us -> 52.6 us  [dot(): return jnp.dot(left, right, preferred_element_type=F32)]
  transfers between devices with their start and end apart: 86 -> 44, of which waited for: 29 -> 20; matrix products, arithmetic and copies ran while one was open for 37% -> 18% of each run, Pallas kernels for 4% -> 4%
where the time goes in v2:
time: 916 us; the launch traced here: 902 us
  Pallas kernels  384 us (42%)
  matrix products  185 us (20%)
  waiting for transfers between devices  162 us (18%)
  starting transfers between devices  65.6 us (7%)
  local copies, waits for them, and re-layouts  61.5 us (7%)
  other arithmetic  38.6 us (4%)
    pallas_call x2, Pallas kernels, move(): pl.pallas_call(kernel, in_specs=[pl.BlockSpec(memory_space=pl.ANY)] * n_i...  340 us
    ppermute x26, waiting for transfers between devices, swap(): return lax.ppermute(block, axis, [(i, i ^ mask) for i in range(n)])  114 us
    dot_general x16, matrix products, dot_nt(): lax.dot_general(left, right, (((1,), (1,)), ((), ())), preferred_element_...  94.5 us
    dot_general x14, matrix products, dot(): return jnp.dot(left, right, preferred_element_type=F32)  52.6 us
    ppermute x18, starting transfers between devices, shift(): return lax.ppermute(block, axis, [(i, (i + step) % n) for i in range(n)])  52.1 us
    ppermute x18, waiting for transfers between devices, shift(): return lax.ppermute(block, axis, [(i, (i + step) % n) for i in range(n)])  47.7 us
    dot_general x36, matrix products, dot_tn(): lax.dot_general(left, right, (((0,), (0,)), ((), ())), preferred_element_...  38 us
    dynamic_update_slice x46, local copies, waits for them, and re-layouts, put(): return lax.dynamic_update_slice(array, block, starts)  31.2 us
  transfers between devices with their start and end apart: 44, of which 20 were waited for; matrix products, arithmetic and copies ran while one was open for 18% of the time, Pallas kernels for 4%

profile of v2, /device:TPU:0, one launch (start us, length us, event | category | flops | bytes accessed | tf_op | source)
XLA Modules:
  0.0 901.6 jit_solution(2883100310643368957)
XLA Ops:
  13.5 116.9 %shard_map.258 = (bf16[2,4,64,2048]{3,2,1,0:T(8,128)(2,1)S(1)}, bf16[2432,3072]{1,0:T(8,128)(2,1)}) custom-call(bf16[8,64,2048]{2,1,0:T(8,128)(2,1)S(1)} %copy-done.8, bf16[3,512,1024]{2,1,0:T(8,128)(2,1)S(1)} %copy-done.4, bf16[384,3072]{1,0:T(8,128)(2,1)S(1)} %fusion.18.refs_2_), custom_call_target="tpu_custom_call" | custom-call | tf_op jit(solution)/shard_map/pallas_call | solution.py:371
  131.8 11.6 %convolution_convert_fusion = bf16[512,3072]{1,0:T(8,128)(2,1)S(1)} fusion(bf16[2432,3072]{1,0:T(8,128)(2,1)} %get-tuple-element.34, bf16[512,384]{1,0:T(8,128)(2,1)S(1)} %copy.39, bf16[512,2048]{1,0:T(8,128)(2,1)S(1)} %bitcast.314), kind=kOutput, calls=%fused_computation.14 | convolution fusion | flops 7656964096 | bytes 20578304 | tf_op jit(solution)/shard_map/dot_general | solution.py:23
  152.3 222.8 %shard_map.259 = (bf16[2,2,256,1024]{3,2,1,0:T(8,128)(2,1)S(1)}, bf16[2,2,256,1024]{3,2,1,0:T(8,128)(2,1)S(1)}, bf16[2,2,256,1024]{3,2,1,0:T(8,128)(2,1)S(1)}, b...) custom-call(bf16[2,2,256,1024]{3,2,1,0:T(8,128)(2,1)S(1)} %pad_maxim, ...), custom_call_target="tpu_custom_call" | custom-call | tf_op jit(solution)/shard_map/pallas_call | solution.py:371
  375.4 8.7 shard_map.261
  387.4 8.5 shard_map.260
  399.6 13.4 %collective-permute-done.5 = bf16[256,2176]{1,0:T(8,128)(2,1)S(1)} collective-permute-done((bf16[256,2176]{1,0:T(8,128)(2,1)S(1)}, bf16[256,2176]{1,0:T(8,128)(2,1)S(1)}, u32[]{:S(2)}, u32[]{:S(2)}) %collective-permute-start.5) | collective-permute-done | bytes 1114144 | tf_op jit(solution)/shard_map/ppermute | solution.py:41
  414.3 22.2 %collective-permute-done = bf16[256,2176]{1,0:T(8,128)(2,1)S(1)} collective-permute-done((bf16[256,2176]{1,0:T(8,128)(2,1)S(1)}, bf16[256,2176]{1,0:T(8,128)(2,1)S(1)}, u32[]{:S(2)}, u32[]{:S(2)}) %collective-permute-start) | collective-permute-done | bytes 1114144 | tf_op jit(solution)/shard_map/ppermute | solution.py:41
  446.8 11.6 %convolution_convert_fusion.10 = bf16[256,2176]{1,0:T(8,128)(2,1)} fusion(bf16[4096,2176]{1,0:T(8,128)(2,1)} %get-tuple-element.41, f32[256,4096]{1,0:T(8,128)S(1)} %fusion.72), kind=kOutput, calls=%fused_computation.36 | convolution fusion | flops 4573396992 | bytes 23134208 | tf_op jit(solution)/shard_map/dot_general | solution.py:23
  465.4 11.8 %convolution_convert_fusion.9 = bf16[256,2176]{1,0:T(8,128)(2,1)} fusion(bf16[4096,2176]{1,0:T(8,128)(2,1)} %get-tuple-element.41, f32[256,4096]{1,0:T(8,128)S(1)} %fusion.76), kind=kOutput, calls=%fused_computation.35 | convolution fusion | flops 4573396992 | bytes 23134208 | tf_op jit(solution)/shard_map/dot_general | solution.py:23
  488.0 20.7 %collective-permute-done.6 = bf16[256,2176]{1,0:T(8,128)(2,1)} collective-permute-done((bf16[256,2176]{1,0:T(8,128)(2,1)}, bf16[256,2176]{1,0:T(8,128)(2,1)}, u32[]{:S(2)}, u32[]{:S(2)}) %collective-permute-start.6) | collective-permute-done | bytes 1114144 | tf_op jit(solution)/shard_map/ppermute | solution.py:41
  519.6 11.8 %fusion.1 = bf16[256,4096]{1,0:T(8,128)(2,1)} fusion(bf16[4096,2176]{1,0:T(8,128)(2,1)} %get-tuple-element.41, f32[256,4096]{1,0:T(8,128)} %copy-done.89, bf16[256,128]{1,0:T(8,128)(2,1)S(1)} %fusion.62, bf16[256,2048]{1,0:T(8,128)(2,1)S(1)} %get-tuple-element.88), kind=kOutput, calls=%fused_computation.7 | convolution fusion | flops 4586602496 | bytes 25231360 | tf_op jit(solution)/shard_map/dot_general | solution.py:27
  533.5 19.2 %convolution_convert_fusion.6 = bf16[256,2176]{1,0:T(8,128)(2,1)} fusion(bf16[256,4096]{1,0:T(8,128)(2,1)} %fusion.1, bf16[2176,4096]{1,0:T(8,128)(2,1)} %get-tuple-element.40), kind=kOutput, calls=%fused_computation.32 | convolution fusion | flops 4563959808 | bytes 21037056 | tf_op jit(solution)/shard_map/dot_general | solution.py:27
  556.6 11.9 %fusion = bf16[256,4096]{1,0:T(8,128)(2,1)} fusion(bf16[4096,2176]{1,0:T(8,128)(2,1)} %get-tuple-element.41, f32[256,4096]{1,0:T(8,128)} %copy-done.88, bf16[256,128]{1,0:T(8,128)(2,1)S(1)} %fusion.60, bf16[256,2048]{1,0:T(8,128)(2,1)} %get-tuple-element.89), kind=kOutput, calls=%fused_computation.6 | convolution fusion | flops 4586602496 | bytes 25231360 | tf_op jit(solution)/shard_map/dot_general | solution.py:27
  568.5 19.4 %convolution_convert_fusion.8 = bf16[256,2176]{1,0:T(8,128)(2,1)} fusion(bf16[256,4096]{1,0:T(8,128)(2,1)} %fusion, bf16[2176,4096]{1,0:T(8,128)(2,1)} %get-tuple-element.40), kind=kOutput, calls=%fused_computation.34 | convolution fusion | flops 4563959808 | bytes 21037056 | tf_op jit(solution)/shard_map/dot_general | solution.py:27
  624.2 13.6 %shard_map.263 = (bf16[1,256,1024]{2,1,0:T(8,128)(2,1)S(1)}, bf16[2,1,256,1024]{3,2,1,0:T(8,128)(2,1)S(1)}, bf16[2,1,256,1024]{3,2,1,0:T(8,128)(2,1)S(1)}, bf16[...) custom-call(bf16[1,256,1024]{2,1,0:T(8,128)(2,1)S(1)} %copy-done.21, f32[1,1024,128]{2,1,0:T(8,128)S(1)} %copy-done.15, ...), custom_call_target="tpu_custom_call" | custom-call | flops 10737418240 | bytes 9961472 | tf_op jit(solution)/shard_map/pallas_call | solution.py:168
  639.7 13.8 %shard_map.262 = (bf16[1,256,1024]{2,1,0:T(8,128)(2,1)S(1)}, bf16[2,1,256,1024]{3,2,1,0:T(8,128)(2,1)S(1)}, bf16[2,1,256,1024]{3,2,1,0:T(8,128)(2,1)S(1)}, bf16[...) custom-call(bf16[1,256,1024]{2,1,0:T(8,128)(2,1)S(1)} %copy-done.19, f32[1,1024,128]{2,1,0:T(8,128)S(1)} %copy-done.13, ...), custom_call_target="tpu_custom_call" | custom-call | flops 10737418240 | bytes 9961472 | tf_op jit(solution)/shard_map/pallas_call | solution.py:168
  690.4 16.2 %collective-permute-start.9 = (bf16[1,64,2048]{2,1,0:T(8,128)(2,1)S(1)}, bf16[1,64,2048]{2,1,0:T(8,128)(2,1)S(1)}, u32[]{:S(2)}, u32[]{:S(2)}) collective-permute-start(bf16[1,64,2048]{2,1,0:T(8,128)(2,1)S(1)} %get-tuple-element.102), channel_id=1, source_target_pairs={{0,8},{8,16},{16,24},{24,0},{1,9},{9,17},{17,25},{25,1},{2,10},{10... | collective-permute-start | bytes 786440 | tf_op jit(solution)/shard_map/ppermute | solution.py:36
  726.4 9.1 %collective-permute-done.41 = bf16[4,32,3840]{2,1,0:T(8,128)(2,1)} collective-permute-done((bf16[4,32,3840]{2,1,0:T(8,128)(2,1)S(1)}, bf16[4,32,3840]{2,1,0:T(8,128)(2,1)}, u32[]{:S(2)}, u32[]{:S(2)}) %collective-permute-start.41) | collective-permute-done | bytes 983072 | tf_op jit(solution)/shard_map/ppermute | solution.py:41
  740.2 17.6 %collective-permute-done.21 = bf16[2,1,256,1024]{3,2,1,0:T(8,128)(2,1)S(1)} collective-permute-done((bf16[2,1,256,1024]{3,2,1,0:T(8,128)(2,1)S(1)}, bf16[2,1,256,1024]{3,2,1,0:T(8,128)(2,1)S(1)}, u32[]{:S(2)}, u32[]{:S(2)}) %collective-permute-start.21) | collective-permute-done | bytes 1048608 | tf_op jit(solution)/shard_map/ppermute | solution.py:41
  759.8 10.9 %convolution_convert_fusion.5 = bf16[256,2432]{1,0:T(8,128)(2,1)} fusion(bf16[2432,3072]{1,0:T(8,128)(2,1)} %get-tuple-element.34, bf16[256,1024]{1,0:T(8,128)(2,1)} %get-tuple-element.96, bf16[256,1024]{1,0:T(8,128)(2,1)} %get-tuple-element.95, bf16[256,1024]{1,0:T(8,128)(2,1)S(1)} %bitcast.315), kind=kOutput, calls=%fused_computation.31 | convolution fusion | flops 3830546432 | bytes 17760256 | tf_op jit(solution)/shard_map/dot_general | solution.py:27
  771.2 7.3 collective-permute-done.13
  781.8 10.9 %convolution_convert_fusion.7 = bf16[256,2432]{1,0:T(8,128)(2,1)} fusion(bf16[2432,3072]{1,0:T(8,128)(2,1)} %get-tuple-element.34, bf16[256,1024]{1,0:T(8,128)(2,1)} %get-tuple-element.101, bf16[256,1024]{1,0:T(8,128)(2,1)S(1)} %get-tuple-element.100, bf16[256,1024]{1,0:T(8,128)(2,1)S(1)} %bitcast.316), kind=kOutput, calls=%fused_computation.33 | convolution fusion | flops 3830546432 | bytes 17760256 | tf_op jit(solution)/shard_map/dot_general | solution.py:27
  838.8 14.2 %collective-permute-done.16 = bf16[1,64,2048]{2,1,0:T(8,128)(2,1)S(1)} collective-permute-done((bf16[1,64,2048]{2,1,0:T(8,128)(2,1)S(1)}, bf16[1,64,2048]{2,1,0:T(8,128)(2,1)S(1)}, u32[]{:S(2)}, u32[]{:S(2)}) %collective-permute-start.16) | collective-permute-done | bytes 262176 | tf_op jit(solution)/shard_map/ppermute | solution.py:36
  868.9 9.9 %collective-permute-start.25 = (bf16[1,64,2048]{2,1,0:T(8,128)(2,1)S(1)}, bf16[1,64,2048]{2,1,0:T(8,128)(2,1)S(1)}, u32[]{:S(2)}, u32[]{:S(2)}) collective-permute-start(bf16[1,64,2048]{2,1,0:T(8,128)(2,1)S(1)} %get-tuple-element.92), channel_id=1, source_target_pairs={{0,8},{8,16},{16,24},{24,0},{1,9},{9,17},{17,25},{25,1},{2,10},{10... | collective-permute-start | bytes 786440 | tf_op jit(solution)/shard_map/ppermute | solution.py:36
  (485 shorter events, 263.2 us)
Async XLA Ops:
  385.6 27.4 %collective-permute-start.5 = (bf16[256,2176]{1,0:T(8,128)(2,1)S(1)}, bf16[256,2176]{1,0:T(8,128)(2,1)S(1)}, u32[]{:S(2)}, u32[]{:S(2)}) collective-permute-start(bf16[256,2176]{1,0:T(8,128)(2,1)S(1)} %convolution_convert_fusion.11), channel_id=1, source_target_pairs={{0,1},{1,0},{2,3},{3,2},{4,5},{5,4},{6,7},{7,6},{8,9},{9,8},{10,11... | collective-permute-start | bytes 3342344 | tf_op jit(solution)/shard_map/ppermute | solution.py:41
  397.3 39.1 %collective-permute-start = (bf16[256,2176]{1,0:T(8,128)(2,1)S(1)}, bf16[256,2176]{1,0:T(8,128)(2,1)S(1)}, u32[]{:S(2)}, u32[]{:S(2)}) collective-permute-start(bf16[256,2176]{1,0:T(8,128)(2,1)S(1)} %convolution_convert_fusion.12), channel_id=1, source_target_pairs={{0,1},{1,0},{2,3},{3,2},{4,5},{5,4},{6,7},{7,6},{8,9},{9,8},{10,11... | collective-permute-start | bytes 3342344 | tf_op jit(solution)/shard_map/ppermute | solution.py:41
  458.4 27.8 %collective-permute-start.1 = (bf16[256,2176]{1,0:T(8,128)(2,1)}, bf16[256,2176]{1,0:T(8,128)(2,1)}, u32[]{:S(2)}, u32[]{:S(2)}) collective-permute-start(bf16[256,2176]{1,0:T(8,128)(2,1)} %convolution_convert_fusion.10), channel_id=1, source_target_pairs={{0,1},{1,0},{2,3},{3,2},{4,5},{5,4},{6,7},{7,6},{8,9},{9,8},{10,11... | collective-permute-start | bytes 3342344 | tf_op jit(solution)/shard_map/ppermute | solution.py:41
  477.2 31.6 %collective-permute-start.6 = (bf16[256,2176]{1,0:T(8,128)(2,1)}, bf16[256,2176]{1,0:T(8,128)(2,1)}, u32[]{:S(2)}, u32[]{:S(2)}) collective-permute-start(bf16[256,2176]{1,0:T(8,128)(2,1)} %convolution_convert_fusion.9), channel_id=1, source_target_pairs={{0,1},{1,0},{2,3},{3,2},{4,5},{5,4},{6,7},{7,6},{8,9},{9,8},{10,11... | collective-permute-start | bytes 3342344 | tf_op jit(solution)/shard_map/ppermute | solution.py:41
  552.7 44.4 %collective-permute-start.18 = (bf16[256,2176]{1,0:T(8,128)(2,1)}, bf16[256,2176]{1,0:T(8,128)(2,1)}, u32[]{:S(2)}, u32[]{:S(2)}) collective-permute-start(bf16[256,2176]{1,0:T(8,128)(2,1)} %convolution_convert_fusion.6), channel_id=1, source_target_pairs={{0,1},{1,0},{2,3},{3,2},{4,5},{5,4},{6,7},{7,6},{8,9},{9,8},{10,11... | collective-permute-start | bytes 3342344 | tf_op jit(solution)/shard_map/ppermute | solution.py:41
  589.6 25.2 %collective-permute-start.10 = (bf16[256,2176]{1,0:T(8,128)(2,1)}, bf16[256,2176]{1,0:T(8,128)(2,1)S(1)}, u32[]{:S(2)}, u32[]{:S(2)}) collective-permute-start(bf16[256,2176]{1,0:T(8,128)(2,1)} %convolution_convert_fusion.8), channel_id=1, source_target_pairs={{0,1},{1,0},{2,3},{3,2},{4,5},{5,4},{6,7},{7,6},{8,9},{9,8},{10,11... | collective-permute-start | bytes 3342344 | tf_op jit(solution)/shard_map/ppermute | solution.py:41
  623.6 31.8 %collective-permute-start.36 = (bf16[32,3840]{1,0:T(8,128)(2,1)}, bf16[32,3840]{1,0:T(8,128)(2,1)}, u32[]{:S(2)}, u32[]{:S(2)}) collective-permute-start(bf16[32,3840]{1,0:T(8,128)(2,1)} %get-tuple-element.109), channel_id=1, source_target_pairs={{0,2},{2,0},{4,6},{6,4},{1,3},{3,1},{5,7},{7,5},{8,10},{10,8},{12,... | collective-permute-start | bytes 737288 | tf_op jit(solution)/shard_map/ppermute | solution.py:41
  623.6 43.5 %collective-permute-start.35 = (bf16[32,3840]{1,0:T(8,128)(2,1)}, bf16[32,3840]{1,0:T(8,128)(2,1)}, u32[]{:S(2)}, u32[]{:S(2)}) collective-permute-start(bf16[32,3840]{1,0:T(8,128)(2,1)} %get-tuple-element.108), channel_id=1, source_target_pairs={{0,2},{2,0},{4,6},{6,4},{1,3},{3,1},{5,7},{7,5},{8,10},{10,8},{12,... | collective-permute-start | bytes 737288 | tf_op jit(solution)/shard_map/ppermute | solution.py:41
  637.8 85.2 %collective-permute-start.20 = (bf16[2,1,256,1024]{3,2,1,0:T(8,128)(2,1)S(1)}, bf16[2,1,256,1024]{3,2,1,0:T(8,128)(2,1)S(1)}, u32[]{:S(2)}, u32[]{:S(2)}) collective-permute-start(bf16[2,1,256,1024]{3,2,1,0:T(8,128)(2,1)S(1)} %get-tuple-element.55), channel_id=1, source_target_pairs={{0,2},{2,0},{4,6},{6,4},{1,3},{3,1},{5,7},{7,5},{8,10},{10,8},{12,... | collective-permute-start | bytes 3145736 | tf_op jit(solution)/shard_map/ppermute | solution.py:41
  638.8 22.3 %collective-permute-start.3 = (bf16[1,64,2048]{2,1,0:T(8,128)(2,1)}, bf16[1,64,2048]{2,1,0:T(8,128)(2,1)S(1)}, u32[]{:S(2)}, u32[]{:S(2)}) collective-permute-start(bf16[1,64,2048]{2,1,0:T(8,128)(2,1)} %get-tuple-element.106), channel_id=1, source_target_pairs={{0,16},{8,24},{16,0},{24,8},{1,17},{9,25},{17,1},{25,9},{2,18},{10... | collective-permute-start | bytes 786440 | tf_op jit(solution)/shard_map/ppermute | solution.py:36
  676.0 64.1 %collective-permute-start.19 = (bf16[2,1,256,1024]{3,2,1,0:T(8,128)(2,1)S(1)}, bf16[2,1,256,1024]{3,2,1,0:T(8,128)(2,1)S(1)}, u32[]{:S(2)}, u32[]{:S(2)}) collective-permute-start(bf16[2,1,256,1024]{3,2,1,0:T(8,128)(2,1)S(1)} %get-tuple-element.53), channel_id=1, source_target_pairs={{0,2},{2,0},{4,6},{6,4},{1,3},{3,1},{5,7},{7,5},{8,10},{10,8},{12,... | collective-permute-start | bytes 3145736 | tf_op jit(solution)/shard_map/ppermute | solution.py:41
  682.4 41.6 %collective-permute-start.12 = (bf16[2,1,256,1024]{3,2,1,0:T(8,128)(2,1)S(1)}, bf16[2,1,256,1024]{3,2,1,0:T(8,128)(2,1)S(1)}, u32[]{:S(2)}, u32[]{:S(2)}) collective-permute-start(bf16[2,1,256,1024]{3,2,1,0:T(8,128)(2,1)S(1)} %get-tuple-element.49), channel_id=1, source_target_pairs={{0,2},{2,0},{4,6},{6,4},{1,3},{3,1},{5,7},{7,5},{8,10},{10,8},{12,... | collective-permute-start | bytes 3145736 | tf_op jit(solution)/shard_map/ppermute | solution.py:41
  710.6 24.8 %collective-permute-start.41 = (bf16[4,32,3840]{2,1,0:T(8,128)(2,1)S(1)}, bf16[4,32,3840]{2,1,0:T(8,128)(2,1)}, u32[]{:S(2)}, u32[]{:S(2)}) collective-permute-start(bf16[4,32,3840]{2,1,0:T(8,128)(2,1)S(1)} %pad_maximum_fusion.3), channel_id=1, source_target_pairs={{0,4},{2,6},{4,0},{6,2},{1,5},{3,7},{5,1},{7,3},{8,12},{10,14},{12... | collective-permute-start | bytes 2949128 | tf_op jit(solution)/shard_map/ppermute | solution.py:41
  711.3 59.9 %collective-permute-start.11 = (bf16[2,1,256,1024]{3,2,1,0:T(8,128)(2,1)}, bf16[2,1,256,1024]{3,2,1,0:T(8,128)(2,1)}, u32[]{:S(2)}, u32[]{:S(2)}) collective-permute-start(bf16[2,1,256,1024]{3,2,1,0:T(8,128)(2,1)} %get-tuple-element.47), channel_id=1, source_target_pairs={{0,2},{2,0},{4,6},{6,4},{1,3},{3,1},{5,7},{7,5},{8,10},{10,8},{12,... | collective-permute-start | bytes 3145736 | tf_op jit(solution)/shard_map/ppermute | solution.py:41
  724.0 33.8 %collective-permute-start.21 = (bf16[2,1,256,1024]{3,2,1,0:T(8,128)(2,1)S(1)}, bf16[2,1,256,1024]{3,2,1,0:T(8,128)(2,1)S(1)}, u32[]{:S(2)}, u32[]{:S(2)}) collective-permute-start(bf16[2,1,256,1024]{3,2,1,0:T(8,128)(2,1)S(1)} %add_convert_fusion.3), channel_id=1, source_target_pairs={{0,4},{2,6},{4,0},{6,2},{1,5},{3,7},{5,1},{7,3},{8,12},{10,14},{12... | collective-permute-start | bytes 3145736 | tf_op jit(solution)/shard_map/ppermute | solution.py:41
  735.4 43.0 %collective-permute-start.13 = (bf16[2,1,256,1024]{3,2,1,0:T(8,128)(2,1)}, bf16[2,1,256,1024]{3,2,1,0:T(8,128)(2,1)}, u32[]{:S(2)}, u32[]{:S(2)}) collective-permute-start(bf16[2,1,256,1024]{3,2,1,0:T(8,128)(2,1)} %add_convert_fusion.6), channel_id=1, source_target_pairs={{0,4},{2,6},{4,0},{6,2},{1,5},{3,7},{5,1},{7,3},{8,12},{10,14},{12... | collective-permute-start | bytes 3145736 | tf_op jit(solution)/shard_map/ppermute | solution.py:41
  739.9 57.5 %collective-permute-start.43 = (bf16[4,32,3840]{2,1,0:T(8,128)(2,1)}, bf16[4,32,3840]{2,1,0:T(8,128)(2,1)}, u32[]{:S(2)}, u32[]{:S(2)}) collective-permute-start(bf16[4,32,3840]{2,1,0:T(8,128)(2,1)} %collective-permute-done.41), channel_id=1, source_target_pairs={{0,2},{2,0},{4,6},{6,4},{1,3},{3,1},{5,7},{7,5},{8,10},{10,8},{12,... | collective-permute-start | bytes 2949128 | tf_op jit(solution)/shard_map/ppermute | solution.py:41
  770.7 45.8 %collective-permute-start.22 = (bf16[256,2432]{1,0:T(8,128)(2,1)}, bf16[256,2432]{1,0:T(8,128)(2,1)}, u32[]{:S(2)}, u32[]{:S(2)}) collective-permute-start(bf16[256,2432]{1,0:T(8,128)(2,1)} %convolution_convert_fusion.5), channel_id=1, source_target_pairs={{0,1},{1,0},{2,3},{3,2},{4,5},{5,4},{6,7},{7,6},{8,9},{9,8},{10,11... | collective-permute-start | bytes 3735560 | tf_op jit(solution)/shard_map/ppermute | solution.py:41
  792.6 30.5 %collective-permute-start.14 = (bf16[256,2432]{1,0:T(8,128)(2,1)}, bf16[256,2432]{1,0:T(8,128)(2,1)S(1)}, u32[]{:S(2)}, u32[]{:S(2)}) collective-permute-start(bf16[256,2432]{1,0:T(8,128)(2,1)} %convolution_convert_fusion.7), channel_id=1, source_target_pairs={{0,1},{1,0},{2,3},{3,2},{4,5},{5,4},{6,7},{7,6},{8,9},{9,8},{10,11... | collective-permute-start | bytes 3735560 | tf_op jit(solution)/shard_map/ppermute | solution.py:41
  824.6 29.0 %collective-permute-start.26 = (bf16[32,2304]{1,0:T(8,128)(2,1)S(1)}, bf16[32,2304]{1,0:T(8,128)(2,1)S(1)}, u32[]{:S(2)}, u32[]{:S(2)}) collective-permute-start(bf16[32,2304]{1,0:T(8,128)(2,1)S(1)} %get-tuple-element.113), channel_id=1, source_target_pairs={{0,2},{2,0},{4,6},{6,4},{1,3},{3,1},{5,7},{7,5},{8,10},{10,8},{12,... | collective-permute-start | bytes 442376 | tf_op jit(solution)/shard_map/ppermute | solution.py:41
  828.3 24.7 %collective-permute-start.16 = (bf16[1,64,2048]{2,1,0:T(8,128)(2,1)S(1)}, bf16[1,64,2048]{2,1,0:T(8,128)(2,1)S(1)}, u32[]{:S(2)}, u32[]{:S(2)}) collective-permute-start(bf16[1,64,2048]{2,1,0:T(8,128)(2,1)S(1)} %get-tuple-element.98), channel_id=1, source_target_pairs={{0,16},{8,24},{16,0},{24,8},{1,17},{9,25},{17,1},{25,9},{2,18},{10... | collective-permute-start | bytes 786440 | tf_op jit(solution)/shard_map/ppermute | solution.py:36
  828.3 25.2 %collective-permute-start.17 = (bf16[1,64,2048]{2,1,0:T(8,128)(2,1)S(1)}, bf16[1,64,2048]{2,1,0:T(8,128)(2,1)S(1)}, u32[]{:S(2)}, u32[]{:S(2)}) collective-permute-start(bf16[1,64,2048]{2,1,0:T(8,128)(2,1)S(1)} %get-tuple-element.97), channel_id=1, source_target_pairs={{0,8},{8,16},{16,24},{24,0},{1,9},{9,17},{17,25},{25,1},{2,10},{10... | collective-permute-start | bytes 786440 | tf_op jit(solution)/shard_map/ppermute | solution.py:36
  830.3 54.2 %collective-permute-start.23 = (bf16[1,64,2048]{2,1,0:T(8,128)(2,1)S(1)}, bf16[1,64,2048]{2,1,0:T(8,128)(2,1)S(1)}, u32[]{:S(2)}, u32[]{:S(2)}) collective-permute-start(bf16[1,64,2048]{2,1,0:T(8,128)(2,1)S(1)} %get-tuple-element.94), channel_id=1, source_target_pairs={{0,24},{8,0},{16,8},{24,16},{1,25},{9,1},{17,9},{25,17},{2,26},{10... | collective-permute-start | bytes 786440 | tf_op jit(solution)/shard_map/ppermute | solution.py:36
  838.7 45.9 %collective-permute-start.24 = (bf16[1,64,2048]{2,1,0:T(8,128)(2,1)S(1)}, bf16[1,64,2048]{2,1,0:T(8,128)(2,1)S(1)}, u32[]{:S(2)}, u32[]{:S(2)}) collective-permute-start(bf16[1,64,2048]{2,1,0:T(8,128)(2,1)S(1)} %get-tuple-element.93), channel_id=1, source_target_pairs={{0,16},{8,24},{16,0},{24,8},{1,17},{9,25},{17,1},{25,9},{2,18},{10... | collective-permute-start | bytes 786440 | tf_op jit(solution)/shard_map/ppermute | solution.py:36
  (120 other events, 1931.6 us)

commit v3 on v2

--- a/solution.py
+++ b/solution.py
@@ -73,8 +73,7 @@
     return pieces[0]
 
 
-def both(part):
-    low = part.astype(BF16)
+def both(low):
     for mask in masks_of(lax.axis_size("tp")):
         total = low.astype(F32) + swap(low, "tp", mask).astype(F32)
         low = total.astype(BF16)
@@ -337,7 +336,7 @@
     return out
 
 
-def move(make, kinds, inputs, outputs, n_fsdp, n_ctx, local_shapes, ident, ahead=2):
+def move(make, kinds, inputs, outputs, n_fsdp, n_ctx, local_shapes, ident, ahead=2, foot=None):
     n_in = len(inputs)
     n_copy = copies_of(kinds, n_fsdp, n_ctx)
 
@@ -345,6 +344,9 @@
         ins, outs = refs[:n_in], refs[n_in : n_in + len(outputs)]
         send, recv, here = refs[n_in + len(outputs) : n_in + len(outputs) + 3]
         room = refs[n_in + len(outputs) + 3 :]
+        if foot is not None:
+            blocks_ref, ins = ins[-1], ins[:-1]
+            strip = room[-1]
         mover = Mover(n_fsdp, n_ctx, send, recv)
         items, stay = make(ins, outs, mover.z)
         mover.greet()
@@ -357,10 +359,19 @@
                 mover.relay(items[i])
                 if i + ahead < len(items):
                     mover.begin(items[i + ahead])
+            if i == 0 and foot is not None:
+                strip[...] = jnp.zeros_like(strip)
+                high, wide = blocks_ref.shape[1:]
+                for j in range(blocks_ref.shape[0]):
+                    strip[j * high : (j + 1) * high, j * wide : (j + 1) * wide] = blocks_ref[j]
+                set_foot = pltpu.make_async_copy(strip, foot[1](outs), here.at[2 * len(local_shapes)])
+                set_foot.start()
+                kept.append((None, set_foot))
             if i == 0:
                 for first, second in kept:
-                    first.wait()
-                    second.start()
+                    if first is not None:
+                        first.wait()
+                        second.start()
             for level in range(levels):
                 if 0 <= i - 1 - level < len(items):
                     mover.finish(items[i - 1 - level], level)
@@ -368,17 +379,25 @@
             second.wait()
         mover.close()
 
+    spaces = [pl.BlockSpec(memory_space=pl.ANY)] * n_in
+    room_shapes = list(local_shapes)
+    if foot is not None:
+        blocks = foot[0]
+        inputs = inputs + (blocks,)
+        n_in += 1
+        spaces.append(pl.BlockSpec(memory_space=pltpu.VMEM))
+        room_shapes.append((blocks.shape[0] * blocks.shape[1], blocks.shape[0] * blocks.shape[2]))
     return pl.pallas_call(
         kernel,
-        in_specs=[pl.BlockSpec(memory_space=pl.ANY)] * n_in,
+        in_specs=spaces,
         out_specs=[pl.BlockSpec(memory_space=pl.ANY)] * len(outputs),
         out_shape=[jax.ShapeDtypeStruct(shape, BF16) for shape in outputs],
         scratch_shapes=[
             pltpu.SemaphoreType.DMA((n_copy,)),
             pltpu.SemaphoreType.DMA((n_copy,)),
-            pltpu.SemaphoreType.DMA((2 * len(local_shapes),)),
+            pltpu.SemaphoreType.DMA((2 * len(local_shapes) + 1,)),
         ]
-        + [pltpu.VMEM(shape, BF16) for shape in local_shapes],
+        + [pltpu.VMEM(shape, BF16) for shape in room_shapes],
         compiler_params=pltpu.CompilerParams(
             collective_id=ident, has_side_effects=True, vmem_limit_bytes=32 << 20
         ),
@@ -395,6 +414,144 @@
     first = jnp.mean(dhat, axis=-1, keepdims=True)
     second = jnp.mean(dhat * hat, axis=-1, keepdims=True)
     return rstd * (dhat - first - hat * second)
+
+
+def mm(left, right, nt, finish, tile, n_out=1, beside=None):
+    rows, depth = left.shape
+    columns = right.shape[0] if nt else right.shape[1]
+    extra = [] if beside is None else [beside]
+    sub = 128 if nt else tile
+
+    def kernel(left_ref, right_ref, *refs):
+        n_extra = len(extra)
+        outs = refs[n_extra : n_extra + n_out]
+        if nt:
+            turned = refs[-1]
+
+            @pl.when(pl.program_id(0) == 0)
+            def _():
+                turned[...] = left_ref[...].T
+
+        for k in range(tile // sub):
+            at = slice(k * sub, (k + 1) * sub)
+            if nt:
+                block = dot(right_ref[at, :], turned[...]).T
+            else:
+                block = dot(left_ref[...], right_ref[:, at])
+            values = finish(block, *[ref[:, at] for ref in refs[:n_extra]])
+            for ref, value in zip(outs, values):
+                ref[:, at] = value
+
+    part = pl.BlockSpec((rows, tile), lambda j: (0, j))
+    out = pl.pallas_call(
+        kernel,
+        grid=(pl.cdiv(columns, tile),),
+        in_specs=[
+            pl.BlockSpec((rows, depth), lambda j: (0, 0)),
+            pl.BlockSpec((tile, depth), lambda j: (j, 0))
+            if nt
+            else pl.BlockSpec((depth, tile), lambda j: (0, j)),
+        ]
+        + [part] * len(extra),
+        out_specs=[part] * n_out,
+        out_shape=[jax.ShapeDtypeStruct((rows, columns), BF16)] * n_out,
+        scratch_shapes=[pltpu.VMEM((depth, rows), BF16)] if nt else [],
+        compiler_params=pltpu.CompilerParams(vmem_limit_bytes=48 << 20),
+        cost_estimate=pl.CostEstimate(
+            flops=2 * rows * depth * columns,
+            bytes_accessed=2 * (rows * depth + 2 * depth * columns + rows * columns * n_out),
+            transcendentals=0,
+        ),
+    )(left, right, *extra)
+    return out[0] if n_out == 1 else out
+
+
+def compact(pairs, n_part):
+    rows = pairs[0][0].shape[0]
+    sizes = [values.shape[1] // n_part for _, values in pairs]
+    total = sum(sizes)
+
+    def kernel(*refs):
+        out_ref = refs[-1]
+        column = lax.broadcasted_iota(jnp.int32, (NR, RANK), 0)
+        rank = lax.broadcasted_iota(jnp.int32, (NR, RANK), 1)
+        used = jnp.where(lax.rem(column, RANK) == rank, 1.0, 0.0).astype(BF16)
+        start = 0
+        for i, size in enumerate(sizes):
+            codes = dot(refs[2 * i][...], used).astype(BF16)
+            block = dot_tn(codes, refs[2 * i + 1][...]).astype(BF16)
+            for part in range(n_part):
+                out_ref[part, :, start : start + size] = block[:, part * size : (part + 1) * size]
+            start += size
+
+    flat = [array for pair in pairs for array in pair]
+    return pl.pallas_call(
+        kernel,
+        in_specs=[pl.BlockSpec(memory_space=pltpu.VMEM)] * len(flat),
+        out_specs=pl.BlockSpec(memory_space=pltpu.VMEM),
+        out_shape=jax.ShapeDtypeStruct((n_part, RANK, total), BF16),
+        compiler_params=pltpu.CompilerParams(vmem_limit_bytes=40 << 20),
+        cost_estimate=pl.CostEstimate(
+            flops=2 * rows * RANK * total * n_part * 8,
+            bytes_accessed=2 * rows * total * n_part,
+            transcendentals=0,
+        ),
+    )(*flat)
+
+
+def combine(pieces, chosen, shapes):
+    n_part = len(pieces)
+    n_fsdp, rows, columns = pieces[0].shape
+    flat = []
+    for i, shape in enumerate(shapes):
+        for lead in range(shape[0] if len(shape) == 3 else 1):
+            flat.append((i, lead if len(shape) == 3 else None, shape[-2:]))
+
+    def kernel(chosen_ref, *refs):
+        piece_refs, outs = refs[:n_part], refs[n_part:]
+        z, ct = lax.axis_index("fsdp"), lax.axis_index("ctx")
+        for k, offset in enumerate(offsets(n_part)):
+            part = flip(ct, offset)
+            ordered = jnp.concatenate(
+                [piece_refs[k][lax.rem(z - a + n_fsdp, n_fsdp)] for a in range(n_fsdp)], axis=0
+            )
+            start = 0
+            for i, lead, (high, wide) in flat:
+                out_ref = outs[i] if lead is None else outs[i].at[lead]
+                tall = wide == NR and high != NR
+                size = (high if tall else wide) // n_part
+                block = ordered[:, start : start + size]
+                at = pl.ds(pl.multiple_of(part * size, size), size)
+                if tall:
+                    out_ref[at, :] = dot_tn(block, chosen_ref[...])
+                else:
+                    out_ref[:, at] = dot_tn(chosen_ref[...], block)
+                start += size
+
+    return pl.pallas_call(
+        kernel,
+        in_specs=[pl.BlockSpec(memory_space=pltpu.VMEM)] * (1 + n_part),
+        out_specs=[pl.BlockSpec(memory_space=pltpu.VMEM)] * len(shapes),
+        out_shape=[jax.ShapeDtypeStruct(shape, F32) for shape in shapes],
+        compiler_params=pltpu.CompilerParams(vmem_limit_bytes=48 << 20),
+        cost_estimate=pl.CostEstimate(
+            flops=2 * NR * n_fsdp * rows * columns * n_part,
+            bytes_accessed=2 * n_fsdp * rows * columns * n_part + 4 * NR * columns * n_part,
+            transcendentals=0,
+        ),
+    )(chosen, *pieces)
+
+
+def as_low(block):
+    return (block.astype(BF16),)
+
+
+def times(block, factor):
+    return ((block * factor.astype(F32)).astype(BF16),)
+
+
+def after(value, *first):
+    return lax.optimization_barrier((value,) + first)[0]
 
 
 def gelu_both(pre):
@@ -452,13 +609,11 @@
         return out
 
     units = w_up.shape[1]
-    bands = [jnp.pad(b_qkv[j], ((0, 0), (j * heads_width, (2 - j) * heads_width))) for j in range(3)]
-    qkv_foot = jnp.concatenate(bands, axis=0)
     rows_shape = (per, n_fsdp, piece, width)
     zq, zu = w_qkv.shape[1], w_up.shape[0]
 
     def first_items(ins, outs, z):
-        x_ref, w_ref, foot_ref = ins
+        x_ref, w_ref = ins
         rows_ref, whole_ref = outs
 
         def deal(g):
@@ -480,19 +635,19 @@
                 pl.ds(pl.multiple_of(z * zq, zq), zq), pl.ds(j * heads_width, heads_width)
             ]
             stay.append((w_ref.at[j], own))
-        stay.append((foot_ref, whole_ref.at[pl.ds(width, 3 * NR)]))
-        items = [weight(0), deal(0), weight(1), weight(2)] + [deal(g) for g in range(1, per)]
+        items = [weight(j) for j in range(3)] + [deal(g) for g in range(per)]
         return items, stay
 
     x_all, qkv_x = move(
         first_items,
         [Weight] * 3 + [Deal] * per,
-        (x_in, w_qkv, qkv_foot),
+        (x_in, w_qkv),
         (rows_shape, (width + 3 * NR, 3 * heads_width)),
         n_fsdp,
         n_ctx,
-        ((piece, width),) * per + (w_qkv.shape[1:],) * 3 + (qkv_foot.shape,),
+        ((piece, width),) * per + (w_qkv.shape[1:],) * 3,
         0,
+        foot=(b_qkv, lambda outs: outs[1].at[pl.ds(width, 3 * NR)]),
     )
 
     def second_items(ins, outs, z):
@@ -556,7 +711,7 @@
     pick_all = jnp.repeat(picked, loc, axis=0)
     x_flat = x_all.reshape(per * loc, width)
     adapt_all = (dot(x_flat, a_in) * jnp.concatenate([pick_all] * 3, axis=1)).astype(BF16)
-    proj_all = dot(jnp.concatenate([x_flat, adapt_all], axis=1), qkv_x).astype(BF16)
+    proj_all = mm(jnp.concatenate([x_flat, adapt_all], axis=1), qkv_x, False, as_low, 1024)
     kv_own = jnp.stack([proj_all[:, heads_width : 2 * heads_width], proj_all[:, 2 * heads_width :]])
     kv_own = kv_own.reshape(2, per, loc, heads_width)
     moved = move(
@@ -580,86 +735,104 @@
     cot_all, out_x, up_x, down_x = moved[n_ctx - 1 :]
     cot_flat = cot_all.reshape(per * loc, width)
 
-    acts, ins = [], []
-    early, late = [], []
-    for group in range(n_group):
-        mine = slice(group * g_rows, (group + 1) * g_rows)
-        pick = jnp.repeat(take(picked, group * g_per, g_per), loc, axis=0)
-        pick3 = jnp.concatenate([pick] * 3, axis=1)
-        bias = bias_all[group * g_per : (group + 1) * g_per]
-        x_rows = x_flat[mine]
-        grad_out = cot_flat[mine]
-        adapt_in = adapt_all[mine]
-        query = proj_all[mine, :heads_width].reshape(g_per, loc, heads_width)
-        first = group * g_per
-
-        def compact(codes, values, j=0):
-            out = []
-            for n in range(g_per):
-                first = my_ids[group * g_per + n] * RANK + j * NR
-                rows = slice(n * loc, (n + 1) * loc)
-                out.append(dot_tn(take(codes[rows], first, RANK, 1), values[rows]).astype(BF16))
-            return jnp.concatenate(out, axis=0)
-
-        context, log_total = attend(query, kv_all, bias, first)
-        ctx_rows = context.reshape(g_rows, heads_width)
-        summed = both(dot(ctx_rows, out_x))
-        adapt_out = (summed[:, width:] * pick).astype(BF16)
-        hat1, rstd1 = norm_parts(x_rows.astype(F32) + summed[:, :width] + dot(adapt_out, b_out))
-        hidden = hat1 * ln_gain[0] + ln_bias[0]
-        hidden_low = hidden.astype(BF16)
-        adapt_up = (dot(hidden_low, a_up) * pick).astype(BF16)
-        gelu_out, slope = gelu_both(dot(jnp.concatenate([hidden_low, adapt_up], axis=1), up_x))
-        summed = both(dot(gelu_out, down_x))
-        adapt_down = (summed[:, width:] * pick).astype(BF16)
-        hat2, rstd2 = norm_parts(hidden + summed[:, :width] + dot(adapt_down, b_down))
-        layer_out = (hat2 * ln_gain[1] + ln_bias[1]).astype(BF16)
-        acts.append(undeal(layer_out, group))
-
-        dy2 = norm_back(hat2, rstd2, grad_out.astype(F32) * ln_gain[1])
-        d_down = dy2.astype(BF16)
-        dadapt_down = (dot_nt(d_down, b_down) * pick).astype(BF16)
-        d_gelu = dot_nt(jnp.concatenate([d_down, dadapt_down], axis=1), down_x)
-        d_pre = (d_gelu * slope.astype(F32)).astype(BF16)
-        summed = both(dot_nt(d_pre, up_x))
-        dadapt_up = (summed[:, width:] * pick).astype(BF16)
-        dh1 = dy2 + summed[:, :width] + dot_nt(dadapt_up, a_up)
-        dy1 = norm_back(hat1, rstd1, dh1 * ln_gain[0])
-        d_attn = dy1.astype(BF16)
-        dadapt_out = (dot_nt(d_attn, b_out) * pick).astype(BF16)
-        d_context = dot_nt(jnp.concatenate([d_attn, dadapt_out], axis=1), out_x).astype(BF16)
-        early.append(
-            jnp.concatenate(
-                [
-                    compact(adapt_down, d_down),
-                    compact(dadapt_down, gelu_out),
-                    compact(adapt_up, d_pre),
-                    compact(dadapt_up, hidden_low),
-                    compact(adapt_out, d_attn),
-                    compact(dadapt_out, ctx_rows),
-                ],
-                axis=1,
-            )
+    groups = range(n_group)
+    picks = [jnp.repeat(take(picked, g * g_per, g_per), loc, axis=0) for g in groups]
+    biases = [bias_all[g * g_per : (g + 1) * g_per] for g in groups]
+    part = [slice(g * g_rows, (g + 1) * g_rows) for g in groups]
+    seq = [slice(n * loc, (n + 1) * loc) for n in range(g_per)]
+    x_rows = [x_flat[part[g]] for g in groups]
+    query = [proj_all[part[g], :heads_width].reshape(g_per, loc, heads_width) for g in groups]
+
+    attended = [attend(query[g], kv_all, biases[g], g * g_per) for g in groups]
+    ctx_rows = [attended[g][0].reshape(g_rows, heads_width) for g in groups]
+    summed = [both(mm(ctx_rows[g], out_x, False, as_low, 768)) for g in groups]
+    adapt_out, hat1, rstd1, hidden, hidden_low, adapt_up, gelu_out, slope = ([] for _ in range(8))
+    for g in groups:
+        adapt_out.append((summed[g][:, width:] * picks[g]).astype(BF16))
+        y1 = x_rows[g].astype(F32) + summed[g][:, :width] + dot(adapt_out[g], b_out)
+        parts = norm_parts(y1)
+        hat1.append(parts[0])
+        rstd1.append(parts[1])
+        hidden.append(parts[0] * ln_gain[0] + ln_bias[0])
+        hidden_low.append(hidden[g].astype(BF16))
+        adapt_up.append((dot(hidden_low[g], a_up) * picks[g]).astype(BF16))
+        wide = jnp.concatenate([hidden_low[g], adapt_up[g]], axis=1)
+        pair = mm(wide, up_x, False, gelu_both, 1024, 2)
+        gelu_out.append(pair[0])
+        slope.append(pair[1])
+    summed = [both(mm(gelu_out[g], down_x, False, as_low, 768)) for g in groups]
+    adapt_down, acts, dy2, d_down, dadapt_down, d_pre = ([] for _ in range(6))
+    for g in groups:
+        adapt_down.append((summed[g][:, width:] * picks[g]).astype(BF16))
+        hat2, rstd2 = norm_parts(hidden[g] + summed[g][:, :width] + dot(adapt_down[g], b_down))
+        acts.append(undeal((hat2 * ln_gain[1] + ln_bias[1]).astype(BF16), g))
+        dy2.append(norm_back(hat2, rstd2, cot_flat[part[g]].astype(F32) * ln_gain[1]))
+        d_down.append(dy2[g].astype(BF16))
+        dadapt_down.append((dot_nt(d_down[g], b_down) * picks[g]).astype(BF16))
+        wide = jnp.concatenate([d_down[g], dadapt_down[g]], axis=1)
+        d_pre.append(mm(wide, down_x, True, times, 1024, 1, slope[g]))
+    summed = [both(mm(d_pre[g], up_x, True, as_low, 768)) for g in groups]
+    dadapt_up, dy1, d_attn, dadapt_out, backs = ([] for _ in range(5))
+    for g in groups:
+        dadapt_up.append((summed[g][:, width:] * picks[g]).astype(BF16))
+        dh1 = dy2[g] + summed[g][:, :width] + dot_nt(dadapt_up[g], a_up)
+        dy1.append(norm_back(hat1[g], rstd1[g], dh1 * ln_gain[0]))
+        d_attn.append(dy1[g].astype(BF16))
+        dadapt_out.append((dot_nt(d_attn[g], b_out) * picks[g]).astype(BF16))
+        wide = jnp.concatenate([d_attn[g], dadapt_out[g]], axis=1)
+        d_context = mm(wide, out_x, True, as_low, 512).reshape(g_per, loc, heads_width)
+        backs.append(
+            attend_back(query[g], kv_all, biases[g], d_context, attended[g][1], g * g_per)
         )
-        d_query, d_kv = attend_back(
-            query, kv_all, bias, d_context.reshape(g_per, loc, heads_width), log_total, first
+
+    def gathered(parts):
+        mine = jnp.concatenate(parts, axis=1)
+        blocks = [
+            lax.dynamic_index_in_dim(mine, ct ^ offset, 0, False) for offset in offsets(n_ctx)
+        ]
+        own = fold(blocks, "ctx")
+        got = jnp.stack([own] + [shift(own, "fsdp", step) for step in range(1, n_fsdp)])
+        return spread([got], "ctx")
+
+    early_in = []
+    for g in groups:
+        pairs = (
+            (adapt_down[g], d_down[g]),
+            (dadapt_down[g], gelu_out[g]),
+            (adapt_up[g], d_pre[g]),
+            (dadapt_up[g], hidden_low[g]),
+            (adapt_out[g], d_attn[g]),
+            (dadapt_out[g], ctx_rows[g]),
         )
-        d_pair = fold(d_kv, "ctx").reshape(2, g_rows, heads_width)
-        d_proj = jnp.concatenate([d_query.reshape(g_rows, heads_width), d_pair[0], d_pair[1]], axis=1)
-        summed = both(dot_nt(d_proj, qkv_x))
-        dadapt_in = (summed[:, width:] * pick3).astype(BF16)
-        d_x = (dy1 + summed[:, :width] + dot_nt(dadapt_in, a_in)).astype(BF16)
-        ins.append(undeal(d_x, group))
-        late.append(
-            jnp.concatenate(
-                [
-                    compact(adapt_in, d_proj[:, j * heads_width : (j + 1) * heads_width], j)
-                    for j in range(3)
-                ]
-                + [compact(dadapt_in, x_rows, j) for j in range(3)],
-                axis=1,
-            )
-        )
+        early_in.append(pairs)
+    early_in = after(early_in, backs[-1][0])
+    early = gathered(
+        [compact([(c[r], v[r]) for c, v in early_in[g]], n_ctx) for g in groups for r in seq]
+    )
+
+    d_proj, ins, late = [], [], []
+    summed = []
+    for g in groups:
+        d_pair = fold(backs[g][1], "ctx").reshape(2, g_rows, heads_width)
+        d_query = backs[g][0].reshape(g_rows, heads_width)
+        d_proj.append(jnp.concatenate([d_query, d_pair[0], d_pair[1]], axis=1))
+        summed.append(both(mm(d_proj[g], qkv_x, True, as_low, 640)))
+    for g in groups:
+        pick3 = jnp.concatenate([picks[g]] * 3, axis=1)
+        dadapt_in = (summed[g][:, width:] * pick3).astype(BF16)
+        d_x = (dy1[g] + summed[g][:, :width] + dot_nt(dadapt_in, a_in)).astype(BF16)
+        ins.append(undeal(d_x, g))
+        adapt_in = adapt_all[part[g]]
+        for r in seq:
+            pairs = []
+            for j in range(3):
+                codes = slice(j * NR, (j + 1) * NR)
+                columns = slice(j * heads_width, (j + 1) * heads_width)
+                pairs.append((adapt_in[r, codes], d_proj[g][r, columns]))
+            for j in range(3):
+                pairs.append((dadapt_in[r, j * NR : (j + 1) * NR], x_rows[g][r]))
+            late.append(compact(pairs, n_ctx))
+    late = gathered(late)
 
     def assemble(parts):
         full = jnp.zeros((seqs, piece, width), BF16)
@@ -671,42 +844,14 @@
 
     codes = (adapter_ids[:, None] * RANK + jnp.arange(RANK)[None, :]).reshape(-1)
     chosen = (codes[:, None] == jnp.arange(NR)[None, :]).astype(BF16)
-
-    def everywhere(parts):
-        mine = jnp.concatenate(parts, axis=0)
-        rows, columns = mine.shape
-        size = columns // n_ctx
-        blocks = [take(mine, (ct ^ offset) * size, size, 1) for offset in offsets(n_ctx)]
-        own = fold(blocks, "ctx")
-        got = jnp.stack([own] + [shift(own, "fsdp", step) for step in range(1, n_fsdp)])
-        full = jnp.zeros((n_fsdp * rows, columns), BF16)
-        for offset, block in zip(offsets(n_ctx), spread([got], "ctx")):
-            for step in range(n_fsdp):
-                owner = lax.rem(z - step + n_fsdp, n_fsdp)
-                full = put(full, block[step], owner * rows, (ct ^ offset) * size)
-        return full
-
-    def split(full, sizes):
-        out, at = [], 0
-        for size in sizes:
-            out.append(full[:, at : at + size])
-            at += size
-        return out
-
-    e = split(everywhere(early), [width, units, units, width, width, heads_width])
-    l = split(everywhere(late), [heads_width] * 3 + [width] * 3)
-    return (
-        assemble(acts),
-        assemble(ins),
-        jnp.stack([dot_tn(l[3 + j], chosen) for j in range(3)]),
-        jnp.stack([dot_tn(chosen, l[j]) for j in range(3)]),
-        dot_tn(e[5], chosen),
-        dot_tn(chosen, e[4]),
-        dot_tn(e[3], chosen),
-        dot_tn(chosen, e[2]),
-        dot_tn(e[1], chosen),
-        dot_tn(chosen, e[0]),
+    early, acts = after((early, acts), summed[-1])
+    e = combine(
+        early,
+        chosen,
+        [(NR, width), (units, NR), (NR, units), (width, NR), (NR, width), (heads_width, NR)],
     )
+    l = combine(late, chosen, [(3, NR, heads_width), (3, width, NR)])
+    return assemble(acts), assemble(ins), l[1], l[0], e[5], e[4], e[3], e[2], e[1], e[0]
 
 
 def solution(mesh):

time: 916 us -> 865 us (0.944)
  matrix products: 185 us -> 13 us
  Pallas kernels: 384 us -> 503 us
  waiting for transfers between devices: 162 us -> 203 us
  local copies, waits for them, and re-layouts: 61.5 us -> 48.6 us
  other arithmetic: 38.6 us -> 27.7 us
    pallas_call x2 -> x23, Pallas kernels: 340 us -> 459 us  [the longest x2 323 us: move(): pl.pallas_call(kernel, in_specs=spaces, out_specs=[pl.BlockSpec(memory_sp...]
    dot_general x16 -> x8, matrix products: 94.5 us -> 6.73 us  [dot_nt(): lax.dot_general(left, right, (((1,), (1,)), ((), ())), preferred_element_...]
    ppermute x26, waiting for transfers between devices: 114 us -> 179 us  [swap(): return lax.ppermute(block, axis, [(i, i ^ mask) for i in range(n)])]
    dot_general x14 -> x7, matrix products: 52.6 us -> 6.22 us  [dot(): return jnp.dot(left, right, preferred_element_type=F32)]
    dot_general x36 -> x0, matrix products: 38 us -> none  [dot_tn(): lax.dot_general(left, right, (((0,), (0,)), ((), ())), preferred_element_...]
    dynamic_update_slice x46 -> x16, local copies, waits for them, and re-layouts: 31.2 us -> 0.34 us  [put(): return lax.dynamic_update_slice(array, block, starts)]
    unnamed x202 -> x275, local copies, waits for them, and re-layouts: 18.1 us -> 42.5 us
    ppermute x18, waiting for transfers between devices: 47.7 us -> 23.9 us  [shift(): return lax.ppermute(block, axis, [(i, (i + step) % n) for i in range(n)])]
  transfers between devices with their start and end apart: 44 -> 44, of which waited for: 20 -> 17; matrix products, arithmetic and copies ran while one was open for 18% -> 3% of each run, Pallas kernels for 4% -> 11%
where the time goes in v3:
time: 865 us; the launch traced here: 856 us
  Pallas kernels  503 us (58%)
  waiting for transfers between devices  203 us (23%)
  starting transfers between devices  57.5 us (7%)
  local copies, waits for them, and re-layouts  48.6 us (6%)
  other arithmetic  27.7 us (3%)
  matrix products  13 us (2%)
    pallas_call x2, Pallas kernels, move(): pl.pallas_call(kernel, in_specs=spaces, out_specs=[pl.BlockSpec(memory_sp...  323 us
    ppermute x26, waiting for transfers between devices, swap(): return lax.ppermute(block, axis, [(i, i ^ mask) for i in range(n)])  179 us
    pallas_call x15, Pallas kernels, mm(): pl.pallas_call(kernel, grid=(pl.cdiv(columns, tile),), in_specs=[pl.Block...  121 us
    unnamed x275, local copies, waits for them, and re-layouts  42.5 us
    ppermute x18, starting transfers between devices, shift(): return lax.ppermute(block, axis, [(i, (i + step) % n) for i in range(n)])  36.1 us
    pallas_call x2, Pallas kernels, attend_back(): pl.pallas_call(lambda *refs: attend_back_kernel(n_piece, *refs), grid=(n_...  27.3 us
    ppermute x18, waiting for transfers between devices, shift(): return lax.ppermute(block, axis, [(i, (i + step) % n) for i in range(n)])  23.9 us
    ppermute x26, starting transfers between devices, swap(): return lax.ppermute(block, axis, [(i, i ^ mask) for i in range(n)])  21.3 us
  transfers between devices with their start and end apart: 44, of which 17 were waited for; matrix products, arithmetic and copies ran while one was open for 3% of the time, Pallas kernels for 11%

profile of v3, /device:TPU:0, one launch (start us, length us, event | category | flops | bytes accessed | tf_op | source)
XLA Modules:
  0.0 856.4 jit_solution(14968002926335141710)
XLA Ops:
  5.5 100.0 %shard_map.258 = (bf16[2,4,64,2048]{3,2,1,0:T(8,128)(2,1)S(1)}, bf16[2432,3072]{1,0:T(8,128)(2,1)}) custom-call(bf16[8,64,2048]{2,1,0:T(8,128)(2,1)S(1)} %copy-done.29, bf16[3,512,1024]{2,1,0:T(8,128)(2,1)S(1)} %copy-done.28, bf16[3,128,1024]{2,1,0:T(8,128)(2,1)S(1)} %copy-done.48), custom_call_target="tpu_custom_call" | custom-call | tf_op jit(solution)/shard_map/pallas_call | solution.py:390
  107.6 11.2 %shard_map.259 = bf16[512,3072]{1,0:T(8,128)(2,1)S(1)} custom-call(bf16[512,2432]{1,0:T(8,128)(2,1)S(1)} %pad_maximum_fusion.left_ref, bf16[2432,3072]{1,0:T(8,128)(2,1)} %get-tuple-element.82.right_ref), custom_call_target="tpu_custom_call" | custom-call | flops 7650410496 | bytes 35520512 | tf_op jit(solution)/shard_map/pallas_call | solution.py:446
  127.8 222.9 %shard_map.260 = (bf16[2,2,256,1024]{3,2,1,0:T(8,128)(2,1)S(1)}, bf16[2,2,256,1024]{3,2,1,0:T(8,128)(2,1)S(1)}, bf16[2,2,256,1024]{3,2,1,0:T(8,128)(2,1)S(1)}, b...) custom-call(bf16[2,2,256,1024]{3,2,1,0:T(8,128)(2,1)S(1)} %pad_maxim, ...), custom_call_target="tpu_custom_call" | custom-call | tf_op jit(solution)/shard_map/pallas_call | solution.py:390
  382.8 31.5 %collective-permute-done = bf16[256,2176]{1,0:T(8,128)(2,1)} collective-permute-done((bf16[256,2176]{1,0:T(8,128)(2,1)}, bf16[256,2176]{1,0:T(8,128)(2,1)}, u32[]{:S(2)}, u32[]{:S(2)}) %collective-permute-start) | collective-permute-done | bytes 1114144 | tf_op jit(solution)/shard_map/ppermute | solution.py:41
  418.9 10.7 %shard_map.263 = (bf16[256,4096]{1,0:T(8,128)(2,1)S(1)}, bf16[256,4096]{1,0:T(8,128)(2,1)S(1)}) custom-call(bf16[256,2176]{1,0:T(8,128)(2,1)S(1)} %pad_maximum_fusion.4.left_ref, bf16[2176,4096]{1,0:T(8,128)(2,1)} %get-tuple-element.88.right_ref), custom_call_target="tpu_custom_call" | custom-call | flops 4563402752 | bytes 40960000 | tf_op jit(solution)/shard_map/pallas_call | solution.py:446
  430.9 9.7 %shard_map.264 = bf16[256,2176]{1,0:T(8,128)(2,1)S(1)} custom-call(bf16[256,4096]{1,0:T(8,128)(2,1)S(1)} %get-tuple-element.101.left_ref.refs_3_, bf16[4096,2176]{1,0:T(8,128)(2,1)} %get-tuple-element.90.right_ref), custom_call_target="tpu_custom_call" | custom-call | flops 4563402752 | bytes 38862848 | tf_op jit(solution)/shard_map/pallas_call | solution.py:446
  445.0 21.9 %collective-permute-done.1 = bf16[256,2176]{1,0:T(8,128)(2,1)S(1)} collective-permute-done((bf16[256,2176]{1,0:T(8,128)(2,1)S(1)}, bf16[256,2176]{1,0:T(8,128)(2,1)S(1)}, u32[]{:S(2)}, u32[]{:S(2)}) %collective-permute-start.1) | collective-permute-done | bytes 1114144 | tf_op jit(solution)/shard_map/ppermute | solution.py:41
  470.5 10.7 %shard_map.269 = (bf16[256,4096]{1,0:T(8,128)(2,1)S(1)}, bf16[256,4096]{1,0:T(8,128)(2,1)S(1)}) custom-call(bf16[256,2176]{1,0:T(8,128)(2,1)S(1)} %pad_maximum_fusion.6.left_ref, bf16[2176,4096]{1,0:T(8,128)(2,1)} %get-tuple-element.88.right_ref), custom_call_target="tpu_custom_call" | custom-call | flops 4563402752 | bytes 40960000 | tf_op jit(solution)/shard_map/pallas_call | solution.py:446
  482.5 11.0 %shard_map.270 = bf16[256,2176]{1,0:T(8,128)(2,1)} custom-call(bf16[256,4096]{1,0:T(8,128)(2,1)S(1)} %get-tuple-element.113.left_ref.refs_3_, bf16[4096,2176]{1,0:T(8,128)(2,1)} %get-tuple-element.90.right_ref), custom_call_target="tpu_custom_call" | custom-call | flops 4563402752 | bytes 38862848 | tf_op jit(solution)/shard_map/pallas_call | solution.py:446
  498.2 21.0 %collective-permute-done.4 = bf16[256,2176]{1,0:T(8,128)(2,1)} collective-permute-done((bf16[256,2176]{1,0:T(8,128)(2,1)}, bf16[256,2176]{1,0:T(8,128)(2,1)}, u32[]{:S(2)}, u32[]{:S(2)}) %collective-permute-start.4) | collective-permute-done | bytes 1114144 | tf_op jit(solution)/shard_map/ppermute | solution.py:41
  530.4 9.7 %shard_map.271.left_ref.refs_5_ = bf16[256,4096]{1,0:T(8,128)(2,1)S(1)} custom-call(bf16[256,2176]{1,0:T(8,128)(2,1)S(1)} %pad_maximum_fusion.7.left_ref, bf16[4096,2176]{1,0:T(8,128)(2,1)} %get-tuple-element.90.right_ref, bf16[256,4096]{1,0:T(8,128)(2,1)S(1)} %copy-done.40), custom_call_target="tpu_custom_call" | custom-call | flops 4563402752 | bytes 38862848 | tf_op jit(solution)/shard_map/pallas_call | solution.py:446
  540.1 10.5 %shard_map.272 = bf16[256,2176]{1,0:T(8,128)(2,1)S(1)} custom-call(bf16[256,4096]{1,0:T(8,128)(2,1)S(1)} %shard_map.271.left_ref.refs_5_, bf16[2176,4096]{1,0:T(8,128)(2,1)} %get-tuple-element.88.right_ref), custom_call_target="tpu_custom_call" | custom-call | flops 4563402752 | bytes 38862848 | tf_op jit(solution)/shard_map/pallas_call | solution.py:446
  552.8 9.7 %shard_map.265.left_ref.refs_5_ = bf16[256,4096]{1,0:T(8,128)(2,1)S(1)} custom-call(bf16[256,2176]{1,0:T(8,128)(2,1)S(1)} %pad_maximum_fusion.5.left_ref, bf16[4096,2176]{1,0:T(8,128)(2,1)} %get-tuple-element.90.right_ref, bf16[256,4096]{1,0:T(8,128)(2,1)S(1)} %copy-done.38), custom_call_target="tpu_custom_call" | custom-call | flops 4563402752 | bytes 38862848 | tf_op jit(solution)/shard_map/pallas_call | solution.py:446
  562.6 10.0 %shard_map.266 = bf16[256,2176]{1,0:T(8,128)(2,1)S(1)} custom-call(bf16[256,4096]{1,0:T(8,128)(2,1)S(1)} %shard_map.265.left_ref.refs_5_, bf16[2176,4096]{1,0:T(8,128)(2,1)} %get-tuple-element.88.right_ref), custom_call_target="tpu_custom_call" | custom-call | flops 4563402752 | bytes 38862848 | tf_op jit(solution)/shard_map/pallas_call | solution.py:446
  586.0 13.1 %collective-permute-done.2 = bf16[256,2176]{1,0:T(8,128)(2,1)} collective-permute-done((bf16[256,2176]{1,0:T(8,128)(2,1)S(1)}, bf16[256,2176]{1,0:T(8,128)(2,1)}, u32[]{:S(2)}, u32[]{:S(2)}) %collective-permute-start.2) | collective-permute-done | bytes 1114144 | tf_op jit(solution)/shard_map/ppermute | solution.py:41
  606.0 13.9 %shard_map.274 = (bf16[1,256,1024]{2,1,0:T(8,128)(2,1)S(1)}, bf16[2,1,256,1024]{3,2,1,0:T(8,128)(2,1)S(1)}, bf16[2,1,256,1024]{3,2,1,0:T(8,128)(2,1)S(1)}, bf16[...) custom-call(bf16[1,256,1024]{2,1,0:T(8,128)(2,1)S(1)} %copy-done.65, f32[1,1024,128]{2,1,0:T(8,128)S(1)} %copy-done.61, ...), custom_call_target="tpu_custom_call" | custom-call | flops 10737418240 | bytes 9961472 | tf_op jit(solution)/shard_map/pallas_call | solution.py:167
  639.7 13.4 %shard_map.279 = (bf16[1,256,1024]{2,1,0:T(8,128)(2,1)S(1)}, bf16[2,1,256,1024]{3,2,1,0:T(8,128)(2,1)S(1)}, bf16[2,1,256,1024]{3,2,1,0:T(8,128)(2,1)S(1)}, bf16[...) custom-call(bf16[1,256,1024]{2,1,0:T(8,128)(2,1)S(1)} %copy-done.63, f32[1,1024,128]{2,1,0:T(8,128)S(1)} %copy-done.59, ...), custom_call_target="tpu_custom_call" | custom-call | flops 10737418240 | bytes 9961472 | tf_op jit(solution)/shard_map/pallas_call | solution.py:167
  680.6 9.5 %collective-permute-done.23 = bf16[2,1,256,1024]{3,2,1,0:T(8,128)(2,1)S(1)} collective-permute-done((bf16[2,1,256,1024]{3,2,1,0:T(8,128)(2,1)S(1)}, bf16[2,1,256,1024]{3,2,1,0:T(8,128)(2,1)S(1)}, u32[]{:S(2)}, u32[]{:S(2)}) %collective-permute-start.23) | collective-permute-done | bytes 1048608 | tf_op jit(solution)/shard_map/ppermute | solution.py:41
  703.4 28.5 %collective-permute-done.27 = bf16[2,1,256,1024]{3,2,1,0:T(8,128)(2,1)S(1)} collective-permute-done((bf16[2,1,256,1024]{3,2,1,0:T(8,128)(2,1)S(1)}, bf16[2,1,256,1024]{3,2,1,0:T(8,128)(2,1)S(1)}, u32[]{:S(2)}, u32[]{:S(2)}) %collective-permute-start.27) | collective-permute-done | bytes 1048608 | tf_op jit(solution)/shard_map/ppermute | solution.py:41
  746.7 12.7 %collective-permute-done.24 = bf16[256,2432]{1,0:T(8,128)(2,1)S(1)} collective-permute-done((bf16[256,2432]{1,0:T(8,128)(2,1)S(1)}, bf16[256,2432]{1,0:T(8,128)(2,1)S(1)}, u32[]{:S(2)}, u32[]{:S(2)}) %collective-permute-start.24) | collective-permute-done | bytes 1245216 | tf_op jit(solution)/shard_map/ppermute | solution.py:41
  765.3 20.8 %collective-permute-done.28 = bf16[256,2432]{1,0:T(8,128)(2,1)S(1)} collective-permute-done((bf16[256,2432]{1,0:T(8,128)(2,1)S(1)}, bf16[256,2432]{1,0:T(8,128)(2,1)S(1)}, u32[]{:S(2)}, u32[]{:S(2)}) %collective-permute-start.28) | collective-permute-done | bytes 1245216 | tf_op jit(solution)/shard_map/ppermute | solution.py:41
  809.4 8.9 %collective-permute-start.38 = (bf16[32,2304]{1,0:T(8,128)(2,1)S(1)}, bf16[32,2304]{1,0:T(8,128)(2,1)S(1)}, u32[]{:S(2)}, u32[]{:S(2)}) collective-permute-start(bf16[32,2304]{1,0:T(8,128)(2,1)S(1)} %add_convert_fusion.9), channel_id=1, source_target_pairs={{0,8},{8,16},{16,24},{24,0},{1,9},{9,17},{17,25},{25,1},{2,10},{10... | collective-permute-start | bytes 442376 | tf_op jit(solution)/shard_map/ppermute | solution.py:36
  824.5 10.2 %collective-permute-start.33 = (bf16[1,64,2048]{2,1,0:T(8,128)(2,1)S(1)}, bf16[1,64,2048]{2,1,0:T(8,128)(2,1)S(1)}, u32[]{:S(2)}, u32[]{:S(2)}) collective-permute-start(bf16[1,64,2048]{2,1,0:T(8,128)(2,1)S(1)} %get-tuple-element.187), channel_id=1, source_target_pairs={{0,16},{8,24},{16,0},{24,8},{1,17},{9,25},{17,1},{25,9},{2,18},{10... | collective-permute-start | bytes 786440 | tf_op jit(solution)/shard_map/ppermute | solution.py:36
  837.7 13.3 %collective-permute-done.41.refs_1_ = bf16[4,32,2304]{2,1,0:T(8,128)(2,1)S(1)} collective-permute-done((bf16[4,32,2304]{2,1,0:T(8,128)(2,1)S(1)}, bf16[4,32,2304]{2,1,0:T(8,128)(2,1)S(1)}, u32[]{:S(2)}, u32[]{:S(2)}) %collective-permute-start.41) | collective-permute-done | bytes 589856 | tf_op jit(solution)/shard_map/ppermute | solution.py:41
  (500 shorter events, 218.2 us)
Async XLA Ops:
  363.1 79.2 %collective-permute-start.3 = (bf16[256,2176]{1,0:T(8,128)(2,1)}, bf16[256,2176]{1,0:T(8,128)(2,1)}, u32[]{:S(2)}, u32[]{:S(2)}) collective-permute-start(bf16[256,2176]{1,0:T(8,128)(2,1)} %shard_map.268), channel_id=1, source_target_pairs={{0,1},{1,0},{2,3},{3,2},{4,5},{5,4},{6,7},{7,6},{8,9},{9,8},{10,11... | collective-permute-start | bytes 3342344 | tf_op jit(solution)/shard_map/ppermute | solution.py:41
  380.4 33.8 %collective-permute-start = (bf16[256,2176]{1,0:T(8,128)(2,1)}, bf16[256,2176]{1,0:T(8,128)(2,1)}, u32[]{:S(2)}, u32[]{:S(2)}) collective-permute-start(bf16[256,2176]{1,0:T(8,128)(2,1)} %shard_map.262), channel_id=1, source_target_pairs={{0,1},{1,0},{2,3},{3,2},{4,5},{5,4},{6,7},{7,6},{8,9},{9,8},{10,11... | collective-permute-start | bytes 3342344 | tf_op jit(solution)/shard_map/ppermute | solution.py:41
  440.7 26.2 %collective-permute-start.1 = (bf16[256,2176]{1,0:T(8,128)(2,1)S(1)}, bf16[256,2176]{1,0:T(8,128)(2,1)S(1)}, u32[]{:S(2)}, u32[]{:S(2)}) collective-permute-start(bf16[256,2176]{1,0:T(8,128)(2,1)S(1)} %shard_map.264), channel_id=1, source_target_pairs={{0,1},{1,0},{2,3},{3,2},{4,5},{5,4},{6,7},{7,6},{8,9},{9,8},{10,11... | collective-permute-start | bytes 3342344 | tf_op jit(solution)/shard_map/ppermute | solution.py:41
  493.5 25.6 %collective-permute-start.4 = (bf16[256,2176]{1,0:T(8,128)(2,1)}, bf16[256,2176]{1,0:T(8,128)(2,1)}, u32[]{:S(2)}, u32[]{:S(2)}) collective-permute-start(bf16[256,2176]{1,0:T(8,128)(2,1)} %shard_map.270), channel_id=1, source_target_pairs={{0,1},{1,0},{2,3},{3,2},{4,5},{5,4},{6,7},{7,6},{8,9},{9,8},{10,11... | collective-permute-start | bytes 3342344 | tf_op jit(solution)/shard_map/ppermute | solution.py:41
  550.7 26.7 %collective-permute-start.5 = (bf16[256,2176]{1,0:T(8,128)(2,1)S(1)}, bf16[256,2176]{1,0:T(8,128)(2,1)}, u32[]{:S(2)}, u32[]{:S(2)}) collective-permute-start(bf16[256,2176]{1,0:T(8,128)(2,1)S(1)} %shard_map.272), channel_id=1, source_target_pairs={{0,1},{1,0},{2,3},{3,2},{4,5},{5,4},{6,7},{7,6},{8,9},{9,8},{10,11... | collective-permute-start | bytes 3342344 | tf_op jit(solution)/shard_map/ppermute | solution.py:41
  572.6 26.5 %collective-permute-start.2 = (bf16[256,2176]{1,0:T(8,128)(2,1)S(1)}, bf16[256,2176]{1,0:T(8,128)(2,1)}, u32[]{:S(2)}, u32[]{:S(2)}) collective-permute-start(bf16[256,2176]{1,0:T(8,128)(2,1)S(1)} %shard_map.266), channel_id=1, source_target_pairs={{0,1},{1,0},{2,3},{3,2},{4,5},{5,4},{6,7},{7,6},{8,9},{9,8},{10,11... | collective-permute-start | bytes 3342344 | tf_op jit(solution)/shard_map/ppermute | solution.py:41
  633.0 46.1 %collective-permute-start.21 = (bf16[2,1,256,1024]{3,2,1,0:T(8,128)(2,1)}, bf16[2,1,256,1024]{3,2,1,0:T(8,128)(2,1)}, u32[]{:S(2)}, u32[]{:S(2)}) collective-permute-start(bf16[2,1,256,1024]{3,2,1,0:T(8,128)(2,1)} %get-tuple-element.123), channel_id=1, source_target_pairs={{0,2},{2,0},{4,6},{6,4},{1,3},{3,1},{5,7},{7,5},{8,10},{10,8},{12,... | collective-permute-start | bytes 3145736 | tf_op jit(solution)/shard_map/ppermute | solution.py:41
  653.1 25.5 %collective-permute-start.26 = (bf16[2,1,256,1024]{3,2,1,0:T(8,128)(2,1)S(1)}, bf16[2,1,256,1024]{3,2,1,0:T(8,128)(2,1)S(1)}, u32[]{:S(2)}, u32[]{:S(2)}) collective-permute-start(bf16[2,1,256,1024]{3,2,1,0:T(8,128)(2,1)S(1)} %get-tuple-element.139), channel_id=1, source_target_pairs={{0,2},{2,0},{4,6},{6,4},{1,3},{3,1},{5,7},{7,5},{8,10},{10,8},{12,... | collective-permute-start | bytes 3145736 | tf_op jit(solution)/shard_map/ppermute | solution.py:41
  653.5 23.2 %collective-permute-start.11 = (bf16[32,3840]{1,0:T(8,128)(2,1)S(1)}, bf16[32,3840]{1,0:T(8,128)(2,1)S(1)}, u32[]{:S(2)}, u32[]{:S(2)}) collective-permute-start(bf16[32,3840]{1,0:T(8,128)(2,1)S(1)} %add_convert_fusion.8), channel_id=1, source_target_pairs={{0,24},{8,0},{16,8},{24,16},{1,25},{9,1},{17,9},{25,17},{2,26},{10... | collective-permute-start | bytes 737288 | tf_op jit(solution)/shard_map/ppermute | solution.py:36
  664.1 26.1 %collective-permute-start.23 = (bf16[2,1,256,1024]{3,2,1,0:T(8,128)(2,1)S(1)}, bf16[2,1,256,1024]{3,2,1,0:T(8,128)(2,1)S(1)}, u32[]{:S(2)}, u32[]{:S(2)}) collective-permute-start(bf16[2,1,256,1024]{3,2,1,0:T(8,128)(2,1)S(1)} %add_convert_fusion.4), channel_id=1, source_target_pairs={{0,4},{2,6},{4,0},{6,2},{1,5},{3,7},{5,1},{7,3},{8,12},{10,14},{12... | collective-permute-start | bytes 3145736 | tf_op jit(solution)/shard_map/ppermute | solution.py:41
  673.7 60.5 %collective-permute-start.15 = (bf16[1,64,2048]{2,1,0:T(8,128)(2,1)}, bf16[1,64,2048]{2,1,0:T(8,128)(2,1)S(1)}, u32[]{:S(2)}, u32[]{:S(2)}) collective-permute-start(bf16[1,64,2048]{2,1,0:T(8,128)(2,1)} %get-tuple-element.202), channel_id=1, source_target_pairs={{0,24},{8,0},{16,8},{24,16},{1,25},{9,1},{17,9},{25,17},{2,26},{10... | collective-permute-start | bytes 786440 | tf_op jit(solution)/shard_map/ppermute | solution.py:36
  676.7 58.3 %collective-permute-start.16 = (bf16[1,64,2048]{2,1,0:T(8,128)(2,1)}, bf16[1,64,2048]{2,1,0:T(8,128)(2,1)S(1)}, u32[]{:S(2)}, u32[]{:S(2)}) collective-permute-start(bf16[1,64,2048]{2,1,0:T(8,128)(2,1)} %get-tuple-element.201), channel_id=1, source_target_pairs={{0,16},{8,24},{16,0},{24,8},{1,17},{9,25},{17,1},{25,9},{2,18},{10... | collective-permute-start | bytes 786440 | tf_op jit(solution)/shard_map/ppermute | solution.py:36
  678.6 24.7 %collective-permute-start.25 = (bf16[2,1,256,1024]{3,2,1,0:T(8,128)(2,1)S(1)}, bf16[2,1,256,1024]{3,2,1,0:T(8,128)(2,1)S(1)}, u32[]{:S(2)}, u32[]{:S(2)}) collective-permute-start(bf16[2,1,256,1024]{3,2,1,0:T(8,128)(2,1)S(1)} %get-tuple-element.137), channel_id=1, source_target_pairs={{0,2},{2,0},{4,6},{6,4},{1,3},{3,1},{5,7},{7,5},{8,10},{10,8},{12,... | collective-permute-start | bytes 3145736 | tf_op jit(solution)/shard_map/ppermute | solution.py:41
  679.1 56.0 %collective-permute-start.12 = (bf16[4,32,3840]{2,1,0:T(8,128)(2,1)S(1)}, bf16[4,32,3840]{2,1,0:T(8,128)(2,1)S(1)}, u32[]{:S(2)}, u32[]{:S(2)}) collective-permute-start(bf16[4,32,3840]{2,1,0:T(8,128)(2,1)S(1)} %pad_maximum_fusion.10.refs_0_), channel_id=1, source_target_pairs={{0,4},{2,6},{4,0},{6,2},{1,5},{3,7},{5,1},{7,3},{8,12},{10,14},{12... | collective-permute-start | bytes 2949128 | tf_op jit(solution)/shard_map/ppermute | solution.py:41
  690.2 41.7 %collective-permute-start.27 = (bf16[2,1,256,1024]{3,2,1,0:T(8,128)(2,1)S(1)}, bf16[2,1,256,1024]{3,2,1,0:T(8,128)(2,1)S(1)}, u32[]{:S(2)}, u32[]{:S(2)}) collective-permute-start(bf16[2,1,256,1024]{3,2,1,0:T(8,128)(2,1)S(1)} %add_convert_fusion.1), channel_id=1, source_target_pairs={{0,4},{2,6},{4,0},{6,2},{1,5},{3,7},{5,1},{7,3},{8,12},{10,14},{12... | collective-permute-start | bytes 3145736 | tf_op jit(solution)/shard_map/ppermute | solution.py:41
  703.3 41.2 %collective-permute-start.17 = (bf16[1,64,2048]{2,1,0:T(8,128)(2,1)}, bf16[1,64,2048]{2,1,0:T(8,128)(2,1)S(1)}, u32[]{:S(2)}, u32[]{:S(2)}) collective-permute-start(bf16[1,64,2048]{2,1,0:T(8,128)(2,1)} %get-tuple-element.200), channel_id=1, source_target_pairs={{0,8},{8,16},{16,24},{24,0},{1,9},{9,17},{17,25},{25,1},{2,10},{10... | collective-permute-start | bytes 786440 | tf_op jit(solution)/shard_map/ppermute | solution.py:36
  731.9 27.5 %collective-permute-start.24 = (bf16[256,2432]{1,0:T(8,128)(2,1)S(1)}, bf16[256,2432]{1,0:T(8,128)(2,1)S(1)}, u32[]{:S(2)}, u32[]{:S(2)}) collective-permute-start(bf16[256,2432]{1,0:T(8,128)(2,1)S(1)} %shard_map.277), channel_id=1, source_target_pairs={{0,1},{1,0},{2,3},{3,2},{4,5},{5,4},{6,7},{7,6},{8,9},{9,8},{10,11... | collective-permute-start | bytes 3735560 | tf_op jit(solution)/shard_map/ppermute | solution.py:41
  735.0 30.1 %collective-permute-start.13 = (bf16[4,32,3840]{2,1,0:T(8,128)(2,1)S(1)}, bf16[4,32,3840]{2,1,0:T(8,128)(2,1)S(1)}, u32[]{:S(2)}, u32[]{:S(2)}) collective-permute-start(bf16[4,32,3840]{2,1,0:T(8,128)(2,1)S(1)} %pad_maximum_fusion.10.refs_0_), channel_id=1, source_target_pairs={{0,2},{2,0},{4,6},{6,4},{1,3},{3,1},{5,7},{7,5},{8,10},{10,8},{12,... | collective-permute-start | bytes 2949128 | tf_op jit(solution)/shard_map/ppermute | solution.py:41
  735.1 30.0 %collective-permute-start.14 = (bf16[4,32,3840]{2,1,0:T(8,128)(2,1)S(1)}, bf16[4,32,3840]{2,1,0:T(8,128)(2,1)S(1)}, u32[]{:S(2)}, u32[]{:S(2)}) collective-permute-start(bf16[4,32,3840]{2,1,0:T(8,128)(2,1)S(1)} %collective-permute-done.12.refs_1_), channel_id=1, source_target_pairs={{0,2},{2,0},{4,6},{6,4},{1,3},{3,1},{5,7},{7,5},{8,10},{10,8},{12,... | collective-permute-start | bytes 2949128 | tf_op jit(solution)/shard_map/ppermute | solution.py:41
  759.4 26.7 %collective-permute-start.28 = (bf16[256,2432]{1,0:T(8,128)(2,1)S(1)}, bf16[256,2432]{1,0:T(8,128)(2,1)S(1)}, u32[]{:S(2)}, u32[]{:S(2)}) collective-permute-start(bf16[256,2432]{1,0:T(8,128)(2,1)S(1)} %shard_map.280), channel_id=1, source_target_pairs={{0,1},{1,0},{2,3},{3,2},{4,5},{5,4},{6,7},{7,6},{8,9},{9,8},{10,11... | collective-permute-start | bytes 3735560 | tf_op jit(solution)/shard_map/ppermute | solution.py:41
  793.2 31.3 %collective-permute-start.30 = (bf16[1,64,2048]{2,1,0:T(8,128)(2,1)S(1)}, bf16[1,64,2048]{2,1,0:T(8,128)(2,1)S(1)}, u32[]{:S(2)}, u32[]{:S(2)}) collective-permute-start(bf16[1,64,2048]{2,1,0:T(8,128)(2,1)S(1)} %get-tuple-element.190), channel_id=1, source_target_pairs={{0,16},{8,24},{16,0},{24,8},{1,17},{9,25},{17,1},{25,9},{2,18},{10... | collective-permute-start | bytes 786440 | tf_op jit(solution)/shard_map/ppermute | solution.py:36
  794.2 43.4 %collective-permute-start.31 = (bf16[1,64,2048]{2,1,0:T(8,128)(2,1)S(1)}, bf16[1,64,2048]{2,1,0:T(8,128)(2,1)S(1)}, u32[]{:S(2)}, u32[]{:S(2)}) collective-permute-start(bf16[1,64,2048]{2,1,0:T(8,128)(2,1)S(1)} %get-tuple-element.189), channel_id=1, source_target_pairs={{0,8},{8,16},{16,24},{24,0},{1,9},{9,17},{17,25},{25,1},{2,10},{10... | collective-permute-start | bytes 786440 | tf_op jit(solution)/shard_map/ppermute | solution.py:36
  801.2 49.8 %collective-permute-start.32 = (bf16[1,64,2048]{2,1,0:T(8,128)(2,1)S(1)}, bf16[1,64,2048]{2,1,0:T(8,128)(2,1)S(1)}, u32[]{:S(2)}, u32[]{:S(2)}) collective-permute-start(bf16[1,64,2048]{2,1,0:T(8,128)(2,1)S(1)} %get-tuple-element.188), channel_id=1, source_target_pairs={{0,24},{8,0},{16,8},{24,16},{1,25},{9,1},{17,9},{25,17},{2,26},{10... | collective-permute-start | bytes 786440 | tf_op jit(solution)/shard_map/ppermute | solution.py:36
  824.5 27.9 %collective-permute-start.33 = (bf16[1,64,2048]{2,1,0:T(8,128)(2,1)S(1)}, bf16[1,64,2048]{2,1,0:T(8,128)(2,1)S(1)}, u32[]{:S(2)}, u32[]{:S(2)}) collective-permute-start(bf16[1,64,2048]{2,1,0:T(8,128)(2,1)S(1)} %get-tuple-element.187), channel_id=1, source_target_pairs={{0,16},{8,24},{16,0},{24,8},{1,17},{9,25},{17,1},{25,9},{2,18},{10... | collective-permute-start | bytes 786440 | tf_op jit(solution)/shard_map/ppermute | solution.py:36
  (157 other events, 2971.1 us)

commit v4 on v3

--- a/solution.py
+++ b/solution.py
@@ -73,112 +73,53 @@
     return pieces[0]
 
 
-def both(low):
+def both_in_turn(parts):
+    lows, got = list(parts), None
     for mask in masks_of(lax.axis_size("tp")):
-        total = low.astype(F32) + swap(low, "tp", mask).astype(F32)
-        low = total.astype(BF16)
-    return total
-
-
-def attend_kernel(n_piece, q_ref, bias_ref, *refs):
-    kv_refs, (out_ref, log_ref) = refs[:n_piece], refs[n_piece:]
-    query = q_ref[0]
-    loc = query.shape[0]
-    scores = []
-    for j in range(n_piece):
-        bias = bias_ref[0, pl.ds(j * loc, loc), :]
-        bias = jnp.concatenate([bias] * (loc // 128), axis=1)
-        scores.append(dot_nt(kv_refs[j][0, 0], query) * SCALE + bias)
+        got = [swap(low, "tp", mask) for low in lows]
+        for g in range(len(lows) - 1):
+            got[g] = after(got[g], *lows[g + 1 :])
+        totals = [low.astype(F32) + other.astype(F32) for low, other in zip(lows, got)]
+        lows = [total.astype(BF16) for total in totals]
+    return totals
+
+
+def attend_head(query, keys, values, biases):
+    scores = [dot_nt(k, query) * SCALE + bias for k, bias in zip(keys, biases)]
     top = scores[0].max(axis=0, keepdims=True)
     for s in scores[1:]:
         top = jnp.maximum(top, s.max(axis=0, keepdims=True))
     total = jnp.zeros_like(top)
     mixed = None
-    for j in range(n_piece):
-        probs = jnp.exp(scores[j] - top)
+    for s, v in zip(scores, values):
+        probs = jnp.exp(s - top)
         total = total + probs.sum(axis=0, keepdims=True)
-        term = dot_tn(kv_refs[j][1, 0], probs.astype(BF16))
+        term = dot_tn(v, probs.astype(BF16))
         mixed = term if mixed is None else mixed + term
-    out_ref[0] = (mixed / total).T.astype(BF16)
-    log_ref[0, 0] = top + jnp.log(total)
-
-
-def attend_back_kernel(n_piece, q_ref, bias_ref, g_ref, log_ref, *refs):
-    kv_refs, dq_ref, dkv_refs = refs[:n_piece], refs[n_piece], refs[n_piece + 1 :]
-    query = q_ref[0]
-    grad = g_ref[0]
-    log_total = log_ref[0, 0]
-    loc = query.shape[0]
-    probs, dprobs = [], []
+    return (mixed / total).T.astype(BF16), top + jnp.log(total)
+
+
+def attend_back_head(query, grad, log_total, keys, values, biases):
+    probs, dprobs, dvalues = [], [], []
     delta = jnp.zeros_like(log_total)
-    for j in range(n_piece):
-        bias = bias_ref[0, pl.ds(j * loc, loc), :]
-        bias = jnp.concatenate([bias] * (loc // 128), axis=1)
-        p = jnp.exp(dot_nt(kv_refs[j][0, 0], query) * SCALE + bias - log_total)
-        dp = dot_nt(kv_refs[j][1, 0], grad)
-        dkv_refs[j][1, 0] = dot(p.astype(BF16), grad).astype(BF16)
+    for k, v, bias in zip(keys, values, biases):
+        p = jnp.exp(dot_nt(k, query) * SCALE + bias - log_total)
+        dp = dot_nt(v, grad)
+        dvalues.append(dot(p.astype(BF16), grad).astype(BF16))
         delta = delta + (p * dp).sum(axis=0, keepdims=True)
         probs.append(p)
         dprobs.append(dp)
-    dq = None
-    for j in range(n_piece):
-        ds = (probs[j] * (dprobs[j] - delta)).astype(BF16)
-        dkv_refs[j][0, 0] = (dot(ds, query) * SCALE).astype(BF16)
-        term = dot_tn(kv_refs[j][0, 0], ds)
-        dq = term if dq is None else dq + term
-    dq_ref[0] = (dq * SCALE).T.astype(BF16)
-
-
-def attend_specs(n_seq, loc, n_piece, first):
-    row = pl.BlockSpec((1, loc, HEAD_DIM), lambda s, h: (s, 0, h))
-    bias = pl.BlockSpec((1, n_piece * loc, 128), lambda s, h: (s, 0, 0))
-    pair = pl.BlockSpec((2, 1, loc, HEAD_DIM), lambda s, h: (0, s + first, 0, h))
-    grads = pl.BlockSpec((2, 1, loc, HEAD_DIM), lambda s, h: (0, s, 0, h))
-    log = pl.BlockSpec((1, 1, 1, loc), lambda s, h: (s, h, 0, 0))
-    return row, bias, pair, log, grads
-
-
-def attend(query, kv, bias, first):
-    n_seq, loc, width = query.shape
-    n_piece, heads = len(kv), width // HEAD_DIM
-    row, bias_spec, pair, log, grads = attend_specs(n_seq, loc, n_piece, first)
-    return pl.pallas_call(
-        lambda *refs: attend_kernel(n_piece, *refs),
-        grid=(n_seq, heads),
-        in_specs=[row, bias_spec] + [pair] * n_piece,
-        out_specs=[row, log],
-        out_shape=[
-            jax.ShapeDtypeStruct(query.shape, BF16),
-            jax.ShapeDtypeStruct((n_seq, heads, 1, loc), F32),
-        ],
-        compiler_params=pltpu.CompilerParams(vmem_limit_bytes=32 << 20),
-        cost_estimate=pl.CostEstimate(
-            flops=n_seq * heads * 4 * loc * loc * n_piece * HEAD_DIM * 4,
-            bytes_accessed=2 * n_seq * loc * width * (2 + 2 * n_piece),
-            transcendentals=n_seq * heads * loc * loc * n_piece,
-        ),
-    )(query, bias, *kv)
-
-
-def attend_back(query, kv, bias, grad, log_total, first):
-    n_seq, loc, width = query.shape
-    n_piece, heads = len(kv), width // HEAD_DIM
-    row, bias_spec, pair, log, grads = attend_specs(n_seq, loc, n_piece, first)
-    out = pl.pallas_call(
-        lambda *refs: attend_back_kernel(n_piece, *refs),
-        grid=(n_seq, heads),
-        in_specs=[row, bias_spec, row, log] + [pair] * n_piece,
-        out_specs=[row] + [grads] * n_piece,
-        out_shape=[jax.ShapeDtypeStruct(query.shape, BF16)]
-        + [jax.ShapeDtypeStruct((2, n_seq, loc, width), BF16)] * n_piece,
-        compiler_params=pltpu.CompilerParams(vmem_limit_bytes=40 << 20),
-        cost_estimate=pl.CostEstimate(
-            flops=n_seq * heads * 10 * loc * loc * n_piece * HEAD_DIM * 4,
-            bytes_accessed=2 * n_seq * loc * width * (3 + 4 * n_piece),
-            transcendentals=n_seq * heads * loc * loc * n_piece,
-        ),
-    )(query, bias, grad, log_total, *kv)
-    return out[0], list(out[1:])
+    dquery, dkeys = None, []
+    for k, p, dp in zip(keys, probs, dprobs):
+        ds = (p * (dp - delta)).astype(BF16)
+        dkeys.append((dot(ds, query) * SCALE).astype(BF16))
+        term = dot_tn(k, ds)
+        dquery = term if dquery is None else dquery + term
+    return (dquery * SCALE).T.astype(BF16), dkeys, dvalues
+
+
+def ds(start, size):
+    return pl.ds(pl.multiple_of(start, size), size)
 
 
 def flip(ct, offset):
@@ -216,10 +157,12 @@
         self.offsets = offsets(n_ctx)
         self.came, self.waiting = {}, {}
 
-    def greet(self):
+    def greet(self, tp=False):
         barrier = pltpu.get_barrier_semaphore()
         others = [{"fsdp": lax.rem(self.z + s, self.n_fsdp)} for s in range(1, self.n_fsdp)]
         others += [{"ctx": flip(self.ct, mask)} for mask in self.masks]
+        if tp:
+            others.append({"tp": 1 - lax.axis_index("tp")})
         for other in others:
             pl.semaphore_signal(
                 barrier, inc=1, device_id=other, device_id_type=pl.DeviceIdType.MESH
@@ -404,6 +347,313 @@
     )(*inputs)
 
 
+def forward_and_gather(query, kv_own, bias, shards, maps, n_fsdp, n_ctx):
+    per, loc, width_here = query.shape
+    cot, w_out, w_up, w_down = shards
+    piece, width = cot.shape[1:]
+    heads, units = width_here // HEAD_DIM, w_up.shape[1]
+    zu, zo = w_up.shape[0], w_out.shape[1]
+    so, su, sd = w_out.shape[0] // n_ctx, zu // n_ctx, w_down.shape[0] // n_ctx
+    wide = width + NR
+    stay_shapes = [(piece, width)] * per + [x.shape for x in (w_out, w_up, w_down) + maps]
+    n_stay = len(stay_shapes)
+    halves = 2
+    n_copy = (n_fsdp - 1) * n_ctx * (1 + 2 * halves) + per * (n_fsdp - 1 + n_ctx - 1 + 1)
+
+    def kernel(*refs):
+        q_ref, bias_ref, kv_ref, cot_ref, wo_ref, wu_ref, wd_ref, ao_ref, bu_ref, ad_ref = refs[:10]
+        slots = refs[10 : 9 + n_ctx]
+        rows_ref, out_ref, up_ref, down_ref, ctx_ref, log_ref, part_ref, other_ref = refs[
+            9 + n_ctx : 17 + n_ctx
+        ]
+        send, recv, here, load, kv_room, out_room = refs[17 + n_ctx : 23 + n_ctx]
+        room = refs[23 + n_ctx :]
+        mover = Mover(n_fsdp, n_ctx, send, recv)
+        z = mover.z
+
+        def deal(g):
+            return Deal(lambda to: cot_ref.at[to * per + g], lambda s: rows_ref.at[g, s])
+
+        def pair(g):
+            return Pair(lambda k: kv_ref.at[:, g] if k == 0 else slots[k - 1].at[:, g])
+
+        out_item = Weight(
+            lambda c: wo_ref.at[ds(c * so, so)],
+            lambda o, c: out_ref.at[ds(c * so, so), ds(o * zo, zo)],
+        )
+
+        def up_item(h):
+            columns = pl.ds(h * (units // halves), units // halves)
+            return Weight(
+                lambda c: wu_ref.at[ds(c * su, su), columns],
+                lambda o, c: up_ref.at[ds(o * zu + c * su, su), columns],
+            )
+
+        def down_item(h):
+            size = sd // halves
+            return Weight(
+                lambda c: wd_ref.at[ds(c * sd + h * size, size)],
+                lambda o, c: down_ref.at[ds(c * sd + h * size, size), ds(o * zo, zo)],
+            )
+
+        pairs = [pair(g) for g in range(per)]
+        items = [out_item] + [up_item(h) for h in range(halves)]
+        items += [down_item(h) for h in range(halves)] + [deal(g) for g in range(per)]
+        stay = [(cot_ref.at[z * per + g], rows_ref.at[g, 0]) for g in range(per)]
+        stay += [
+            (wo_ref, out_ref.at[:, ds(z * zo, zo)]),
+            (wu_ref, up_ref.at[ds(z * zu, zu)]),
+            (wd_ref, down_ref.at[:, ds(z * zo, zo)]),
+            (ao_ref, out_ref.at[:, pl.ds(width, NR)]),
+            (bu_ref, up_ref.at[pl.ds(width, NR)]),
+            (ad_ref, down_ref.at[:, pl.ds(width, NR)]),
+        ]
+
+        def attend(g):
+            for level in range(len(mover.masks)):
+                mover.finish(pairs[g], level)
+            loads = []
+            for k in range(n_ctx):
+                copy = pltpu.make_async_copy(pairs[g].slot_at(k), kv_room.at[k], load.at[k])
+                copy.start()
+                loads.append(copy)
+            for copy in loads:
+                copy.wait()
+
+            def one(h, carry):
+                at = ds(h * HEAD_DIM, HEAD_DIM)
+                biases = []
+                for k in range(n_ctx):
+                    block = bias_ref[g, k * loc : (k + 1) * loc, :]
+                    biases.append(jnp.concatenate([block] * (loc // 128), axis=1))
+                context, log = attend_head(
+                    q_ref[g, :, at],
+                    [kv_room[k, 0, :, at] for k in range(n_ctx)],
+                    [kv_room[k, 1, :, at] for k in range(n_ctx)],
+                    biases,
+                )
+                ctx_ref[g, :, at] = context
+                log_ref[g, h] = log
+                return carry
+
+            lax.fori_loop(0, heads, one, 0)
+
+        def project():
+            copy = pltpu.make_async_copy(out_ref, out_room, load.at[n_ctx])
+            copy.start()
+            copy.wait()
+            for g in range(per):
+                for start in range(0, wide, 1024):
+                    at = slice(start, min(start + 1024, wide))
+                    part_ref[g, :, at] = dot(ctx_ref[g], out_room[:, at]).astype(BF16)
+                swapped.append(
+                    mover.go(
+                        part_ref.at[g], other_ref.at[g], {"tp": 1 - lax.axis_index("tp")}
+                    )
+                )
+
+        swapped = []
+        tasks = {i: (lambda g=i: attend(g)) for i in range(per)}
+        tasks[per] = project
+        mover.greet(tp=True)
+        for item in pairs + items[:2]:
+            mover.begin(item)
+        kept = keep(stay, room, here)
+        levels = len(mover.masks)
+        for i in range(len(items) + levels):
+            if i < len(items):
+                mover.relay(items[i])
+                if i + 2 < len(items):
+                    mover.begin(items[i + 2])
+            if i == 0:
+                for first, second in kept:
+                    first.wait()
+                    second.start()
+            for level in range(levels):
+                if 0 <= i - 1 - level < len(items):
+                    mover.finish(items[i - 1 - level], level)
+            if i == per:
+                for _, second in kept:
+                    second.wait()
+            if i in tasks:
+                tasks[i]()
+        for copy in swapped:
+            copy.wait_recv()
+        mover.close()
+
+    row = (per, loc, width_here)
+    vmem, anywhere = pl.BlockSpec(memory_space=pltpu.VMEM), pl.BlockSpec(memory_space=pl.ANY)
+    outputs = [(kv_own.shape, BF16, anywhere)] * (n_ctx - 1) + [
+        ((per, n_fsdp, piece, width), BF16, anywhere),
+        ((width_here, wide), BF16, anywhere),
+        ((wide, units), BF16, anywhere),
+        ((units, wide), BF16, anywhere),
+        (row, BF16, vmem),
+        ((per, heads, 1, loc), F32, vmem),
+        ((per, loc, wide), BF16, vmem),
+        ((per, loc, wide), BF16, anywhere),
+    ]
+    return pl.pallas_call(
+        kernel,
+        in_specs=[vmem, vmem] + [anywhere] * 8,
+        out_specs=[space for _, _, space in outputs],
+        out_shape=[jax.ShapeDtypeStruct(shape, dtype) for shape, dtype, _ in outputs],
+        scratch_shapes=[
+            pltpu.SemaphoreType.DMA((n_copy,)),
+            pltpu.SemaphoreType.DMA((n_copy,)),
+            pltpu.SemaphoreType.DMA((2 * n_stay,)),
+            pltpu.SemaphoreType.DMA((n_ctx + 1,)),
+            pltpu.VMEM((n_ctx, 2, loc, width_here), BF16),
+            pltpu.VMEM((width_here, wide), BF16),
+        ]
+        + [pltpu.VMEM(shape, BF16) for shape in stay_shapes],
+        compiler_params=pltpu.CompilerParams(
+            collective_id=1, has_side_effects=True, vmem_limit_bytes=50 << 20
+        ),
+    )(query, bias, kv_own, cot, w_out, w_up, w_down, *maps)
+
+
+def attend_back(query, kv_own, slots, bias, grad, log_total, acts, n_fsdp, n_ctx):
+    per, loc, width_here = query.shape
+    piece, width = acts.shape[2:]
+    heads = width_here // HEAD_DIM
+    cuts = 2
+    high = heads // cuts
+    columns = high * HEAD_DIM
+    masks = masks_of(n_ctx)
+    units = [(g, c) for g in range(per) for c in range(cuts)]
+    n_copy = per * (n_fsdp - 1) + len(units) * (n_ctx - 1)
+
+    def kernel(*refs):
+        q_ref, bias_ref, g_ref, log_ref, acts_ref, kv_ref = refs[:6]
+        slot_refs = refs[6 : 5 + n_ctx]
+        dq_ref, dkv_ref, out_ref = refs[5 + n_ctx : 8 + n_ctx]
+        send, recv, load, kv_room, own, came, act_room = refs[8 + n_ctx :]
+        mover = Mover(n_fsdp, n_ctx, send, recv)
+        z, ct = mover.z, mover.ct
+        loads = []
+        for g in range(per):
+            loads.append([])
+            for k in range(n_ctx):
+                source = kv_ref if k == 0 else slot_refs[k - 1]
+                copy = pltpu.make_async_copy(
+                    source.at[:, g], kv_room.at[g, k], load.at[g * n_ctx + k]
+                )
+                copy.start()
+                loads[g].append(copy)
+        kept = []
+        for g in range(per):
+            at = per * n_ctx + 2 * g
+            first = pltpu.make_async_copy(acts_ref.at[g, 0], act_room.at[g], load.at[at])
+            first.start()
+            second = pltpu.make_async_copy(
+                act_room.at[g], out_ref.at[z * per + g], load.at[at + 1]
+            )
+            kept.append((first, second))
+        mover.greet()
+        dealt = []
+        for g in range(per):
+            for s in range(1, n_fsdp):
+                to = lax.rem(z - s + n_fsdp, n_fsdp)
+                dealt.append(
+                    mover.go(acts_ref.at[g, s], out_ref.at[z * per + g], {"fsdp": to})
+                )
+        flying = {}
+
+        def compute(u):
+            g, c = units[u]
+            if c == 0:
+                for copy in loads[g]:
+                    copy.wait()
+
+            def one(h, carry):
+                at = ds(c * columns + h * HEAD_DIM, HEAD_DIM)
+                to = ds(h * HEAD_DIM, HEAD_DIM)
+                biases = []
+                for k in range(n_ctx):
+                    block = bias_ref[g, k * loc : (k + 1) * loc, :]
+                    biases.append(jnp.concatenate([block] * (loc // 128), axis=1))
+                dquery, dkeys, dvalues = attend_back_head(
+                    q_ref[g, :, at],
+                    g_ref[g, :, at],
+                    log_ref[g, c * high + h],
+                    [kv_room[g, k, 0, :, at] for k in range(n_ctx)],
+                    [kv_room[g, k, 1, :, at] for k in range(n_ctx)],
+                    biases,
+                )
+                dq_ref[g, :, at] = dquery
+                for k in range(n_ctx):
+                    own[u, k, 0, :, to] = dkeys[k]
+                    own[u, k, 1, :, to] = dvalues[k]
+                return carry
+
+            lax.fori_loop(0, high, one, 0)
+
+        def hand(u, level):
+            half = 2**level
+            device = {"ctx": flip(ct, masks[level])}
+            flying[u, level] = [
+                mover.go(own.at[u, half + i], came.at[u, half - 1 + i], device) for i in range(half)
+            ]
+
+        def take_in(u, level):
+            half = 2**level
+            for i, copy in enumerate(flying[u, level]):
+                copy.wait_recv()
+                for j in range(2):
+                    total = own[u, i, j].astype(F32) + came[u, half - 1 + i, j].astype(F32)
+                    if level:
+                        own[u, i, j] = total.astype(BF16)
+                    else:
+                        g, c = units[u]
+                        dkv_ref[j, g, :, c * columns : (c + 1) * columns] = total.astype(BF16)
+
+        last = len(masks) - 1
+        for t in range(len(units) + last + 1):
+            if t < len(units):
+                compute(t)
+                hand(t, last)
+            if t == 0:
+                for first, second in kept:
+                    first.wait()
+                    second.start()
+            for k in range(last + 1):
+                u, level = t - 1 - k, last - k
+                if 0 <= u < len(units):
+                    take_in(u, level)
+                    if level:
+                        hand(u, level - 1)
+        for _, second in kept:
+            second.wait()
+        for copy in dealt:
+            copy.wait_recv()
+        mover.close()
+
+    vmem, anywhere = pl.BlockSpec(memory_space=pltpu.VMEM), pl.BlockSpec(memory_space=pl.ANY)
+    return pl.pallas_call(
+        kernel,
+        in_specs=[vmem] * 4 + [anywhere] * (1 + n_ctx),
+        out_specs=[vmem, vmem, anywhere],
+        out_shape=[
+            jax.ShapeDtypeStruct(query.shape, BF16),
+            jax.ShapeDtypeStruct(kv_own.shape, BF16),
+            jax.ShapeDtypeStruct((per * n_fsdp, piece, width), BF16),
+        ],
+        scratch_shapes=[
+            pltpu.SemaphoreType.DMA((n_copy,)),
+            pltpu.SemaphoreType.DMA((n_copy,)),
+            pltpu.SemaphoreType.DMA((per * (n_ctx + 2),)),
+            pltpu.VMEM((per, n_ctx, 2, loc, width_here), BF16),
+            pltpu.VMEM((len(units), n_ctx, 2, loc, columns), BF16),
+            pltpu.VMEM((len(units), n_ctx - 1, 2, loc, columns), BF16),
+            pltpu.VMEM((per, piece, width), BF16),
+        ],
+        compiler_params=pltpu.CompilerParams(
+            collective_id=2, has_side_effects=True, vmem_limit_bytes=56 << 20
+        ),
+    )(query, bias, grad, log_total, acts, kv_own, *slots)
+
+
 def norm_parts(values):
     center = values - jnp.mean(values, axis=-1, keepdims=True)
     rstd = lax.rsqrt(jnp.mean(center * center, axis=-1, keepdims=True) + NORM_EPS)
@@ -650,50 +900,6 @@
         foot=(b_qkv, lambda outs: outs[1].at[pl.ds(width, 3 * NR)]),
     )
 
-    def second_items(ins, outs, z):
-        kv_ref, cot_ref, wo_ref, wu_ref, wd_ref, ao_ref, bu_ref, ad_ref = ins
-        slots, (rows_ref, out_ref, up_ref, down_ref) = outs[: n_ctx - 1], outs[n_ctx - 1 :]
-
-        def ds(start, size):
-            return pl.ds(pl.multiple_of(start, size), size)
-
-        def deal(g):
-            return Deal(lambda to: cot_ref.at[to * per + g], lambda s: rows_ref.at[g, s])
-
-        zo = wo_ref.shape[1]
-        so, su, sd = wo_ref.shape[0] // n_ctx, zu // n_ctx, wd_ref.shape[0] // n_ctx
-        out_item = Weight(
-            lambda c: wo_ref.at[ds(c * so, so)],
-            lambda o, c: out_ref.at[ds(c * so, so), ds(o * zo, zo)],
-        )
-
-        def up_item(h):
-            columns = pl.ds(h * (units // 2), units // 2)
-            return Weight(
-                lambda c: wu_ref.at[ds(c * su, su), columns],
-                lambda o, c: up_ref.at[ds(o * zu + c * su, su), columns],
-            )
-
-        def down_item(h):
-            half = sd // 2
-            return Weight(
-                lambda c: wd_ref.at[ds(c * sd + h * half, half)],
-                lambda o, c: down_ref.at[ds(c * sd + h * half, half), ds(o * zo, zo)],
-            )
-
-        pair = Pair(lambda k: kv_ref if k == 0 else slots[k - 1])
-        stay = [(cot_ref.at[z * per + g], rows_ref.at[g, 0]) for g in range(per)]
-        stay += [
-            (wo_ref, out_ref.at[:, ds(z * zo, zo)]),
-            (wu_ref, up_ref.at[ds(z * zu, zu)]),
-            (wd_ref, down_ref.at[:, ds(z * zo, zo)]),
-            (ao_ref, out_ref.at[:, pl.ds(width, NR)]),
-            (bu_ref, up_ref.at[pl.ds(width, NR)]),
-            (ad_ref, down_ref.at[:, pl.ds(width, NR)]),
-        ]
-        items = [pair, out_item, up_item(0), up_item(1), down_item(0), down_item(1)]
-        return items + [deal(g) for g in range(per)], stay
-
     a_in = a_qkv.transpose(1, 0, 2).reshape(width, 3 * NR)
 
     my_lengths = take(lengths, z * per, per)
@@ -714,38 +920,29 @@
     proj_all = mm(jnp.concatenate([x_flat, adapt_all], axis=1), qkv_x, False, as_low, 1024)
     kv_own = jnp.stack([proj_all[:, heads_width : 2 * heads_width], proj_all[:, 2 * heads_width :]])
     kv_own = kv_own.reshape(2, per, loc, heads_width)
-    moved = move(
-        second_items,
-        [Pair] + [Weight] * 5 + [Deal] * per,
-        (kv_own, cotangent, w_out, w_up, w_down, a_out, b_up, a_down),
-        ((2, per, loc, heads_width),) * (n_ctx - 1)
-        + (
-            rows_shape,
-            (heads_width, width + NR),
-            (width + NR, units),
-            (units, width + NR),
-        ),
+    moved = forward_and_gather(
+        proj_all[:, :heads_width].reshape(per, loc, heads_width),
+        kv_own,
+        bias_all,
+        (cotangent, w_out, w_up, w_down),
+        (a_out, b_up, a_down),
         n_fsdp,
         n_ctx,
-        ((piece, width),) * per
-        + (w_out.shape, w_up.shape, w_down.shape, a_out.shape, b_up.shape, a_down.shape),
-        1,
     )
     kv_all = [kv_own] + list(moved[: n_ctx - 1])
-    cot_all, out_x, up_x, down_x = moved[n_ctx - 1 :]
+    cot_all, out_x, up_x, down_x, context, log_total, part_out, other_out = moved[n_ctx - 1 :]
     cot_flat = cot_all.reshape(per * loc, width)
 
     groups = range(n_group)
     picks = [jnp.repeat(take(picked, g * g_per, g_per), loc, axis=0) for g in groups]
-    biases = [bias_all[g * g_per : (g + 1) * g_per] for g in groups]
     part = [slice(g * g_rows, (g + 1) * g_rows) for g in groups]
     seq = [slice(n * loc, (n + 1) * loc) for n in range(g_per)]
     x_rows = [x_flat[part[g]] for g in groups]
-    query = [proj_all[part[g], :heads_width].reshape(g_per, loc, heads_width) for g in groups]
-
-    attended = [attend(query[g], kv_all, biases[g], g * g_per) for g in groups]
-    ctx_rows = [attended[g][0].reshape(g_rows, heads_width) for g in groups]
-    summed = [both(mm(ctx_rows[g], out_x, False, as_low, 768)) for g in groups]
+
+    ctx_flat = context.reshape(per * loc, heads_width)
+    ctx_rows = [ctx_flat[part[g]] for g in groups]
+    summed = (part_out.astype(F32) + other_out.astype(F32)).reshape(per * loc, width + NR)
+    summed = [summed[part[g]] for g in groups]
     adapt_out, hat1, rstd1, hidden, hidden_low, adapt_up, gelu_out, slope = ([] for _ in range(8))
     for g in groups:
         adapt_out.append((summed[g][:, width:] * picks[g]).astype(BF16))
@@ -760,18 +957,18 @@
         pair = mm(wide, up_x, False, gelu_both, 1024, 2)
         gelu_out.append(pair[0])
         slope.append(pair[1])
-    summed = [both(mm(gelu_out[g], down_x, False, as_low, 768)) for g in groups]
+    summed = both_in_turn([mm(gelu_out[g], down_x, False, as_low, 768) for g in groups])
     adapt_down, acts, dy2, d_down, dadapt_down, d_pre = ([] for _ in range(6))
     for g in groups:
         adapt_down.append((summed[g][:, width:] * picks[g]).astype(BF16))
         hat2, rstd2 = norm_parts(hidden[g] + summed[g][:, :width] + dot(adapt_down[g], b_down))
-        acts.append(undeal((hat2 * ln_gain[1] + ln_bias[1]).astype(BF16), g))
+        acts.append((hat2 * ln_gain[1] + ln_bias[1]).astype(BF16))
         dy2.append(norm_back(hat2, rstd2, cot_flat[part[g]].astype(F32) * ln_gain[1]))
         d_down.append(dy2[g].astype(BF16))
         dadapt_down.append((dot_nt(d_down[g], b_down) * picks[g]).astype(BF16))
         wide = jnp.concatenate([d_down[g], dadapt_down[g]], axis=1)
         d_pre.append(mm(wide, down_x, True, times, 1024, 1, slope[g]))
-    summed = [both(mm(d_pre[g], up_x, True, as_low, 768)) for g in groups]
+    summed = both_in_turn([mm(d_pre[g], up_x, True, as_low, 768) for g in groups])
     dadapt_up, dy1, d_attn, dadapt_out, backs = ([] for _ in range(5))
     for g in groups:
         dadapt_up.append((summed[g][:, width:] * picks[g]).astype(BF16))
@@ -780,10 +977,20 @@
         d_attn.append(dy1[g].astype(BF16))
         dadapt_out.append((dot_nt(d_attn[g], b_out) * picks[g]).astype(BF16))
         wide = jnp.concatenate([d_attn[g], dadapt_out[g]], axis=1)
-        d_context = mm(wide, out_x, True, as_low, 512).reshape(g_per, loc, heads_width)
-        backs.append(
-            attend_back(query[g], kv_all, biases[g], d_context, attended[g][1], g * g_per)
-        )
+        backs.append(mm(wide, out_x, True, as_low, 512).reshape(g_per, loc, heads_width))
+    d_query, d_pair, activations = attend_back(
+        proj_all[:, :heads_width].reshape(per, loc, heads_width),
+        kv_own,
+        kv_all[1:],
+        bias_all,
+        jnp.concatenate(backs, axis=0),
+        log_total,
+        jnp.concatenate(acts, axis=0).reshape(per, n_fsdp, piece, width),
+        n_fsdp,
+        n_ctx,
+    )
+    d_query = d_query.reshape(per * loc, heads_width)
+    d_pair = d_pair.reshape(2, per * loc, heads_width)
 
     def gathered(parts):
         mine = jnp.concatenate(parts, axis=1)
@@ -805,18 +1012,17 @@
             (dadapt_out[g], ctx_rows[g]),
         )
         early_in.append(pairs)
-    early_in = after(early_in, backs[-1][0])
+    early_in = after(early_in, d_query)
     early = gathered(
         [compact([(c[r], v[r]) for c, v in early_in[g]], n_ctx) for g in groups for r in seq]
     )
 
-    d_proj, ins, late = [], [], []
-    summed = []
-    for g in groups:
-        d_pair = fold(backs[g][1], "ctx").reshape(2, g_rows, heads_width)
-        d_query = backs[g][0].reshape(g_rows, heads_width)
-        d_proj.append(jnp.concatenate([d_query, d_pair[0], d_pair[1]], axis=1))
-        summed.append(both(mm(d_proj[g], qkv_x, True, as_low, 640)))
+    ins, late = [], []
+    d_proj = [
+        jnp.concatenate([d_query[part[g]], d_pair[0, part[g]], d_pair[1, part[g]]], axis=1)
+        for g in groups
+    ]
+    summed = both_in_turn([mm(d_proj[g], qkv_x, True, as_low, 640) for g in groups])
     for g in groups:
         pick3 = jnp.concatenate([picks[g]] * 3, axis=1)
         dadapt_in = (summed[g][:, width:] * pick3).astype(BF16)
@@ -844,14 +1050,14 @@
 
     codes = (adapter_ids[:, None] * RANK + jnp.arange(RANK)[None, :]).reshape(-1)
     chosen = (codes[:, None] == jnp.arange(NR)[None, :]).astype(BF16)
-    early, acts = after((early, acts), summed[-1])
+    early = after(early, summed[-1])
     e = combine(
         early,
         chosen,
         [(NR, width), (units, NR), (NR, units), (width, NR), (NR, width), (heads_width, NR)],
     )
     l = combine(late, chosen, [(3, NR, heads_width), (3, width, NR)])
-    return assemble(acts), assemble(ins), l[1], l[0], e[5], e[4], e[3], e[2], e[1], e[0]
+    return activations, assemble(ins), l[1], l[0], e[5], e[4], e[3], e[2], e[1], e[0]
 
 
 def solution(mesh):

time: 865 us -> 768 us (0.89)
  waiting for transfers between devices: 203 us -> 130 us
  local copies, waits for them, and re-layouts: 48.6 us -> 24.3 us
  starting transfers between devices: 57.5 us -> 41.7 us
  Pallas kernels: 503 us -> 517 us
    pallas_call x4 -> x2, Pallas kernels: 44.2 us -> 287 us  [the longest x1 225 us: forward_and_gather(): pl.pallas_call(kernel, in_specs=[vmem, vmem] + [anywhere] * 8, out_specs=...]
    pallas_call x2 -> x1, Pallas kernels: 323 us -> 100 us  [move(): pl.pallas_call(kernel, in_specs=spaces, out_specs=[pl.BlockSpec(memory_sp...]
    ppermute x26 -> x18, waiting for transfers between devices: 179 us -> 95.3 us  [swap(): return lax.ppermute(block, axis, [(i, i ^ mask) for i in range(n)])]
    unnamed x275 -> x130, local copies, waits for them, and re-layouts: 42.5 us -> 15.7 us
    ppermute x18 -> x12, waiting for transfers between devices: 23.9 us -> 34.2 us  [shift(): return lax.ppermute(block, axis, [(i, (i + step) % n) for i in range(n)])]
    ppermute x18 -> x12, starting transfers between devices: 36.1 us -> 26 us  [shift(): return lax.ppermute(block, axis, [(i, (i + step) % n) for i in range(n)])]
    pallas_call x15 -> x13, Pallas kernels: 121 us -> 114 us  [mm(): pl.pallas_call(kernel, grid=(pl.cdiv(columns, tile),), in_specs=[pl.Block...]
    ppermute x26 -> x18, starting transfers between devices: 21.3 us -> 15.7 us  [swap(): return lax.ppermute(block, axis, [(i, i ^ mask) for i in range(n)])]
  transfers between devices with their start and end apart: 44 -> 30, of which waited for: 17 -> 15; matrix products, arithmetic and copies ran while one was open for 3% -> 3% of each run, Pallas kernels for 11% -> 15%
where the time goes in v4:
time: 768 us; the launch traced here: 758 us
  Pallas kernels  517 us (67%)
  waiting for transfers between devices  130 us (17%)
  starting transfers between devices  41.7 us (5%)
  other arithmetic  30.8 us (4%)
  local copies, waits for them, and re-layouts  24.3 us (3%)
  matrix products  12.3 us (2%)
    pallas_call x1, Pallas kernels, forward_and_gather(): pl.pallas_call(kernel, in_specs=[vmem, vmem] + [anywhere] * 8, out_specs=...  225 us
    pallas_call x13, Pallas kernels, mm(): pl.pallas_call(kernel, grid=(pl.cdiv(columns, tile),), in_specs=[pl.Block...  114 us
    pallas_call x1, Pallas kernels, move(): pl.pallas_call(kernel, in_specs=spaces, out_specs=[pl.BlockSpec(memory_sp...  100 us
    ppermute x18, waiting for transfers between devices, swap(): return lax.ppermute(block, axis, [(i, i ^ mask) for i in range(n)])  95.3 us
    pallas_call x1, Pallas kernels, attend_back(): pl.pallas_call(kernel, in_specs=[vmem] * 4 + [anywhere] * (1 + n_ctx), ou...  62.5 us
    ppermute x12, waiting for transfers between devices, shift(): return lax.ppermute(block, axis, [(i, (i + step) % n) for i in range(n)])  34.2 us
    ppermute x12, starting transfers between devices, shift(): return lax.ppermute(block, axis, [(i, (i + step) % n) for i in range(n)])  26 us
    ppermute x18, starting transfers between devices, swap(): return lax.ppermute(block, axis, [(i, i ^ mask) for i in range(n)])  15.7 us
  transfers between devices with their start and end apart: 30, of which 15 were waited for; matrix products, arithmetic and copies ran while one was open for 3% of the time, Pallas kernels for 15%

profile of v4, /device:TPU:0, one launch (start us, length us, event | category | flops | bytes accessed | tf_op | source)
XLA Modules:
  0.0 757.8 jit_solution(14799166536441372114)
XLA Ops:
  5.5 100.0 %shard_map.258 = (bf16[2,4,64,2048]{3,2,1,0:T(8,128)(2,1)S(1)}, bf16[2432,3072]{1,0:T(8,128)(2,1)}) custom-call(bf16[8,64,2048]{2,1,0:T(8,128)(2,1)S(1)} %copy-done.17, bf16[3,512,1024]{2,1,0:T(8,128)(2,1)S(1)} %copy-done.16, bf16[3,128,1024]{2,1,0:T(8,128)(2,1)S(1)} %copy-done.23), custom_call_target="tpu_custom_call" | custom-call | tf_op jit(solution)/shard_map/pallas_call | solution.py:333
  109.0 11.2 %shard_map.259 = bf16[512,3072]{1,0:T(8,128)(2,1)S(1)} custom-call(bf16[512,2432]{1,0:T(8,128)(2,1)S(1)} %pad_maximum_fusion.left_ref, bf16[2432,3072]{1,0:T(8,128)(2,1)} %get-tuple-element.70.right_ref), custom_call_target="tpu_custom_call" | custom-call | flops 7650410496 | bytes 35520512 | tf_op jit(solution)/shard_map/pallas_call | solution.py:696
  125.9 224.8 %shard_map.260 = (bf16[2,2,256,1024]{3,2,1,0:T(8,128)(2,1)}, bf16[2,2,256,1024]{3,2,1,0:T(8,128)(2,1)}, bf16[2,2,256,1024]{3,2,1,0:T(8,128)(2,1)}, bf16[2,4,64,2...) custom-call(bf16[2,256,1024]{2,1,0:T(8,128)(2,1)S(1)} %bitcast.159, ...), custom_call_target="tpu_custom_call" | custom-call | tf_op jit(solution)/shard_map/pallas_call | solution.py:496
  359.0 10.7 %shard_map.263 = (bf16[256,4096]{1,0:T(8,128)(2,1)S(1)}, bf16[256,4096]{1,0:T(8,128)(2,1)S(1)}) custom-call(bf16[256,2176]{1,0:T(8,128)(2,1)S(1)} %pad_maximum_fusion.6.left_ref, bf16[2176,4096]{1,0:T(8,128)(2,1)} %get-tuple-element.73.right_ref), custom_call_target="tpu_custom_call" | custom-call | flops 4563402752 | bytes 40960000 | tf_op jit(solution)/shard_map/pallas_call | solution.py:696
  371.0 10.5 %shard_map.264 = bf16[256,2176]{1,0:T(8,128)(2,1)} custom-call(bf16[256,4096]{1,0:T(8,128)(2,1)S(1)} %get-tuple-element.109.left_ref.refs_3_, bf16[4096,2176]{1,0:T(8,128)(2,1)} %get-tuple-element.75.right_ref), custom_call_target="tpu_custom_call" | custom-call | flops 4563402752 | bytes 38862848 | tf_op jit(solution)/shard_map/pallas_call | solution.py:696
  390.7 18.1 %collective-permute-done.2 = bf16[256,2176]{1,0:T(8,128)(2,1)} collective-permute-done((bf16[256,2176]{1,0:T(8,128)(2,1)}, bf16[256,2176]{1,0:T(8,128)(2,1)}, u32[]{:S(2)}, u32[]{:S(2)}) %collective-permute-start.2) | collective-permute-done | bytes 1114144 | tf_op jit(solution)/shard_map/ppermute | solution.py:41
  412.2 11.1 %shard_map.261 = (bf16[256,4096]{1,0:T(8,128)(2,1)S(1)}, bf16[256,4096]{1,0:T(8,128)(2,1)S(1)}) custom-call(bf16[256,2176]{1,0:T(8,128)(2,1)S(1)} %pad_maximum_fusion.5.left_ref, bf16[2176,4096]{1,0:T(8,128)(2,1)} %get-tuple-element.73.right_ref), custom_call_target="tpu_custom_call" | custom-call | flops 4563402752 | bytes 40960000 | tf_op jit(solution)/shard_map/pallas_call | solution.py:696
  423.3 9.8 %shard_map.262 = bf16[256,2176]{1,0:T(8,128)(2,1)S(1)} custom-call(bf16[256,4096]{1,0:T(8,128)(2,1)S(1)} %get-tuple-element.97.left_ref.refs_3_, bf16[4096,2176]{1,0:T(8,128)(2,1)} %get-tuple-element.75.right_ref), custom_call_target="tpu_custom_call" | custom-call | flops 4563402752 | bytes 38862848 | tf_op jit(solution)/shard_map/pallas_call | solution.py:696
  436.6 22.7 %collective-permute-done = bf16[256,2176]{1,0:T(8,128)(2,1)S(1)} collective-permute-done((bf16[256,2176]{1,0:T(8,128)(2,1)S(1)}, bf16[256,2176]{1,0:T(8,128)(2,1)S(1)}, u32[]{:S(2)}, u32[]{:S(2)}) %collective-permute-start) | collective-permute-done | bytes 1114144 | tf_op jit(solution)/shard_map/ppermute | solution.py:41
  467.0 9.7 %shard_map.265.left_ref.refs_5_ = bf16[256,4096]{1,0:T(8,128)(2,1)S(1)} custom-call(bf16[256,2176]{1,0:T(8,128)(2,1)S(1)} %pad_maximum_fusion.7.left_ref, bf16[4096,2176]{1,0:T(8,128)(2,1)} %get-tuple-element.75.right_ref, bf16[256,4096]{1,0:T(8,128)(2,1)S(1)} %get-tuple-element.79.refs_0_), custom_call_target="tpu_custom_call" | custom-call | flops 4563402752 | bytes 38862848 | tf_op jit(solution)/shard_map/pallas_call | solution.py:696
  476.7 9.8 %shard_map.266 = bf16[256,2176]{1,0:T(8,128)(2,1)S(1)} custom-call(bf16[256,4096]{1,0:T(8,128)(2,1)S(1)} %shard_map.265.left_ref.refs_5_, bf16[2176,4096]{1,0:T(8,128)(2,1)} %get-tuple-element.73.right_ref), custom_call_target="tpu_custom_call" | custom-call | flops 4563402752 | bytes 38862848 | tf_op jit(solution)/shard_map/pallas_call | solution.py:696
  488.7 9.9 %shard_map.267.left_ref.refs_5_ = bf16[256,4096]{1,0:T(8,128)(2,1)S(1)} custom-call(bf16[256,2176]{1,0:T(8,128)(2,1)S(1)} %pad_maximum_fusion.8.left_ref, bf16[4096,2176]{1,0:T(8,128)(2,1)} %get-tuple-element.75.right_ref, bf16[256,4096]{1,0:T(8,128)(2,1)S(1)} %copy-done.20), custom_call_target="tpu_custom_call" | custom-call | flops 4563402752 | bytes 38862848 | tf_op jit(solution)/shard_map/pallas_call | solution.py:696
  498.6 9.9 %shard_map.268 = bf16[256,2176]{1,0:T(8,128)(2,1)S(1)} custom-call(bf16[256,4096]{1,0:T(8,128)(2,1)S(1)} %shard_map.267.left_ref.refs_5_, bf16[2176,4096]{1,0:T(8,128)(2,1)} %get-tuple-element.73.right_ref), custom_call_target="tpu_custom_call" | custom-call | flops 4563402752 | bytes 38862848 | tf_op jit(solution)/shard_map/pallas_call | solution.py:696
  519.1 16.6 %collective-permute-done.3 = bf16[256,2176]{1,0:T(8,128)(2,1)S(1)} collective-permute-done((bf16[256,2176]{1,0:T(8,128)(2,1)S(1)}, bf16[256,2176]{1,0:T(8,128)(2,1)S(1)}, u32[]{:S(2)}, u32[]{:S(2)}) %collective-permute-start.3) | collective-permute-done | bytes 1114144 | tf_op jit(solution)/shard_map/ppermute | solution.py:41
  554.0 62.5 %shard_map.271 = (bf16[2,256,1024]{2,1,0:T(8,128)(2,1)}, bf16[2,2,256,1024]{3,2,1,0:T(8,128)(2,1)}, bf16[8,64,2048]{2,1,0:T(8,128)(2,1)}) custom-call(bf16[2,256,1024]{2,1,0:T(8,128)(2,1)} %bitcast.158, f32[2,1024,128]{2,1,0:T(8,128)} %copy-done.8, bf16[2,256,1024]{2,1,0:T(8,128)(2,1)} %pad_maximum_fusion.11.refs_2_, f32[2,8,1,256]{3,2,1,0:T(1,128)} %copy-done.32, ...), custom_call_target="tpu_custom_call" | custom-call | tf_op jit(solution)/shard_map/pallas_call | solution.py:633
  618.5 8.7 %shard_map.273 = bf16[256,2432]{1,0:T(8,128)(2,1)S(1)} custom-call(bf16[256,3072]{1,0:T(8,128)(2,1)S(1)} %pad_maximum_fusion.4.left_ref, bf16[2432,3072]{1,0:T(8,128)(2,1)} %get-tuple-element.70.right_ref), custom_call_target="tpu_custom_call" | custom-call | flops 3825205248 | bytes 32702464 | tf_op jit(solution)/shard_map/pallas_call | solution.py:696
  630.5 4.9 collective-permute-done.23
  639.4 8.9 %shard_map.272 = bf16[256,2432]{1,0:T(8,128)(2,1)S(1)} custom-call(bf16[256,3072]{1,0:T(8,128)(2,1)S(1)} %pad_maximum_fusion.3.left_ref, bf16[2432,3072]{1,0:T(8,128)(2,1)} %get-tuple-element.70.right_ref), custom_call_target="tpu_custom_call" | custom-call | flops 3825205248 | bytes 32702464 | tf_op jit(solution)/shard_map/pallas_call | solution.py:696
  658.0 24.1 %collective-permute-done.4 = bf16[256,2432]{1,0:T(8,128)(2,1)S(1)} collective-permute-done((bf16[256,2432]{1,0:T(8,128)(2,1)S(1)}, bf16[256,2432]{1,0:T(8,128)(2,1)S(1)}, u32[]{:S(2)}, u32[]{:S(2)}) %collective-permute-start.4) | collective-permute-done | bytes 1245216 | tf_op jit(solution)/shard_map/ppermute | solution.py:41
  690.8 7.7 %collective-permute-done.5 = bf16[1,64,2048]{2,1,0:T(8,128)(2,1)S(1)} collective-permute-done((bf16[1,64,2048]{2,1,0:T(8,128)(2,1)S(1)}, bf16[1,64,2048]{2,1,0:T(8,128)(2,1)S(1)}, u32[]{:S(2)}, u32[]{:S(2)}) %collective-permute-start.5) | collective-permute-done | bytes 262176 | tf_op jit(solution)/shard_map/ppermute | solution.py:36
  707.2 7.5 collective-permute-done.6
  717.8 6.7 collective-permute-start.9
  731.4 8.8 %collective-permute-start.11 = (bf16[1,64,2048]{2,1,0:T(8,128)(2,1)S(1)}, bf16[1,64,2048]{2,1,0:T(8,128)(2,1)S(1)}, u32[]{:S(2)}, u32[]{:S(2)}) collective-permute-start(bf16[1,64,2048]{2,1,0:T(8,128)(2,1)S(1)} %get-tuple-element.164), channel_id=1, source_target_pairs={{0,8},{8,16},{16,24},{24,0},{1,9},{9,17},{17,25},{25,1},{2,10},{10... | collective-permute-start | bytes 786440 | tf_op jit(solution)/shard_map/ppermute | solution.py:36
  740.2 8.0 %collective-permute-done.10 = bf16[1,64,2048]{2,1,0:T(8,128)(2,1)S(1)} collective-permute-done((bf16[1,64,2048]{2,1,0:T(8,128)(2,1)S(1)}, bf16[1,64,2048]{2,1,0:T(8,128)(2,1)S(1)}, u32[]{:S(2)}, u32[]{:S(2)}) %collective-permute-start.10) | collective-permute-done | bytes 262176 | tf_op jit(solution)/shard_map/ppermute | solution.py:36
  (307 shorter events, 132.8 us)
Async XLA Ops:
  381.5 27.3 %collective-permute-start.2 = (bf16[256,2176]{1,0:T(8,128)(2,1)}, bf16[256,2176]{1,0:T(8,128)(2,1)}, u32[]{:S(2)}, u32[]{:S(2)}) collective-permute-start(bf16[256,2176]{1,0:T(8,128)(2,1)} %shard_map.264), channel_id=1, source_target_pairs={{0,1},{1,0},{2,3},{3,2},{4,5},{5,4},{6,7},{7,6},{8,9},{9,8},{10,11... | collective-permute-start | bytes 3342344 | tf_op jit(solution)/shard_map/ppermute | solution.py:41
  433.1 26.2 %collective-permute-start = (bf16[256,2176]{1,0:T(8,128)(2,1)S(1)}, bf16[256,2176]{1,0:T(8,128)(2,1)S(1)}, u32[]{:S(2)}, u32[]{:S(2)}) collective-permute-start(bf16[256,2176]{1,0:T(8,128)(2,1)S(1)} %shard_map.262), channel_id=1, source_target_pairs={{0,1},{1,0},{2,3},{3,2},{4,5},{5,4},{6,7},{7,6},{8,9},{9,8},{10,11... | collective-permute-start | bytes 3342344 | tf_op jit(solution)/shard_map/ppermute | solution.py:41
  486.5 27.6 %collective-permute-start.1 = (bf16[256,2176]{1,0:T(8,128)(2,1)S(1)}, bf16[256,2176]{1,0:T(8,128)(2,1)}, u32[]{:S(2)}, u32[]{:S(2)}) collective-permute-start(bf16[256,2176]{1,0:T(8,128)(2,1)S(1)} %shard_map.266), channel_id=1, source_target_pairs={{0,1},{1,0},{2,3},{3,2},{4,5},{5,4},{6,7},{7,6},{8,9},{9,8},{10,11... | collective-permute-start | bytes 3342344 | tf_op jit(solution)/shard_map/ppermute | solution.py:41
  508.5 27.2 %collective-permute-start.3 = (bf16[256,2176]{1,0:T(8,128)(2,1)S(1)}, bf16[256,2176]{1,0:T(8,128)(2,1)S(1)}, u32[]{:S(2)}, u32[]{:S(2)}) collective-permute-start(bf16[256,2176]{1,0:T(8,128)(2,1)S(1)} %shard_map.268), channel_id=1, source_target_pairs={{0,1},{1,0},{2,3},{3,2},{4,5},{5,4},{6,7},{7,6},{8,9},{9,8},{10,11... | collective-permute-start | bytes 3342344 | tf_op jit(solution)/shard_map/ppermute | solution.py:41
  547.4 81.4 %collective-permute-start.22 = (bf16[32,3840]{1,0:T(8,128)(2,1)S(1)}, bf16[32,3840]{1,0:T(8,128)(2,1)S(1)}, u32[]{:S(2)}, u32[]{:S(2)}) collective-permute-start(bf16[32,3840]{1,0:T(8,128)(2,1)S(1)} %get-tuple-element.173), channel_id=1, source_target_pairs={{0,2},{2,0},{4,6},{6,4},{1,3},{3,1},{5,7},{7,5},{8,10},{10,8},{12,... | collective-permute-start | bytes 737288 | tf_op jit(solution)/shard_map/ppermute | solution.py:41
  547.5 83.0 %collective-permute-start.21 = (bf16[32,3840]{1,0:T(8,128)(2,1)S(1)}, bf16[32,3840]{1,0:T(8,128)(2,1)S(1)}, u32[]{:S(2)}, u32[]{:S(2)}) collective-permute-start(bf16[32,3840]{1,0:T(8,128)(2,1)S(1)} %get-tuple-element.172), channel_id=1, source_target_pairs={{0,2},{2,0},{4,6},{6,4},{1,3},{3,1},{5,7},{7,5},{8,10},{10,8},{12,... | collective-permute-start | bytes 737288 | tf_op jit(solution)/shard_map/ppermute | solution.py:41
  627.2 30.4 %collective-permute-start.8 = (bf16[256,2432]{1,0:T(8,128)(2,1)S(1)}, bf16[256,2432]{1,0:T(8,128)(2,1)S(1)}, u32[]{:S(2)}, u32[]{:S(2)}) collective-permute-start(bf16[256,2432]{1,0:T(8,128)(2,1)S(1)} %shard_map.273), channel_id=1, source_target_pairs={{0,1},{1,0},{2,3},{3,2},{4,5},{5,4},{6,7},{7,6},{8,9},{9,8},{10,11... | collective-permute-start | bytes 3735560 | tf_op jit(solution)/shard_map/ppermute | solution.py:41
  635.5 13.4 %collective-permute-start.24 = (bf16[32,3840]{1,0:T(8,128)(2,1)S(1)}, bf16[32,3840]{1,0:T(8,128)(2,1)S(1)}, u32[]{:S(2)}, u32[]{:S(2)}) collective-permute-start(bf16[32,3840]{1,0:T(8,128)(2,1)S(1)} %add_convert_fusion.2), channel_id=1, source_target_pairs={{0,8},{8,16},{16,24},{24,0},{1,9},{9,17},{17,25},{25,1},{2,10},{10... | collective-permute-start | bytes 737288 | tf_op jit(solution)/shard_map/ppermute | solution.py:36
  635.6 18.1 %collective-permute-start.25 = (bf16[32,3840]{1,0:T(8,128)(2,1)S(1)}, bf16[32,3840]{1,0:T(8,128)(2,1)S(1)}, u32[]{:S(2)}, u32[]{:S(2)}) collective-permute-start(bf16[32,3840]{1,0:T(8,128)(2,1)S(1)} %add_convert_fusion.2), channel_id=1, source_target_pairs={{0,16},{8,24},{16,0},{24,8},{1,17},{9,25},{17,1},{25,9},{2,18},{10... | collective-permute-start | bytes 737288 | tf_op jit(solution)/shard_map/ppermute | solution.py:36
  637.2 16.5 %collective-permute-start.26 = (bf16[32,3840]{1,0:T(8,128)(2,1)S(1)}, bf16[32,3840]{1,0:T(8,128)(2,1)S(1)}, u32[]{:S(2)}, u32[]{:S(2)}) collective-permute-start(bf16[32,3840]{1,0:T(8,128)(2,1)S(1)} %add_convert_fusion.2), channel_id=1, source_target_pairs={{0,24},{8,0},{16,8},{24,16},{1,25},{9,1},{17,9},{25,17},{2,26},{10... | collective-permute-start | bytes 737288 | tf_op jit(solution)/shard_map/ppermute | solution.py:36
  648.3 33.8 %collective-permute-start.4 = (bf16[256,2432]{1,0:T(8,128)(2,1)S(1)}, bf16[256,2432]{1,0:T(8,128)(2,1)S(1)}, u32[]{:S(2)}, u32[]{:S(2)}) collective-permute-start(bf16[256,2432]{1,0:T(8,128)(2,1)S(1)} %shard_map.272), channel_id=1, source_target_pairs={{0,1},{1,0},{2,3},{3,2},{4,5},{5,4},{6,7},{7,6},{8,9},{9,8},{10,11... | collective-permute-start | bytes 3735560 | tf_op jit(solution)/shard_map/ppermute | solution.py:41
  653.8 74.5 %collective-permute-start.27 = (bf16[4,32,3840]{2,1,0:T(8,128)(2,1)S(1)}, bf16[4,32,3840]{2,1,0:T(8,128)(2,1)S(1)}, u32[]{:S(2)}, u32[]{:S(2)}) collective-permute-start(bf16[4,32,3840]{2,1,0:T(8,128)(2,1)S(1)} %pad_maximum_fusion.12.refs_0_), channel_id=1, source_target_pairs={{0,4},{2,6},{4,0},{6,2},{1,5},{3,7},{5,1},{7,3},{8,12},{10,14},{12... | collective-permute-start | bytes 2949128 | tf_op jit(solution)/shard_map/ppermute | solution.py:41
  655.4 93.4 %collective-permute-start.28 = (bf16[4,32,3840]{2,1,0:T(8,128)(2,1)S(1)}, bf16[4,32,3840]{2,1,0:T(8,128)(2,1)S(1)}, u32[]{:S(2)}, u32[]{:S(2)}) collective-permute-start(bf16[4,32,3840]{2,1,0:T(8,128)(2,1)S(1)} %pad_maximum_fusion.12.refs_0_), channel_id=1, source_target_pairs={{0,2},{2,0},{4,6},{6,4},{1,3},{3,1},{5,7},{7,5},{8,10},{10,8},{12,... | collective-permute-start | bytes 2949128 | tf_op jit(solution)/shard_map/ppermute | solution.py:41
  686.2 13.8 %collective-permute-start.12 = (bf16[32,2304]{1,0:T(8,128)(2,1)S(1)}, bf16[32,2304]{1,0:T(8,128)(2,1)S(1)}, u32[]{:S(2)}, u32[]{:S(2)}) collective-permute-start(bf16[32,2304]{1,0:T(8,128)(2,1)S(1)} %get-tuple-element.174), channel_id=1, source_target_pairs={{0,2},{2,0},{4,6},{6,4},{1,3},{3,1},{5,7},{7,5},{8,10},{10,8},{12,... | collective-permute-start | bytes 442376 | tf_op jit(solution)/shard_map/ppermute | solution.py:41
  690.6 24.0 %collective-permute-start.6 = (bf16[1,64,2048]{2,1,0:T(8,128)(2,1)S(1)}, bf16[1,64,2048]{2,1,0:T(8,128)(2,1)S(1)}, u32[]{:S(2)}, u32[]{:S(2)}) collective-permute-start(bf16[1,64,2048]{2,1,0:T(8,128)(2,1)S(1)} %get-tuple-element.168), channel_id=1, source_target_pairs={{0,16},{8,24},{16,0},{24,8},{1,17},{9,25},{17,1},{25,9},{2,18},{10... | collective-permute-start | bytes 786440 | tf_op jit(solution)/shard_map/ppermute | solution.py:36
  703.7 11.2 %collective-permute-start.15 = (bf16[32,2304]{1,0:T(8,128)(2,1)S(1)}, bf16[32,2304]{1,0:T(8,128)(2,1)S(1)}, u32[]{:S(2)}, u32[]{:S(2)}) collective-permute-start(bf16[32,2304]{1,0:T(8,128)(2,1)S(1)} %add_convert_fusion.3), channel_id=1, source_target_pairs={{0,8},{8,16},{16,24},{24,0},{1,9},{9,17},{17,25},{25,1},{2,10},{10... | collective-permute-start | bytes 442376 | tf_op jit(solution)/shard_map/ppermute | solution.py:36
  703.8 14.0 %collective-permute-start.16 = (bf16[32,2304]{1,0:T(8,128)(2,1)S(1)}, bf16[32,2304]{1,0:T(8,128)(2,1)S(1)}, u32[]{:S(2)}, u32[]{:S(2)}) collective-permute-start(bf16[32,2304]{1,0:T(8,128)(2,1)S(1)} %add_convert_fusion.3), channel_id=1, source_target_pairs={{0,16},{8,24},{16,0},{24,8},{1,17},{9,25},{17,1},{25,9},{2,18},{10... | collective-permute-start | bytes 442376 | tf_op jit(solution)/shard_map/ppermute | solution.py:36
  714.6 12.0 %collective-permute-start.17 = (bf16[32,2304]{1,0:T(8,128)(2,1)S(1)}, bf16[32,2304]{1,0:T(8,128)(2,1)S(1)}, u32[]{:S(2)}, u32[]{:S(2)}) collective-permute-start(bf16[32,2304]{1,0:T(8,128)(2,1)S(1)} %add_convert_fusion.3), channel_id=1, source_target_pairs={{0,24},{8,0},{16,8},{24,16},{1,25},{9,1},{17,9},{25,17},{2,26},{10... | collective-permute-start | bytes 442376 | tf_op jit(solution)/shard_map/ppermute | solution.py:36
  715.0 11.7 %collective-permute-start.7 = (bf16[1,64,2048]{2,1,0:T(8,128)(2,1)S(1)}, bf16[1,64,2048]{2,1,0:T(8,128)(2,1)S(1)}, u32[]{:S(2)}, u32[]{:S(2)}) collective-permute-start(bf16[1,64,2048]{2,1,0:T(8,128)(2,1)S(1)} %get-tuple-element.167), channel_id=1, source_target_pairs={{0,8},{8,16},{16,24},{24,0},{1,9},{9,17},{17,25},{25,1},{2,10},{10... | collective-permute-start | bytes 786440 | tf_op jit(solution)/shard_map/ppermute | solution.py:36
  717.8 13.6 %collective-permute-start.9 = (bf16[1,64,2048]{2,1,0:T(8,128)(2,1)S(1)}, bf16[1,64,2048]{2,1,0:T(8,128)(2,1)S(1)}, u32[]{:S(2)}, u32[]{:S(2)}) collective-permute-start(bf16[1,64,2048]{2,1,0:T(8,128)(2,1)S(1)} %get-tuple-element.166), channel_id=1, source_target_pairs={{0,24},{8,0},{16,8},{24,16},{1,25},{9,1},{17,9},{25,17},{2,26},{10... | collective-permute-start | bytes 786440 | tf_op jit(solution)/shard_map/ppermute | solution.py:36
  726.6 21.6 %collective-permute-start.10 = (bf16[1,64,2048]{2,1,0:T(8,128)(2,1)S(1)}, bf16[1,64,2048]{2,1,0:T(8,128)(2,1)S(1)}, u32[]{:S(2)}, u32[]{:S(2)}) collective-permute-start(bf16[1,64,2048]{2,1,0:T(8,128)(2,1)S(1)} %get-tuple-element.165), channel_id=1, source_target_pairs={{0,16},{8,24},{16,0},{24,8},{1,17},{9,25},{17,1},{25,9},{2,18},{10... | collective-permute-start | bytes 786440 | tf_op jit(solution)/shard_map/ppermute | solution.py:36
  726.7 21.5 %collective-permute-start.18 = (bf16[4,32,2304]{2,1,0:T(8,128)(2,1)S(1)}, bf16[4,32,2304]{2,1,0:T(8,128)(2,1)S(1)}, u32[]{:S(2)}, u32[]{:S(2)}) collective-permute-start(bf16[4,32,2304]{2,1,0:T(8,128)(2,1)S(1)} %pad_maximum_fusion.13.refs_0_), channel_id=1, source_target_pairs={{0,4},{2,6},{4,0},{6,2},{1,5},{3,7},{5,1},{7,3},{8,12},{10,14},{12... | collective-permute-start | bytes 1769480 | tf_op jit(solution)/shard_map/ppermute | solution.py:41
  728.3 20.5 %collective-permute-start.29 = (bf16[4,32,3840]{2,1,0:T(8,128)(2,1)S(1)}, bf16[4,32,3840]{2,1,0:T(8,128)(2,1)S(1)}, u32[]{:S(2)}, u32[]{:S(2)}) collective-permute-start(bf16[4,32,3840]{2,1,0:T(8,128)(2,1)S(1)} %collective-permute-done.27.refs_1_), channel_id=1, source_target_pairs={{0,2},{2,0},{4,6},{6,4},{1,3},{3,1},{5,7},{7,5},{8,10},{10,8},{12,... | collective-permute-start | bytes 2949128 | tf_op jit(solution)/shard_map/ppermute | solution.py:41
  731.4 17.3 %collective-permute-start.11 = (bf16[1,64,2048]{2,1,0:T(8,128)(2,1)S(1)}, bf16[1,64,2048]{2,1,0:T(8,128)(2,1)S(1)}, u32[]{:S(2)}, u32[]{:S(2)}) collective-permute-start(bf16[1,64,2048]{2,1,0:T(8,128)(2,1)S(1)} %get-tuple-element.164), channel_id=1, source_target_pairs={{0,8},{8,16},{16,24},{24,0},{1,9},{9,17},{17,25},{25,1},{2,10},{10... | collective-permute-start | bytes 786440 | tf_op jit(solution)/shard_map/ppermute | solution.py:36
  (70 other events, 1164.3 us)

commit v5 on v4

--- a/solution.py
+++ b/solution.py
@@ -654,6 +654,34 @@
     )(query, bias, grad, log_total, acts, kv_own, *slots)
 
 
+class Ring:
+    def __init__(self, room, sems, at, tile_at):
+        self.room, self.sems, self.at, self.tile_at = room, sems, at, tile_at
+
+    def copy(self, t):
+        slot = lax.rem(t, 2)
+        return pltpu.make_async_copy(
+            self.tile_at(t), self.room.at[slot], self.sems.at[self.at + slot]
+        )
+
+    def prefetch(self):
+        self.copy(0).start()
+        self.copy(1).start()
+
+    def run(self, n, body):
+        def step(t, carry):
+            self.copy(t).wait()
+            body(t, self.room.at[lax.rem(t, 2)])
+
+            @pl.when(t + 2 < n)
+            def _():
+                self.copy(t + 2).start()
+
+            return carry
+
+        lax.fori_loop(0, n, step, 0)
+
+
 def norm_parts(values):
     center = values - jnp.mean(values, axis=-1, keepdims=True)
     rstd = lax.rsqrt(jnp.mean(center * center, axis=-1, keepdims=True) + NORM_EPS)
@@ -664,6 +692,265 @@
     first = jnp.mean(dhat, axis=-1, keepdims=True)
     second = jnp.mean(dhat * hat, axis=-1, keepdims=True)
     return rstd * (dhat - first - hat * second)
+
+
+def gelu_both(pre):
+    square = pre * pre
+    bent = jnp.tanh(GELU_COEF * (pre + 0.044715 * square * pre))
+    out = 0.5 * pre * (1.0 + bent)
+    slope = 0.5 * (1.0 + bent) + 0.5 * pre * (1.0 - bent * bent) * GELU_COEF * (
+        1.0 + 3.0 * 0.044715 * square
+    )
+    return out.astype(BF16), slope.astype(BF16)
+
+
+def middle(x_all, part_out, other_out, cot_all, picked, gain, shift_by, weights, maps):
+    per, loc, width = x_all.shape
+    out_x, up_x, down_x = weights
+    a_up, b_out, b_down, a_down, b_up = maps
+    wide, units = up_x.shape
+    width_here = out_x.shape[0]
+    tile = 512
+    chunk = 32
+    n_wide = width // tile
+    n_swap = n_wide + 1
+
+    def kernel(*refs):
+        pick_ref, gain_ref, shift_ref, a_up_ref, b_out_ref, b_down_ref, a_down_ref, b_up_ref = refs[:8]
+        x_ref, first_ref, second_ref, cot_ref, out_ref, up_ref, down_ref = refs[8:15]
+        h_out, gelu_out, acts_out, dd_out, dpre_out, dy1_out, da_out = refs[15:22]
+        adapt_out_ref, adapt_down_ref, dadapt_up_ref, ctx_ref = refs[22:26]
+        (send, recv, ring_sem, sems) = refs[26:30]
+        (up_room, down_room, down_rows, up_rows) = refs[30:34]
+        (stage, part, got, hat1, rstd1, keep32, slope, gelu, wide_v, turned, dpre_t) = refs[34:]
+        partner = {"tp": 1 - lax.axis_index("tp")}
+
+        up = Ring(up_room, ring_sem, 0, lambda t: up_ref.at[:, ds(t * tile, tile)])
+        down = Ring(down_room, ring_sem, 2, lambda t: down_ref.at[:, ds(t * tile, tile)])
+        down_r = Ring(down_rows, ring_sem, 4, lambda t: down_ref.at[ds(t * tile, tile)])
+        up_r = Ring(up_rows, ring_sem, 6, lambda t: up_ref.at[ds(t * tile, tile)])
+        out_r = Ring(down_rows, ring_sem, 4, lambda t: out_ref.at[ds(t * tile, tile)])
+
+        busy = {}
+        used = [0]
+
+        def move(source, target, key):
+            copy = pltpu.make_async_copy(source, target, sems.at[used[0]])
+            used[0] += 1
+            copy.start()
+            busy.setdefault(key, []).append(copy)
+
+        def free(*keys):
+            for key in keys:
+                for copy in busy.pop(key, []):
+                    copy.wait()
+
+        def swap_copy(turn, g, t, size):
+            at = ds(t * tile, size)
+            sem = (turn * per + g) * n_swap + t
+            return pltpu.make_async_remote_copy(
+                src_ref=part.at[g, :, at],
+                dst_ref=got.at[turn, g, :, at],
+                send_sem=send.at[sem],
+                recv_sem=recv.at[sem],
+                device_id=partner,
+                device_id_type=pl.DeviceIdType.MESH,
+            )
+
+        def swapped(turn, g):
+            for t in range(n_swap):
+                copy = swap_copy(turn, g, t, tile if t < n_wide else NR)
+                copy.wait_recv()
+                copy.wait_send()
+
+        def by_rows(body):
+            def step(r, carry):
+                body(pl.ds(pl.multiple_of(r * chunk, chunk), chunk))
+                return carry
+
+            lax.fori_loop(0, loc // chunk, step, 0)
+
+        barrier = pltpu.get_barrier_semaphore()
+        pl.semaphore_signal(
+            barrier, inc=1, device_id=partner, device_id_type=pl.DeviceIdType.MESH
+        )
+        for g in range(per):
+            move(x_ref.at[g], stage.at[g], ("stage", g))
+            move(first_ref.at[g], part.at[g], ("part", g))
+            move(second_ref.at[g], slope.at[g, :, pl.ds(0, wide)], ("slope", g))
+        up.prefetch()
+        down.prefetch()
+        pl.semaphore_wait(barrier, 1)
+
+        for g in range(per):
+            free(("stage", g), ("part", g), ("slope", g), "wide", "gelu")
+            pick = pick_ref[g]
+
+            def first_norm(rows, g=g, pick=pick):
+                total = part[g, rows, :].astype(F32) + slope[g, rows, :wide].astype(F32)
+                code = (total[:, width:] * pick).astype(BF16)
+                adapt_out_ref[g, rows, :] = code
+                y1 = stage[g, rows, :].astype(F32) + total[:, :width] + dot(code, b_out_ref[...])
+                hat, rstd = norm_parts(y1)
+                hat1[g, rows, :] = hat
+                rstd1[g, rows, :] = jnp.broadcast_to(rstd, (chunk, 128))
+                low = (hat * gain_ref[0:1, :] + shift_ref[0:1, :]).astype(BF16)
+                wide_v[rows, :width] = low
+                wide_v[rows, width:] = (dot(low, a_up_ref[...]) * pick).astype(BF16)
+
+            by_rows(first_norm)
+            move(wide_v, h_out.at[g], "wide")
+            move(cot_ref.at[g], stage.at[g], ("stage", g))
+
+            def up_tile(t, room, g=g):
+                at = ds(t * tile, tile)
+                value, factor = gelu_both(dot(wide_v[...], room[...]))
+                gelu[:, at] = value
+                slope[g, :, at] = factor
+
+            up.run(units // tile, up_tile)
+            if g + 1 < per:
+                up.prefetch()
+            else:
+                down_r.prefetch()
+            move(gelu, gelu_out.at[g], "gelu")
+
+            def down_tile(t, room, g=g):
+                part[g, :, ds(t * tile, tile)] = dot(gelu[...], room[...]).astype(BF16)
+                swap_copy(0, g, t, tile).start()
+
+            down.run(n_wide, down_tile)
+            if g + 1 < per:
+                down.prefetch()
+            else:
+                up_r.prefetch()
+            part[g, :, width:] = dot(gelu[...], a_down_ref[...]).astype(BF16)
+            swap_copy(0, g, n_wide, NR).start()
+
+        for g in range(per):
+            swapped(0, g)
+            free(("stage", g), "wide")
+            pick = pick_ref[g]
+
+            def second_norm(rows, g=g, pick=pick):
+                total = part[g, rows, :].astype(F32) + got[0, g, rows, :].astype(F32)
+                code = (total[:, width:] * pick).astype(BF16)
+                adapt_down_ref[g, rows, :] = code
+                hidden = hat1[g, rows, :] * gain_ref[0:1, :] + shift_ref[0:1, :]
+                hat, rstd = norm_parts(hidden + total[:, :width] + dot(code, b_down_ref[...]))
+                part[g, rows, :width] = (hat * gain_ref[1:2, :] + shift_ref[1:2, :]).astype(BF16)
+                dy2 = norm_back(hat, rstd, stage[g, rows, :].astype(F32) * gain_ref[1:2, :])
+                keep32[g, rows, :] = dy2
+                low = dy2.astype(BF16)
+                wide_v[rows, :width] = low
+                wide_v[rows, width:] = (dot_nt(low, b_down_ref[...]) * pick).astype(BF16)
+
+            by_rows(second_norm)
+            move(part.at[g, :, pl.ds(0, width)], acts_out.at[g], ("part", g))
+            move(wide_v, dd_out.at[g], "wide")
+            turned[...] = wide_v[...].T
+
+            def down_back(t, room, g=g):
+                at = ds(t * tile, tile)
+                block = dot(room[...], turned[...]).T
+                low = (block * slope[g, :, at].astype(F32)).astype(BF16)
+                slope[g, :, at] = low
+                dpre_t[at, :] = low.T
+
+            down_r.run(units // tile, down_back)
+            (down_r if g + 1 < per else out_r).prefetch()
+            move(slope.at[g], dpre_out.at[g], ("slope", g))
+            free(("part", g))
+
+            def up_back(t, room, g=g):
+                part[g, :, ds(t * tile, tile)] = dot(room[...], dpre_t[...]).T.astype(BF16)
+                swap_copy(1, g, t, tile).start()
+
+            up_r.run(n_wide, up_back)
+            if g + 1 < per:
+                up_r.prefetch()
+            part[g, :, width:] = dot(b_up_ref[...], dpre_t[...]).T.astype(BF16)
+            swap_copy(1, g, n_wide, NR).start()
+
+        for g in range(per):
+            swapped(1, g)
+            free("wide")
+            pick = pick_ref[g]
+
+            def first_back(rows, g=g, pick=pick):
+                total = part[g, rows, :].astype(F32) + got[1, g, rows, :].astype(F32)
+                code = (total[:, width:] * pick).astype(BF16)
+                dadapt_up_ref[g, rows, :] = code
+                dh1 = keep32[g, rows, :] + total[:, :width] + dot_nt(code, a_up_ref[...])
+                rstd = rstd1[g, rows, 0:1]
+                dy1 = norm_back(hat1[g, rows, :], rstd, dh1 * gain_ref[0:1, :])
+                keep32[g, rows, :] = dy1
+                low = dy1.astype(BF16)
+                wide_v[rows, :width] = low
+                wide_v[rows, width:] = (dot_nt(low, b_out_ref[...]) * pick).astype(BF16)
+
+            by_rows(first_back)
+            move(keep32.at[g], dy1_out.at[g], "dy1")
+            move(wide_v, da_out.at[g], "wide")
+            turned[...] = wide_v[...].T
+
+            def out_back(t, room, g=g):
+                ctx_ref[g, :, ds(t * tile, tile)] = dot(room[...], turned[...]).T.astype(BF16)
+
+            out_r.run(width_here // tile, out_back)
+            if g + 1 < per:
+                out_r.prefetch()
+        free(*list(busy))
+
+    vmem, anywhere = pl.BlockSpec(memory_space=pltpu.VMEM), pl.BlockSpec(memory_space=pl.ANY)
+    row = (per, loc)
+    outputs = [
+        (row + (wide,), BF16, anywhere),
+        (row + (units,), BF16, anywhere),
+        (row + (width,), BF16, anywhere),
+        (row + (wide,), BF16, anywhere),
+        (row + (units,), BF16, anywhere),
+        (row + (width,), F32, anywhere),
+        (row + (wide,), BF16, anywhere),
+        (row + (NR,), BF16, vmem),
+        (row + (NR,), BF16, vmem),
+        (row + (NR,), BF16, vmem),
+        (row + (width_here,), BF16, vmem),
+    ]
+    n_copy = 2 * per * n_swap
+    return pl.pallas_call(
+        kernel,
+        in_specs=[vmem] * 8 + [anywhere] * 7,
+        out_specs=[space for _, _, space in outputs],
+        out_shape=[jax.ShapeDtypeStruct(shape, dtype) for shape, dtype, _ in outputs],
+        scratch_shapes=[
+            pltpu.SemaphoreType.DMA((n_copy,)),
+            pltpu.SemaphoreType.DMA((n_copy,)),
+            pltpu.SemaphoreType.DMA((8,)),
+            pltpu.SemaphoreType.DMA((11 * per,)),
+            pltpu.VMEM((2, wide, tile), BF16),
+            pltpu.VMEM((2, units, tile), BF16),
+            pltpu.VMEM((2, tile, wide), BF16),
+            pltpu.VMEM((2, tile, units), BF16),
+            pltpu.VMEM(row + (width,), BF16),
+            pltpu.VMEM(row + (wide,), BF16),
+            pltpu.VMEM((2,) + row + (wide,), BF16),
+            pltpu.VMEM(row + (width,), F32),
+            pltpu.VMEM(row + (128,), F32),
+            pltpu.VMEM(row + (width,), F32),
+            pltpu.VMEM(row + (units,), BF16),
+            pltpu.VMEM((loc, units), BF16),
+            pltpu.VMEM((loc, wide), BF16),
+            pltpu.VMEM((wide, loc), BF16),
+            pltpu.VMEM((units, loc), BF16),
+        ],
+        compiler_params=pltpu.CompilerParams(
+            collective_id=3, has_side_effects=True, vmem_limit_bytes=62 << 20
+        ),
+    )(
+        picked, gain, shift_by, a_up, b_out, b_down, a_down, b_up,
+        x_all, part_out, other_out, cot_all, out_x, up_x, down_x,
+    )
 
 
 def mm(left, right, nt, finish, tile, n_out=1, beside=None):
@@ -716,9 +1003,9 @@
     return out[0] if n_out == 1 else out
 
 
-def compact(pairs, n_part):
-    rows = pairs[0][0].shape[0]
-    sizes = [values.shape[1] // n_part for _, values in pairs]
+def compact(arrays, pairs, n_part):
+    per, loc = arrays[0].shape[:2]
+    sizes = [values[2] // n_part for _, values in pairs]
     total = sum(sizes)
 
     def kernel(*refs):
@@ -727,26 +1014,27 @@
         rank = lax.broadcasted_iota(jnp.int32, (NR, RANK), 1)
         used = jnp.where(lax.rem(column, RANK) == rank, 1.0, 0.0).astype(BF16)
         start = 0
-        for i, size in enumerate(sizes):
-            codes = dot(refs[2 * i][...], used).astype(BF16)
-            block = dot_tn(codes, refs[2 * i + 1][...]).astype(BF16)
+        for (codes, values), size in zip(pairs, sizes):
+            code = refs[codes[0]][0, :, codes[1] : codes[1] + codes[2]]
+            value = refs[values[0]][0, :, values[1] : values[1] + values[2]]
+            block = dot_tn(dot(code, used).astype(BF16), value).astype(BF16)
             for part in range(n_part):
                 out_ref[part, :, start : start + size] = block[:, part * size : (part + 1) * size]
             start += size
 
-    flat = [array for pair in pairs for array in pair]
     return pl.pallas_call(
         kernel,
-        in_specs=[pl.BlockSpec(memory_space=pltpu.VMEM)] * len(flat),
-        out_specs=pl.BlockSpec(memory_space=pltpu.VMEM),
-        out_shape=jax.ShapeDtypeStruct((n_part, RANK, total), BF16),
-        compiler_params=pltpu.CompilerParams(vmem_limit_bytes=40 << 20),
+        grid=(per,),
+        in_specs=[pl.BlockSpec((1,) + x.shape[1:], lambda n: (n, 0, 0)) for x in arrays],
+        out_specs=pl.BlockSpec((n_part, RANK, total), lambda n: (0, n, 0)),
+        out_shape=jax.ShapeDtypeStruct((n_part, per * RANK, total), BF16),
+        compiler_params=pltpu.CompilerParams(vmem_limit_bytes=48 << 20),
         cost_estimate=pl.CostEstimate(
-            flops=2 * rows * RANK * total * n_part * 8,
-            bytes_accessed=2 * rows * total * n_part,
+            flops=2 * per * loc * RANK * total * n_part * 8,
+            bytes_accessed=2 * per * loc * total * n_part,
             transcendentals=0,
         ),
-    )(*flat)
+    )(*arrays)
 
 
 def combine(pieces, chosen, shapes):
@@ -794,10 +1082,6 @@
 
 def as_low(block):
     return (block.astype(BF16),)
-
-
-def times(block, factor):
-    return ((block * factor.astype(F32)).astype(BF16),)
 
 
 def after(value, *first):
@@ -931,69 +1215,38 @@
     )
     kv_all = [kv_own] + list(moved[: n_ctx - 1])
     cot_all, out_x, up_x, down_x, context, log_total, part_out, other_out = moved[n_ctx - 1 :]
-    cot_flat = cot_all.reshape(per * loc, width)
 
     groups = range(n_group)
     picks = [jnp.repeat(take(picked, g * g_per, g_per), loc, axis=0) for g in groups]
     part = [slice(g * g_rows, (g + 1) * g_rows) for g in groups]
-    seq = [slice(n * loc, (n + 1) * loc) for n in range(g_per)]
     x_rows = [x_flat[part[g]] for g in groups]
 
-    ctx_flat = context.reshape(per * loc, heads_width)
-    ctx_rows = [ctx_flat[part[g]] for g in groups]
-    summed = (part_out.astype(F32) + other_out.astype(F32)).reshape(per * loc, width + NR)
-    summed = [summed[part[g]] for g in groups]
-    adapt_out, hat1, rstd1, hidden, hidden_low, adapt_up, gelu_out, slope = ([] for _ in range(8))
-    for g in groups:
-        adapt_out.append((summed[g][:, width:] * picks[g]).astype(BF16))
-        y1 = x_rows[g].astype(F32) + summed[g][:, :width] + dot(adapt_out[g], b_out)
-        parts = norm_parts(y1)
-        hat1.append(parts[0])
-        rstd1.append(parts[1])
-        hidden.append(parts[0] * ln_gain[0] + ln_bias[0])
-        hidden_low.append(hidden[g].astype(BF16))
-        adapt_up.append((dot(hidden_low[g], a_up) * picks[g]).astype(BF16))
-        wide = jnp.concatenate([hidden_low[g], adapt_up[g]], axis=1)
-        pair = mm(wide, up_x, False, gelu_both, 1024, 2)
-        gelu_out.append(pair[0])
-        slope.append(pair[1])
-    summed = both_in_turn([mm(gelu_out[g], down_x, False, as_low, 768) for g in groups])
-    adapt_down, acts, dy2, d_down, dadapt_down, d_pre = ([] for _ in range(6))
-    for g in groups:
-        adapt_down.append((summed[g][:, width:] * picks[g]).astype(BF16))
-        hat2, rstd2 = norm_parts(hidden[g] + summed[g][:, :width] + dot(adapt_down[g], b_down))
-        acts.append((hat2 * ln_gain[1] + ln_bias[1]).astype(BF16))
-        dy2.append(norm_back(hat2, rstd2, cot_flat[part[g]].astype(F32) * ln_gain[1]))
-        d_down.append(dy2[g].astype(BF16))
-        dadapt_down.append((dot_nt(d_down[g], b_down) * picks[g]).astype(BF16))
-        wide = jnp.concatenate([d_down[g], dadapt_down[g]], axis=1)
-        d_pre.append(mm(wide, down_x, True, times, 1024, 1, slope[g]))
-    summed = both_in_turn([mm(d_pre[g], up_x, True, as_low, 768) for g in groups])
-    dadapt_up, dy1, d_attn, dadapt_out, backs = ([] for _ in range(5))
-    for g in groups:
-        dadapt_up.append((summed[g][:, width:] * picks[g]).astype(BF16))
-        dh1 = dy2[g] + summed[g][:, :width] + dot_nt(dadapt_up[g], a_up)
-        dy1.append(norm_back(hat1[g], rstd1[g], dh1 * ln_gain[0]))
-        d_attn.append(dy1[g].astype(BF16))
-        dadapt_out.append((dot_nt(d_attn[g], b_out) * picks[g]).astype(BF16))
-        wide = jnp.concatenate([d_attn[g], dadapt_out[g]], axis=1)
-        backs.append(mm(wide, out_x, True, as_low, 512).reshape(g_per, loc, heads_width))
+    (wide_h, gelu_out, acts, wide_d, d_pre, dy1, wide_a, adapt_out, adapt_down, dadapt_up, d_context) = middle(
+        x_all.reshape(per, loc, width),
+        part_out,
+        other_out,
+        cot_all.reshape(per, loc, width),
+        picked[:, None, :],
+        ln_gain,
+        ln_bias,
+        (out_x, up_x, down_x),
+        (a_up, b_out, b_down, a_down, b_up),
+    )
     d_query, d_pair, activations = attend_back(
         proj_all[:, :heads_width].reshape(per, loc, heads_width),
         kv_own,
         kv_all[1:],
         bias_all,
-        jnp.concatenate(backs, axis=0),
+        d_context,
         log_total,
-        jnp.concatenate(acts, axis=0).reshape(per, n_fsdp, piece, width),
+        acts.reshape(per, n_fsdp, piece, width),
         n_fsdp,
         n_ctx,
     )
     d_query = d_query.reshape(per * loc, heads_width)
     d_pair = d_pair.reshape(2, per * loc, heads_width)
 
-    def gathered(parts):
-        mine = jnp.concatenate(parts, axis=1)
+    def gathered(mine):
         blocks = [
             lax.dynamic_index_in_dim(mine, ct ^ offset, 0, False) for offset in offsets(n_ctx)
         ]
@@ -1001,23 +1254,24 @@
         got = jnp.stack([own] + [shift(own, "fsdp", step) for step in range(1, n_fsdp)])
         return spread([got], "ctx")
 
-    early_in = []
-    for g in groups:
-        pairs = (
-            (adapt_down[g], d_down[g]),
-            (dadapt_down[g], gelu_out[g]),
-            (adapt_up[g], d_pre[g]),
-            (dadapt_up[g], hidden_low[g]),
-            (adapt_out[g], d_attn[g]),
-            (dadapt_out[g], ctx_rows[g]),
-        )
-        early_in.append(pairs)
-    early_in = after(early_in, d_query)
-    early = gathered(
-        [compact([(c[r], v[r]) for c, v in early_in[g]], n_ctx) for g in groups for r in seq]
+    early_in = after(
+        (adapt_down, wide_d, gelu_out, wide_h, d_pre, dadapt_up, adapt_out, wide_a, context),
+        d_query,
     )
-
-    ins, late = [], []
+    code, row, unit = (0, NR), (0, width), (0, units)
+    tail = (width, NR)
+    early_pairs = [
+        ((0,) + code, (1,) + row),
+        ((1,) + tail, (2,) + unit),
+        ((3,) + tail, (4,) + unit),
+        ((5,) + code, (3,) + row),
+        ((6,) + code, (7,) + row),
+        ((7,) + tail, (8, 0, heads_width)),
+    ]
+    early = gathered(compact(early_in, early_pairs, n_ctx))
+
+    dy1_flat = dy1.reshape(per * loc, width)
+    ins, dadapt_all = [], []
     d_proj = [
         jnp.concatenate([d_query[part[g]], d_pair[0, part[g]], d_pair[1, part[g]]], axis=1)
         for g in groups
@@ -1026,19 +1280,19 @@
     for g in groups:
         pick3 = jnp.concatenate([picks[g]] * 3, axis=1)
         dadapt_in = (summed[g][:, width:] * pick3).astype(BF16)
-        d_x = (dy1[g] + summed[g][:, :width] + dot_nt(dadapt_in, a_in)).astype(BF16)
+        d_x = (dy1_flat[part[g]] + summed[g][:, :width] + dot_nt(dadapt_in, a_in)).astype(BF16)
         ins.append(undeal(d_x, g))
-        adapt_in = adapt_all[part[g]]
-        for r in seq:
-            pairs = []
-            for j in range(3):
-                codes = slice(j * NR, (j + 1) * NR)
-                columns = slice(j * heads_width, (j + 1) * heads_width)
-                pairs.append((adapt_in[r, codes], d_proj[g][r, columns]))
-            for j in range(3):
-                pairs.append((dadapt_in[r, j * NR : (j + 1) * NR], x_rows[g][r]))
-            late.append(compact(pairs, n_ctx))
-    late = gathered(late)
+        dadapt_all.append(dadapt_in)
+    late_in = (
+        adapt_all.reshape(per, loc, 3 * NR),
+        jnp.concatenate(dadapt_all, axis=0).reshape(per, loc, 3 * NR),
+        jnp.concatenate(d_proj, axis=0).reshape(per, loc, 3 * heads_width),
+        x_flat.reshape(per, loc, width),
+    )
+    late_pairs = [
+        ((0, j * NR, NR), (2, j * heads_width, heads_width)) for j in range(3)
+    ] + [((1, j * NR, NR), (3,) + row) for j in range(3)]
+    late = gathered(compact(late_in, late_pairs, n_ctx))
 
     def assemble(parts):
         full = jnp.zeros((seqs, piece, width), BF16)

time: 768 us -> 717 us (0.934)
  waiting for transfers between devices: 130 us -> 59.2 us
  Pallas kernels: 517 us -> 563 us
  other arithmetic: 30.8 us -> 18.1 us
  matrix products: 12.3 us -> 2.81 us
    pallas_call x4 -> x3, Pallas kernels: 7.8 us -> 140 us  [the longest x1 128 us: middle(): pl.pallas_call(kernel, in_specs=[vmem] * 8 + [anywhere] * 7, out_specs=[s...]
    pallas_call x13 -> x3, Pallas kernels: 114 us -> 28.6 us  [mm(): pl.pallas_call(kernel, grid=(pl.cdiv(columns, tile),), in_specs=[pl.Block...]
    ppermute x18 -> x14, waiting for transfers between devices: 95.3 us -> 14.8 us  [swap(): return lax.ppermute(block, axis, [(i, i ^ mask) for i in range(n)])]
    ppermute x12, waiting for transfers between devices: 34.2 us -> 44.4 us  [shift(): return lax.ppermute(block, axis, [(i, (i + step) % n) for i in range(n)])]
    convert_element_type x10 -> x0, other arithmetic: 8.64 us -> none  [the longest x2 4.07 us: local(): d_attn.append(dy1[g].astype(BF16))]
    ppermute x18 -> x14, starting transfers between devices: 15.7 us -> 9.73 us  [swap(): return lax.ppermute(block, axis, [(i, i ^ mask) for i in range(n)])]
    unnamed x130 -> x66, local copies, waits for them, and re-layouts: 15.7 us -> 18.5 us
  transfers between devices with their start and end apart: 30 -> 26, of which waited for: 15 -> 11; matrix products, arithmetic and copies ran while one was open for 3% -> 3% of each run, Pallas kernels for 15% -> 13%
where the time goes in v5:
time: 717 us; the launch traced here: 705 us
  Pallas kernels  563 us (79%)
  waiting for transfers between devices  59.2 us (8%)
  starting transfers between devices  35.8 us (5%)
  local copies, waits for them, and re-layouts  23.6 us (3%)
  other arithmetic  18.1 us (3%)
    pallas_call x1, Pallas kernels, forward_and_gather(): pl.pallas_call(kernel, in_specs=[vmem, vmem] + [anywhere] * 8, out_specs=...  225 us
    pallas_call x1, Pallas kernels, middle(): pl.pallas_call(kernel, in_specs=[vmem] * 8 + [anywhere] * 7, out_specs=[s...  128 us
    pallas_call x1, Pallas kernels, move(): pl.pallas_call(kernel, in_specs=spaces, out_specs=[pl.BlockSpec(memory_sp...  100 us
    pallas_call x1, Pallas kernels, attend_back(): pl.pallas_call(kernel, in_specs=[vmem] * 4 + [anywhere] * (1 + n_ctx), ou...  62.8 us
    ppermute x12, waiting for transfers between devices, shift(): return lax.ppermute(block, axis, [(i, (i + step) % n) for i in range(n)])  44.4 us
    pallas_call x3, Pallas kernels, mm(): pl.pallas_call(kernel, grid=(pl.cdiv(columns, tile),), in_specs=[pl.Block...  28.6 us
    ppermute x12, starting transfers between devices, shift(): return lax.ppermute(block, axis, [(i, (i + step) % n) for i in range(n)])  26.1 us
    unnamed x66, local copies, waits for them, and re-layouts  18.5 us
  transfers between devices with their start and end apart: 26, of which 11 were waited for; matrix products, arithmetic and copies ran while one was open for 3% of the time, Pallas kernels for 13%

profile of v5, /device:TPU:0, one launch (start us, length us, event | category | flops | bytes accessed | tf_op | source)
XLA Modules:
  0.0 704.6 jit_solution(9843306890930652277)
XLA Ops:
  8.2 100.0 %shard_map.258 = (bf16[2,4,64,2048]{3,2,1,0:T(8,128)(2,1)S(1)}, bf16[2432,3072]{1,0:T(8,128)(2,1)}) custom-call(bf16[8,64,2048]{2,1,0:T(8,128)(2,1)S(1)} %copy-done.6, bf16[3,512,1024]{2,1,0:T(8,128)(2,1)S(1)} %copy-done.4, bf16[3,128,1024]{2,1,0:T(8,128)(2,1)S(1)} %copy-done.11), custom_call_target="tpu_custom_call" | custom-call | tf_op jit(solution)/shard_map/pallas_call | solution.py:333
  110.4 11.2 %shard_map.259 = bf16[512,3072]{1,0:T(8,128)(2,1)S(1)} custom-call(bf16[512,2432]{1,0:T(8,128)(2,1)S(1)} %pad_maximum_fusion.left_ref, bf16[2432,3072]{1,0:T(8,128)(2,1)} %get-tuple-element.60.right_ref), custom_call_target="tpu_custom_call" | custom-call | flops 7650410496 | bytes 35520512 | tf_op jit(solution)/shard_map/pallas_call | solution.py:983
  124.5 224.6 %shard_map.260 = (bf16[2,2,256,1024]{3,2,1,0:T(8,128)(2,1)}, bf16[2,2,256,1024]{3,2,1,0:T(8,128)(2,1)}, bf16[2,2,256,1024]{3,2,1,0:T(8,128)(2,1)}, bf16[2,4,64,2...) custom-call(bf16[2,256,1024]{2,1,0:T(8,128)(2,1)S(1)} %bitcast.95, ...), custom_call_target="tpu_custom_call" | custom-call | tf_op jit(solution)/shard_map/pallas_call | solution.py:496
  350.7 127.7 %shard_map.261 = (bf16[2,256,2176]{2,1,0:T(8,128)(2,1)}, bf16[2,256,4096]{2,1,0:T(8,128)(2,1)}, bf16[2,256,2048]{2,1,0:T(8,128)(2,1)}, bf16[2,256,2176]{2,1,0:T(...) custom-call(f32[2,1,128]{2,1,0:T(1,128)} %compare_convert_fusion.ref, ...), custom_call_target="tpu_custom_call" | custom-call | tf_op jit(solution)/shard_map/pallas_call | solution.py:921
  484.1 7.4 %shard_map.267 = bf16[4,32,3840]{2,1,0:T(8,128)(2,1)S(1)} custom-call(bf16[2,256,128]{2,1,0:T(8,128)(2,1)S(1)} %copy-done.14, bf16[2,256,2176]{2,1,0:T(8,128)(2,1)S(1)} %copy-done.5, bf16[2,256,4096]{2,1,0:T(8,128)(2,1)} %get-tuple-element.91.refs_2_, bf16[2,256,2176]{2,1,0:T(8,128)(2,1)} %get-tuple-element.92.refs_3_, ...), custom_call_target="tpu_custom_call" | custom-call | flops 2013265920 | bytes 15728640 | tf_op jit(solution)/shard_map/pallas_call | solution.py:1025
  492.8 62.8 %shard_map.262 = (bf16[2,256,1024]{2,1,0:T(8,128)(2,1)}, bf16[2,2,256,1024]{3,2,1,0:T(8,128)(2,1)}, bf16[8,64,2048]{2,1,0:T(8,128)(2,1)}) custom-call(bf16[2,256,1024]{2,1,0:T(8,128)(2,1)} %bitcast.96, f32[2,1024,128]{2,1,0:T(8,128)} %copy-done.2, bf16[2,256,1024]{2,1,0:T(8,128)(2,1)} %get-tuple-element.67.refs_2_, f32[2,8,1,256]{3,2,1,0:T(1,128)} %copy-done.16, ...), custom_call_target="tpu_custom_call" | custom-call | tf_op jit(solution)/shard_map/pallas_call | solution.py:633
  558.6 8.7 %shard_map.264 = bf16[256,2432]{1,0:T(8,128)(2,1)S(1)} custom-call(bf16[256,3072]{1,0:T(8,128)(2,1)S(1)} %pad_maximum_fusion.3.left_ref, bf16[2432,3072]{1,0:T(8,128)(2,1)} %get-tuple-element.60.right_ref), custom_call_target="tpu_custom_call" | custom-call | flops 3825205248 | bytes 32702464 | tf_op jit(solution)/shard_map/pallas_call | solution.py:983
  568.0 8.7 %shard_map.263 = bf16[256,2432]{1,0:T(8,128)(2,1)S(1)} custom-call(bf16[256,3072]{1,0:T(8,128)(2,1)S(1)} %pad_maximum_fusion.2.left_ref, bf16[2432,3072]{1,0:T(8,128)(2,1)} %get-tuple-element.60.right_ref), custom_call_target="tpu_custom_call" | custom-call | flops 3825205248 | bytes 32702464 | tf_op jit(solution)/shard_map/pallas_call | solution.py:983
  578.2 7.0 maximum_maximum_fusion
  588.5 5.5 collective-permute-done.19
  599.9 7.0 collective-permute-done.20
  606.8 7.6 %collective-permute-done.21 = bf16[32,3840]{1,0:T(8,128)(2,1)S(1)} collective-permute-done((bf16[32,3840]{1,0:T(8,128)(2,1)}, bf16[32,3840]{1,0:T(8,128)(2,1)S(1)}, u32[]{:S(2)}, u32[]{:S(2)}) %collective-permute-start.21) | collective-permute-done | bytes 245792 | tf_op jit(solution)/shard_map/ppermute | solution.py:36
  617.1 5.8 collective-permute-done
  630.2 4.9 shard_map.265
  637.4 7.6 %collective-permute-done.1 = bf16[1,64,2048]{2,1,0:T(8,128)(2,1)S(1)} collective-permute-done((bf16[1,64,2048]{2,1,0:T(8,128)(2,1)S(1)}, bf16[1,64,2048]{2,1,0:T(8,128)(2,1)S(1)}, u32[]{:S(2)}, u32[]{:S(2)}) %collective-permute-start.1) | collective-permute-done | bytes 262176 | tf_op jit(solution)/shard_map/ppermute | solution.py:36
  646.7 3.4 collective-permute-done.10
  650.3 3.5 collective-permute-start.12
  653.8 7.5 %collective-permute-done.2 = bf16[1,64,2048]{2,1,0:T(8,128)(2,1)S(1)} collective-permute-done((bf16[1,64,2048]{2,1,0:T(8,128)(2,1)S(1)}, bf16[1,64,2048]{2,1,0:T(8,128)(2,1)S(1)}, u32[]{:S(2)}, u32[]{:S(2)}) %collective-permute-start.2) | collective-permute-done | bytes 262176 | tf_op jit(solution)/shard_map/ppermute | solution.py:36
  664.4 6.7 collective-permute-start.5
  675.0 3.1 collective-permute-done.5
  678.1 8.7 %collective-permute-start.7 = (bf16[1,64,2048]{2,1,0:T(8,128)(2,1)S(1)}, bf16[1,64,2048]{2,1,0:T(8,128)(2,1)S(1)}, u32[]{:S(2)}, u32[]{:S(2)}) collective-permute-start(bf16[1,64,2048]{2,1,0:T(8,128)(2,1)S(1)} %get-tuple-element.115), channel_id=1, source_target_pairs={{0,8},{8,16},{16,24},{24,0},{1,9},{9,17},{17,25},{25,1},{2,10},{10... | collective-permute-start | bytes 786440 | tf_op jit(solution)/shard_map/ppermute | solution.py:36
  686.8 8.1 %collective-permute-done.6 = bf16[1,64,2048]{2,1,0:T(8,128)(2,1)S(1)} collective-permute-done((bf16[1,64,2048]{2,1,0:T(8,128)(2,1)S(1)}, bf16[1,64,2048]{2,1,0:T(8,128)(2,1)S(1)}, u32[]{:S(2)}, u32[]{:S(2)}) %collective-permute-start.6) | collective-permute-done | bytes 262176 | tf_op jit(solution)/shard_map/ppermute | solution.py:36
  695.6 4.3 shard_map.268
  699.9 2.9 shard_map.266
  (159 shorter events, 58.0 us)
Async XLA Ops:
  492.3 92.9 %collective-permute-start.18 = (bf16[32,3840]{1,0:T(8,128)(2,1)}, bf16[32,3840]{1,0:T(8,128)(2,1)}, u32[]{:S(2)}, u32[]{:S(2)}) collective-permute-start(bf16[32,3840]{1,0:T(8,128)(2,1)} %get-tuple-element.124), channel_id=1, source_target_pairs={{0,2},{2,0},{4,6},{6,4},{1,3},{3,1},{5,7},{7,5},{8,10},{10,8},{12,... | collective-permute-start | bytes 737288 | tf_op jit(solution)/shard_map/ppermute | solution.py:41
  492.3 96.2 %collective-permute-start.17 = (bf16[32,3840]{1,0:T(8,128)(2,1)}, bf16[32,3840]{1,0:T(8,128)(2,1)}, u32[]{:S(2)}, u32[]{:S(2)}) collective-permute-start(bf16[32,3840]{1,0:T(8,128)(2,1)} %get-tuple-element.123), channel_id=1, source_target_pairs={{0,2},{2,0},{4,6},{6,4},{1,3},{3,1},{5,7},{7,5},{8,10},{10,8},{12,... | collective-permute-start | bytes 737288 | tf_op jit(solution)/shard_map/ppermute | solution.py:41
  567.3 57.1 %collective-permute-start.4 = (bf16[256,2432]{1,0:T(8,128)(2,1)S(1)}, bf16[256,2432]{1,0:T(8,128)(2,1)}, u32[]{:S(2)}, u32[]{:S(2)}) collective-permute-start(bf16[256,2432]{1,0:T(8,128)(2,1)S(1)} %shard_map.264), channel_id=1, source_target_pairs={{0,1},{1,0},{2,3},{3,2},{4,5},{5,4},{6,7},{7,6},{8,9},{9,8},{10,11... | collective-permute-start | bytes 3735560 | tf_op jit(solution)/shard_map/ppermute | solution.py:41
  576.7 46.2 %collective-permute-start = (bf16[256,2432]{1,0:T(8,128)(2,1)S(1)}, bf16[256,2432]{1,0:T(8,128)(2,1)}, u32[]{:S(2)}, u32[]{:S(2)}) collective-permute-start(bf16[256,2432]{1,0:T(8,128)(2,1)S(1)} %shard_map.263), channel_id=1, source_target_pairs={{0,1},{1,0},{2,3},{3,2},{4,5},{5,4},{6,7},{7,6},{8,9},{9,8},{10,11... | collective-permute-start | bytes 3735560 | tf_op jit(solution)/shard_map/ppermute | solution.py:41
  586.9 7.1 %collective-permute-start.19 = (bf16[32,3840]{1,0:T(8,128)(2,1)}, bf16[32,3840]{1,0:T(8,128)(2,1)}, u32[]{:S(2)}, u32[]{:S(2)}) collective-permute-start(bf16[32,3840]{1,0:T(8,128)(2,1)} %fusion.4), channel_id=1, source_target_pairs={{0,4},{2,6},{4,0},{6,2},{1,5},{3,7},{5,1},{7,3},{8,12},{10,14},{12... | collective-permute-start | bytes 737288 | tf_op jit(solution)/shard_map/ppermute | solution.py:41
  595.9 11.0 %collective-permute-start.20 = (bf16[32,3840]{1,0:T(8,128)(2,1)}, bf16[32,3840]{1,0:T(8,128)(2,1)S(1)}, u32[]{:S(2)}, u32[]{:S(2)}) collective-permute-start(bf16[32,3840]{1,0:T(8,128)(2,1)} %add_convert_fusion), channel_id=1, source_target_pairs={{0,8},{8,16},{16,24},{24,0},{1,9},{9,17},{17,25},{25,1},{2,10},{10... | collective-permute-start | bytes 737288 | tf_op jit(solution)/shard_map/ppermute | solution.py:36
  595.9 18.6 %collective-permute-start.21 = (bf16[32,3840]{1,0:T(8,128)(2,1)}, bf16[32,3840]{1,0:T(8,128)(2,1)S(1)}, u32[]{:S(2)}, u32[]{:S(2)}) collective-permute-start(bf16[32,3840]{1,0:T(8,128)(2,1)} %add_convert_fusion), channel_id=1, source_target_pairs={{0,16},{8,24},{16,0},{24,8},{1,17},{9,25},{17,1},{25,9},{2,18},{10... | collective-permute-start | bytes 737288 | tf_op jit(solution)/shard_map/ppermute | solution.py:36
  597.5 17.0 %collective-permute-start.22 = (bf16[32,3840]{1,0:T(8,128)(2,1)}, bf16[32,3840]{1,0:T(8,128)(2,1)S(1)}, u32[]{:S(2)}, u32[]{:S(2)}) collective-permute-start(bf16[32,3840]{1,0:T(8,128)(2,1)} %add_convert_fusion), channel_id=1, source_target_pairs={{0,24},{8,0},{16,8},{24,16},{1,25},{9,1},{17,9},{25,17},{2,26},{10... | collective-permute-start | bytes 737288 | tf_op jit(solution)/shard_map/ppermute | solution.py:36
  615.5 59.3 %collective-permute-start.23 = (bf16[4,32,3840]{2,1,0:T(8,128)(2,1)S(1)}, bf16[4,32,3840]{2,1,0:T(8,128)(2,1)S(1)}, u32[]{:S(2)}, u32[]{:S(2)}) collective-permute-start(bf16[4,32,3840]{2,1,0:T(8,128)(2,1)S(1)} %pad_maximum_fusion.4.refs_0_), channel_id=1, source_target_pairs={{0,4},{2,6},{4,0},{6,2},{1,5},{3,7},{5,1},{7,3},{8,12},{10,14},{12... | collective-permute-start | bytes 2949128 | tf_op jit(solution)/shard_map/ppermute | solution.py:41
  617.1 78.5 %collective-permute-start.24 = (bf16[4,32,3840]{2,1,0:T(8,128)(2,1)S(1)}, bf16[4,32,3840]{2,1,0:T(8,128)(2,1)S(1)}, u32[]{:S(2)}, u32[]{:S(2)}) collective-permute-start(bf16[4,32,3840]{2,1,0:T(8,128)(2,1)S(1)} %pad_maximum_fusion.4.refs_0_), channel_id=1, source_target_pairs={{0,2},{2,0},{4,6},{6,4},{1,3},{3,1},{5,7},{7,5},{8,10},{10,8},{12,... | collective-permute-start | bytes 2949128 | tf_op jit(solution)/shard_map/ppermute | solution.py:41
  635.2 11.4 %collective-permute-start.8 = (bf16[32,2304]{1,0:T(8,128)(2,1)S(1)}, bf16[32,2304]{1,0:T(8,128)(2,1)S(1)}, u32[]{:S(2)}, u32[]{:S(2)}) collective-permute-start(bf16[32,2304]{1,0:T(8,128)(2,1)S(1)} %get-tuple-element.125), channel_id=1, source_target_pairs={{0,2},{2,0},{4,6},{6,4},{1,3},{3,1},{5,7},{7,5},{8,10},{10,8},{12,... | collective-permute-start | bytes 442376 | tf_op jit(solution)/shard_map/ppermute | solution.py:41
  635.8 9.2 %collective-permute-start.1 = (bf16[1,64,2048]{2,1,0:T(8,128)(2,1)S(1)}, bf16[1,64,2048]{2,1,0:T(8,128)(2,1)S(1)}, u32[]{:S(2)}, u32[]{:S(2)}) collective-permute-start(bf16[1,64,2048]{2,1,0:T(8,128)(2,1)S(1)} %get-tuple-element.120), channel_id=1, source_target_pairs={{0,24},{8,0},{16,8},{24,16},{1,25},{9,1},{17,9},{25,17},{2,26},{10... | collective-permute-start | bytes 786440 | tf_op jit(solution)/shard_map/ppermute | solution.py:36
  637.2 24.0 %collective-permute-start.2 = (bf16[1,64,2048]{2,1,0:T(8,128)(2,1)S(1)}, bf16[1,64,2048]{2,1,0:T(8,128)(2,1)S(1)}, u32[]{:S(2)}, u32[]{:S(2)}) collective-permute-start(bf16[1,64,2048]{2,1,0:T(8,128)(2,1)S(1)} %get-tuple-element.119), channel_id=1, source_target_pairs={{0,16},{8,24},{16,0},{24,8},{1,17},{9,25},{17,1},{25,9},{2,18},{10... | collective-permute-start | bytes 786440 | tf_op jit(solution)/shard_map/ppermute | solution.py:36
  645.0 5.1 collective-permute-start.10
  650.2 11.4 %collective-permute-start.11 = (bf16[32,2304]{1,0:T(8,128)(2,1)S(1)}, bf16[32,2304]{1,0:T(8,128)(2,1)S(1)}, u32[]{:S(2)}, u32[]{:S(2)}) collective-permute-start(bf16[32,2304]{1,0:T(8,128)(2,1)S(1)} %add_convert_fusion.1), channel_id=1, source_target_pairs={{0,8},{8,16},{16,24},{24,0},{1,9},{9,17},{17,25},{25,1},{2,10},{10... | collective-permute-start | bytes 442376 | tf_op jit(solution)/shard_map/ppermute | solution.py:36
  650.3 14.1 %collective-permute-start.12 = (bf16[32,2304]{1,0:T(8,128)(2,1)S(1)}, bf16[32,2304]{1,0:T(8,128)(2,1)S(1)}, u32[]{:S(2)}, u32[]{:S(2)}) collective-permute-start(bf16[32,2304]{1,0:T(8,128)(2,1)S(1)} %add_convert_fusion.1), channel_id=1, source_target_pairs={{0,16},{8,24},{16,0},{24,8},{1,17},{9,25},{17,1},{25,9},{2,18},{10... | collective-permute-start | bytes 442376 | tf_op jit(solution)/shard_map/ppermute | solution.py:36
  661.2 12.3 %collective-permute-start.13 = (bf16[32,2304]{1,0:T(8,128)(2,1)S(1)}, bf16[32,2304]{1,0:T(8,128)(2,1)S(1)}, u32[]{:S(2)}, u32[]{:S(2)}) collective-permute-start(bf16[32,2304]{1,0:T(8,128)(2,1)S(1)} %add_convert_fusion.1), channel_id=1, source_target_pairs={{0,24},{8,0},{16,8},{24,16},{1,25},{9,1},{17,9},{25,17},{2,26},{10... | collective-permute-start | bytes 442376 | tf_op jit(solution)/shard_map/ppermute | solution.py:36
  661.6 12.0 %collective-permute-start.3 = (bf16[1,64,2048]{2,1,0:T(8,128)(2,1)S(1)}, bf16[1,64,2048]{2,1,0:T(8,128)(2,1)S(1)}, u32[]{:S(2)}, u32[]{:S(2)}) collective-permute-start(bf16[1,64,2048]{2,1,0:T(8,128)(2,1)S(1)} %get-tuple-element.118), channel_id=1, source_target_pairs={{0,8},{8,16},{16,24},{24,0},{1,9},{9,17},{17,25},{25,1},{2,10},{10... | collective-permute-start | bytes 786440 | tf_op jit(solution)/shard_map/ppermute | solution.py:36
  664.4 13.7 %collective-permute-start.5 = (bf16[1,64,2048]{2,1,0:T(8,128)(2,1)S(1)}, bf16[1,64,2048]{2,1,0:T(8,128)(2,1)S(1)}, u32[]{:S(2)}, u32[]{:S(2)}) collective-permute-start(bf16[1,64,2048]{2,1,0:T(8,128)(2,1)S(1)} %get-tuple-element.117), channel_id=1, source_target_pairs={{0,24},{8,0},{16,8},{24,16},{1,25},{9,1},{17,9},{25,17},{2,26},{10... | collective-permute-start | bytes 786440 | tf_op jit(solution)/shard_map/ppermute | solution.py:36
  673.5 21.4 %collective-permute-start.6 = (bf16[1,64,2048]{2,1,0:T(8,128)(2,1)S(1)}, bf16[1,64,2048]{2,1,0:T(8,128)(2,1)S(1)}, u32[]{:S(2)}, u32[]{:S(2)}) collective-permute-start(bf16[1,64,2048]{2,1,0:T(8,128)(2,1)S(1)} %get-tuple-element.116), channel_id=1, source_target_pairs={{0,16},{8,24},{16,0},{24,8},{1,17},{9,25},{17,1},{25,9},{2,18},{10... | collective-permute-start | bytes 786440 | tf_op jit(solution)/shard_map/ppermute | solution.py:36
  673.6 21.3 %collective-permute-start.14 = (bf16[4,32,2304]{2,1,0:T(8,128)(2,1)S(1)}, bf16[4,32,2304]{2,1,0:T(8,128)(2,1)S(1)}, u32[]{:S(2)}, u32[]{:S(2)}) collective-permute-start(bf16[4,32,2304]{2,1,0:T(8,128)(2,1)S(1)} %pad_maximum_fusion.5.refs_0_), channel_id=1, source_target_pairs={{0,4},{2,6},{4,0},{6,2},{1,5},{3,7},{5,1},{7,3},{8,12},{10,14},{12... | collective-permute-start | bytes 1769480 | tf_op jit(solution)/shard_map/ppermute | solution.py:41
  674.9 20.7 %collective-permute-start.25 = (bf16[4,32,3840]{2,1,0:T(8,128)(2,1)S(1)}, bf16[4,32,3840]{2,1,0:T(8,128)(2,1)S(1)}, u32[]{:S(2)}, u32[]{:S(2)}) collective-permute-start(bf16[4,32,3840]{2,1,0:T(8,128)(2,1)S(1)} %collective-permute-done.23.refs_1_), channel_id=1, source_target_pairs={{0,2},{2,0},{4,6},{6,4},{1,3},{3,1},{5,7},{7,5},{8,10},{10,8},{12,... | collective-permute-start | bytes 2949128 | tf_op jit(solution)/shard_map/ppermute | solution.py:41
  678.1 17.4 %collective-permute-start.7 = (bf16[1,64,2048]{2,1,0:T(8,128)(2,1)S(1)}, bf16[1,64,2048]{2,1,0:T(8,128)(2,1)S(1)}, u32[]{:S(2)}, u32[]{:S(2)}) collective-permute-start(bf16[1,64,2048]{2,1,0:T(8,128)(2,1)S(1)} %get-tuple-element.115), channel_id=1, source_target_pairs={{0,8},{8,16},{16,24},{24,0},{1,9},{9,17},{17,25},{25,1},{2,10},{10... | collective-permute-start | bytes 786440 | tf_op jit(solution)/shard_map/ppermute | solution.py:36
  694.9 5.0 collective-permute-start.15
  (34 other events, 426.8 us)

commit v6 on v5

--- a/solution.py
+++ b/solution.py
@@ -31,16 +31,6 @@
     return lax.dot_general(left, right, (((0,), (0,)), ((), ())), preferred_element_type=F32)
 
 
-def shift(block, axis, step):
-    n = lax.axis_size(axis)
-    return lax.ppermute(block, axis, [(i, (i + step) % n) for i in range(n)])
-
-
-def swap(block, axis, mask):
-    n = lax.axis_size(axis)
-    return lax.ppermute(block, axis, [(i, i ^ mask) for i in range(n)])
-
-
 def masks_of(n):
     out = []
     while n > 1:
@@ -49,39 +39,11 @@
     return out
 
 
-def spread(pieces, axis):
-    for mask in masks_of(lax.axis_size(axis)):
-        pieces = pieces + [swap(piece, axis, mask) for piece in pieces]
-    return pieces
-
-
 def offsets(n):
     out = [0]
     for mask in masks_of(n):
         out = out + [o ^ mask for o in out]
     return out
-
-
-def fold(pieces, axis):
-    for mask in reversed(masks_of(lax.axis_size(axis))):
-        half = len(pieces) // 2
-        got = [swap(piece, axis, mask) for piece in pieces[half:]]
-        pieces = [
-            (mine.astype(F32) + other.astype(F32)).astype(BF16)
-            for mine, other in zip(pieces[:half], got)
-        ]
-    return pieces[0]
-
-
-def both_in_turn(parts):
-    lows, got = list(parts), None
-    for mask in masks_of(lax.axis_size("tp")):
-        got = [swap(low, "tp", mask) for low in lows]
-        for g in range(len(lows) - 1):
-            got[g] = after(got[g], *lows[g + 1 :])
-        totals = [low.astype(F32) + other.astype(F32) for low, other in zip(lows, got)]
-        lows = [total.astype(BF16) for total in totals]
-    return totals
 
 
 def attend_head(query, keys, values, biases):
@@ -132,8 +94,8 @@
 
 
 class Weight:
-    def __init__(self, shard_at, whole_at):
-        self.shard_at, self.whole_at = shard_at, whole_at
+    def __init__(self, shard_at, whole_at, own=None):
+        self.shard_at, self.whole_at, self.own = shard_at, whole_at, own
 
 
 class Deal:
@@ -231,6 +193,15 @@
             return
         self.waiting[item] = [[] for _ in self.masks]
         n = self.n_fsdp
+        if item.own is not None:
+
+            def mine(k):
+                return item.own if k == 0 else item.whole_at(self.z, flip(self.ct, self.offsets[k]))
+
+            def lands(k, level):
+                return item.whole_at(self.z, flip(self.ct, self.offsets[k]))
+
+            self.cast(item, mine, lands, 0, 0)
         for i in range(n - 1):
             s = i // 2 + 1 if i % 2 == 0 else n - 1 - i // 2
             owner = lax.rem(self.z - s + n, n)
@@ -517,7 +488,7 @@
     per, loc, width_here = query.shape
     piece, width = acts.shape[2:]
     heads = width_here // HEAD_DIM
-    cuts = 2
+    cuts = 4
     high = heads // cuts
     columns = high * HEAD_DIM
     masks = masks_of(n_ctx)
@@ -1003,89 +974,285 @@
     return out[0] if n_out == 1 else out
 
 
-def compact(arrays, pairs, n_part):
-    per, loc = arrays[0].shape[:2]
-    sizes = [values[2] // n_part for _, values in pairs]
-    total = sum(sizes)
-
-    def kernel(*refs):
-        out_ref = refs[-1]
-        column = lax.broadcasted_iota(jnp.int32, (NR, RANK), 0)
-        rank = lax.broadcasted_iota(jnp.int32, (NR, RANK), 1)
-        used = jnp.where(lax.rem(column, RANK) == rank, 1.0, 0.0).astype(BF16)
-        start = 0
-        for (codes, values), size in zip(pairs, sizes):
-            code = refs[codes[0]][0, :, codes[1] : codes[1] + codes[2]]
-            value = refs[values[0]][0, :, values[1] : values[1] + values[2]]
-            block = dot_tn(dot(code, used).astype(BF16), value).astype(BF16)
-            for part in range(n_part):
-                out_ref[part, :, start : start + size] = block[:, part * size : (part + 1) * size]
-            start += size
-
-    return pl.pallas_call(
-        kernel,
-        grid=(per,),
-        in_specs=[pl.BlockSpec((1,) + x.shape[1:], lambda n: (n, 0, 0)) for x in arrays],
-        out_specs=pl.BlockSpec((n_part, RANK, total), lambda n: (0, n, 0)),
-        out_shape=jax.ShapeDtypeStruct((n_part, per * RANK, total), BF16),
-        compiler_params=pltpu.CompilerParams(vmem_limit_bytes=48 << 20),
-        cost_estimate=pl.CostEstimate(
-            flops=2 * per * loc * RANK * total * n_part * 8,
-            bytes_accessed=2 * per * loc * total * n_part,
-            transcendentals=0,
-        ),
-    )(*arrays)
-
-
 def combine(pieces, chosen, shapes):
-    n_part = len(pieces)
-    n_fsdp, rows, columns = pieces[0].shape
+    n_part, n_fsdp = pieces.shape[:2]
     flat = []
     for i, shape in enumerate(shapes):
         for lead in range(shape[0] if len(shape) == 3 else 1):
             flat.append((i, lead if len(shape) == 3 else None, shape[-2:]))
 
-    def kernel(chosen_ref, *refs):
-        piece_refs, outs = refs[:n_part], refs[n_part:]
-        z, ct = lax.axis_index("fsdp"), lax.axis_index("ctx")
-        for k, offset in enumerate(offsets(n_part)):
-            part = flip(ct, offset)
-            ordered = jnp.concatenate(
-                [piece_refs[k][lax.rem(z - a + n_fsdp, n_fsdp)] for a in range(n_fsdp)], axis=0
-            )
+    def kernel(chosen_ref, piece_ref, *outs):
+        for part in range(n_part):
+            ordered = jnp.concatenate([piece_ref[part, a] for a in range(n_fsdp)], axis=0)
             start = 0
             for i, lead, (high, wide) in flat:
                 out_ref = outs[i] if lead is None else outs[i].at[lead]
                 tall = wide == NR and high != NR
                 size = (high if tall else wide) // n_part
                 block = ordered[:, start : start + size]
-                at = pl.ds(pl.multiple_of(part * size, size), size)
+                at = slice(part * size, (part + 1) * size)
                 if tall:
                     out_ref[at, :] = dot_tn(block, chosen_ref[...])
                 else:
                     out_ref[:, at] = dot_tn(chosen_ref[...], block)
                 start += size
 
+    vmem = pl.BlockSpec(memory_space=pltpu.VMEM)
     return pl.pallas_call(
         kernel,
-        in_specs=[pl.BlockSpec(memory_space=pltpu.VMEM)] * (1 + n_part),
-        out_specs=[pl.BlockSpec(memory_space=pltpu.VMEM)] * len(shapes),
+        in_specs=[vmem, vmem],
+        out_specs=[vmem] * len(shapes),
         out_shape=[jax.ShapeDtypeStruct(shape, F32) for shape in shapes],
         compiler_params=pltpu.CompilerParams(vmem_limit_bytes=48 << 20),
-        cost_estimate=pl.CostEstimate(
-            flops=2 * NR * n_fsdp * rows * columns * n_part,
-            bytes_accessed=2 * n_fsdp * rows * columns * n_part + 4 * NR * columns * n_part,
-            transcendentals=0,
+    )(chosen, pieces)
+
+
+def last(d_query, d_pair, x_all, adapt_all, dy1, qkv_x, a_in, picked, early, pairs, n_fsdp, n_ctx):
+    per, loc, width_here = d_query.shape
+    piece, width = loc // n_fsdp, x_all.shape[2]
+    depth = 3 * width_here
+    foot = 3 * NR
+    wide = width + foot
+    tile, chunk = 512, 32
+    n_wide = width // tile
+    n_swap = n_wide + 1
+    n_early = len(early)
+    early_sizes = [values[2] // n_ctx for _, values in pairs] + [width_here // n_ctx] * 3
+    late_sizes = [width // n_ctx] * 3
+    gathers = 2
+    n_copy = per * (n_fsdp - 1) + gathers * ((n_fsdp - 1) * n_ctx + 2 * (n_ctx - 1))
+
+    def kernel(*refs):
+        dq_ref, dkv_ref, x_ref, adapt_ref, a_ref, pick_ref = refs[:6]
+        dy1_ref, w_ref = refs[6:8]
+        early_refs = refs[8 : 8 + n_early]
+        in_ref, early_out, late_out = refs[8 + n_early : 11 + n_early]
+        send, recv, swap_send, swap_recv, ring_sem, sems = refs[11 + n_early : 17 + n_early]
+        rows_room, foot_room, dy1_room, turned, part, got, codes_in, dx = refs[
+            17 + n_early : 25 + n_early
+        ]
+        early_part, early_came, late_part, late_came = refs[25 + n_early : 29 + n_early]
+        staged = refs[29 + n_early :]
+        mover = Mover(n_fsdp, n_ctx, send, recv)
+        z, ct, masks = mover.z, mover.ct, mover.masks
+        partner = {"tp": 1 - lax.axis_index("tp")}
+        ring = Ring(rows_room, ring_sem, 0, lambda t: w_ref.at[ds(t * tile, tile)])
+        used = [0]
+
+        def move(source, target):
+            copy = pltpu.make_async_copy(source, target, sems.at[used[0]])
+            used[0] += 1
+            copy.start()
+            return copy
+
+        def swap_copy(g, t, size):
+            at = ds(t * tile, tile) if size == tile else pl.ds(width, size)
+            sem = g * n_swap + t
+            return pltpu.make_async_remote_copy(
+                src_ref=part.at[g, :, at],
+                dst_ref=got.at[g, :, at],
+                send_sem=swap_send.at[sem],
+                recv_sem=swap_recv.at[sem],
+                device_id=partner,
+                device_id_type=pl.DeviceIdType.MESH,
+            )
+
+        def compact(out_ref, n, entries, sizes):
+            column = lax.broadcasted_iota(jnp.int32, (NR, RANK), 0)
+            rank = lax.broadcasted_iota(jnp.int32, (NR, RANK), 1)
+            used_columns = jnp.where(lax.rem(column, RANK) == rank, 1.0, 0.0).astype(BF16)
+            start = 0
+            for (code, value), size in zip(entries, sizes):
+                short = dot(code(), used_columns).astype(BF16)
+                block = dot_tn(short, value()).astype(BF16)
+                for k in range(n_ctx):
+                    out_ref[k, n * RANK : (n + 1) * RANK, start : start + size] = block[
+                        :, k * size : (k + 1) * size
+                    ]
+                start += size
+
+        class Fold:
+            def __init__(self, parts, came):
+                self.parts, self.came, self.flying = parts, came, {}
+
+            def at(self, k):
+                return flip(ct, mover.offsets[k])
+
+            def hand(self, level):
+                half = 2**level
+                self.flying[level] = [
+                    mover.go(
+                        self.parts.at[self.at(half + i)],
+                        self.came.at[half - 1 + i],
+                        {"ctx": flip(ct, masks[level])},
+                    )
+                    for i in range(half)
+                ]
+
+            def take(self, level):
+                for i, copy in enumerate(self.flying[level]):
+                    copy.wait_recv()
+                    total = self.parts[self.at(i)].astype(F32) + self.came[2**level - 1 + i].astype(F32)
+                    self.parts[self.at(i)] = total.astype(BF16)
+
+        lasting = len(masks) - 1
+        load_foot = move(w_ref.at[pl.ds(width, foot)], foot_room)
+        ring.prefetch()
+        loads = [move(ref, room) for ref, room in zip(early_refs, staged)]
+        load_dy1 = move(dy1_ref, dy1_room)
+        mover.greet(tp=True)
+        folds = [Fold(early_part, early_came), Fold(late_part, late_came)]
+        for g in range(per):
+            turned[0:width_here, :] = dq_ref[g].T
+            turned[width_here : 2 * width_here, :] = dkv_ref[0, g].T
+            turned[2 * width_here :, :] = dkv_ref[1, g].T
+            if g == 0:
+                load_foot.wait()
+            part[g, :, width:] = dot(foot_room[...], turned[...]).T.astype(BF16)
+            swap_copy(g, n_wide, foot).start()
+
+            def back(t, room, g=g):
+                part[g, :, ds(t * tile, tile)] = dot(room[...], turned[...]).T.astype(BF16)
+                swap_copy(g, t, tile).start()
+
+            ring.run(n_wide, back)
+            if g + 1 < per:
+                ring.prefetch()
+            if g == 0:
+                for copy in loads:
+                    copy.wait()
+                for n in range(per):
+                    entries = []
+                    for (i, first, size), (j, start, count) in pairs:
+                        entries.append(
+                            (
+                                lambda n=n, i=i, f=first, c=size: staged[i][n, :, f : f + c],
+                                lambda n=n, i=j, f=start, c=count: staged[i][n, :, f : f + c],
+                            )
+                        )
+                    values = [
+                        lambda n=n: dq_ref[n],
+                        lambda n=n: dkv_ref[0, n],
+                        lambda n=n: dkv_ref[1, n],
+                    ]
+                    for j in range(3):
+                        entries.append(
+                            (lambda n=n, j=j: adapt_ref[n, :, j * NR : (j + 1) * NR], values[j])
+                        )
+                    compact(early_part, n, entries, early_sizes)
+                folds[0].hand(lasting)
+        for level in range(lasting, -1, -1):
+            folds[0].take(level)
+            if level:
+                folds[0].hand(level - 1)
+
+        def gather(parts, out_ref):
+            own = parts.at[ct]
+            kept.append(move(own, out_ref.at[ct, z]))
+            item = Weight(lambda c: parts.at[c], lambda o, c: out_ref.at[c, o], own)
+            mover.begin(item)
+            return item
+
+        kept = []
+        first = gather(early_part, early_out)
+        load_dy1.wait()
+        dealt = []
+
+        def finish_rows(g):
+            for t in range(n_swap):
+                copy = swap_copy(g, t, tile if t < n_wide else foot)
+                copy.wait_recv()
+                copy.wait_send()
+            pick = jnp.concatenate([pick_ref[g]] * 3, axis=1)
+
+            def step(r, carry):
+                rows = ds(r * chunk, chunk)
+                total = part[g, rows, :].astype(F32) + got[g, rows, :].astype(F32)
+                code = (total[:, width:] * pick).astype(BF16)
+                codes_in[g, rows, :] = code
+                value = dy1_room[g, rows, :] + total[:, :width] + dot_nt(code, a_ref[...])
+                dx[g, rows, :] = value.astype(BF16)
+                return carry
+
+            lax.fori_loop(0, loc // chunk, step, 0)
+            kept.append(move(dx.at[g, pl.ds(0, piece)], in_ref.at[z * per + g]))
+            for s in range(1, n_fsdp):
+                to = lax.rem(z - s + n_fsdp, n_fsdp)
+                dealt.append(
+                    mover.go(
+                        dx.at[g, pl.ds(s * piece, piece)], in_ref.at[z * per + g], {"fsdp": to}
+                    )
+                )
+
+        for g in range(per):
+            finish_rows(g)
+            if g == 0:
+                mover.relay(first)
+        for n in range(per):
+            entries = []
+            for j in range(3):
+                entries.append(
+                    (
+                        lambda n=n, j=j: codes_in[n, :, j * NR : (j + 1) * NR],
+                        lambda n=n: x_ref[n],
+                    )
+                )
+            compact(late_part, n, entries, late_sizes)
+        folds[1].hand(lasting)
+        for level in range(lasting, -1, -1):
+            folds[1].take(level)
+            if level:
+                folds[1].hand(level - 1)
+        second = gather(late_part, late_out)
+        for level in range(len(masks)):
+            mover.finish(first, level)
+        mover.relay(second)
+        for level in range(len(masks)):
+            mover.finish(second, level)
+        for copy in dealt:
+            copy.wait_recv()
+        for copy in kept:
+            copy.wait()
+        mover.close()
+
+    vmem, anywhere = pl.BlockSpec(memory_space=pltpu.VMEM), pl.BlockSpec(memory_space=pl.ANY)
+    parts = [(n_ctx, per * RANK, sum(early_sizes)), (n_ctx, per * RANK, sum(late_sizes))]
+    rooms = [
+        ((2, tile, depth), BF16),
+        ((foot, depth), BF16),
+        (dy1.shape, F32),
+        ((depth, loc), BF16),
+        ((per, loc, wide), BF16),
+        ((per, loc, wide), BF16),
+        ((per, loc, foot), BF16),
+        ((per, loc, width), BF16),
+    ]
+    for shape in parts:
+        rooms += [(shape, BF16), ((n_ctx - 1,) + shape[1:], BF16)]
+    rooms += [(x.shape, BF16) for x in early]
+    return pl.pallas_call(
+        kernel,
+        in_specs=[vmem] * 6 + [anywhere] * (2 + n_early),
+        out_specs=[anywhere] * 3,
+        out_shape=[jax.ShapeDtypeStruct((per * n_fsdp, piece, width), BF16)]
+        + [jax.ShapeDtypeStruct((n_ctx, n_fsdp) + shape[1:], BF16) for shape in parts],
+        scratch_shapes=[
+            pltpu.SemaphoreType.DMA((n_copy,)),
+            pltpu.SemaphoreType.DMA((n_copy,)),
+            pltpu.SemaphoreType.DMA((per * n_swap,)),
+            pltpu.SemaphoreType.DMA((per * n_swap,)),
+            pltpu.SemaphoreType.DMA((2,)),
+            pltpu.SemaphoreType.DMA((4 + n_early + per,)),
+        ]
+        + [pltpu.VMEM(shape, dtype) for shape, dtype in rooms],
+        compiler_params=pltpu.CompilerParams(
+            collective_id=4, has_side_effects=True, vmem_limit_bytes=60 << 20
         ),
-    )(chosen, *pieces)
+    )(d_query, d_pair, x_all, adapt_all, a_in, picked, dy1, qkv_x, *early)
 
 
 def as_low(block):
     return (block.astype(BF16),)
-
-
-def after(value, *first):
-    return lax.optimization_barrier((value,) + first)[0]
 
 
 def gelu_both(pre):
@@ -1131,17 +1298,6 @@
     def take(array, start, size, axis=0):
         return lax.dynamic_slice_in_dim(array, start, size, axis)
 
-    def put(array, block, *starts):
-        return lax.dynamic_update_slice(array, block, starts)
-
-    def undeal(rows, group_out):
-        rows = rows.reshape(g_per, n_fsdp, piece, width)
-        out = []
-        for step in range(n_fsdp):
-            block = rows[:, step]
-            out.append(block if step == 0 else shift(block, "fsdp", -step))
-        return out
-
     units = w_up.shape[1]
     rows_shape = (per, n_fsdp, piece, width)
     zq, zu = w_qkv.shape[1], w_up.shape[0]
@@ -1243,21 +1399,6 @@
         n_fsdp,
         n_ctx,
     )
-    d_query = d_query.reshape(per * loc, heads_width)
-    d_pair = d_pair.reshape(2, per * loc, heads_width)
-
-    def gathered(mine):
-        blocks = [
-            lax.dynamic_index_in_dim(mine, ct ^ offset, 0, False) for offset in offsets(n_ctx)
-        ]
-        own = fold(blocks, "ctx")
-        got = jnp.stack([own] + [shift(own, "fsdp", step) for step in range(1, n_fsdp)])
-        return spread([got], "ctx")
-
-    early_in = after(
-        (adapt_down, wide_d, gelu_out, wide_h, d_pre, dadapt_up, adapt_out, wide_a, context),
-        d_query,
-    )
     code, row, unit = (0, NR), (0, width), (0, units)
     tail = (width, NR)
     early_pairs = [
@@ -1268,50 +1409,35 @@
         ((6,) + code, (7,) + row),
         ((7,) + tail, (8, 0, heads_width)),
     ]
-    early = gathered(compact(early_in, early_pairs, n_ctx))
-
-    dy1_flat = dy1.reshape(per * loc, width)
-    ins, dadapt_all = [], []
-    d_proj = [
-        jnp.concatenate([d_query[part[g]], d_pair[0, part[g]], d_pair[1, part[g]]], axis=1)
-        for g in groups
-    ]
-    summed = both_in_turn([mm(d_proj[g], qkv_x, True, as_low, 640) for g in groups])
-    for g in groups:
-        pick3 = jnp.concatenate([picks[g]] * 3, axis=1)
-        dadapt_in = (summed[g][:, width:] * pick3).astype(BF16)
-        d_x = (dy1_flat[part[g]] + summed[g][:, :width] + dot_nt(dadapt_in, a_in)).astype(BF16)
-        ins.append(undeal(d_x, g))
-        dadapt_all.append(dadapt_in)
-    late_in = (
+    early_in = (
+        adapt_down, wide_d, gelu_out, wide_h, d_pre, dadapt_up, adapt_out, wide_a, context,
+    )
+    input_grad, early, late = last(
+        d_query,
+        d_pair,
+        x_all.reshape(per, loc, width),
         adapt_all.reshape(per, loc, 3 * NR),
-        jnp.concatenate(dadapt_all, axis=0).reshape(per, loc, 3 * NR),
-        jnp.concatenate(d_proj, axis=0).reshape(per, loc, 3 * heads_width),
-        x_flat.reshape(per, loc, width),
+        dy1,
+        qkv_x,
+        a_in,
+        picked[:, None, :],
+        early_in,
+        early_pairs,
+        n_fsdp,
+        n_ctx,
     )
-    late_pairs = [
-        ((0, j * NR, NR), (2, j * heads_width, heads_width)) for j in range(3)
-    ] + [((1, j * NR, NR), (3,) + row) for j in range(3)]
-    late = gathered(compact(late_in, late_pairs, n_ctx))
-
-    def assemble(parts):
-        full = jnp.zeros((seqs, piece, width), BF16)
-        for group, blocks in enumerate(parts):
-            for step, block in enumerate(blocks):
-                owner = lax.rem(z + step, n_fsdp)
-                full = put(full, block, owner * per + group * g_per, 0, 0)
-        return full
-
     codes = (adapter_ids[:, None] * RANK + jnp.arange(RANK)[None, :]).reshape(-1)
     chosen = (codes[:, None] == jnp.arange(NR)[None, :]).astype(BF16)
-    early = after(early, summed[-1])
     e = combine(
         early,
         chosen,
-        [(NR, width), (units, NR), (NR, units), (width, NR), (NR, width), (heads_width, NR)],
+        [
+            (NR, width), (units, NR), (NR, units), (width, NR), (NR, width), (heads_width, NR),
+            (3, NR, heads_width),
+        ],
     )
-    l = combine(late, chosen, [(3, NR, heads_width), (3, width, NR)])
-    return activations, assemble(ins), l[1], l[0], e[5], e[4], e[3], e[2], e[1], e[0]
+    (a_qkv_grad,) = combine(late, chosen, [(3, width, NR)])
+    return activations, input_grad, a_qkv_grad, e[6], e[5], e[4], e[3], e[2], e[1], e[0]
 
 
 def solution(mesh):

time: 717 us -> 684 us (0.954)
  Pallas kernels: 563 us -> 649 us
  waiting for transfers between devices: 59.2 us -> 0 us
  starting transfers between devices: 35.8 us -> 0 us
  other arithmetic: 18.1 us -> 2.81 us
    pallas_call x4 -> x3, Pallas kernels: 19.5 us -> 127 us  [the longest x1 120 us: last(): pl.pallas_call(kernel, in_specs=[vmem] * 6 + [anywhere] * (2 + n_early),...]
    ppermute x26 -> x0, waiting for transfers between devices: 59.2 us -> none  [the longest x12 44.4 us: shift(): return lax.ppermute(block, axis, [(i, (i + step) % n) for i in range(n)])]
    ppermute x26 -> x0, starting transfers between devices: 35.8 us -> none  [the longest x12 26.1 us: shift(): return lax.ppermute(block, axis, [(i, (i + step) % n) for i in range(n)])]
    pallas_call x3 -> x1, Pallas kernels: 28.6 us -> 11.2 us  [mm(): pl.pallas_call(kernel, grid=(pl.cdiv(columns, tile),), in_specs=[pl.Block...]
    concatenate x4 -> x0, other arithmetic: 7.22 us -> none  [the longest x1 6.97 us: local(): jnp.concatenate(d_proj, axis=0).reshape(per, loc, 3 * heads_width)]
    unnamed x66 -> x39, local copies, waits for them, and re-layouts: 18.5 us -> 16.1 us
  transfers between devices with their start and end apart: 26 -> 0, of which waited for: 11 -> 0; matrix products, arithmetic and copies ran while one was open for 3% -> 0% of each run, Pallas kernels for 13% -> 0%
where the time goes in v6:
time: 684 us; the launch traced here: 675 us
  Pallas kernels  649 us (95%)
  local copies, waits for them, and re-layouts  19.3 us (3%)
    pallas_call x1, Pallas kernels, forward_and_gather(): pl.pallas_call(kernel, in_specs=[vmem, vmem] + [anywhere] * 8, out_specs=...  225 us
    pallas_call x1, Pallas kernels, middle(): pl.pallas_call(kernel, in_specs=[vmem] * 8 + [anywhere] * 7, out_specs=[s...  128 us
    pallas_call x1, Pallas kernels, last(): pl.pallas_call(kernel, in_specs=[vmem] * 6 + [anywhere] * (2 + n_early),...  120 us
    pallas_call x1, Pallas kernels, move(): pl.pallas_call(kernel, in_specs=spaces, out_specs=[pl.BlockSpec(memory_sp...  100 us
    pallas_call x1, Pallas kernels, attend_back(): pl.pallas_call(kernel, in_specs=[vmem] * 4 + [anywhere] * (1 + n_ctx), ou...  58.1 us
    unnamed x39, local copies, waits for them, and re-layouts  16.1 us

profile of v6, /device:TPU:0, one launch (start us, length us, event | category | flops | bytes accessed | tf_op | source)
XLA Modules:
  0.0 675.1 jit_solution(13490468334021508032)
XLA Ops:
  0.6 0.7 dynamic_slice.6
  1.5 1.9 copy-done.4
  3.4 1.6 copy-done.5
  5.0 1.1 copy-done.8
  6.1 100.0 %shard_map.258 = (bf16[2,4,64,2048]{3,2,1,0:T(8,128)(2,1)S(1)}, bf16[2432,3072]{1,0:T(8,128)(2,1)}) custom-call(bf16[8,64,2048]{2,1,0:T(8,128)(2,1)S(1)} %copy-done.5, bf16[3,512,1024]{2,1,0:T(8,128)(2,1)S(1)} %copy-done.4, bf16[3,128,1024]{2,1,0:T(8,128)(2,1)S(1)} %copy-done.8), custom_call_target="tpu_custom_call" | custom-call | tf_op jit(solution)/shard_map/pallas_call | solution.py:304
  106.1 3.3 copy.30
  109.4 2.7 fusion
  112.3 0.5 copy-done.14
  112.9 11.2 %shard_map.259 = bf16[512,3072]{1,0:T(8,128)(2,1)S(1)} custom-call(bf16[512,2432]{1,0:T(8,128)(2,1)S(1)} %pad_maximum_fusion.left_ref, bf16[2432,3072]{1,0:T(8,128)(2,1)} %get-tuple-element.48.right_ref.refs_7_), custom_call_target="tpu_custom_call" | custom-call | flops 7650410496 | bytes 35520512 | tf_op jit(solution)/shard_map/pallas_call | solution.py:954
  124.5 1.5 pad_maximum_fusion.1.refs_2_.refs_5_
  126.8 224.7 %shard_map.260 = (bf16[2,2,256,1024]{3,2,1,0:T(8,128)(2,1)}, bf16[2,2,256,1024]{3,2,1,0:T(8,128)(2,1)}, bf16[2,2,256,1024]{3,2,1,0:T(8,128)(2,1)}, bf16[2,4,64,2...) custom-call(bf16[2,256,1024]{2,1,0:T(8,128)(2,1)S(1)} %bitcast.18, ...), custom_call_target="tpu_custom_call" | custom-call | tf_op jit(solution)/shard_map/pallas_call | solution.py:467
  351.5 1.0 copy-done.7
  352.5 0.6 copy-done.10
  353.1 0.6 compare_convert_fusion.refs_0_.refs_5_
  353.7 127.8 %shard_map.261 = (bf16[2,256,2176]{2,1,0:T(8,128)(2,1)}, bf16[2,256,4096]{2,1,0:T(8,128)(2,1)}, bf16[2,256,2048]{2,1,0:T(8,128)(2,1)}, bf16[2,256,2176]{2,1,0:T(...) custom-call(f32[2,1,128]{2,1,0:T(1,128)} %compare_convert_fusion.ref, ...), custom_call_target="tpu_custom_call" | custom-call | tf_op jit(solution)/shard_map/pallas_call | solution.py:892
  481.5 58.1 %shard_map.262 = (bf16[2,256,1024]{2,1,0:T(8,128)(2,1)}, bf16[2,2,256,1024]{3,2,1,0:T(8,128)(2,1)}, bf16[8,64,2048]{2,1,0:T(8,128)(2,1)}) custom-call(bf16[2,256,1024]{2,1,0:T(8,128)(2,1)} %bitcast.19, f32[2,1024,128]{2,1,0:T(8,128)} %copy-done.1, bf16[2,256,1024]{2,1,0:T(8,128)(2,1)} %get-tuple-element.55.refs_2_, f32[2,8,1,256]{3,2,1,0:T(1,128)} %copy-done.10, ...), custom_call_target="tpu_custom_call" | custom-call | tf_op jit(solution)/shard_map/pallas_call | solution.py:604
  539.6 1.6 copy.31.refs_4_
  541.2 119.9 %shard_map.263 = (bf16[8,64,2048]{2,1,0:T(8,128)(2,1)}, bf16[4,4,32,4608]{3,2,1,0:T(8,128)(2,1)}, bf16[4,4,32,1536]{3,2,1,0:T(8,128)(2,1)}) custom-call(bf16[2,256,1024]{2,1,0:T(8,128)(2,1)} %get-tuple-element.62.refs_0_, bf16[2,2,256,1024]{3,2,1,0:T(8,128)(2,1)} %get-tuple-element.63.refs_1_, bf16[2,256,2048]{2,1,0:T(8,128)(2,1)} %bitcast.17, ...), custom_call_target="tpu_custom_call" | custom-call | tf_op jit(solution)/shard_map/pallas_call | solution.py:1233
  661.4 2.3 copy-done.3
  663.8 4.9 shard_map.265
  668.7 2.3 shard_map.264
  671.0 1.3 copy.34
  672.3 1.0 copy-done.13
  673.3 1.3 copy.35
  (44 shorter events, 1.7 us)
Async XLA Ops:
  1.5 1.9 copy-start.4
  3.4 1.6 copy-start.5
  5.0 1.1 copy-start.8
  106.1 6.0 copy-start
  112.1 0.7 copy-start.14
  124.4 2.3 copy-start.2
  124.5 1.5 copy-start.16
  124.5 1.6 copy-start.15
  124.5 2.3 copy-start.9
  126.7 224.7 %copy-start.1 = (f32[2,1024,128]{2,1,0:T(8,128)}, f32[2,1024,128]{2,1,0:T(8,128)S(1)}, u32[]{:S(2)}) copy-start(f32[2,1024,128]{2,1,0:T(8,128)S(1)} %broadcast_in_dim.15.refs_1_) | copy-start | bytes 3145732
  351.5 1.0 copy-start.7
  352.5 0.6 copy-start.10
  481.5 58.2 %copy-start.11 = (bf16[3,2048,128]{1,2,0:T(8,128)(2,1)S(1)}, bf16[3,2048,128]{1,2,0:T(8,128)(2,1)}, u32[]{:S(2)}) copy-start(bf16[3,2048,128]{1,2,0:T(8,128)(2,1)} %copy.30) | copy-start | bytes 4718596
  541.2 119.9 %copy-start.17 = (s32[8]{0:T(128)S(1)}, s32[8]{0:T(128)}, u32[]{:S(2)}) copy-start(s32[8]{0:T(128)} %param.22) | copy-start | bytes 100
  661.4 2.3 copy-start.3
  663.8 4.9 copy-start.6
  668.7 2.3 copy-start.12
  671.0 2.3 copy-start.13

commit v7 on v6

--- a/solution.py
+++ b/solution.py
@@ -14,7 +14,6 @@
 NORM_EPS = 1e-06
 GELU_COEF = 0.7978845608028654
 SCALE = 1.0 / math.sqrt(HEAD_DIM)
-GROUPS = 2
 F32 = jnp.float32
 BF16 = jnp.bfloat16
 
@@ -94,8 +93,8 @@
 
 
 class Weight:
-    def __init__(self, shard_at, whole_at, own=None):
-        self.shard_at, self.whole_at, self.own = shard_at, whole_at, own
+    def __init__(self, shard_at, whole_at, own=None, skip=0):
+        self.shard_at, self.whole_at, self.own, self.skip = shard_at, whole_at, own, skip
 
 
 class Deal:
@@ -117,7 +116,13 @@
         self.open = []
         self.masks = masks_of(n_ctx)
         self.offsets = offsets(n_ctx)
-        self.came, self.waiting = {}, {}
+        self.came, self.waiting, self.done = {}, {}, {}
+
+    def skip(self, item):
+        return item.skip if isinstance(item, Weight) else 0
+
+    def part(self, item):
+        return lax.rem(self.ct, self.n_ctx >> item.skip) if item.skip else self.ct
 
     def greet(self, tp=False):
         barrier = pltpu.get_barrier_semaphore()
@@ -151,7 +156,7 @@
         return copy
 
     def along(self, item, owner, right, ok, source, slot):
-        target = item.whole_at(owner, self.ct)
+        target = item.whole_at(owner, self.part(item))
         device = {"fsdp": lax.rem(self.z + (1 if right else self.n_fsdp - 1), self.n_fsdp)}
         copy = self.copy(source, target, device, self.came[item] + slot - 1)
         pl.when(ok)(copy.start)
@@ -165,7 +170,7 @@
         if isinstance(item, Weight):
             self.came[item] = self.used
             self.used += self.n_fsdp - 1
-            source = item.shard_at(self.ct)
+            source = item.shard_at(self.part(item))
             self.along(item, self.z, True, self.z < self.n_fsdp - 1, source, 1)
             self.along(item, self.z, False, self.z > 0, source, self.n_fsdp - 1)
             return
@@ -179,33 +184,33 @@
         ]
 
     def cast(self, item, source_at, target_at, k, first):
-        for level in range(first, len(self.masks)):
-            device = {"ctx": flip(self.ct, self.masks[level])}
+        skip = self.skip(item)
+        for level in range(first, len(self.masks) - skip):
+            device = {"ctx": flip(self.ct, self.masks[level + skip])}
             copy = self.go(source_at(k), target_at(k, level), device)
             self.waiting[item][level].append((copy, k + 2**level, source_at, target_at))
 
     def relay(self, item):
-        if isinstance(item, Pair):
-            return
         if isinstance(item, Deal):
             for copy in self.came[item]:
                 copy.wait_recv()
             return
-        self.waiting[item] = [[] for _ in self.masks]
-        n = self.n_fsdp
+        self.waiting[item] = [[] for _ in self.masks[item.skip :]]
+        n, part = self.n_fsdp, self.part(item)
+        others = offsets(self.n_ctx >> item.skip)
         if item.own is not None:
 
             def mine(k):
-                return item.own if k == 0 else item.whole_at(self.z, flip(self.ct, self.offsets[k]))
+                return item.own if k == 0 else item.whole_at(self.z, flip(part, others[k]))
 
             def lands(k, level):
-                return item.whole_at(self.z, flip(self.ct, self.offsets[k]))
+                return item.whole_at(self.z, flip(part, others[k]))
 
             self.cast(item, mine, lands, 0, 0)
         for i in range(n - 1):
             s = i // 2 + 1 if i % 2 == 0 else n - 1 - i // 2
             owner = lax.rem(self.z - s + n, n)
-            here = item.whole_at(owner, self.ct)
+            here = item.whole_at(owner, part)
             self.copy(here, here, {"fsdp": owner}, self.came[item] + s - 1).wait_recv()
             if s < n - 1:
                 ok = (self.z >= s) & (self.z < n - 1)
@@ -215,16 +220,23 @@
                 self.along(item, owner, False, ok, here, s - 1)
 
             def at(k, owner=owner):
-                return item.whole_at(owner, flip(self.ct, self.offsets[k]))
+                return item.whole_at(owner, flip(part, others[k]))
 
             self.cast(item, at, lambda k, level, at=at: at(k), 0, 0)
 
     def finish(self, item, level):
-        if isinstance(item, Deal):
+        if isinstance(item, Deal) or level != self.done.get(item, 0):
+            return
+        if level == len(self.waiting[item]):
             return
         for copy, k, source_at, target_at in self.waiting[item][level]:
             copy.wait_recv()
             self.cast(item, source_at, target_at, k, level + 1)
+        self.done[item] = level + 1
+
+    def complete(self, item):
+        while self.done.get(item, 0) < len(self.waiting[item]):
+            self.finish(item, self.done.get(item, 0))
 
     def close(self):
         for ok, copy in self.open:
@@ -313,40 +325,49 @@
         ]
         + [pltpu.VMEM(shape, BF16) for shape in room_shapes],
         compiler_params=pltpu.CompilerParams(
-            collective_id=ident, has_side_effects=True, vmem_limit_bytes=32 << 20
+            collective_id=ident, has_side_effects=True, vmem_limit_bytes=60 << 20
         ),
     )(*inputs)
 
 
-def forward_and_gather(query, kv_own, bias, shards, maps, n_fsdp, n_ctx):
-    per, loc, width_here = query.shape
-    cot, w_out, w_up, w_down = shards
-    piece, width = cot.shape[1:]
+def forward_and_gather(x_rows, qkv_x, a_qkv, picked, bias, shards, maps, n_fsdp, n_ctx):
+    per, loc, width = x_rows.shape
+    w_out, w_up, w_down = shards
+    width_here = qkv_x.shape[1] // 3
     heads, units = width_here // HEAD_DIM, w_up.shape[1]
     zu, zo = w_up.shape[0], w_out.shape[1]
+    n_part = n_ctx // 2 if n_ctx > 1 else 1
     so, su, sd = w_out.shape[0] // n_ctx, zu // n_ctx, w_down.shape[0] // n_ctx
     wide = width + NR
-    stay_shapes = [(piece, width)] * per + [x.shape for x in (w_out, w_up, w_down) + maps]
-    n_stay = len(stay_shapes)
-    halves = 2
-    n_copy = (n_fsdp - 1) * n_ctx * (1 + 2 * halves) + per * (n_fsdp - 1 + n_ctx - 1 + 1)
+    wide_x = width + 3 * NR
+    cuts = 4
+    paired = cuts // 2 if n_ctx > 1 else 0
+    tile = 512
+    per_kind = width_here // tile
+    n_tile = 3 * per_kind
+    n_copy = (n_fsdp - 1) * n_ctx * (1 + 2 * cuts) + 2 * per * (n_ctx - 1) + 6 + per
+    lag = 4
 
     def kernel(*refs):
-        q_ref, bias_ref, kv_ref, cot_ref, wo_ref, wu_ref, wd_ref, ao_ref, bu_ref, ad_ref = refs[:10]
-        slots = refs[10 : 9 + n_ctx]
-        rows_ref, out_ref, up_ref, down_ref, ctx_ref, log_ref, part_ref, other_ref = refs[
-            9 + n_ctx : 17 + n_ctx
+        bias_ref, a_ref, pick_ref, x_ref, w_ref = refs[:5]
+        wo_ref, wu_ref, wd_ref, ao_ref, bu_ref, ad_ref = refs[5:11]
+        slots = refs[11 : 10 + n_ctx]
+        q_ref, kv_ref, adapt_ref, out_ref, up_ref, down_ref, ctx_ref, log_ref, part_ref, other_ref = refs[
+            10 + n_ctx : 20 + n_ctx
         ]
-        send, recv, here, load, kv_room, out_room = refs[17 + n_ctx : 23 + n_ctx]
-        room = refs[23 + n_ctx :]
+        send, recv, here, load, ring_sem, x_room, w_room, proj, kv_room, out_room = refs[20 + n_ctx :]
         mover = Mover(n_fsdp, n_ctx, send, recv)
+        ring = Ring(
+            w_room,
+            ring_sem,
+            0,
+            lambda t: w_ref.at[:, ds(lax.rem(t + per_kind, n_tile) * tile, tile)],
+        )
         z = mover.z
-
-        def deal(g):
-            return Deal(lambda to: cot_ref.at[to * per + g], lambda s: rows_ref.at[g, s])
-
-        def pair(g):
-            return Pair(lambda k: kv_ref.at[:, g] if k == 0 else slots[k - 1].at[:, g])
+        rows = [pl.ds(g * loc, loc) for g in range(per)]
+
+        def columns(j):
+            return pl.ds(j * width_here, width_here)
 
         out_item = Weight(
             lambda c: wo_ref.at[ds(c * so, so)],
@@ -354,40 +375,62 @@
         )
 
         def up_item(h):
-            columns = pl.ds(h * (units // halves), units // halves)
+            at = pl.ds(h * (units // cuts), units // cuts)
             return Weight(
-                lambda c: wu_ref.at[ds(c * su, su), columns],
-                lambda o, c: up_ref.at[ds(o * zu + c * su, su), columns],
+                lambda c: wu_ref.at[ds(c * su, su), at],
+                lambda o, c: up_ref.at[ds(o * zu + c * su, su), at],
             )
 
         def down_item(h):
-            size = sd // halves
+            size = sd // cuts
             return Weight(
                 lambda c: wd_ref.at[ds(c * sd + h * size, size)],
                 lambda o, c: down_ref.at[ds(c * sd + h * size, size), ds(o * zo, zo)],
             )
 
-        pairs = [pair(g) for g in range(per)]
-        items = [out_item] + [up_item(h) for h in range(halves)]
-        items += [down_item(h) for h in range(halves)] + [deal(g) for g in range(per)]
-        stay = [(cot_ref.at[z * per + g], rows_ref.at[g, 0]) for g in range(per)]
-        stay += [
-            (wo_ref, out_ref.at[:, ds(z * zo, zo)]),
-            (wu_ref, up_ref.at[ds(z * zu, zu)]),
-            (wd_ref, down_ref.at[:, ds(z * zo, zo)]),
-            (ao_ref, out_ref.at[:, pl.ds(width, NR)]),
-            (bu_ref, up_ref.at[pl.ds(width, NR)]),
-            (ad_ref, down_ref.at[:, pl.ds(width, NR)]),
-        ]
+        def down_pair(h):
+            size = sd // cuts
+
+            def at(c, p):
+                return ds((c + p * n_part) * sd + h * size, size)
+
+            def half(p):
+                return Weight(
+                    lambda c: wd_ref.at[at(c, p)],
+                    lambda o, c: down_ref.at[at(c, p), ds(o * zo, zo)],
+                    skip=1,
+                )
+
+            return [half(p) for p in range(2)]
+
+        def pair(g, j):
+            return Pair(
+                lambda k: proj.at[rows[g], columns(1 + j)] if k == 0 else slots[k - 1].at[j, g]
+            )
+
+        pairs = [pair(g, j) for g in range(per) for j in range(2)]
+        items = [out_item] + [up_item(h) for h in range(cuts)]
+        items += [down_item(h) for h in range(cuts - paired)]
+        for h in range(cuts - paired, cuts):
+            items += down_pair(h)
+        used = [0]
+
+        def move(source, target):
+            copy = pltpu.make_async_copy(source, target, here.at[used[0]])
+            used[0] += 1
+            copy.start()
+            return copy
 
         def attend(g):
-            for level in range(len(mover.masks)):
-                mover.finish(pairs[g], level)
+            for j in range(2):
+                mover.complete(pairs[2 * g + j])
             loads = []
-            for k in range(n_ctx):
-                copy = pltpu.make_async_copy(pairs[g].slot_at(k), kv_room.at[k], load.at[k])
+            for k in range(1, n_ctx):
+                copy = pltpu.make_async_copy(slots[k - 1].at[:, g], kv_room.at[k], load.at[k])
                 copy.start()
                 loads.append(copy)
+            for j in range(2):
+                kv_room[0, j] = proj[g * loc : (g + 1) * loc, (1 + j) * width_here : (2 + j) * width_here]
             for copy in loads:
                 copy.wait()
 
@@ -398,7 +441,7 @@
                     block = bias_ref[g, k * loc : (k + 1) * loc, :]
                     biases.append(jnp.concatenate([block] * (loc // 128), axis=1))
                 context, log = attend_head(
-                    q_ref[g, :, at],
+                    proj[g * loc : (g + 1) * loc, at],
                     [kv_room[k, 0, :, at] for k in range(n_ctx)],
                     [kv_room[k, 1, :, at] for k in range(n_ctx)],
                     biases,
@@ -410,7 +453,10 @@
             lax.fori_loop(0, heads, one, 0)
 
         def project():
-            copy = pltpu.make_async_copy(out_ref, out_room, load.at[n_ctx])
+            mover.complete(out_item)
+            own[0].wait_recv()
+            own[3].wait_recv()
+            copy = pltpu.make_async_copy(out_ref, out_room, load.at[0])
             copy.start()
             copy.wait()
             for g in range(per):
@@ -423,39 +469,73 @@
                     )
                 )
 
-        swapped = []
-        tasks = {i: (lambda g=i: attend(g)) for i in range(per)}
-        tasks[per] = project
+        def tiles(t, room):
+            at = ds(lax.rem(t + per_kind, n_tile) * tile, tile)
+            proj[:, at] = dot(x_room[...], room[...]).astype(BF16)
+
+        swapped, outward = [], []
+        tasks = {1 + g: (lambda g=g: attend(g)) for g in range(per)}
+        tasks[per + 2] = project
+        ring.prefetch()
+        loads = [move(x_ref.at[g], x_room.at[rows[g], pl.ds(0, width)]) for g in range(per)]
         mover.greet(tp=True)
-        for item in pairs + items[:2]:
+        ahead = 3
+        for item in items[:ahead]:
             mover.begin(item)
-        kept = keep(stay, room, here)
-        levels = len(mover.masks)
-        for i in range(len(items) + levels):
+        sibling = {"ctx": flip(mover.ct, 1)}
+        own = [
+            mover.go(source, target, sibling)
+            for source, target in (
+                (wo_ref, out_ref.at[:, ds(z * zo, zo)]),
+                (wu_ref, up_ref.at[ds(z * zu, zu)]),
+                (wd_ref, down_ref.at[:, ds(z * zo, zo)]),
+                (ao_ref, out_ref.at[:, pl.ds(width, NR)]),
+                (bu_ref, up_ref.at[pl.ds(width, NR)]),
+                (ad_ref, down_ref.at[:, pl.ds(width, NR)]),
+            )
+        ]
+        for g in range(per):
+            loads[g].wait()
+            pick = pick_ref[g]
+            for j in range(3):
+                code = dot(x_room[g * loc : (g + 1) * loc, :width], a_ref[j]) * pick
+                x_room[g * loc : (g + 1) * loc, width + j * NR : width + (j + 1) * NR] = code.astype(BF16)
+            outward.append(move(x_room.at[rows[g], pl.ds(width, 3 * NR)], adapt_ref.at[g]))
+        ring.run(2 * per_kind, tiles, 0, n_tile)
+        for item in pairs:
+            mover.begin(item)
+        for g in range(per):
+            for j in range(2):
+                outward.append(move(proj.at[rows[g], columns(1 + j)], kv_ref.at[j, g]))
+        for i in range(len(items) + lag + 2):
             if i < len(items):
                 mover.relay(items[i])
-                if i + 2 < len(items):
-                    mover.begin(items[i + 2])
+                if i + ahead < len(items):
+                    mover.begin(items[i + ahead])
             if i == 0:
-                for first, second in kept:
-                    first.wait()
-                    second.start()
-            for level in range(levels):
-                if 0 <= i - 1 - level < len(items):
-                    mover.finish(items[i - 1 - level], level)
-            if i == per:
-                for _, second in kept:
-                    second.wait()
+                ring.run(n_tile, tiles, 2 * per_kind, n_tile)
+                for g in range(per):
+                    outward.append(move(proj.at[rows[g], columns(0)], q_ref.at[g]))
+            for level in range(len(mover.masks)):
+                if 0 <= i - lag - level < len(items):
+                    mover.finish(items[i - lag - level], level)
             if i in tasks:
                 tasks[i]()
-        for copy in swapped:
+        for item in items:
+            mover.complete(item)
+        for copy in own[1:3] + own[4:] + swapped:
             copy.wait_recv()
+        for copy in outward:
+            copy.wait()
         mover.close()
 
     row = (per, loc, width_here)
+    pair_shape = (2,) + row
     vmem, anywhere = pl.BlockSpec(memory_space=pltpu.VMEM), pl.BlockSpec(memory_space=pl.ANY)
-    outputs = [(kv_own.shape, BF16, anywhere)] * (n_ctx - 1) + [
-        ((per, n_fsdp, piece, width), BF16, anywhere),
+    outputs = [(pair_shape, BF16, anywhere)] * (n_ctx - 1) + [
+        (row, BF16, anywhere),
+        (pair_shape, BF16, anywhere),
+        ((per, loc, 3 * NR), BF16, anywhere),
         ((width_here, wide), BF16, anywhere),
         ((wide, units), BF16, anywhere),
         ((units, wide), BF16, anywhere),
@@ -466,22 +546,25 @@
     ]
     return pl.pallas_call(
         kernel,
-        in_specs=[vmem, vmem] + [anywhere] * 8,
+        in_specs=[vmem] * 3 + [anywhere] * 8,
         out_specs=[space for _, _, space in outputs],
         out_shape=[jax.ShapeDtypeStruct(shape, dtype) for shape, dtype, _ in outputs],
         scratch_shapes=[
             pltpu.SemaphoreType.DMA((n_copy,)),
             pltpu.SemaphoreType.DMA((n_copy,)),
-            pltpu.SemaphoreType.DMA((2 * n_stay,)),
-            pltpu.SemaphoreType.DMA((n_ctx + 1,)),
+            pltpu.SemaphoreType.DMA((5 * per,)),
+            pltpu.SemaphoreType.DMA((n_ctx,)),
+            pltpu.SemaphoreType.DMA((2,)),
+            pltpu.VMEM((per * loc, wide_x), BF16),
+            pltpu.VMEM((2, wide_x, tile), BF16),
+            pltpu.VMEM((per * loc, 3 * width_here), BF16),
             pltpu.VMEM((n_ctx, 2, loc, width_here), BF16),
             pltpu.VMEM((width_here, wide), BF16),
-        ]
-        + [pltpu.VMEM(shape, BF16) for shape in stay_shapes],
+        ],
         compiler_params=pltpu.CompilerParams(
-            collective_id=1, has_side_effects=True, vmem_limit_bytes=50 << 20
+            collective_id=1, has_side_effects=True, vmem_limit_bytes=60 << 20
         ),
-    )(query, bias, kv_own, cot, w_out, w_up, w_down, *maps)
+    )(bias, a_qkv, picked, x_rows, qkv_x, w_out, w_up, w_down, *maps)
 
 
 def attend_back(query, kv_own, slots, bias, grad, log_total, acts, n_fsdp, n_ctx):
@@ -639,18 +722,20 @@
         self.copy(0).start()
         self.copy(1).start()
 
-    def run(self, n, body):
+    def run(self, n, body, first=0, total=None):
+        total = n if total is None else total
+
         def step(t, carry):
             self.copy(t).wait()
             body(t, self.room.at[lax.rem(t, 2)])
 
-            @pl.when(t + 2 < n)
+            @pl.when(t + 2 < total)
             def _():
                 self.copy(t + 2).start()
 
             return carry
 
-        lax.fori_loop(0, n, step, 0)
+        lax.fori_loop(first, n, step, 0)
 
 
 def norm_parts(values):
@@ -675,7 +760,7 @@
     return out.astype(BF16), slope.astype(BF16)
 
 
-def middle(x_all, part_out, other_out, cot_all, picked, gain, shift_by, weights, maps):
+def middle(x_all, part_out, other_out, cot, picked, gain, shift_by, weights, maps, n_fsdp, n_ctx):
     per, loc, width = x_all.shape
     out_x, up_x, down_x = weights
     a_up, b_out, b_down, a_down, b_up = maps
@@ -689,11 +774,12 @@
     def kernel(*refs):
         pick_ref, gain_ref, shift_ref, a_up_ref, b_out_ref, b_down_ref, a_down_ref, b_up_ref = refs[:8]
         x_ref, first_ref, second_ref, cot_ref, out_ref, up_ref, down_ref = refs[8:15]
-        h_out, gelu_out, acts_out, dd_out, dpre_out, dy1_out, da_out = refs[15:22]
-        adapt_out_ref, adapt_down_ref, dadapt_up_ref, ctx_ref = refs[22:26]
-        (send, recv, ring_sem, sems) = refs[26:30]
-        (up_room, down_room, down_rows, up_rows) = refs[30:34]
-        (stage, part, got, hat1, rstd1, keep32, slope, gelu, wide_v, turned, dpre_t) = refs[34:]
+        h_out, gelu_out, acts_out, dd_out, dpre_out, dy1_out, da_out, cot_rows = refs[15:23]
+        adapt_out_ref, adapt_down_ref, dadapt_up_ref, ctx_ref = refs[23:27]
+        (send, recv, deal_send, deal_recv, ring_sem, sems) = refs[27:33]
+        (up_room, down_room, down_rows, up_rows) = refs[33:37]
+        (stage, part, got, hat1, rstd1, keep32, slope, gelu, wide_v, turned, dpre_t) = refs[37:]
+        mover = Mover(n_fsdp, n_ctx, deal_send, deal_recv)
         partner = {"tp": 1 - lax.axis_index("tp")}
 
         up = Ring(up_room, ring_sem, 0, lambda t: up_ref.at[:, ds(t * tile, tile)])
@@ -741,17 +827,20 @@
 
             lax.fori_loop(0, loc // chunk, step, 0)
 
-        barrier = pltpu.get_barrier_semaphore()
-        pl.semaphore_signal(
-            barrier, inc=1, device_id=partner, device_id_type=pl.DeviceIdType.MESH
-        )
+        def deal(g):
+            return Deal(lambda to: cot_ref.at[to * per + g], lambda s: cot_rows.at[g, s])
+
+        deals = [deal(g) for g in range(per)]
         for g in range(per):
             move(x_ref.at[g], stage.at[g], ("stage", g))
+            move(cot_ref.at[mover.z * per + g], cot_rows.at[g, 0], ("cot", g))
             move(first_ref.at[g], part.at[g], ("part", g))
             move(second_ref.at[g], slope.at[g, :, pl.ds(0, wide)], ("slope", g))
         up.prefetch()
         down.prefetch()
-        pl.semaphore_wait(barrier, 1)
+        mover.greet(tp=True)
+        for item in deals:
+            mover.begin(item)
 
         for g in range(per):
             free(("stage", g), ("part", g), ("slope", g), "wide", "gelu")
@@ -771,7 +860,6 @@
 
             by_rows(first_norm)
             move(wide_v, h_out.at[g], "wide")
-            move(cot_ref.at[g], stage.at[g], ("stage", g))
 
             def up_tile(t, room, g=g):
                 at = ds(t * tile, tile)
@@ -799,6 +887,11 @@
             swap_copy(0, g, n_wide, NR).start()
 
         for g in range(per):
+            mover.relay(deals[g])
+            free(("cot", g))
+            for s in range(n_fsdp):
+                at = pl.ds(s * cot.shape[1], cot.shape[1])
+                move(cot_rows.at[g, s], stage.at[g, at], ("stage", g))
             swapped(0, g)
             free(("stage", g), "wide")
             pick = pick_ref[g]
@@ -872,6 +965,7 @@
             if g + 1 < per:
                 out_r.prefetch()
         free(*list(busy))
+        mover.close()
 
     vmem, anywhere = pl.BlockSpec(memory_space=pltpu.VMEM), pl.BlockSpec(memory_space=pl.ANY)
     row = (per, loc)
@@ -883,6 +977,7 @@
         (row + (units,), BF16, anywhere),
         (row + (width,), F32, anywhere),
         (row + (wide,), BF16, anywhere),
+        ((per, n_fsdp) + cot.shape[1:], BF16, anywhere),
         (row + (NR,), BF16, vmem),
         (row + (NR,), BF16, vmem),
         (row + (NR,), BF16, vmem),
@@ -897,8 +992,10 @@
         scratch_shapes=[
             pltpu.SemaphoreType.DMA((n_copy,)),
             pltpu.SemaphoreType.DMA((n_copy,)),
+            pltpu.SemaphoreType.DMA((per * (n_fsdp - 1),)),
+            pltpu.SemaphoreType.DMA((per * (n_fsdp - 1),)),
             pltpu.SemaphoreType.DMA((8,)),
-            pltpu.SemaphoreType.DMA((11 * per,)),
+            pltpu.SemaphoreType.DMA(((11 + n_fsdp) * per,)),
             pltpu.VMEM((2, wide, tile), BF16),
             pltpu.VMEM((2, units, tile), BF16),
             pltpu.VMEM((2, tile, wide), BF16),
@@ -920,58 +1017,8 @@
         ),
     )(
         picked, gain, shift_by, a_up, b_out, b_down, a_down, b_up,
-        x_all, part_out, other_out, cot_all, out_x, up_x, down_x,
+        x_all, part_out, other_out, cot, out_x, up_x, down_x,
     )
-
-
-def mm(left, right, nt, finish, tile, n_out=1, beside=None):
-    rows, depth = left.shape
-    columns = right.shape[0] if nt else right.shape[1]
-    extra = [] if beside is None else [beside]
-    sub = 128 if nt else tile
-
-    def kernel(left_ref, right_ref, *refs):
-        n_extra = len(extra)
-        outs = refs[n_extra : n_extra + n_out]
-        if nt:
-            turned = refs[-1]
-
-            @pl.when(pl.program_id(0) == 0)
-            def _():
-                turned[...] = left_ref[...].T
-
-        for k in range(tile // sub):
-            at = slice(k * sub, (k + 1) * sub)
-            if nt:
-                block = dot(right_ref[at, :], turned[...]).T
-            else:
-                block = dot(left_ref[...], right_ref[:, at])
-            values = finish(block, *[ref[:, at] for ref in refs[:n_extra]])
-            for ref, value in zip(outs, values):
-                ref[:, at] = value
-
-    part = pl.BlockSpec((rows, tile), lambda j: (0, j))
-    out = pl.pallas_call(
-        kernel,
-        grid=(pl.cdiv(columns, tile),),
-        in_specs=[
-            pl.BlockSpec((rows, depth), lambda j: (0, 0)),
-            pl.BlockSpec((tile, depth), lambda j: (j, 0))
-            if nt
-            else pl.BlockSpec((depth, tile), lambda j: (0, j)),
-        ]
-        + [part] * len(extra),
-        out_specs=[part] * n_out,
-        out_shape=[jax.ShapeDtypeStruct((rows, columns), BF16)] * n_out,
-        scratch_shapes=[pltpu.VMEM((depth, rows), BF16)] if nt else [],
-        compiler_params=pltpu.CompilerParams(vmem_limit_bytes=48 << 20),
-        cost_estimate=pl.CostEstimate(
-            flops=2 * rows * depth * columns,
-            bytes_accessed=2 * (rows * depth + 2 * depth * columns + rows * columns * n_out),
-            transcendentals=0,
-        ),
-    )(left, right, *extra)
-    return out[0] if n_out == 1 else out
 
 
 def combine(pieces, chosen, shapes):
@@ -1007,7 +1054,7 @@
     )(chosen, pieces)
 
 
-def last(d_query, d_pair, x_all, adapt_all, dy1, qkv_x, a_in, picked, early, pairs, n_fsdp, n_ctx):
+def last(d_query, d_pair, x_all, adapt_all, dy1, qkv_x, a_qkv, picked, early, pairs, n_fsdp, n_ctx):
     per, loc, width_here = d_query.shape
     piece, width = loc // n_fsdp, x_all.shape[2]
     depth = 3 * width_here
@@ -1170,7 +1217,9 @@
                 total = part[g, rows, :].astype(F32) + got[g, rows, :].astype(F32)
                 code = (total[:, width:] * pick).astype(BF16)
                 codes_in[g, rows, :] = code
-                value = dy1_room[g, rows, :] + total[:, :width] + dot_nt(code, a_ref[...])
+                value = dy1_room[g, rows, :] + total[:, :width]
+                for j in range(3):
+                    value = value + dot_nt(code[:, j * NR : (j + 1) * NR], a_ref[j])
                 dx[g, rows, :] = value.astype(BF16)
                 return carry
 
@@ -1248,11 +1297,7 @@
         compiler_params=pltpu.CompilerParams(
             collective_id=4, has_side_effects=True, vmem_limit_bytes=60 << 20
         ),
-    )(d_query, d_pair, x_all, adapt_all, a_in, picked, dy1, qkv_x, *early)
-
-
-def as_low(block):
-    return (block.astype(BF16),)
+    )(d_query, d_pair, x_all, adapt_all, a_qkv, picked, dy1, qkv_x, *early)
 
 
 def gelu_both(pre):
@@ -1291,16 +1336,12 @@
     per = seqs // n_fsdp
     loc = n_fsdp * piece
     heads_width = w_qkv.shape[2]
-    n_group = GROUPS if per % GROUPS == 0 else 1
-    g_per = per // n_group
-    g_rows = g_per * loc
-
     def take(array, start, size, axis=0):
         return lax.dynamic_slice_in_dim(array, start, size, axis)
 
     units = w_up.shape[1]
     rows_shape = (per, n_fsdp, piece, width)
-    zq, zu = w_qkv.shape[1], w_up.shape[0]
+    zq = w_qkv.shape[1]
 
     def first_items(ins, outs, z):
         x_ref, w_ref = ins
@@ -1340,8 +1381,6 @@
         foot=(b_qkv, lambda outs: outs[1].at[pl.ds(width, 3 * NR)]),
     )
 
-    a_in = a_qkv.transpose(1, 0, 2).reshape(width, 3 * NR)
-
     my_lengths = take(lengths, z * per, per)
     my_ids = take(adapter_ids, z * per, per)
     picked = (my_ids[:, None] == jnp.arange(NR)[None, :] // RANK).astype(F32)
@@ -1354,44 +1393,34 @@
     bias_all = jnp.where(key_pos[None, :] < my_lengths[:, None], 0.0, -1e30).astype(F32)
     bias_all = jnp.broadcast_to(bias_all[:, :, None], bias_all.shape + (128,))
 
-    pick_all = jnp.repeat(picked, loc, axis=0)
-    x_flat = x_all.reshape(per * loc, width)
-    adapt_all = (dot(x_flat, a_in) * jnp.concatenate([pick_all] * 3, axis=1)).astype(BF16)
-    proj_all = mm(jnp.concatenate([x_flat, adapt_all], axis=1), qkv_x, False, as_low, 1024)
-    kv_own = jnp.stack([proj_all[:, heads_width : 2 * heads_width], proj_all[:, 2 * heads_width :]])
-    kv_own = kv_own.reshape(2, per, loc, heads_width)
+    picked = picked[:, None, :]
+    x_rows = x_all.reshape(per, loc, width)
     moved = forward_and_gather(
-        proj_all[:, :heads_width].reshape(per, loc, heads_width),
-        kv_own,
-        bias_all,
-        (cotangent, w_out, w_up, w_down),
-        (a_out, b_up, a_down),
-        n_fsdp,
-        n_ctx,
+        x_rows, qkv_x, a_qkv, picked, bias_all, (w_out, w_up, w_down), (a_out, b_up, a_down), n_fsdp, n_ctx
     )
-    kv_all = [kv_own] + list(moved[: n_ctx - 1])
-    cot_all, out_x, up_x, down_x, context, log_total, part_out, other_out = moved[n_ctx - 1 :]
-
-    groups = range(n_group)
-    picks = [jnp.repeat(take(picked, g * g_per, g_per), loc, axis=0) for g in groups]
-    part = [slice(g * g_rows, (g + 1) * g_rows) for g in groups]
-    x_rows = [x_flat[part[g]] for g in groups]
-
-    (wide_h, gelu_out, acts, wide_d, d_pre, dy1, wide_a, adapt_out, adapt_down, dadapt_up, d_context) = middle(
-        x_all.reshape(per, loc, width),
+    slots = moved[: n_ctx - 1]
+    (query, kv_own, adapt_all, out_x, up_x, down_x, context, log_total, part_out, other_out) = moved[
+        n_ctx - 1 :
+    ]
+    (
+        wide_h, gelu_out, acts, wide_d, d_pre, dy1, wide_a, _, adapt_out, adapt_down, dadapt_up, d_context,
+    ) = middle(
+        x_rows,
         part_out,
         other_out,
-        cot_all.reshape(per, loc, width),
-        picked[:, None, :],
+        cotangent,
+        picked,
         ln_gain,
         ln_bias,
         (out_x, up_x, down_x),
         (a_up, b_out, b_down, a_down, b_up),
+        n_fsdp,
+        n_ctx,
     )
     d_query, d_pair, activations = attend_back(
-        proj_all[:, :heads_width].reshape(per, loc, heads_width),
+        query,
         kv_own,
-        kv_all[1:],
+        slots,
         bias_all,
         d_context,
         log_total,
@@ -1415,12 +1444,12 @@
     input_grad, early, late = last(
         d_query,
         d_pair,
-        x_all.reshape(per, loc, width),
-        adapt_all.reshape(per, loc, 3 * NR),
+        x_rows,
+        adapt_all,
         dy1,
         qkv_x,
-        a_in,
-        picked[:, None, :],
+        a_qkv,
+        picked,
         early_in,
         early_pairs,
         n_fsdp,

time: 684 us -> 637 us (0.931)
  Pallas kernels: 649 us -> 621 us
  local copies, waits for them, and re-layouts: 19.3 us -> 8.94 us
    pallas_call x2 -> x1, Pallas kernels: 236 us -> 202 us  [forward_and_gather(): pl.pallas_call(kernel, in_specs=[vmem] * 3 + [anywhere] * 8, out_specs=[s...]
    unnamed x39 -> x12, local copies, waits for them, and re-layouts: 16.1 us -> 6.01 us
where the time goes in v7:
time: 637 us; the launch traced here: 633 us
  Pallas kernels  621 us (97%)
  local copies, waits for them, and re-layouts  8.94 us (1%)
    pallas_call x1, Pallas kernels, forward_and_gather(): pl.pallas_call(kernel, in_specs=[vmem] * 3 + [anywhere] * 8, out_specs=[s...  202 us
    pallas_call x1, Pallas kernels, middle(): pl.pallas_call(kernel, in_specs=[vmem] * 8 + [anywhere] * 7, out_specs=[s...  131 us
    pallas_call x1, Pallas kernels, last(): pl.pallas_call(kernel, in_specs=[vmem] * 6 + [anywhere] * (2 + n_early),...  122 us
    pallas_call x1, Pallas kernels, move(): pl.pallas_call(kernel, in_specs=spaces, out_specs=[pl.BlockSpec(memory_sp...  101 us
    pallas_call x1, Pallas kernels, attend_back(): pl.pallas_call(kernel, in_specs=[vmem] * 4 + [anywhere] * (1 + n_ctx), ou...  58.2 us

profile of v7, /device:TPU:0, one launch (start us, length us, event | category | flops | bytes accessed | tf_op | source)
XLA Modules:
  0.0 633.0 jit_solution(10388492645552050638)
XLA Ops:
  0.6 0.7 dynamic_slice.6
  1.4 0.7 fusion.2
  2.0 0.1 add_multiply_fusion
  2.1 0.1 iota_add_fusion
  2.2 0.1 add.82
  2.3 0.1 compare_select_fusion
  2.4 1.3 broadcast_in_dim.12.refs_0_.refs_1_
  3.7 0.7 dynamic_slice.7
  4.4 0.6 compare_convert_fusion.refs_2_.refs_0_.refs_5_
  5.0 101.4 %shard_map.258 = (bf16[2,4,64,2048]{3,2,1,0:T(8,128)(2,1)}, bf16[2432,3072]{1,0:T(8,128)(2,1)}) custom-call(bf16[8,64,2048]{2,1,0:T(8,128)(2,1)} %refs_0_.1, bf16[3,512,1024]{2,1,0:T(8,128)(2,1)} %refs_1_.3, bf16[3,128,1024]{2,1,0:T(8,128)(2,1)} %refs_2_.2), custom_call_target="tpu_custom_call" | custom-call | tf_op jit(solution)/shard_map/pallas_call | solution.py:316
  106.4 201.8 %shard_map.259 = (bf16[2,2,256,1024]{3,2,1,0:T(8,128)(2,1)}, bf16[2,2,256,1024]{3,2,1,0:T(8,128)(2,1)}, bf16[2,2,256,1024]{3,2,1,0:T(8,128)(2,1)}, bf16[2,256,10...) custom-call(f32[2,1024,128]{2,1,0:T(8,128)} %broadcast_in_dim.12.ref, ...), custom_call_target="tpu_custom_call" | custom-call | tf_op jit(solution)/shard_map/pallas_call | solution.py:547
  308.2 130.5 %shard_map.260 = (bf16[2,256,2176]{2,1,0:T(8,128)(2,1)}, bf16[2,256,4096]{2,1,0:T(8,128)(2,1)}, bf16[2,256,2048]{2,1,0:T(8,128)(2,1)}, bf16[2,256,2176]{2,1,0:T(...) custom-call(f32[2,1,128]{2,1,0:T(1,128)} %compare_convert_fusion.ref, ...), custom_call_target="tpu_custom_call" | custom-call | tf_op jit(solution)/shard_map/pallas_call | solution.py:987
  438.8 58.2 %shard_map.261 = (bf16[2,256,1024]{2,1,0:T(8,128)(2,1)}, bf16[2,2,256,1024]{3,2,1,0:T(8,128)(2,1)}, bf16[8,64,2048]{2,1,0:T(8,128)(2,1)}) custom-call(bf16[2,256,1024]{2,1,0:T(8,128)(2,1)} %get-tuple-element.51.refs_0_, f32[2,1024,128]{2,1,0:T(8,128)} %broadcast_in_dim.12.refs_0_.refs_1_, bf16[2,256,1024]{2,1,0:T(8,128)(2,1)} %get-tuple-element.57.refs_2_, ...), custom_call_target="tpu_custom_call" | custom-call | tf_op jit(solution)/shard_map/pallas_call | solution.py:687
  497.0 0.0 copy-start.4
  497.0 122.3 %shard_map.262 = (bf16[8,64,2048]{2,1,0:T(8,128)(2,1)}, bf16[4,4,32,4608]{3,2,1,0:T(8,128)(2,1)}, bf16[4,4,32,1536]{3,2,1,0:T(8,128)(2,1)}) custom-call(bf16[2,256,1024]{2,1,0:T(8,128)(2,1)} %get-tuple-element.65.refs_0_, bf16[2,2,256,1024]{3,2,1,0:T(8,128)(2,1)} %get-tuple-element.66.refs_1_, bf16[2,256,2048]{2,1,0:T(8,128)(2,1)} %bitcast.4, ...), custom_call_target="tpu_custom_call" | custom-call | tf_op jit(solution)/shard_map/pallas_call | solution.py:1282
  619.4 0.1 iota_add_fusion.1
  619.4 0.1 add.87
  619.5 0.1 fusion.chosen_ref
  619.6 2.3 copy-done
  621.9 4.9 shard_map.264
  626.9 2.3 shard_map.263
  629.2 1.3 copy.31
  630.5 1.0 copy-done.3
  631.5 1.3 copy.32
  (9 shorter events, 0.0 us)
Async XLA Ops:
  497.0 122.3 %copy-start.4 = (s32[8]{0:T(128)S(1)}, s32[8]{0:T(128)}, u32[]{:S(2)}) copy-start(s32[8]{0:T(128)} %param.22) | copy-start | bytes 100
  619.6 2.3 copy-start
  621.9 5.0 copy-start.1
  626.9 2.3 copy-start.2
  629.2 2.3 copy-start.3

commit v8 on v7

--- a/solution.py
+++ b/solution.py
@@ -330,7 +330,9 @@
     )(*inputs)
 
 
-def forward_and_gather(x_rows, qkv_x, a_qkv, picked, bias, shards, maps, n_fsdp, n_ctx):
+def forward_and_gather(
+    x_rows, qkv_x, a_qkv, picked, bias, gain, shift_by, first_maps, shards, maps, n_fsdp, n_ctx
+):
     per, loc, width = x_rows.shape
     w_out, w_up, w_down = shards
     width_here = qkv_x.shape[1] // 3
@@ -344,18 +346,25 @@
     paired = cuts // 2 if n_ctx > 1 else 0
     tile = 512
     per_kind = width_here // tile
+    chunk = 32
     n_tile = 3 * per_kind
     n_copy = (n_fsdp - 1) * n_ctx * (1 + 2 * cuts) + 2 * per * (n_ctx - 1) + 6 + per
     lag = 4
 
     def kernel(*refs):
-        bias_ref, a_ref, pick_ref, x_ref, w_ref = refs[:5]
-        wo_ref, wu_ref, wd_ref, ao_ref, bu_ref, ad_ref = refs[5:11]
-        slots = refs[11 : 10 + n_ctx]
-        q_ref, kv_ref, adapt_ref, out_ref, up_ref, down_ref, ctx_ref, log_ref, part_ref, other_ref = refs[
-            10 + n_ctx : 20 + n_ctx
+        bias_ref, a_ref, pick_ref, gain_ref, shift_ref, a_up_ref, b_out_ref, x_ref, w_ref = refs[:9]
+        wo_ref, wu_ref, wd_ref, ao_ref, bu_ref, ad_ref = refs[9:15]
+        slots = refs[15 : 14 + n_ctx]
+        q_ref, kv_ref, adapt_ref, out_ref, up_ref, down_ref, ctx_ref, log_ref = refs[
+            14 + n_ctx : 22 + n_ctx
         ]
-        send, recv, here, load, ring_sem, x_room, w_room, proj, kv_room, out_room = refs[20 + n_ctx :]
+        h_ref, gelu_ref, slope_ref, hat_ref, rstd_ref, adapt_out_ref, adapt_up_ref = refs[
+            22 + n_ctx : 29 + n_ctx
+        ]
+        send, recv, here, load, ring_sem, x_room, w_room, proj, kv_room, out_room = refs[
+            29 + n_ctx : 39 + n_ctx
+        ]
+        part_ref, other_ref, up_room, wide_v, hat1, gelu, slope = refs[39 + n_ctx :]
         mover = Mover(n_fsdp, n_ctx, send, recv)
         ring = Ring(
             w_room,
@@ -473,9 +482,58 @@
             at = ds(lax.rem(t + per_kind, n_tile) * tile, tile)
             proj[:, at] = dot(x_room[...], room[...]).astype(BF16)
 
+        up_ring = Ring(up_room, ring_sem, 2, lambda t: up_ref.at[:, ds(t * tile, tile)])
+
+        def first_norm(g):
+            swapped[g].wait_recv()
+            pick = pick_ref[g]
+
+            def step(r, carry):
+                rows_r = ds(r * chunk, chunk)
+                total = part_ref[g, rows_r, :].astype(F32) + other_ref[g, rows_r, :].astype(F32)
+                code = (total[:, width:] * pick).astype(BF16)
+                adapt_out_ref[g, rows_r, :] = code
+                x = x_room[ds(g * loc + r * chunk, chunk), :width].astype(F32)
+                hat, rstd = norm_parts(x + total[:, :width] + dot(code, b_out_ref[...]))
+                hat1[g, rows_r, :] = hat
+                rstd_ref[g, rows_r, :] = jnp.broadcast_to(rstd, (chunk, 128))
+                low = (hat * gain_ref[0:1, :] + shift_ref[0:1, :]).astype(BF16)
+                wide_v[g, rows_r, :width] = low
+                code = (dot(low, a_up_ref[...]) * pick).astype(BF16)
+                wide_v[g, rows_r, width:] = code
+                adapt_up_ref[g, rows_r, :] = code
+                return carry
+
+            lax.fori_loop(0, loc // chunk, step, 0)
+            outward.append(move(hat1.at[g], hat_ref.at[g]))
+            outward.append(move(wide_v.at[g], h_ref.at[g]))
+
+        def feed(g):
+            if g == 0:
+                for item in items[1 : 1 + cuts]:
+                    mover.complete(item)
+                own[1].wait_recv()
+                own[4].wait_recv()
+                up_ring.prefetch()
+
+            def up_tile(t, room):
+                at = ds(t * tile, tile)
+                value, factor = gelu_both(dot(wide_v[g], room[...]))
+                gelu[g, :, at] = value
+                slope[g, :, at] = factor
+
+            up_ring.run(units // tile, up_tile)
+            if g + 1 < per:
+                up_ring.prefetch()
+            outward.append(move(gelu.at[g], gelu_ref.at[g]))
+            outward.append(move(slope.at[g], slope_ref.at[g]))
+
         swapped, outward = [], []
         tasks = {1 + g: (lambda g=g: attend(g)) for g in range(per)}
         tasks[per + 2] = project
+        tasks[per + 5] = lambda: [first_norm(g) for g in range(per)]
+        for g in range(per):
+            tasks[per + 6 + g] = lambda g=g: feed(g)
         ring.prefetch()
         loads = [move(x_ref.at[g], x_room.at[rows[g], pl.ds(0, width)]) for g in range(per)]
         mover.greet(tp=True)
@@ -523,7 +581,7 @@
                 tasks[i]()
         for item in items:
             mover.complete(item)
-        for copy in own[1:3] + own[4:] + swapped:
+        for copy in (own[2], own[5]):
             copy.wait_recv()
         for copy in outward:
             copy.wait()
@@ -541,30 +599,42 @@
         ((units, wide), BF16, anywhere),
         (row, BF16, vmem),
         ((per, heads, 1, loc), F32, vmem),
-        ((per, loc, wide), BF16, vmem),
         ((per, loc, wide), BF16, anywhere),
+        ((per, loc, units), BF16, anywhere),
+        ((per, loc, units), BF16, anywhere),
+        ((per, loc, width), F32, anywhere),
+        ((per, loc, 128), F32, vmem),
+        ((per, loc, NR), BF16, vmem),
+        ((per, loc, NR), BF16, vmem),
     ]
     return pl.pallas_call(
         kernel,
-        in_specs=[vmem] * 3 + [anywhere] * 8,
+        in_specs=[vmem] * 7 + [anywhere] * 8,
         out_specs=[space for _, _, space in outputs],
         out_shape=[jax.ShapeDtypeStruct(shape, dtype) for shape, dtype, _ in outputs],
         scratch_shapes=[
             pltpu.SemaphoreType.DMA((n_copy,)),
             pltpu.SemaphoreType.DMA((n_copy,)),
-            pltpu.SemaphoreType.DMA((5 * per,)),
+            pltpu.SemaphoreType.DMA((9 * per,)),
             pltpu.SemaphoreType.DMA((n_ctx,)),
-            pltpu.SemaphoreType.DMA((2,)),
+            pltpu.SemaphoreType.DMA((4,)),
             pltpu.VMEM((per * loc, wide_x), BF16),
             pltpu.VMEM((2, wide_x, tile), BF16),
             pltpu.VMEM((per * loc, 3 * width_here), BF16),
             pltpu.VMEM((n_ctx, 2, loc, width_here), BF16),
             pltpu.VMEM((width_here, wide), BF16),
+            pltpu.VMEM((per, loc, wide), BF16),
+            pltpu.VMEM((per, loc, wide), BF16),
+            pltpu.VMEM((2, wide, tile), BF16),
+            pltpu.VMEM((per, loc, wide), BF16),
+            pltpu.VMEM((per, loc, width), F32),
+            pltpu.VMEM((per, loc, units), BF16),
+            pltpu.VMEM((per, loc, units), BF16),
         ],
         compiler_params=pltpu.CompilerParams(
             collective_id=1, has_side_effects=True, vmem_limit_bytes=60 << 20
         ),
-    )(bias, a_qkv, picked, x_rows, qkv_x, w_out, w_up, w_down, *maps)
+    )(bias, a_qkv, picked, gain, shift_by, *first_maps, x_rows, qkv_x, w_out, w_up, w_down, *maps)
 
 
 def attend_back(query, kv_own, slots, bias, grad, log_total, acts, n_fsdp, n_ctx):
@@ -738,6 +808,58 @@
         lax.fori_loop(first, n, step, 0)
 
 
+def compact(out_ref, n, entries, sizes):
+    column = lax.broadcasted_iota(jnp.int32, (NR, RANK), 0)
+    rank = lax.broadcasted_iota(jnp.int32, (NR, RANK), 1)
+    used = jnp.where(lax.rem(column, RANK) == rank, 1.0, 0.0).astype(BF16)
+    start = 0
+    for (code, value), size in zip(entries, sizes):
+        short = dot(code(), used).astype(BF16)
+        block = dot_tn(short, value()).astype(BF16)
+        for k in range(out_ref.shape[0]):
+            out_ref[k, n * RANK : (n + 1) * RANK, start : start + size] = block[
+                :, k * size : (k + 1) * size
+            ]
+        start += size
+
+
+class Fold:
+    def __init__(self, mover, parts, came, out_ref):
+        self.mover, self.parts, self.came, self.out_ref = mover, parts, came, out_ref
+        self.flying = {}
+
+    def at(self, k):
+        return flip(self.mover.ct, self.mover.offsets[k])
+
+    def hand(self, level):
+        half = 2**level
+        self.flying[level] = [
+            self.mover.go(
+                self.parts.at[self.at(half + i)],
+                self.came.at[half - 1 + i],
+                {"ctx": flip(self.mover.ct, self.mover.masks[level])},
+            )
+            for i in range(half)
+        ]
+
+    def take(self, level):
+        for i, copy in enumerate(self.flying[level]):
+            copy.wait_recv()
+            total = self.parts[self.at(i)].astype(F32) + self.came[2**level - 1 + i].astype(F32)
+            self.parts[self.at(i)] = total.astype(BF16)
+
+    def next(self, level):
+        self.take(level)
+        if level:
+            self.hand(level - 1)
+
+    def gather(self):
+        own = self.parts.at[self.mover.ct]
+        item = Weight(lambda c: self.parts.at[c], lambda o, c: self.out_ref.at[c, o], own)
+        self.mover.begin(item)
+        return own, self.out_ref.at[self.mover.ct, self.mover.z], item
+
+
 def norm_parts(values):
     center = values - jnp.mean(values, axis=-1, keepdims=True)
     rstd = lax.rsqrt(jnp.mean(center * center, axis=-1, keepdims=True) + NORM_EPS)
@@ -760,8 +882,8 @@
     return out.astype(BF16), slope.astype(BF16)
 
 
-def middle(x_all, part_out, other_out, cot, picked, gain, shift_by, weights, maps, n_fsdp, n_ctx):
-    per, loc, width = x_all.shape
+def middle(hats, rstds, gelus, slopes, adapt_up, cot, picked, gain, shift_by, weights, maps, n_fsdp, n_ctx):
+    per, loc, width = hats.shape
     out_x, up_x, down_x = weights
     a_up, b_out, b_down, a_down, b_up = maps
     wide, units = up_x.shape
@@ -770,20 +892,22 @@
     chunk = 32
     n_wide = width // tile
     n_swap = n_wide + 1
+    sizes = [width // n_ctx, units // n_ctx, units // n_ctx]
 
     def kernel(*refs):
-        pick_ref, gain_ref, shift_ref, a_up_ref, b_out_ref, b_down_ref, a_down_ref, b_up_ref = refs[:8]
-        x_ref, first_ref, second_ref, cot_ref, out_ref, up_ref, down_ref = refs[8:15]
-        h_out, gelu_out, acts_out, dd_out, dpre_out, dy1_out, da_out, cot_rows = refs[15:23]
-        adapt_out_ref, adapt_down_ref, dadapt_up_ref, ctx_ref = refs[23:27]
-        (send, recv, deal_send, deal_recv, ring_sem, sems) = refs[27:33]
-        (up_room, down_room, down_rows, up_rows) = refs[33:37]
-        (stage, part, got, hat1, rstd1, keep32, slope, gelu, wide_v, turned, dpre_t) = refs[37:]
+        pick_ref, gain_ref, shift_ref, rstd1, code_up_ref = refs[:5]
+        a_up_ref, b_out_ref, b_down_ref, a_down_ref, b_up_ref = refs[5:10]
+        hat_ref, gelu_ref, slope_ref, cot_ref, out_ref, up_ref, down_ref = refs[10:17]
+        acts_out, dy1_out, da_out, cot_rows, grads_out = refs[17:22]
+        dadapt_up_ref, ctx_ref = refs[22:24]
+        (send, recv, deal_send, deal_recv, ring_sem, sems) = refs[24:30]
+        (down_room, down_rows, up_rows) = refs[30:33]
+        (stage, part, got, hat1, keep32, slope, gelu, wide_v, turned, dpre_t) = refs[33:43]
+        codes_down, grads_part, grads_came = refs[43:]
         mover = Mover(n_fsdp, n_ctx, deal_send, deal_recv)
         partner = {"tp": 1 - lax.axis_index("tp")}
 
-        up = Ring(up_room, ring_sem, 0, lambda t: up_ref.at[:, ds(t * tile, tile)])
-        down = Ring(down_room, ring_sem, 2, lambda t: down_ref.at[:, ds(t * tile, tile)])
+        down = Ring(down_room, ring_sem, 0, lambda t: down_ref.at[:, ds(t * tile, tile)])
         down_r = Ring(down_rows, ring_sem, 4, lambda t: down_ref.at[ds(t * tile, tile)])
         up_r = Ring(up_rows, ring_sem, 6, lambda t: up_ref.at[ds(t * tile, tile)])
         out_r = Ring(down_rows, ring_sem, 4, lambda t: out_ref.at[ds(t * tile, tile)])
@@ -832,50 +956,23 @@
 
         deals = [deal(g) for g in range(per)]
         for g in range(per):
-            move(x_ref.at[g], stage.at[g], ("stage", g))
+            move(gelu_ref.at[g], gelu.at[g], ("gelu", g))
+            if g == 0:
+                down.prefetch()
             move(cot_ref.at[mover.z * per + g], cot_rows.at[g, 0], ("cot", g))
-            move(first_ref.at[g], part.at[g], ("part", g))
-            move(second_ref.at[g], slope.at[g, :, pl.ds(0, wide)], ("slope", g))
-        up.prefetch()
-        down.prefetch()
+        for g in range(per):
+            move(hat_ref.at[g], hat1.at[g], ("hat", g))
+            move(slope_ref.at[g], slope.at[g], ("slope", g))
         mover.greet(tp=True)
-        for item in deals:
-            mover.begin(item)
+        mover.begin(deals[0])
 
         for g in range(per):
-            free(("stage", g), ("part", g), ("slope", g), "wide", "gelu")
-            pick = pick_ref[g]
-
-            def first_norm(rows, g=g, pick=pick):
-                total = part[g, rows, :].astype(F32) + slope[g, rows, :wide].astype(F32)
-                code = (total[:, width:] * pick).astype(BF16)
-                adapt_out_ref[g, rows, :] = code
-                y1 = stage[g, rows, :].astype(F32) + total[:, :width] + dot(code, b_out_ref[...])
-                hat, rstd = norm_parts(y1)
-                hat1[g, rows, :] = hat
-                rstd1[g, rows, :] = jnp.broadcast_to(rstd, (chunk, 128))
-                low = (hat * gain_ref[0:1, :] + shift_ref[0:1, :]).astype(BF16)
-                wide_v[rows, :width] = low
-                wide_v[rows, width:] = (dot(low, a_up_ref[...]) * pick).astype(BF16)
-
-            by_rows(first_norm)
-            move(wide_v, h_out.at[g], "wide")
-
-            def up_tile(t, room, g=g):
-                at = ds(t * tile, tile)
-                value, factor = gelu_both(dot(wide_v[...], room[...]))
-                gelu[:, at] = value
-                slope[g, :, at] = factor
-
-            up.run(units // tile, up_tile)
-            if g + 1 < per:
-                up.prefetch()
-            else:
+            if g + 1 == per:
                 down_r.prefetch()
-            move(gelu, gelu_out.at[g], "gelu")
+            free(("gelu", g))
 
             def down_tile(t, room, g=g):
-                part[g, :, ds(t * tile, tile)] = dot(gelu[...], room[...]).astype(BF16)
+                part[g, :, ds(t * tile, tile)] = dot(gelu[g], room[...]).astype(BF16)
                 swap_copy(0, g, t, tile).start()
 
             down.run(n_wide, down_tile)
@@ -883,36 +980,37 @@
                 down.prefetch()
             else:
                 up_r.prefetch()
-            part[g, :, width:] = dot(gelu[...], a_down_ref[...]).astype(BF16)
+            part[g, :, width:] = dot(gelu[g], a_down_ref[...]).astype(BF16)
             swap_copy(0, g, n_wide, NR).start()
 
         for g in range(per):
             mover.relay(deals[g])
+            if g + 1 < per:
+                mover.begin(deals[g + 1])
             free(("cot", g))
             for s in range(n_fsdp):
                 at = pl.ds(s * cot.shape[1], cot.shape[1])
                 move(cot_rows.at[g, s], stage.at[g, at], ("stage", g))
             swapped(0, g)
-            free(("stage", g), "wide")
+            free(("stage", g), ("hat", g), ("slope", g))
             pick = pick_ref[g]
 
             def second_norm(rows, g=g, pick=pick):
                 total = part[g, rows, :].astype(F32) + got[0, g, rows, :].astype(F32)
                 code = (total[:, width:] * pick).astype(BF16)
-                adapt_down_ref[g, rows, :] = code
+                codes_down[g, rows, :] = code
                 hidden = hat1[g, rows, :] * gain_ref[0:1, :] + shift_ref[0:1, :]
                 hat, rstd = norm_parts(hidden + total[:, :width] + dot(code, b_down_ref[...]))
                 part[g, rows, :width] = (hat * gain_ref[1:2, :] + shift_ref[1:2, :]).astype(BF16)
                 dy2 = norm_back(hat, rstd, stage[g, rows, :].astype(F32) * gain_ref[1:2, :])
                 keep32[g, rows, :] = dy2
                 low = dy2.astype(BF16)
-                wide_v[rows, :width] = low
-                wide_v[rows, width:] = (dot_nt(low, b_down_ref[...]) * pick).astype(BF16)
+                wide_v[g, rows, :width] = low
+                wide_v[g, rows, width:] = (dot_nt(low, b_down_ref[...]) * pick).astype(BF16)
 
             by_rows(second_norm)
             move(part.at[g, :, pl.ds(0, width)], acts_out.at[g], ("part", g))
-            move(wide_v, dd_out.at[g], "wide")
-            turned[...] = wide_v[...].T
+            turned[...] = wide_v[g].T
 
             def down_back(t, room, g=g):
                 at = ds(t * tile, tile)
@@ -923,7 +1021,6 @@
 
             down_r.run(units // tile, down_back)
             (down_r if g + 1 < per else out_r).prefetch()
-            move(slope.at[g], dpre_out.at[g], ("slope", g))
             free(("part", g))
 
             def up_back(t, room, g=g):
@@ -937,8 +1034,18 @@
             swap_copy(1, g, n_wide, NR).start()
 
         for g in range(per):
+            entries = [
+                (lambda g=g: codes_down[g], lambda g=g: wide_v[g, :, :width]),
+                (lambda g=g: wide_v[g, :, width:], lambda g=g: gelu[g]),
+                (lambda g=g: code_up_ref[g], lambda g=g: slope[g]),
+            ]
+            compact(grads_part, g, entries, sizes)
+
+        fold = Fold(mover, grads_part, grads_came, grads_out)
+        lasting = len(mover.masks) - 1
+        fold.hand(lasting)
+        for g in range(per):
             swapped(1, g)
-            free("wide")
             pick = pick_ref[g]
 
             def first_back(rows, g=g, pick=pick):
@@ -950,13 +1057,15 @@
                 dy1 = norm_back(hat1[g, rows, :], rstd, dh1 * gain_ref[0:1, :])
                 keep32[g, rows, :] = dy1
                 low = dy1.astype(BF16)
-                wide_v[rows, :width] = low
-                wide_v[rows, width:] = (dot_nt(low, b_out_ref[...]) * pick).astype(BF16)
+                wide_v[g, rows, :width] = low
+                wide_v[g, rows, width:] = (dot_nt(low, b_out_ref[...]) * pick).astype(BF16)
 
             by_rows(first_back)
+            if g == 0:
+                fold.next(lasting)
             move(keep32.at[g], dy1_out.at[g], "dy1")
-            move(wide_v, da_out.at[g], "wide")
-            turned[...] = wide_v[...].T
+            move(wide_v.at[g], da_out.at[g], "wide")
+            turned[...] = wide_v[g].T
 
             def out_back(t, room, g=g):
                 ctx_ref[g, :, ds(t * tile, tile)] = dot(room[...], turned[...]).T.astype(BF16)
@@ -964,39 +1073,42 @@
             out_r.run(width_here // tile, out_back)
             if g + 1 < per:
                 out_r.prefetch()
+            if g == 0:
+                for level in range(lasting - 1, -1, -1):
+                    fold.next(level)
+                source, target, item = fold.gather()
+                move(source, target, "grads")
+                mover.relay(item)
+        mover.complete(item)
         free(*list(busy))
         mover.close()
 
     vmem, anywhere = pl.BlockSpec(memory_space=pltpu.VMEM), pl.BlockSpec(memory_space=pl.ANY)
     row = (per, loc)
+    grads_shape = (n_ctx, per * RANK, sum(sizes))
     outputs = [
-        (row + (wide,), BF16, anywhere),
-        (row + (units,), BF16, anywhere),
         (row + (width,), BF16, anywhere),
-        (row + (wide,), BF16, anywhere),
-        (row + (units,), BF16, anywhere),
         (row + (width,), F32, anywhere),
         (row + (wide,), BF16, anywhere),
         ((per, n_fsdp) + cot.shape[1:], BF16, anywhere),
-        (row + (NR,), BF16, vmem),
-        (row + (NR,), BF16, vmem),
+        ((n_ctx, n_fsdp) + grads_shape[1:], BF16, anywhere),
         (row + (NR,), BF16, vmem),
         (row + (width_here,), BF16, vmem),
     ]
     n_copy = 2 * per * n_swap
+    n_deal = per * (n_fsdp - 1) + (n_fsdp - 1) * n_ctx + 2 * (n_ctx - 1)
     return pl.pallas_call(
         kernel,
-        in_specs=[vmem] * 8 + [anywhere] * 7,
+        in_specs=[vmem] * 10 + [anywhere] * 7,
         out_specs=[space for _, _, space in outputs],
         out_shape=[jax.ShapeDtypeStruct(shape, dtype) for shape, dtype, _ in outputs],
         scratch_shapes=[
             pltpu.SemaphoreType.DMA((n_copy,)),
             pltpu.SemaphoreType.DMA((n_copy,)),
-            pltpu.SemaphoreType.DMA((per * (n_fsdp - 1),)),
-            pltpu.SemaphoreType.DMA((per * (n_fsdp - 1),)),
+            pltpu.SemaphoreType.DMA((n_deal,)),
+            pltpu.SemaphoreType.DMA((n_deal,)),
             pltpu.SemaphoreType.DMA((8,)),
-            pltpu.SemaphoreType.DMA(((11 + n_fsdp) * per,)),
-            pltpu.VMEM((2, wide, tile), BF16),
+            pltpu.SemaphoreType.DMA(((7 + n_fsdp) * per + 1,)),
             pltpu.VMEM((2, units, tile), BF16),
             pltpu.VMEM((2, tile, wide), BF16),
             pltpu.VMEM((2, tile, units), BF16),
@@ -1004,51 +1116,65 @@
             pltpu.VMEM(row + (wide,), BF16),
             pltpu.VMEM((2,) + row + (wide,), BF16),
             pltpu.VMEM(row + (width,), F32),
-            pltpu.VMEM(row + (128,), F32),
             pltpu.VMEM(row + (width,), F32),
             pltpu.VMEM(row + (units,), BF16),
-            pltpu.VMEM((loc, units), BF16),
-            pltpu.VMEM((loc, wide), BF16),
+            pltpu.VMEM(row + (units,), BF16),
+            pltpu.VMEM(row + (wide,), BF16),
             pltpu.VMEM((wide, loc), BF16),
             pltpu.VMEM((units, loc), BF16),
+            pltpu.VMEM(row + (NR,), BF16),
+            pltpu.VMEM(grads_shape, BF16),
+            pltpu.VMEM((n_ctx - 1,) + grads_shape[1:], BF16),
         ],
         compiler_params=pltpu.CompilerParams(
             collective_id=3, has_side_effects=True, vmem_limit_bytes=62 << 20
         ),
     )(
-        picked, gain, shift_by, a_up, b_out, b_down, a_down, b_up,
-        x_all, part_out, other_out, cot, out_x, up_x, down_x,
+        picked, gain, shift_by, rstds, adapt_up, a_up, b_out, b_down, a_down, b_up,
+        hats, gelus, slopes, cot, out_x, up_x, down_x,
     )
 
 
 def combine(pieces, chosen, shapes):
-    n_part, n_fsdp = pieces.shape[:2]
-    flat = []
+    n_part, n_fsdp, rows, columns = pieces.shape
+    flat, specs = [], []
     for i, shape in enumerate(shapes):
-        for lead in range(shape[0] if len(shape) == 3 else 1):
-            flat.append((i, lead if len(shape) == 3 else None, shape[-2:]))
+        high, wide = shape[-2:]
+        tall = wide == NR and high != NR
+        size = (high if tall else wide) // n_part
+        block = (size, NR) if tall else (NR, size)
+        lead = shape[0] if len(shape) == 3 else None
+        for j in range(lead or 1):
+            flat.append((i, None if lead is None else j, tall, size))
+        if lead is None:
+            specs.append(pl.BlockSpec(block, (lambda c: (c, 0)) if tall else (lambda c: (0, c))))
+        else:
+            specs.append(
+                pl.BlockSpec(
+                    (lead,) + block, (lambda c: (0, c, 0)) if tall else (lambda c: (0, 0, c))
+                )
+            )
 
     def kernel(chosen_ref, piece_ref, *outs):
-        for part in range(n_part):
-            ordered = jnp.concatenate([piece_ref[part, a] for a in range(n_fsdp)], axis=0)
-            start = 0
-            for i, lead, (high, wide) in flat:
-                out_ref = outs[i] if lead is None else outs[i].at[lead]
-                tall = wide == NR and high != NR
-                size = (high if tall else wide) // n_part
-                block = ordered[:, start : start + size]
-                at = slice(part * size, (part + 1) * size)
-                if tall:
-                    out_ref[at, :] = dot_tn(block, chosen_ref[...])
-                else:
-                    out_ref[:, at] = dot_tn(chosen_ref[...], block)
-                start += size
-
-    vmem = pl.BlockSpec(memory_space=pltpu.VMEM)
+        ordered = jnp.concatenate([piece_ref[0, a] for a in range(n_fsdp)], axis=0)
+        start = 0
+        for i, lead, tall, size in flat:
+            block = ordered[:, start : start + size]
+            value = dot_tn(block, chosen_ref[...]) if tall else dot_tn(chosen_ref[...], block)
+            if lead is None:
+                outs[i][...] = value
+            else:
+                outs[i][lead] = value
+            start += size
+
     return pl.pallas_call(
         kernel,
-        in_specs=[vmem, vmem],
-        out_specs=[vmem] * len(shapes),
+        grid=(n_part,),
+        in_specs=[
+            pl.BlockSpec(chosen.shape, lambda c: (0, 0)),
+            pl.BlockSpec((1, n_fsdp, rows, columns), lambda c: (c, 0, 0, 0)),
+        ],
+        out_specs=specs,
         out_shape=[jax.ShapeDtypeStruct(shape, F32) for shape in shapes],
         compiler_params=pltpu.CompilerParams(vmem_limit_bytes=48 << 20),
     )(chosen, pieces)
@@ -1104,51 +1230,16 @@
                 device_id_type=pl.DeviceIdType.MESH,
             )
 
-        def compact(out_ref, n, entries, sizes):
-            column = lax.broadcasted_iota(jnp.int32, (NR, RANK), 0)
-            rank = lax.broadcasted_iota(jnp.int32, (NR, RANK), 1)
-            used_columns = jnp.where(lax.rem(column, RANK) == rank, 1.0, 0.0).astype(BF16)
-            start = 0
-            for (code, value), size in zip(entries, sizes):
-                short = dot(code(), used_columns).astype(BF16)
-                block = dot_tn(short, value()).astype(BF16)
-                for k in range(n_ctx):
-                    out_ref[k, n * RANK : (n + 1) * RANK, start : start + size] = block[
-                        :, k * size : (k + 1) * size
-                    ]
-                start += size
-
-        class Fold:
-            def __init__(self, parts, came):
-                self.parts, self.came, self.flying = parts, came, {}
-
-            def at(self, k):
-                return flip(ct, mover.offsets[k])
-
-            def hand(self, level):
-                half = 2**level
-                self.flying[level] = [
-                    mover.go(
-                        self.parts.at[self.at(half + i)],
-                        self.came.at[half - 1 + i],
-                        {"ctx": flip(ct, masks[level])},
-                    )
-                    for i in range(half)
-                ]
-
-            def take(self, level):
-                for i, copy in enumerate(self.flying[level]):
-                    copy.wait_recv()
-                    total = self.parts[self.at(i)].astype(F32) + self.came[2**level - 1 + i].astype(F32)
-                    self.parts[self.at(i)] = total.astype(BF16)
-
         lasting = len(masks) - 1
         load_foot = move(w_ref.at[pl.ds(width, foot)], foot_room)
         ring.prefetch()
         loads = [move(ref, room) for ref, room in zip(early_refs, staged)]
         load_dy1 = move(dy1_ref, dy1_room)
         mover.greet(tp=True)
-        folds = [Fold(early_part, early_came), Fold(late_part, late_came)]
+        folds = [
+            Fold(mover, early_part, early_came, early_out),
+            Fold(mover, late_part, late_came, late_out),
+        ]
         for g in range(per):
             turned[0:width_here, :] = dq_ref[g].T
             turned[width_here : 2 * width_here, :] = dkv_ref[0, g].T
@@ -1189,54 +1280,15 @@
                     compact(early_part, n, entries, early_sizes)
                 folds[0].hand(lasting)
         for level in range(lasting, -1, -1):
-            folds[0].take(level)
-            if level:
-                folds[0].hand(level - 1)
-
-        def gather(parts, out_ref):
-            own = parts.at[ct]
-            kept.append(move(own, out_ref.at[ct, z]))
-            item = Weight(lambda c: parts.at[c], lambda o, c: out_ref.at[c, o], own)
-            mover.begin(item)
-            return item
-
+            folds[0].next(level)
         kept = []
-        first = gather(early_part, early_out)
-        load_dy1.wait()
-        dealt = []
-
-        def finish_rows(g):
-            for t in range(n_swap):
-                copy = swap_copy(g, t, tile if t < n_wide else foot)
-                copy.wait_recv()
-                copy.wait_send()
+        source, target, first = folds[0].gather()
+        kept.append(move(source, target))
+        for g in range(per):
+            swap_copy(g, n_wide, foot).wait_recv()
             pick = jnp.concatenate([pick_ref[g]] * 3, axis=1)
-
-            def step(r, carry):
-                rows = ds(r * chunk, chunk)
-                total = part[g, rows, :].astype(F32) + got[g, rows, :].astype(F32)
-                code = (total[:, width:] * pick).astype(BF16)
-                codes_in[g, rows, :] = code
-                value = dy1_room[g, rows, :] + total[:, :width]
-                for j in range(3):
-                    value = value + dot_nt(code[:, j * NR : (j + 1) * NR], a_ref[j])
-                dx[g, rows, :] = value.astype(BF16)
-                return carry
-
-            lax.fori_loop(0, loc // chunk, step, 0)
-            kept.append(move(dx.at[g, pl.ds(0, piece)], in_ref.at[z * per + g]))
-            for s in range(1, n_fsdp):
-                to = lax.rem(z - s + n_fsdp, n_fsdp)
-                dealt.append(
-                    mover.go(
-                        dx.at[g, pl.ds(s * piece, piece)], in_ref.at[z * per + g], {"fsdp": to}
-                    )
-                )
-
-        for g in range(per):
-            finish_rows(g)
-            if g == 0:
-                mover.relay(first)
+            total = part[g, :, width:].astype(F32) + got[g, :, width:].astype(F32)
+            codes_in[g] = (total * pick).astype(BF16)
         for n in range(per):
             entries = []
             for j in range(3):
@@ -1248,16 +1300,47 @@
                 )
             compact(late_part, n, entries, late_sizes)
         folds[1].hand(lasting)
-        for level in range(lasting, -1, -1):
-            folds[1].take(level)
-            if level:
-                folds[1].hand(level - 1)
-        second = gather(late_part, late_out)
-        for level in range(len(masks)):
-            mover.finish(first, level)
-        mover.relay(second)
-        for level in range(len(masks)):
-            mover.finish(second, level)
+        mover.relay(first)
+        load_dy1.wait()
+        dealt = []
+
+        def finish_rows(g):
+            for t in range(n_swap):
+                copy = swap_copy(g, t, tile if t < n_wide else foot)
+                if t < n_wide:
+                    copy.wait_recv()
+                copy.wait_send()
+
+            def step(r, carry):
+                rows = ds(r * chunk, chunk)
+                code = codes_in[g, rows, :]
+                total = part[g, rows, :width].astype(F32) + got[g, rows, :width].astype(F32)
+                value = dy1_room[g, rows, :] + total
+                for j in range(3):
+                    value = value + dot_nt(code[:, j * NR : (j + 1) * NR], a_ref[j])
+                dx[g, rows, :] = value.astype(BF16)
+                return carry
+
+            lax.fori_loop(0, loc // chunk, step, 0)
+            kept.append(move(dx.at[g, pl.ds(0, piece)], in_ref.at[z * per + g]))
+            for s in range(1, n_fsdp):
+                to = lax.rem(z - s + n_fsdp, n_fsdp)
+                dealt.append(
+                    mover.go(
+                        dx.at[g, pl.ds(s * piece, piece)], in_ref.at[z * per + g], {"fsdp": to}
+                    )
+                )
+
+        for g in range(per):
+            finish_rows(g)
+            if g == 0:
+                for level in range(lasting, -1, -1):
+                    folds[1].next(level)
+                source, target, second = folds[1].gather()
+                kept.append(move(source, target))
+                mover.relay(second)
+                mover.complete(first)
+        mover.complete(second)
         for copy in dealt:
             copy.wait_recv()
         for copy in kept:
@@ -1396,26 +1479,17 @@
     picked = picked[:, None, :]
     x_rows = x_all.reshape(per, loc, width)
     moved = forward_and_gather(
-        x_rows, qkv_x, a_qkv, picked, bias_all, (w_out, w_up, w_down), (a_out, b_up, a_down), n_fsdp, n_ctx
+        x_rows, qkv_x, a_qkv, picked, bias_all, ln_gain, ln_bias, (a_up, b_out), (w_out, w_up, w_down),
+        (a_out, b_up, a_down), n_fsdp, n_ctx,
     )
     slots = moved[: n_ctx - 1]
-    (query, kv_own, adapt_all, out_x, up_x, down_x, context, log_total, part_out, other_out) = moved[
-        n_ctx - 1 :
-    ]
     (
-        wide_h, gelu_out, acts, wide_d, d_pre, dy1, wide_a, _, adapt_out, adapt_down, dadapt_up, d_context,
-    ) = middle(
-        x_rows,
-        part_out,
-        other_out,
-        cotangent,
-        picked,
-        ln_gain,
-        ln_bias,
-        (out_x, up_x, down_x),
-        (a_up, b_out, b_down, a_down, b_up),
-        n_fsdp,
-        n_ctx,
+        query, kv_own, adapt_all, out_x, up_x, down_x, context, log_total, wide_h, gelus, slopes, hats, rstds,
+        adapt_out, adapt_up,
+    ) = moved[n_ctx - 1 :]
+    acts, dy1, wide_a, _, grads, dadapt_up, d_context = middle(
+        hats, rstds, gelus, slopes, adapt_up, cotangent, picked, ln_gain, ln_bias, (out_x, up_x, down_x),
+        (a_up, b_out, b_down, a_down, b_up), n_fsdp, n_ctx,
     )
     d_query, d_pair, activations = attend_back(
         query,
@@ -1428,19 +1502,12 @@
         n_fsdp,
         n_ctx,
     )
-    code, row, unit = (0, NR), (0, width), (0, units)
-    tail = (width, NR)
+    early_in = (dadapt_up, wide_h, adapt_out, wide_a, context)
     early_pairs = [
-        ((0,) + code, (1,) + row),
-        ((1,) + tail, (2,) + unit),
-        ((3,) + tail, (4,) + unit),
-        ((5,) + code, (3,) + row),
-        ((6,) + code, (7,) + row),
-        ((7,) + tail, (8, 0, heads_width)),
+        ((0, 0, NR), (1, 0, width)),
+        ((2, 0, NR), (3, 0, width)),
+        ((3, width, NR), (4, 0, heads_width)),
     ]
-    early_in = (
-        adapt_down, wide_d, gelu_out, wide_h, d_pre, dadapt_up, adapt_out, wide_a, context,
-    )
     input_grad, early, late = last(
         d_query,
         d_pair,
@@ -1457,16 +1524,17 @@
     )
     codes = (adapter_ids[:, None] * RANK + jnp.arange(RANK)[None, :]).reshape(-1)
     chosen = (codes[:, None] == jnp.arange(NR)[None, :]).astype(BF16)
-    e = combine(
-        early,
-        chosen,
-        [
-            (NR, width), (units, NR), (NR, units), (width, NR), (NR, width), (heads_width, NR),
-            (3, NR, heads_width),
-        ],
+    b_down_grad, a_down_grad, b_up_grad = combine(
+        grads, chosen, [(NR, width), (units, NR), (NR, units)]
+    )
+    a_up_grad, b_out_grad, a_out_grad, b_qkv_grad = combine(
+        early, chosen, [(width, NR), (NR, width), (heads_width, NR), (3, NR, heads_width)]
     )
     (a_qkv_grad,) = combine(late, chosen, [(3, width, NR)])
-    return activations, input_grad, a_qkv_grad, e[6], e[5], e[4], e[3], e[2], e[1], e[0]
+    return (
+        activations, input_grad, a_qkv_grad, b_qkv_grad, a_out_grad, b_out_grad, a_up_grad, b_up_grad,
+        a_down_grad, b_down_grad,
+    )
 
 
 def solution(mesh):

time: 637 us -> 625 us (0.981)
  Pallas kernels: 621 us -> 608 us
    pallas_call x1, Pallas kernels: 122 us -> 106 us  [last(): pl.pallas_call(kernel, in_specs=[vmem] * 6 + [anywhere] * (2 + n_early),...]
    pallas_call x4 -> x5, Pallas kernels: 340 us -> 341 us  [the longest x1 206 us: forward_and_gather(): pl.pallas_call(kernel, in_specs=[vmem] * 7 + [anywhere] * 8, out_specs=[s...]
where the time goes in v8:
time: 625 us; the launch traced here: 619 us
  Pallas kernels  608 us (97%)
  local copies, waits for them, and re-layouts  8.2 us (1%)
    pallas_call x1, Pallas kernels, forward_and_gather(): pl.pallas_call(kernel, in_specs=[vmem] * 7 + [anywhere] * 8, out_specs=[s...  206 us
    pallas_call x1, Pallas kernels, middle(): pl.pallas_call(kernel, in_specs=[vmem] * 10 + [anywhere] * 7, out_specs=[...  126 us
    pallas_call x1, Pallas kernels, last(): pl.pallas_call(kernel, in_specs=[vmem] * 6 + [anywhere] * (2 + n_early),...  106 us
    pallas_call x1, Pallas kernels, move(): pl.pallas_call(kernel, in_specs=spaces, out_specs=[pl.BlockSpec(memory_sp...  101 us
    pallas_call x1, Pallas kernels, attend_back(): pl.pallas_call(kernel, in_specs=[vmem] * 4 + [anywhere] * (1 + n_ctx), ou...  60 us

profile of v8, /device:TPU:0, one launch (start us, length us, event | category | flops | bytes accessed | tf_op | source)
XLA Modules:
  0.0 618.9 jit_solution(4757268792905973519)
XLA Ops:
  0.6 0.7 dynamic_slice.6
  1.4 0.7 fusion.2
  2.0 0.1 add_multiply_fusion
  2.1 0.1 iota_add_fusion
  2.2 0.1 add.82
  2.3 0.1 compare_select_fusion
  2.4 1.3 broadcast_in_dim.12.refs_0_.refs_1_
  3.7 0.7 dynamic_slice.7
  4.4 0.6 compare_convert_fusion.refs_2_.refs_0_.refs_5_
  5.0 101.4 %shard_map.258 = (bf16[2,4,64,2048]{3,2,1,0:T(8,128)(2,1)}, bf16[2432,3072]{1,0:T(8,128)(2,1)}) custom-call(bf16[8,64,2048]{2,1,0:T(8,128)(2,1)} %refs_0_.1, bf16[3,512,1024]{2,1,0:T(8,128)(2,1)} %refs_1_.3, bf16[3,128,1024]{2,1,0:T(8,128)(2,1)} %refs_2_.2), custom_call_target="tpu_custom_call" | custom-call | tf_op jit(solution)/shard_map/pallas_call | solution.py:316
  106.4 206.5 %shard_map.259 = (bf16[2,2,256,1024]{3,2,1,0:T(8,128)(2,1)}, bf16[2,2,256,1024]{3,2,1,0:T(8,128)(2,1)}, bf16[2,2,256,1024]{3,2,1,0:T(8,128)(2,1)}, bf16[2,256,10...) custom-call(f32[2,1024,128]{2,1,0:T(8,128)} %broadcast_in_dim.12.ref, ...), custom_call_target="tpu_custom_call" | custom-call | tf_op jit(solution)/shard_map/pallas_call | solution.py:610
  312.9 125.9 %shard_map.260 = (bf16[2,256,2048]{2,1,0:T(8,128)(2,1)}, f32[2,256,2048]{2,1,0:T(8,128)}, bf16[2,256,2176]{2,1,0:T(8,128)(2,1)}, bf16[2,4,64,2048]{3,2,1,0:T(8,1...) custom-call(f32[2,1,128]{2,1,0:T(1,128)} %compare_convert_fusion.refs_2_.ref, ...), custom_call_target="tpu_custom_call" | custom-call | tf_op jit(solution)/shard_map/pallas_call | solution.py:1100
  438.8 60.0 %shard_map.261 = (bf16[2,256,1024]{2,1,0:T(8,128)(2,1)}, bf16[2,2,256,1024]{3,2,1,0:T(8,128)(2,1)}, bf16[8,64,2048]{2,1,0:T(8,128)(2,1)}) custom-call(bf16[2,256,1024]{2,1,0:T(8,128)(2,1)} %get-tuple-element.51.refs_0_, f32[2,1024,128]{2,1,0:T(8,128)} %broadcast_in_dim.12.refs_0_.refs_1_, bf16[2,256,1024]{2,1,0:T(8,128)(2,1)} %get-tuple-element.60.refs_2_, ...), custom_call_target="tpu_custom_call" | custom-call | tf_op jit(solution)/shard_map/pallas_call | solution.py:757
  498.8 105.8 %shard_map.262 = (bf16[8,64,2048]{2,1,0:T(8,128)(2,1)}, bf16[4,4,32,2048]{3,2,1,0:T(8,128)(2,1)}, bf16[4,4,32,1536]{3,2,1,0:T(8,128)(2,1)}) custom-call(bf16[2,256,1024]{2,1,0:T(8,128)(2,1)} %get-tuple-element.68.refs_0_, bf16[2,2,256,1024]{3,2,1,0:T(8,128)(2,1)} %get-tuple-element.69.refs_1_, bf16[2,256,2048]{2,1,0:T(8,128)(2,1)} %bitcast.3, ...), custom_call_target="tpu_custom_call" | custom-call | tf_op jit(solution)/shard_map/pallas_call | solution.py:1365
  604.7 0.1 iota_add_fusion.1
  604.7 0.1 add.87
  604.8 0.1 fusion.chosen_ref
  604.9 1.6 copy-done.1
  606.5 2.8 shard_map.264
  609.3 2.7 shard_map.263
  612.0 3.1 shard_map.265
  615.1 1.3 copy.31
  616.4 1.0 copy-done.4
  617.4 1.3 copy.32
  (12 shorter events, 0.0 us)
Async XLA Ops:
  498.8 105.9 %copy-start.5 = (s32[8]{0:T(128)S(1)}, s32[8]{0:T(128)}, u32[]{:S(2)}) copy-start(s32[8]{0:T(128)} %param.22) | copy-start | bytes 100
  604.9 1.6 copy-start.1
  606.5 2.8 copy-start.2
  609.3 2.7 copy-start
  612.0 3.1 copy-start.3
  615.1 2.3 copy-start.4

commit v9 on v8

--- a/solution.py
+++ b/solution.py
@@ -637,147 +637,6 @@
     )(bias, a_qkv, picked, gain, shift_by, *first_maps, x_rows, qkv_x, w_out, w_up, w_down, *maps)
 
 
-def attend_back(query, kv_own, slots, bias, grad, log_total, acts, n_fsdp, n_ctx):
-    per, loc, width_here = query.shape
-    piece, width = acts.shape[2:]
-    heads = width_here // HEAD_DIM
-    cuts = 4
-    high = heads // cuts
-    columns = high * HEAD_DIM
-    masks = masks_of(n_ctx)
-    units = [(g, c) for g in range(per) for c in range(cuts)]
-    n_copy = per * (n_fsdp - 1) + len(units) * (n_ctx - 1)
-
-    def kernel(*refs):
-        q_ref, bias_ref, g_ref, log_ref, acts_ref, kv_ref = refs[:6]
-        slot_refs = refs[6 : 5 + n_ctx]
-        dq_ref, dkv_ref, out_ref = refs[5 + n_ctx : 8 + n_ctx]
-        send, recv, load, kv_room, own, came, act_room = refs[8 + n_ctx :]
-        mover = Mover(n_fsdp, n_ctx, send, recv)
-        z, ct = mover.z, mover.ct
-        loads = []
-        for g in range(per):
-            loads.append([])
-            for k in range(n_ctx):
-                source = kv_ref if k == 0 else slot_refs[k - 1]
-                copy = pltpu.make_async_copy(
-                    source.at[:, g], kv_room.at[g, k], load.at[g * n_ctx + k]
-                )
-                copy.start()
-                loads[g].append(copy)
-        kept = []
-        for g in range(per):
-            at = per * n_ctx + 2 * g
-            first = pltpu.make_async_copy(acts_ref.at[g, 0], act_room.at[g], load.at[at])
-            first.start()
-            second = pltpu.make_async_copy(
-                act_room.at[g], out_ref.at[z * per + g], load.at[at + 1]
-            )
-            kept.append((first, second))
-        mover.greet()
-        dealt = []
-        for g in range(per):
-            for s in range(1, n_fsdp):
-                to = lax.rem(z - s + n_fsdp, n_fsdp)
-                dealt.append(
-                    mover.go(acts_ref.at[g, s], out_ref.at[z * per + g], {"fsdp": to})
-                )
-        flying = {}
-
-        def compute(u):
-            g, c = units[u]
-            if c == 0:
-                for copy in loads[g]:
-                    copy.wait()
-
-            def one(h, carry):
-                at = ds(c * columns + h * HEAD_DIM, HEAD_DIM)
-                to = ds(h * HEAD_DIM, HEAD_DIM)
-                biases = []
-                for k in range(n_ctx):
-                    block = bias_ref[g, k * loc : (k + 1) * loc, :]
-                    biases.append(jnp.concatenate([block] * (loc // 128), axis=1))
-                dquery, dkeys, dvalues = attend_back_head(
-                    q_ref[g, :, at],
-                    g_ref[g, :, at],
-                    log_ref[g, c * high + h],
-                    [kv_room[g, k, 0, :, at] for k in range(n_ctx)],
-                    [kv_room[g, k, 1, :, at] for k in range(n_ctx)],
-                    biases,
-                )
-                dq_ref[g, :, at] = dquery
-                for k in range(n_ctx):
-                    own[u, k, 0, :, to] = dkeys[k]
-                    own[u, k, 1, :, to] = dvalues[k]
-                return carry
-
-            lax.fori_loop(0, high, one, 0)
-
-        def hand(u, level):
-            half = 2**level
-            device = {"ctx": flip(ct, masks[level])}
-            flying[u, level] = [
-                mover.go(own.at[u, half + i], came.at[u, half - 1 + i], device) for i in range(half)
-            ]
-
-        def take_in(u, level):
-            half = 2**level
-            for i, copy in enumerate(flying[u, level]):
-                copy.wait_recv()
-                for j in range(2):
-                    total = own[u, i, j].astype(F32) + came[u, half - 1 + i, j].astype(F32)
-                    if level:
-                        own[u, i, j] = total.astype(BF16)
-                    else:
-                        g, c = units[u]
-                        dkv_ref[j, g, :, c * columns : (c + 1) * columns] = total.astype(BF16)
-
-        last = len(masks) - 1
-        for t in range(len(units) + last + 1):
-            if t < len(units):
-                compute(t)
-                hand(t, last)
-            if t == 0:
-                for first, second in kept:
-                    first.wait()
-                    second.start()
-            for k in range(last + 1):
-                u, level = t - 1 - k, last - k
-                if 0 <= u < len(units):
-                    take_in(u, level)
-                    if level:
-                        hand(u, level - 1)
-        for _, second in kept:
-            second.wait()
-        for copy in dealt:
-            copy.wait_recv()
-        mover.close()
-
-    vmem, anywhere = pl.BlockSpec(memory_space=pltpu.VMEM), pl.BlockSpec(memory_space=pl.ANY)
-    return pl.pallas_call(
-        kernel,
-        in_specs=[vmem] * 4 + [anywhere] * (1 + n_ctx),
-        out_specs=[vmem, vmem, anywhere],
-        out_shape=[
-            jax.ShapeDtypeStruct(query.shape, BF16),
-            jax.ShapeDtypeStruct(kv_own.shape, BF16),
-            jax.ShapeDtypeStruct((per * n_fsdp, piece, width), BF16),
-        ],
-        scratch_shapes=[
-            pltpu.SemaphoreType.DMA((n_copy,)),
-            pltpu.SemaphoreType.DMA((n_copy,)),
-            pltpu.SemaphoreType.DMA((per * (n_ctx + 2),)),
-            pltpu.VMEM((per, n_ctx, 2, loc, width_here), BF16),
-            pltpu.VMEM((len(units), n_ctx, 2, loc, columns), BF16),
-            pltpu.VMEM((len(units), n_ctx - 1, 2, loc, columns), BF16),
-            pltpu.VMEM((per, piece, width), BF16),
-        ],
-        compiler_params=pltpu.CompilerParams(
-            collective_id=2, has_side_effects=True, vmem_limit_bytes=56 << 20
-        ),
-    )(query, bias, grad, log_total, acts, kv_own, *slots)
-
-
 class Ring:
     def __init__(self, room, sems, at, tile_at):
         self.room, self.sems, self.at, self.tile_at = room, sems, at, tile_at
@@ -884,6 +743,7 @@
 
 def middle(hats, rstds, gelus, slopes, adapt_up, cot, picked, gain, shift_by, weights, maps, n_fsdp, n_ctx):
     per, loc, width = hats.shape
+    piece = cot.shape[1]
     out_x, up_x, down_x = weights
     a_up, b_out, b_down, a_down, b_up = maps
     wide, units = up_x.shape
@@ -898,12 +758,12 @@
         pick_ref, gain_ref, shift_ref, rstd1, code_up_ref = refs[:5]
         a_up_ref, b_out_ref, b_down_ref, a_down_ref, b_up_ref = refs[5:10]
         hat_ref, gelu_ref, slope_ref, cot_ref, out_ref, up_ref, down_ref = refs[10:17]
-        acts_out, dy1_out, da_out, cot_rows, grads_out = refs[17:22]
-        dadapt_up_ref, ctx_ref = refs[22:24]
-        (send, recv, deal_send, deal_recv, ring_sem, sems) = refs[24:30]
-        (down_room, down_rows, up_rows) = refs[30:33]
-        (stage, part, got, hat1, keep32, slope, gelu, wide_v, turned, dpre_t) = refs[33:43]
-        codes_down, grads_part, grads_came = refs[43:]
+        acts_out, dy1_out, da_out, cot_rows, grads_out, back_out = refs[17:23]
+        dadapt_up_ref, ctx_ref = refs[23:25]
+        (send, recv, deal_send, deal_recv, ring_sem, sems) = refs[25:31]
+        (down_room, down_rows, up_rows) = refs[31:34]
+        (stage, part, got, hat1, keep32, slope, gelu, wide_v, turned, dpre_t) = refs[34:44]
+        codes_down, grads_part, grads_came = refs[44:]
         mover = Mover(n_fsdp, n_ctx, deal_send, deal_recv)
         partner = {"tp": 1 - lax.axis_index("tp")}
 
@@ -955,6 +815,7 @@
             return Deal(lambda to: cot_ref.at[to * per + g], lambda s: cot_rows.at[g, s])
 
         deals = [deal(g) for g in range(per)]
+        dealt = []
         for g in range(per):
             move(gelu_ref.at[g], gelu.at[g], ("gelu", g))
             if g == 0:
@@ -1010,6 +871,8 @@
 
             by_rows(second_norm)
             move(part.at[g, :, pl.ds(0, width)], acts_out.at[g], ("part", g))
+            own = part.at[g, pl.ds(0, piece), pl.ds(0, width)]
+            move(own, back_out.at[mover.z * per + g], ("part", g))
             turned[...] = wide_v[g].T
 
             def down_back(t, room, g=g):
@@ -1022,6 +885,10 @@
             down_r.run(units // tile, down_back)
             (down_r if g + 1 < per else out_r).prefetch()
             free(("part", g))
+            for s in range(1, n_fsdp):
+                to = lax.rem(mover.z - s + n_fsdp, n_fsdp)
+                rows_s = acts_out.at[g, pl.ds(s * piece, piece)]
+                dealt.append(mover.go(rows_s, back_out.at[mover.z * per + g], {"fsdp": to}))
 
             def up_back(t, room, g=g):
                 part[g, :, ds(t * tile, tile)] = dot(room[...], dpre_t[...]).T.astype(BF16)
@@ -1080,6 +947,8 @@
                 move(source, target, "grads")
                 mover.relay(item)
         mover.complete(item)
+        for copy in dealt:
+            copy.wait_recv()
         free(*list(busy))
         mover.close()
 
@@ -1092,11 +961,12 @@
         (row + (wide,), BF16, anywhere),
         ((per, n_fsdp) + cot.shape[1:], BF16, anywhere),
         ((n_ctx, n_fsdp) + grads_shape[1:], BF16, anywhere),
+        (cot.shape, BF16, anywhere),
         (row + (NR,), BF16, vmem),
         (row + (width_here,), BF16, vmem),
     ]
     n_copy = 2 * per * n_swap
-    n_deal = per * (n_fsdp - 1) + (n_fsdp - 1) * n_ctx + 2 * (n_ctx - 1)
+    n_deal = 2 * per * (n_fsdp - 1) + (n_fsdp - 1) * n_ctx + 2 * (n_ctx - 1)
     return pl.pallas_call(
         kernel,
         in_specs=[vmem] * 10 + [anywhere] * 7,
@@ -1108,7 +978,7 @@
             pltpu.SemaphoreType.DMA((n_deal,)),
             pltpu.SemaphoreType.DMA((n_deal,)),
             pltpu.SemaphoreType.DMA((8,)),
-            pltpu.SemaphoreType.DMA(((7 + n_fsdp) * per + 1,)),
+            pltpu.SemaphoreType.DMA(((8 + n_fsdp) * per + 1,)),
             pltpu.VMEM((2, units, tile), BF16),
             pltpu.VMEM((2, tile, wide), BF16),
             pltpu.VMEM((2, tile, units), BF16),
@@ -1180,37 +1050,47 @@
     )(chosen, pieces)
 
 
-def last(d_query, d_pair, x_all, adapt_all, dy1, qkv_x, a_qkv, picked, early, pairs, n_fsdp, n_ctx):
-    per, loc, width_here = d_query.shape
-    piece, width = loc // n_fsdp, x_all.shape[2]
+def finish(
+    query, kv_own, slots, bias, grad, log_total, x_rows, adapt_in, dy1, qkv_x, a_qkv, picked, early, pairs, n_fsdp, n_ctx
+):
+    per, loc, width_here = query.shape
+    piece, width = loc // n_fsdp, x_rows.shape[2]
+    heads = width_here // HEAD_DIM
+    cuts = 4
+    high = heads // cuts
+    columns = high * HEAD_DIM
+    masks = masks_of(n_ctx)
+    units = [(g, c) for g in range(per) for c in range(cuts)]
     depth = 3 * width_here
     foot = 3 * NR
     wide = width + foot
-    tile, chunk = 512, 32
+    tile = 512
     n_wide = width // tile
     n_swap = n_wide + 1
     n_early = len(early)
-    early_sizes = [values[2] // n_ctx for _, values in pairs] + [width_here // n_ctx] * 3
-    late_sizes = [width // n_ctx] * 3
-    gathers = 2
-    n_copy = per * (n_fsdp - 1) + gathers * ((n_fsdp - 1) * n_ctx + 2 * (n_ctx - 1))
+    early_sizes = [values[2] // n_ctx for _, values in pairs]
+    late_sizes = [width_here // n_ctx] * 3 + [width // n_ctx] * 3
+    n_copy = len(units) * (n_ctx - 1) + per * n_wide * (n_fsdp - 1)
+    n_copy += 2 * ((n_fsdp - 1) * n_ctx + 2 * (n_ctx - 1))
 
     def kernel(*refs):
-        dq_ref, dkv_ref, x_ref, adapt_ref, a_ref, pick_ref = refs[:6]
-        dy1_ref, w_ref = refs[6:8]
-        early_refs = refs[8 : 8 + n_early]
-        in_ref, early_out, late_out = refs[8 + n_early : 11 + n_early]
-        send, recv, swap_send, swap_recv, ring_sem, sems = refs[11 + n_early : 17 + n_early]
-        rows_room, foot_room, dy1_room, turned, part, got, codes_in, dx = refs[
-            17 + n_early : 25 + n_early
-        ]
-        early_part, early_came, late_part, late_came = refs[25 + n_early : 29 + n_early]
-        staged = refs[29 + n_early :]
+        q_ref, bias_ref, g_ref, log_ref, x_ref, adapt_ref, a_ref, pick_ref = refs[:8]
+        dy1_ref, w_ref, kv_ref = refs[8:11]
+        slot_refs = refs[11 : 10 + n_ctx]
+        early_refs = refs[10 + n_ctx : 10 + n_ctx + n_early]
+        at = 10 + n_ctx + n_early
+        in_ref, early_out, late_out = refs[at : at + 3]
+        send, recv, swap_send, swap_recv, ring_sem, load, sems = refs[at + 3 : at + 10]
+        kv_room, own, came, dq, dkv = refs[at + 10 : at + 15]
+        tiles, foot_room, dy1_room, turned, part, got, codes_in, dx = refs[at + 15 : at + 23]
+        early_part, early_came, late_part, late_came = refs[at + 23 : at + 27]
+        staged = refs[at + 27 :]
         mover = Mover(n_fsdp, n_ctx, send, recv)
-        z, ct, masks = mover.z, mover.ct, mover.masks
+        z, ct = mover.z, mover.ct
         partner = {"tp": 1 - lax.axis_index("tp")}
-        ring = Ring(rows_room, ring_sem, 0, lambda t: w_ref.at[ds(t * tile, tile)])
+        ring = Ring(tiles, ring_sem, 0, lambda t: w_ref.at[ds(t * tile, tile)])
         used = [0]
+        kept, dealt, flying = [], [], {}
 
         def move(source, target):
             copy = pltpu.make_async_copy(source, target, sems.at[used[0]])
@@ -1218,8 +1098,74 @@
             copy.start()
             return copy
 
-        def swap_copy(g, t, size):
-            at = ds(t * tile, tile) if size == tile else pl.ds(width, size)
+        loads = []
+        for g in range(per):
+            loads.append([])
+            for k in range(n_ctx):
+                source = kv_ref if k == 0 else slot_refs[k - 1]
+                copy = pltpu.make_async_copy(
+                    source.at[:, g], kv_room.at[g, k], load.at[g * n_ctx + k]
+                )
+                copy.start()
+                loads[g].append(copy)
+        staging = [move(ref, room) for ref, room in zip(early_refs, staged)]
+        load_foot = move(w_ref.at[pl.ds(width, foot)], foot_room)
+        ring.prefetch()
+        load_dy1 = move(dy1_ref, dy1_room)
+        mover.greet(tp=True)
+
+        def compute(u):
+            g, c = units[u]
+            if c == 0:
+                for copy in loads[g]:
+                    copy.wait()
+
+            def one(h, carry):
+                at = ds(c * columns + h * HEAD_DIM, HEAD_DIM)
+                to = ds(h * HEAD_DIM, HEAD_DIM)
+                biases = []
+                for k in range(n_ctx):
+                    block = bias_ref[g, k * loc : (k + 1) * loc, :]
+                    biases.append(jnp.concatenate([block] * (loc // 128), axis=1))
+                dquery, dkeys, dvalues = attend_back_head(
+                    q_ref[g, :, at],
+                    g_ref[g, :, at],
+                    log_ref[g, c * high + h],
+                    [kv_room[g, k, 0, :, at] for k in range(n_ctx)],
+                    [kv_room[g, k, 1, :, at] for k in range(n_ctx)],
+                    biases,
+                )
+                dq[g, :, at] = dquery
+                for k in range(n_ctx):
+                    own[u, k, 0, :, to] = dkeys[k]
+                    own[u, k, 1, :, to] = dvalues[k]
+                return carry
+
+            lax.fori_loop(0, high, one, 0)
+
+        def hand(u, level):
+            half = 2**level
+            device = {"ctx": flip(ct, masks[level])}
+            flying[u, level] = [
+                mover.go(own.at[u, half + i], came.at[u, half - 1 + i], device) for i in range(half)
+            ]
+
+        def take_in(u, level):
+            half = 2**level
+            g, c = units[u]
+            for i, copy in enumerate(flying[u, level]):
+                copy.wait_recv()
+                for j in range(2):
+                    total = own[u, i, j].astype(F32) + came[u, half - 1 + i, j].astype(F32)
+                    if level:
+                        own[u, i, j] = total.astype(BF16)
+                    else:
+                        dkv[j, g, :, c * columns : (c + 1) * columns] = total.astype(BF16)
+            if level:
+                hand(u, level - 1)
+
+        def swap_copy(g, t):
+            at = pl.ds(width, foot) if isinstance(t, int) and t == n_wide else ds(t * tile, tile)
             sem = g * n_swap + t
             return pltpu.make_async_remote_copy(
                 src_ref=part.at[g, :, at],
@@ -1230,117 +1176,123 @@
                 device_id_type=pl.DeviceIdType.MESH,
             )
 
-        lasting = len(masks) - 1
-        load_foot = move(w_ref.at[pl.ds(width, foot)], foot_room)
-        ring.prefetch()
-        loads = [move(ref, room) for ref, room in zip(early_refs, staged)]
-        load_dy1 = move(dy1_ref, dy1_room)
-        mover.greet(tp=True)
-        folds = [
-            Fold(mover, early_part, early_came, early_out),
-            Fold(mover, late_part, late_came, late_out),
-        ]
-        for g in range(per):
-            turned[0:width_here, :] = dq_ref[g].T
-            turned[width_here : 2 * width_here, :] = dkv_ref[0, g].T
-            turned[2 * width_here :, :] = dkv_ref[1, g].T
+        def project_back(g):
+            turned[0:width_here, :] = dq[g].T
+            turned[width_here : 2 * width_here, :] = dkv[0, g].T
+            turned[2 * width_here :, :] = dkv[1, g].T
             if g == 0:
                 load_foot.wait()
             part[g, :, width:] = dot(foot_room[...], turned[...]).T.astype(BF16)
-            swap_copy(g, n_wide, foot).start()
-
-            def back(t, room, g=g):
+            swap_copy(g, n_wide).start()
+
+            def back(t, room):
                 part[g, :, ds(t * tile, tile)] = dot(room[...], turned[...]).T.astype(BF16)
-                swap_copy(g, t, tile).start()
+                swap_copy(g, t).start()
 
             ring.run(n_wide, back)
             if g + 1 < per:
                 ring.prefetch()
-            if g == 0:
-                for copy in loads:
-                    copy.wait()
-                for n in range(per):
-                    entries = []
-                    for (i, first, size), (j, start, count) in pairs:
-                        entries.append(
-                            (
-                                lambda n=n, i=i, f=first, c=size: staged[i][n, :, f : f + c],
-                                lambda n=n, i=j, f=start, c=count: staged[i][n, :, f : f + c],
-                            )
-                        )
-                    values = [
-                        lambda n=n: dq_ref[n],
-                        lambda n=n: dkv_ref[0, n],
-                        lambda n=n: dkv_ref[1, n],
-                    ]
-                    for j in range(3):
-                        entries.append(
-                            (lambda n=n, j=j: adapt_ref[n, :, j * NR : (j + 1) * NR], values[j])
-                        )
-                    compact(early_part, n, entries, early_sizes)
-                folds[0].hand(lasting)
-        for level in range(lasting, -1, -1):
-            folds[0].next(level)
-        kept = []
-        source, target, first = folds[0].gather()
-        kept.append(move(source, target))
-        for g in range(per):
-            swap_copy(g, n_wide, foot).wait_recv()
+
+        def take_codes(g):
+            swap_copy(g, n_wide).wait_recv()
             pick = jnp.concatenate([pick_ref[g]] * 3, axis=1)
             total = part[g, :, width:].astype(F32) + got[g, :, width:].astype(F32)
             codes_in[g] = (total * pick).astype(BF16)
-        for n in range(per):
-            entries = []
+
+        def finish_tile(g, t):
+            swap_copy(g, t).wait_recv()
+            at = slice(t * tile, (t + 1) * tile)
+            value = part[g, :, at].astype(F32) + got[g, :, at].astype(F32) + dy1_room[g, :, at]
             for j in range(3):
-                entries.append(
-                    (
-                        lambda n=n, j=j: codes_in[n, :, j * NR : (j + 1) * NR],
-                        lambda n=n: x_ref[n],
-                    )
-                )
-            compact(late_part, n, entries, late_sizes)
-        folds[1].hand(lasting)
-        mover.relay(first)
-        load_dy1.wait()
-        dealt = []
-
-        def finish_rows(g):
-            for t in range(n_swap):
-                copy = swap_copy(g, t, tile if t < n_wide else foot)
-                if t < n_wide:
-                    copy.wait_recv()
-                copy.wait_send()
-
-            def step(r, carry):
-                rows = ds(r * chunk, chunk)
-                code = codes_in[g, rows, :]
-                total = part[g, rows, :width].astype(F32) + got[g, rows, :width].astype(F32)
-                value = dy1_room[g, rows, :] + total
-                for j in range(3):
-                    value = value + dot_nt(code[:, j * NR : (j + 1) * NR], a_ref[j])
-                dx[g, rows, :] = value.astype(BF16)
-                return carry
-
-            lax.fori_loop(0, loc // chunk, step, 0)
-            kept.append(move(dx.at[g, pl.ds(0, piece)], in_ref.at[z * per + g]))
+                value = value + dot_nt(codes_in[g, :, j * NR : (j + 1) * NR], a_ref[j, at, :])
+            dx[g, :, at] = value.astype(BF16)
+            to_at = pl.ds(t * tile, tile)
+            kept.append(move(dx.at[g, pl.ds(0, piece), to_at], in_ref.at[z * per + g, :, to_at]))
             for s in range(1, n_fsdp):
                 to = lax.rem(z - s + n_fsdp, n_fsdp)
                 dealt.append(
                     mover.go(
-                        dx.at[g, pl.ds(s * piece, piece)], in_ref.at[z * per + g], {"fsdp": to}
+                        dx.at[g, pl.ds(s * piece, piece), to_at],
+                        in_ref.at[z * per + g, :, to_at],
+                        {"fsdp": to},
                     )
                 )
 
+        last = len(masks) - 1
+        for t in range(len(units) + last):
+            if t < len(units):
+                compute(t)
+                hand(t, last)
+            for k in range(last):
+                if 0 <= t - 1 - k < len(units):
+                    take_in(t - 1 - k, last - k)
+        for copy in staging:
+            copy.wait()
+        for n in range(per):
+            entries = []
+            for (i, first, size), (j, start, count) in pairs:
+                entries.append(
+                    (
+                        lambda n=n, i=i, f=first, c=size: staged[i][n, :, f : f + c],
+                        lambda n=n, i=j, f=start, c=count: staged[i][n, :, f : f + c],
+                    )
+                )
+            compact(early_part, n, entries, early_sizes)
+        early_fold = Fold(mover, early_part, early_came, early_out)
+        late_fold = Fold(mover, late_part, late_came, late_out)
+        early_fold.hand(last)
+        done = set()
         for g in range(per):
-            finish_rows(g)
+            for u, (owner, _) in enumerate(units):
+                if owner == g:
+                    take_in(u, 0)
+            project_back(g)
+            take_codes(g)
             if g == 0:
-                for level in range(lasting, -1, -1):
-                    folds[1].next(level)
-                source, target, second = folds[1].gather()
+                for level in range(last, -1, -1):
+                    early_fold.next(level)
+                source, target, first = early_fold.gather()
                 kept.append(move(source, target))
+                load_dy1.wait()
+            if g + 1 < per:
+                for t in range(n_wide // 2):
+                    finish_tile(g, t)
+                    done.add((g, t))
+            if g == 0:
+                mover.relay(first)
+        for n in range(per):
+            values = [
+                lambda n=n: dq[n],
+                lambda n=n: dkv[0, n],
+                lambda n=n: dkv[1, n],
+            ]
+            entries = [
+                (lambda n=n, j=j: adapt_ref[n, :, j * NR : (j + 1) * NR], values[j]) for j in range(3)
+            ]
+            entries += [
+                (lambda n=n, j=j: codes_in[n, :, j * NR : (j + 1) * NR], lambda n=n: x_ref[n])
+                for j in range(3)
+            ]
+            compact(late_part, n, entries, late_sizes)
+        late_fold.hand(last)
+        rest = [(g, t) for g in range(per) for t in range(n_wide) if (g, t) not in done]
+        cut = len(rest) - 2
+        for i, (g, t) in enumerate(rest):
+            finish_tile(g, t)
+            if i == cut - 2:
+                for level in range(last, 0, -1):
+                    late_fold.next(level)
+            if i == cut - 1:
+                late_fold.next(0)
+                source, target, second = late_fold.gather()
+                kept.append(move(source, target))
+                mover.complete(first)
+            if i == cut:
                 mover.relay(second)
-                mover.complete(first)
         mover.complete(second)
+        for g in range(per):
+            for t in range(n_swap):
+                swap_copy(g, t).wait_send()
         for copy in dealt:
             copy.wait_recv()
         for copy in kept:
@@ -1349,22 +1301,28 @@
 
     vmem, anywhere = pl.BlockSpec(memory_space=pltpu.VMEM), pl.BlockSpec(memory_space=pl.ANY)
     parts = [(n_ctx, per * RANK, sum(early_sizes)), (n_ctx, per * RANK, sum(late_sizes))]
+    row = (per, loc)
     rooms = [
+        ((per, n_ctx, 2, loc, width_here), BF16),
+        ((len(units), n_ctx, 2, loc, columns), BF16),
+        ((len(units), n_ctx - 1, 2, loc, columns), BF16),
+        (row + (width_here,), BF16),
+        ((2,) + row + (width_here,), BF16),
         ((2, tile, depth), BF16),
         ((foot, depth), BF16),
         (dy1.shape, F32),
         ((depth, loc), BF16),
-        ((per, loc, wide), BF16),
-        ((per, loc, wide), BF16),
-        ((per, loc, foot), BF16),
-        ((per, loc, width), BF16),
+        (row + (wide,), BF16),
+        (row + (wide,), BF16),
+        (row + (foot,), BF16),
+        (row + (width,), BF16),
     ]
     for shape in parts:
         rooms += [(shape, BF16), ((n_ctx - 1,) + shape[1:], BF16)]
     rooms += [(x.shape, BF16) for x in early]
     return pl.pallas_call(
         kernel,
-        in_specs=[vmem] * 6 + [anywhere] * (2 + n_early),
+        in_specs=[vmem] * 8 + [anywhere] * (2 + n_ctx + n_early),
         out_specs=[anywhere] * 3,
         out_shape=[jax.ShapeDtypeStruct((per * n_fsdp, piece, width), BF16)]
         + [jax.ShapeDtypeStruct((n_ctx, n_fsdp) + shape[1:], BF16) for shape in parts],
@@ -1374,13 +1332,16 @@
             pltpu.SemaphoreType.DMA((per * n_swap,)),
             pltpu.SemaphoreType.DMA((per * n_swap,)),
             pltpu.SemaphoreType.DMA((2,)),
-            pltpu.SemaphoreType.DMA((4 + n_early + per,)),
+            pltpu.SemaphoreType.DMA((per * n_ctx,)),
+            pltpu.SemaphoreType.DMA((4 + n_early + per * n_wide,)),
         ]
         + [pltpu.VMEM(shape, dtype) for shape, dtype in rooms],
         compiler_params=pltpu.CompilerParams(
-            collective_id=4, has_side_effects=True, vmem_limit_bytes=60 << 20
+            collective_id=4, has_side_effects=True, vmem_limit_bytes=63 << 20
         ),
-    )(d_query, d_pair, x_all, adapt_all, a_qkv, picked, dy1, qkv_x, *early)
+    )(
+        query, bias, grad, log_total, x_rows, adapt_in, a_qkv, picked, dy1, qkv_x, kv_own, *slots, *early,
+    )
 
 
 def gelu_both(pre):
@@ -1487,20 +1448,9 @@
         query, kv_own, adapt_all, out_x, up_x, down_x, context, log_total, wide_h, gelus, slopes, hats, rstds,
         adapt_out, adapt_up,
     ) = moved[n_ctx - 1 :]
-    acts, dy1, wide_a, _, grads, dadapt_up, d_context = middle(
+    _, dy1, wide_a, _, grads, activations, dadapt_up, d_context = middle(
         hats, rstds, gelus, slopes, adapt_up, cotangent, picked, ln_gain, ln_bias, (out_x, up_x, down_x),
         (a_up, b_out, b_down, a_down, b_up), n_fsdp, n_ctx,
-    )
-    d_query, d_pair, activations = attend_back(
-        query,
-        kv_own,
-        slots,
-        bias_all,
-        d_context,
-        log_total,
-        acts.reshape(per, n_fsdp, piece, width),
-        n_fsdp,
-        n_ctx,
     )
     early_in = (dadapt_up, wide_h, adapt_out, wide_a, context)
     early_pairs = [
@@ -1508,29 +1458,20 @@
         ((2, 0, NR), (3, 0, width)),
         ((3, width, NR), (4, 0, heads_width)),
     ]
-    input_grad, early, late = last(
-        d_query,
-        d_pair,
-        x_rows,
-        adapt_all,
-        dy1,
-        qkv_x,
-        a_qkv,
-        picked,
-        early_in,
-        early_pairs,
-        n_fsdp,
-        n_ctx,
+    input_grad, early, late = finish(
+        query, kv_own, slots, bias_all, d_context, log_total, x_rows, adapt_all, dy1, qkv_x, a_qkv, picked,
+        early_in, early_pairs, n_fsdp, n_ctx,
     )
+
     codes = (adapter_ids[:, None] * RANK + jnp.arange(RANK)[None, :]).reshape(-1)
     chosen = (codes[:, None] == jnp.arange(NR)[None, :]).astype(BF16)
     b_down_grad, a_down_grad, b_up_grad = combine(
         grads, chosen, [(NR, width), (units, NR), (NR, units)]
     )
-    a_up_grad, b_out_grad, a_out_grad, b_qkv_grad = combine(
-        early, chosen, [(width, NR), (NR, width), (heads_width, NR), (3, NR, heads_width)]
+    a_up_grad, b_out_grad, a_out_grad = combine(
+        early, chosen, [(width, NR), (NR, width), (heads_width, NR)]
     )
-    (a_qkv_grad,) = combine(late, chosen, [(3, width, NR)])
+    b_qkv_grad, a_qkv_grad = combine(late, chosen, [(3, NR, heads_width), (3, width, NR)])
     return (
         activations, input_grad, a_qkv_grad, b_qkv_grad, a_out_grad, b_out_grad, a_up_grad, b_up_grad,
         a_down_grad, b_down_grad,

time: 625 us -> 606 us (0.970)
  Pallas kernels: 608 us -> 590 us
    pallas_call x2 -> x1, Pallas kernels: 166 us -> 139 us  [finish(): pl.pallas_call(kernel, in_specs=[vmem] * 8 + [anywhere] * (2 + n_ctx + n_...]
    pallas_call x1, Pallas kernels: 126 us -> 135 us  [middle(): pl.pallas_call(kernel, in_specs=[vmem] * 10 + [anywhere] * 7, out_specs=[...]
where the time goes in v9:
time: 606 us; the launch traced here: 602 us
  Pallas kernels  590 us (97%)
  local copies, waits for them, and re-layouts  9.72 us (2%)
    pallas_call x1, Pallas kernels, forward_and_gather(): pl.pallas_call(kernel, in_specs=[vmem] * 7 + [anywhere] * 8, out_specs=[s...  206 us
    pallas_call x1, Pallas kernels, finish(): pl.pallas_call(kernel, in_specs=[vmem] * 8 + [anywhere] * (2 + n_ctx + n_...  139 us
    pallas_call x1, Pallas kernels, middle(): pl.pallas_call(kernel, in_specs=[vmem] * 10 + [anywhere] * 7, out_specs=[...  135 us
    pallas_call x1, Pallas kernels, move(): pl.pallas_call(kernel, in_specs=spaces, out_specs=[pl.BlockSpec(memory_sp...  101 us

profile of v9, /device:TPU:0, one launch (start us, length us, event | category | flops | bytes accessed | tf_op | source)
XLA Modules:
  0.0 602.0 jit_solution(9441817408747893859)
XLA Ops:
  0.6 0.7 dynamic_slice.7
  1.4 0.7 fusion.2
  2.0 0.1 add_multiply_fusion
  2.1 0.1 iota_add_fusion
  2.2 0.1 add.83
  2.3 0.1 compare_select_fusion
  2.4 1.3 broadcast_in_dim.12.refs_0_.refs_1_
  3.7 0.7 dynamic_slice.6
  4.4 0.6 compare_convert_fusion.refs_2_.refs_0_.refs_7_
  5.0 101.4 %shard_map.258 = (bf16[2,4,64,2048]{3,2,1,0:T(8,128)(2,1)}, bf16[2432,3072]{1,0:T(8,128)(2,1)}) custom-call(bf16[8,64,2048]{2,1,0:T(8,128)(2,1)} %refs_0_.1, bf16[3,512,1024]{2,1,0:T(8,128)(2,1)} %refs_1_.3, bf16[3,128,1024]{2,1,0:T(8,128)(2,1)} %refs_2_.2), custom_call_target="tpu_custom_call" | custom-call | tf_op jit(solution)/shard_map/pallas_call | solution.py:316
  106.4 206.4 %shard_map.259 = (bf16[2,2,256,1024]{3,2,1,0:T(8,128)(2,1)}, bf16[2,2,256,1024]{3,2,1,0:T(8,128)(2,1)}, bf16[2,2,256,1024]{3,2,1,0:T(8,128)(2,1)}, bf16[2,256,10...) custom-call(f32[2,1024,128]{2,1,0:T(8,128)} %broadcast_in_dim.12.ref, ...), custom_call_target="tpu_custom_call" | custom-call | tf_op jit(solution)/shard_map/pallas_call | solution.py:610
  312.9 134.5 %shard_map.260 = (bf16[2,256,2048]{2,1,0:T(8,128)(2,1)}, f32[2,256,2048]{2,1,0:T(8,128)}, bf16[2,256,2176]{2,1,0:T(8,128)(2,1)}, bf16[2,4,64,2048]{3,2,1,0:T(8,1...) custom-call(f32[2,1,128]{2,1,0:T(1,128)} %compare_convert_fusion.ref, ...), custom_call_target="tpu_custom_call" | custom-call | tf_op jit(solution)/shard_map/pallas_call | solution.py:970
  447.4 138.8 %shard_map.261 = (bf16[8,64,2048]{2,1,0:T(8,128)(2,1)}, bf16[4,4,32,1280]{3,2,1,0:T(8,128)(2,1)}, bf16[4,4,32,2304]{3,2,1,0:T(8,128)(2,1)}) custom-call(bf16[2,256,1024]{2,1,0:T(8,128)(2,1)} %get-tuple-element.58.refs_0_, f32[2,1024,128]{2,1,0:T(8,128)} %broadcast_in_dim.12.refs_0_.refs_1_, bf16[2,256,1024]{2,1,0:T(8,128)(2,1)} %get-tuple-element.59.refs_2_, ...), custom_call_target="tpu_custom_call" | custom-call | tf_op jit(solution)/shard_map/pallas_call | solution.py:1323
  586.3 0.1 iota_add_fusion.1
  586.4 0.1 add.87
  586.4 0.1 fusion.chosen_ref
  586.5 1.8 copy-done.1
  588.3 3.0 shard_map.262
  591.3 1.3 copy-done.2
  592.6 2.4 shard_map.263
  595.0 3.1 shard_map.264
  598.1 1.3 copy.31
  599.4 1.0 copy-done.4
  600.5 1.3 copy.32
  (11 shorter events, 0.0 us)
Async XLA Ops:
  447.4 138.9 %copy-start.5 = (s32[8]{0:T(128)S(1)}, s32[8]{0:T(128)}, u32[]{:S(2)}) copy-start(s32[8]{0:T(128)} %param.22) | copy-start | bytes 100
  586.3 8.8 %copy-start = (bf16[4,4,32,2560]{3,2,1,0:T(8,128)(2,1)S(1)}, bf16[4,4,32,2560]{3,2,1,0:T(8,128)(2,1)}, u32[]{:S(2)}) copy-start(bf16[4,4,32,2560]{3,2,1,0:T(8,128)(2,1)} %get-tuple-element.80.piece_ref) | copy-start | bytes 7864324
  586.5 1.8 copy-start.1
  591.3 1.3 copy-start.2
  592.6 5.5 copy-start.3
  598.1 2.3 copy-start.4

commit v10 on v9

--- a/solution.py
+++ b/solution.py
@@ -93,8 +93,9 @@
 
 
 class Weight:
-    def __init__(self, shard_at, whole_at, own=None, skip=0):
+    def __init__(self, shard_at, whole_at, own=None, skip=0, direct=False):
         self.shard_at, self.whole_at, self.own, self.skip = shard_at, whole_at, own, skip
+        self.direct = direct
 
 
 class Deal:
@@ -166,6 +167,17 @@
         if isinstance(item, Pair):
             self.waiting[item] = [[] for _ in self.masks]
             self.cast(item, item.slot_at, lambda k, level: item.slot_at(k + 2**level), 0, 0)
+            return
+        if isinstance(item, Weight) and item.direct:
+            part = self.part(item)
+            self.came[item] = [
+                self.go(
+                    item.shard_at(part),
+                    item.whole_at(self.z, part),
+                    {"fsdp": lax.rem(self.z + s, self.n_fsdp)},
+                )
+                for s in range(1, self.n_fsdp)
+            ]
             return
         if isinstance(item, Weight):
             self.came[item] = self.used
@@ -211,13 +223,16 @@
             s = i // 2 + 1 if i % 2 == 0 else n - 1 - i // 2
             owner = lax.rem(self.z - s + n, n)
             here = item.whole_at(owner, part)
-            self.copy(here, here, {"fsdp": owner}, self.came[item] + s - 1).wait_recv()
-            if s < n - 1:
-                ok = (self.z >= s) & (self.z < n - 1)
-                self.along(item, owner, True, ok, here, s + 1)
-            if s > 1:
-                ok = (self.z < s) & (self.z > 0)
-                self.along(item, owner, False, ok, here, s - 1)
+            if item.direct:
+                self.came[item][s - 1].wait_recv()
+            else:
+                self.copy(here, here, {"fsdp": owner}, self.came[item] + s - 1).wait_recv()
+                if s < n - 1:
+                    ok = (self.z >= s) & (self.z < n - 1)
+                    self.along(item, owner, True, ok, here, s + 1)
+                if s > 1:
+                    ok = (self.z < s) & (self.z > 0)
+                    self.along(item, owner, False, ok, here, s - 1)
 
             def at(k, owner=owner):
                 return item.whole_at(owner, flip(part, others[k]))
@@ -667,11 +682,10 @@
         lax.fori_loop(first, n, step, 0)
 
 
-def compact(out_ref, n, entries, sizes):
+def compact(out_ref, n, entries, sizes, start=0):
     column = lax.broadcasted_iota(jnp.int32, (NR, RANK), 0)
     rank = lax.broadcasted_iota(jnp.int32, (NR, RANK), 1)
     used = jnp.where(lax.rem(column, RANK) == rank, 1.0, 0.0).astype(BF16)
-    start = 0
     for (code, value), size in zip(entries, sizes):
         short = dot(code(), used).astype(BF16)
         block = dot_tn(short, value()).astype(BF16)
@@ -714,7 +728,9 @@
 
     def gather(self):
         own = self.parts.at[self.mover.ct]
-        item = Weight(lambda c: self.parts.at[c], lambda o, c: self.out_ref.at[c, o], own)
+        item = Weight(
+            lambda c: self.parts.at[c], lambda o, c: self.out_ref.at[c, o], own, direct=True
+        )
         self.mover.begin(item)
         return own, self.out_ref.at[self.mover.ct, self.mover.z], item
 
@@ -758,12 +774,12 @@
         pick_ref, gain_ref, shift_ref, rstd1, code_up_ref = refs[:5]
         a_up_ref, b_out_ref, b_down_ref, a_down_ref, b_up_ref = refs[5:10]
         hat_ref, gelu_ref, slope_ref, cot_ref, out_ref, up_ref, down_ref = refs[10:17]
-        acts_out, dy1_out, da_out, cot_rows, grads_out, back_out = refs[17:23]
+        acts_out, dy1_out, da_out, cot_rows, grads_part, back_out = refs[17:23]
         dadapt_up_ref, ctx_ref = refs[23:25]
         (send, recv, deal_send, deal_recv, ring_sem, sems) = refs[25:31]
         (down_room, down_rows, up_rows) = refs[31:34]
         (stage, part, got, hat1, keep32, slope, gelu, wide_v, turned, dpre_t) = refs[34:44]
-        codes_down, grads_part, grads_came = refs[44:]
+        (codes_down,) = refs[44:]
         mover = Mover(n_fsdp, n_ctx, deal_send, deal_recv)
         partner = {"tp": 1 - lax.axis_index("tp")}
 
@@ -907,10 +923,6 @@
                 (lambda g=g: code_up_ref[g], lambda g=g: slope[g]),
             ]
             compact(grads_part, g, entries, sizes)
-
-        fold = Fold(mover, grads_part, grads_came, grads_out)
-        lasting = len(mover.masks) - 1
-        fold.hand(lasting)
         for g in range(per):
             swapped(1, g)
             pick = pick_ref[g]
@@ -928,8 +940,6 @@
                 wide_v[g, rows, width:] = (dot_nt(low, b_out_ref[...]) * pick).astype(BF16)
 
             by_rows(first_back)
-            if g == 0:
-                fold.next(lasting)
             move(keep32.at[g], dy1_out.at[g], "dy1")
             move(wide_v.at[g], da_out.at[g], "wide")
             turned[...] = wide_v[g].T
@@ -940,13 +950,6 @@
             out_r.run(width_here // tile, out_back)
             if g + 1 < per:
                 out_r.prefetch()
-            if g == 0:
-                for level in range(lasting - 1, -1, -1):
-                    fold.next(level)
-                source, target, item = fold.gather()
-                move(source, target, "grads")
-                mover.relay(item)
-        mover.complete(item)
         for copy in dealt:
             copy.wait_recv()
         free(*list(busy))
@@ -960,13 +963,13 @@
         (row + (width,), F32, anywhere),
         (row + (wide,), BF16, anywhere),
         ((per, n_fsdp) + cot.shape[1:], BF16, anywhere),
-        ((n_ctx, n_fsdp) + grads_shape[1:], BF16, anywhere),
+        (grads_shape, BF16, vmem),
         (cot.shape, BF16, anywhere),
         (row + (NR,), BF16, vmem),
         (row + (width_here,), BF16, vmem),
     ]
     n_copy = 2 * per * n_swap
-    n_deal = 2 * per * (n_fsdp - 1) + (n_fsdp - 1) * n_ctx + 2 * (n_ctx - 1)
+    n_deal = 2 * per * (n_fsdp - 1)
     return pl.pallas_call(
         kernel,
         in_specs=[vmem] * 10 + [anywhere] * 7,
@@ -978,7 +981,7 @@
             pltpu.SemaphoreType.DMA((n_deal,)),
             pltpu.SemaphoreType.DMA((n_deal,)),
             pltpu.SemaphoreType.DMA((8,)),
-            pltpu.SemaphoreType.DMA(((8 + n_fsdp) * per + 1,)),
+            pltpu.SemaphoreType.DMA(((8 + n_fsdp) * per,)),
             pltpu.VMEM((2, units, tile), BF16),
             pltpu.VMEM((2, tile, wide), BF16),
             pltpu.VMEM((2, tile, units), BF16),
@@ -993,8 +996,6 @@
             pltpu.VMEM((wide, loc), BF16),
             pltpu.VMEM((units, loc), BF16),
             pltpu.VMEM(row + (NR,), BF16),
-            pltpu.VMEM(grads_shape, BF16),
-            pltpu.VMEM((n_ctx - 1,) + grads_shape[1:], BF16),
         ],
         compiler_params=pltpu.CompilerParams(
             collective_id=3, has_side_effects=True, vmem_limit_bytes=62 << 20
@@ -1051,7 +1052,7 @@
 
 
 def finish(
-    query, kv_own, slots, bias, grad, log_total, x_rows, adapt_in, dy1, qkv_x, a_qkv, picked, early, pairs, n_fsdp, n_ctx
+    query, kv_own, slots, bias, grad, log_total, x_rows, adapt_in, dy1, qkv_x, a_qkv, picked, grads, early, pairs, n_fsdp, n_ctx
 ):
     per, loc, width_here = query.shape
     piece, width = loc // n_fsdp, x_rows.shape[2]
@@ -1069,22 +1070,23 @@
     n_swap = n_wide + 1
     n_early = len(early)
     early_sizes = [values[2] // n_ctx for _, values in pairs]
+    before = grads.shape[2]
     late_sizes = [width_here // n_ctx] * 3 + [width // n_ctx] * 3
     n_copy = len(units) * (n_ctx - 1) + per * n_wide * (n_fsdp - 1)
     n_copy += 2 * ((n_fsdp - 1) * n_ctx + 2 * (n_ctx - 1))
 
     def kernel(*refs):
         q_ref, bias_ref, g_ref, log_ref, x_ref, adapt_ref, a_ref, pick_ref = refs[:8]
-        dy1_ref, w_ref, kv_ref = refs[8:11]
-        slot_refs = refs[11 : 10 + n_ctx]
-        early_refs = refs[10 + n_ctx : 10 + n_ctx + n_early]
-        at = 10 + n_ctx + n_early
+        dy1_ref, w_ref, grads_ref, kv_ref = refs[8:12]
+        slot_refs = refs[12 : 11 + n_ctx]
+        early_refs = refs[11 + n_ctx : 11 + n_ctx + n_early]
+        at = 11 + n_ctx + n_early
         in_ref, early_out, late_out = refs[at : at + 3]
         send, recv, swap_send, swap_recv, ring_sem, load, sems = refs[at + 3 : at + 10]
         kv_room, own, came, dq, dkv = refs[at + 10 : at + 15]
-        tiles, foot_room, dy1_room, turned, part, got, codes_in, dx = refs[at + 15 : at + 23]
-        early_part, early_came, late_part, late_came = refs[at + 23 : at + 27]
-        staged = refs[at + 27 :]
+        tiles, foot_room, dy1_room, turned, part, got, codes_in = refs[at + 15 : at + 22]
+        early_part, early_came, late_part, late_came = refs[at + 22 : at + 26]
+        staged = refs[at + 26 :]
         mover = Mover(n_fsdp, n_ctx, send, recv)
         z, ct = mover.z, mover.ct
         partner = {"tp": 1 - lax.axis_index("tp")}
@@ -1109,6 +1111,7 @@
                 copy.start()
                 loads[g].append(copy)
         staging = [move(ref, room) for ref, room in zip(early_refs, staged)]
+        staging.append(move(grads_ref, early_part.at[:, :, pl.ds(0, before)]))
         load_foot = move(w_ref.at[pl.ds(width, foot)], foot_room)
         ring.prefetch()
         load_dy1 = move(dy1_ref, dy1_room)
@@ -1201,22 +1204,41 @@
 
         def finish_tile(g, t):
             swap_copy(g, t).wait_recv()
+            swap_copy(g, t).wait_send()
             at = slice(t * tile, (t + 1) * tile)
             value = part[g, :, at].astype(F32) + got[g, :, at].astype(F32) + dy1_room[g, :, at]
             for j in range(3):
                 value = value + dot_nt(codes_in[g, :, j * NR : (j + 1) * NR], a_ref[j, at, :])
-            dx[g, :, at] = value.astype(BF16)
+            part[g, :, at] = value.astype(BF16)
             to_at = pl.ds(t * tile, tile)
-            kept.append(move(dx.at[g, pl.ds(0, piece), to_at], in_ref.at[z * per + g, :, to_at]))
+            kept.append(move(part.at[g, pl.ds(0, piece), to_at], in_ref.at[z * per + g, :, to_at]))
             for s in range(1, n_fsdp):
                 to = lax.rem(z - s + n_fsdp, n_fsdp)
                 dealt.append(
                     mover.go(
-                        dx.at[g, pl.ds(s * piece, piece), to_at],
+                        part.at[g, pl.ds(s * piece, piece), to_at],
                         in_ref.at[z * per + g, :, to_at],
                         {"fsdp": to},
                     )
                 )
+
+        early_fold = Fold(mover, early_part, early_came, early_out)
+        late_fold = Fold(mover, late_part, late_came, late_out)
+
+        def known():
+            for copy in staging:
+                copy.wait()
+            for n in range(per):
+                entries = []
+                for (i, first, size), (j, start, count) in pairs:
+                    entries.append(
+                        (
+                            lambda n=n, i=i, f=first, c=size: staged[i][n, :, f : f + c],
+                            lambda n=n, i=j, f=start, c=count: staged[i][n, :, f : f + c],
+                        )
+                    )
+                compact(early_part, n, entries, early_sizes, before)
+            early_fold.hand(last)
 
         last = len(masks) - 1
         for t in range(len(units) + last):
@@ -1226,40 +1248,30 @@
             for k in range(last):
                 if 0 <= t - 1 - k < len(units):
                     take_in(t - 1 - k, last - k)
-        for copy in staging:
-            copy.wait()
-        for n in range(per):
-            entries = []
-            for (i, first, size), (j, start, count) in pairs:
-                entries.append(
-                    (
-                        lambda n=n, i=i, f=first, c=size: staged[i][n, :, f : f + c],
-                        lambda n=n, i=j, f=start, c=count: staged[i][n, :, f : f + c],
-                    )
-                )
-            compact(early_part, n, entries, early_sizes)
-        early_fold = Fold(mover, early_part, early_came, early_out)
-        late_fold = Fold(mover, late_part, late_came, late_out)
-        early_fold.hand(last)
+            if t == 1:
+                known()
+            if t == 3:
+                for level in range(last, 0, -1):
+                    early_fold.next(level)
+            if t == 6:
+                early_fold.next(0)
+                source, target, first = early_fold.gather()
+                kept.append(move(source, target))
         done = set()
         for g in range(per):
             for u, (owner, _) in enumerate(units):
                 if owner == g:
                     take_in(u, 0)
+            if g + 1 == per:
+                mover.relay(first)
             project_back(g)
             take_codes(g)
             if g == 0:
-                for level in range(last, -1, -1):
-                    early_fold.next(level)
-                source, target, first = early_fold.gather()
-                kept.append(move(source, target))
                 load_dy1.wait()
             if g + 1 < per:
                 for t in range(n_wide // 2):
                     finish_tile(g, t)
                     done.add((g, t))
-            if g == 0:
-                mover.relay(first)
         for n in range(per):
             values = [
                 lambda n=n: dq[n],
@@ -1276,23 +1288,22 @@
             compact(late_part, n, entries, late_sizes)
         late_fold.hand(last)
         rest = [(g, t) for g in range(per) for t in range(n_wide) if (g, t) not in done]
-        cut = len(rest) - 2
         for i, (g, t) in enumerate(rest):
             finish_tile(g, t)
-            if i == cut - 2:
+            if i == 0:
                 for level in range(last, 0, -1):
                     late_fold.next(level)
-            if i == cut - 1:
+            if i == 1:
                 late_fold.next(0)
                 source, target, second = late_fold.gather()
                 kept.append(move(source, target))
+            if i == len(rest) - 3:
                 mover.complete(first)
-            if i == cut:
+            if i == len(rest) - 2:
                 mover.relay(second)
         mover.complete(second)
         for g in range(per):
-            for t in range(n_swap):
-                swap_copy(g, t).wait_send()
+            swap_copy(g, n_wide).wait_send()
         for copy in dealt:
             copy.wait_recv()
         for copy in kept:
@@ -1300,7 +1311,7 @@
         mover.close()
 
     vmem, anywhere = pl.BlockSpec(memory_space=pltpu.VMEM), pl.BlockSpec(memory_space=pl.ANY)
-    parts = [(n_ctx, per * RANK, sum(early_sizes)), (n_ctx, per * RANK, sum(late_sizes))]
+    parts = [(n_ctx, per * RANK, before + sum(early_sizes)), (n_ctx, per * RANK, sum(late_sizes))]
     row = (per, loc)
     rooms = [
         ((per, n_ctx, 2, loc, width_here), BF16),
@@ -1315,14 +1326,13 @@
         (row + (wide,), BF16),
         (row + (wide,), BF16),
         (row + (foot,), BF16),
-        (row + (width,), BF16),
     ]
     for shape in parts:
         rooms += [(shape, BF16), ((n_ctx - 1,) + shape[1:], BF16)]
     rooms += [(x.shape, BF16) for x in early]
     return pl.pallas_call(
         kernel,
-        in_specs=[vmem] * 8 + [anywhere] * (2 + n_ctx + n_early),
+        in_specs=[vmem] * 8 + [anywhere] * (3 + n_ctx + n_early),
         out_specs=[anywhere] * 3,
         out_shape=[jax.ShapeDtypeStruct((per * n_fsdp, piece, width), BF16)]
         + [jax.ShapeDtypeStruct((n_ctx, n_fsdp) + shape[1:], BF16) for shape in parts],
@@ -1333,14 +1343,14 @@
             pltpu.SemaphoreType.DMA((per * n_swap,)),
             pltpu.SemaphoreType.DMA((2,)),
             pltpu.SemaphoreType.DMA((per * n_ctx,)),
-            pltpu.SemaphoreType.DMA((4 + n_early + per * n_wide,)),
+            pltpu.SemaphoreType.DMA((5 + n_early + per * n_wide,)),
         ]
         + [pltpu.VMEM(shape, dtype) for shape, dtype in rooms],
         compiler_params=pltpu.CompilerParams(
             collective_id=4, has_side_effects=True, vmem_limit_bytes=63 << 20
         ),
     )(
-        query, bias, grad, log_total, x_rows, adapt_in, a_qkv, picked, dy1, qkv_x, kv_own, *slots, *early,
+        query, bias, grad, log_total, x_rows, adapt_in, a_qkv, picked, dy1, qkv_x, grads, kv_own, *slots, *early,
     )
 
 
@@ -1460,16 +1470,15 @@
     ]
     input_grad, early, late = finish(
         query, kv_own, slots, bias_all, d_context, log_total, x_rows, adapt_all, dy1, qkv_x, a_qkv, picked,
-        early_in, early_pairs, n_fsdp, n_ctx,
+        grads, early_in, early_pairs, n_fsdp, n_ctx,
     )
 
     codes = (adapter_ids[:, None] * RANK + jnp.arange(RANK)[None, :]).reshape(-1)
     chosen = (codes[:, None] == jnp.arange(NR)[None, :]).astype(BF16)
-    b_down_grad, a_down_grad, b_up_grad = combine(
-        grads, chosen, [(NR, width), (units, NR), (NR, units)]
-    )
-    a_up_grad, b_out_grad, a_out_grad = combine(
-        early, chosen, [(width, NR), (NR, width), (heads_width, NR)]
+    b_down_grad, a_down_grad, b_up_grad, a_up_grad, b_out_grad, a_out_grad = combine(
+        early,
+        chosen,
+        [(NR, width), (units, NR), (NR, units), (width, NR), (NR, width), (heads_width, NR)],
     )
     b_qkv_grad, a_qkv_grad = combine(late, chosen, [(3, NR, heads_width), (3, width, NR)])
     return (

time: 606 us -> 580 us (0.957)
  Pallas kernels: 590 us -> 564 us
    pallas_call x1, Pallas kernels: 135 us -> 115 us  [middle(): pl.pallas_call(kernel, in_specs=[vmem] * 10 + [anywhere] * 7, out_specs=[...]
where the time goes in v10:
time: 580 us; the launch traced here: 576 us
  Pallas kernels  564 us (97%)
  local copies, waits for them, and re-layouts  8.72 us (2%)
    pallas_call x1, Pallas kernels, forward_and_gather(): pl.pallas_call(kernel, in_specs=[vmem] * 7 + [anywhere] * 8, out_specs=[s...  206 us
    pallas_call x1, Pallas kernels, finish(): pl.pallas_call(kernel, in_specs=[vmem] * 8 + [anywhere] * (3 + n_ctx + n_...  134 us
    pallas_call x1, Pallas kernels, middle(): pl.pallas_call(kernel, in_specs=[vmem] * 10 + [anywhere] * 7, out_specs=[...  115 us
    pallas_call x1, Pallas kernels, move(): pl.pallas_call(kernel, in_specs=spaces, out_specs=[pl.BlockSpec(memory_sp...  101 us

profile of v10, /device:TPU:0, one launch (start us, length us, event | category | flops | bytes accessed | tf_op | source)
XLA Modules:
  0.0 575.8 jit_solution(6638158319392716302)
XLA Ops:
  0.6 0.7 dynamic_slice.7
  1.4 0.7 fusion.2
  2.0 0.1 add_multiply_fusion
  2.1 0.1 iota_add_fusion
  2.2 0.1 add.83
  2.3 0.1 compare_select_fusion
  2.4 1.3 broadcast_in_dim.12.refs_0_.refs_1_
  3.7 0.7 dynamic_slice.6
  4.4 0.6 compare_convert_fusion.refs_2_.refs_0_.refs_7_
  5.0 101.4 %shard_map.258 = (bf16[2,4,64,2048]{3,2,1,0:T(8,128)(2,1)}, bf16[2432,3072]{1,0:T(8,128)(2,1)}) custom-call(bf16[8,64,2048]{2,1,0:T(8,128)(2,1)} %refs_0_.1, bf16[3,512,1024]{2,1,0:T(8,128)(2,1)} %refs_1_.3, bf16[3,128,1024]{2,1,0:T(8,128)(2,1)} %refs_2_.2), custom_call_target="tpu_custom_call" | custom-call | tf_op jit(solution)/shard_map/pallas_call | solution.py:331
  106.4 206.5 %shard_map.259 = (bf16[2,2,256,1024]{3,2,1,0:T(8,128)(2,1)}, bf16[2,2,256,1024]{3,2,1,0:T(8,128)(2,1)}, bf16[2,2,256,1024]{3,2,1,0:T(8,128)(2,1)}, bf16[2,256,10...) custom-call(f32[2,1024,128]{2,1,0:T(8,128)} %broadcast_in_dim.12.ref, ...), custom_call_target="tpu_custom_call" | custom-call | tf_op jit(solution)/shard_map/pallas_call | solution.py:625
  312.9 115.4 %shard_map.260 = (bf16[2,256,2048]{2,1,0:T(8,128)(2,1)}, f32[2,256,2048]{2,1,0:T(8,128)}, bf16[2,256,2176]{2,1,0:T(8,128)(2,1)}, bf16[2,4,64,2048]{3,2,1,0:T(8,1...) custom-call(f32[2,1,128]{2,1,0:T(1,128)} %compare_convert_fusion.ref, ...), custom_call_target="tpu_custom_call" | custom-call | tf_op jit(solution)/shard_map/pallas_call | solution.py:973
  428.3 0.0 copy-start.4
  428.3 134.4 %shard_map.261 = (bf16[8,64,2048]{2,1,0:T(8,128)(2,1)}, bf16[4,4,32,3840]{3,2,1,0:T(8,128)(2,1)}, bf16[4,4,32,2304]{3,2,1,0:T(8,128)(2,1)}) custom-call(bf16[2,256,1024]{2,1,0:T(8,128)(2,1)} %get-tuple-element.58.refs_0_, f32[2,1024,128]{2,1,0:T(8,128)} %broadcast_in_dim.12.refs_0_.refs_1_, bf16[2,256,1024]{2,1,0:T(8,128)(2,1)} %get-tuple-element.59.refs_2_, ...), custom_call_target="tpu_custom_call" | custom-call | tf_op jit(solution)/shard_map/pallas_call | solution.py:1333
  562.7 0.0 copy-done.4
  562.8 0.1 iota_add_fusion.1
  562.8 0.1 add.87
  562.9 0.1 fusion.chosen_ref
  563.0 2.1 copy-done
  565.1 3.8 shard_map.263
  569.0 3.0 shard_map.262
  571.9 1.3 copy.31
  573.3 1.0 copy-done.3
  574.3 1.3 copy.32
  (8 shorter events, 0.0 us)
Async XLA Ops:
  428.3 134.4 %copy-start.4 = (s32[8]{0:T(128)S(1)}, s32[8]{0:T(128)}, u32[]{:S(2)}) copy-start(s32[8]{0:T(128)} %param.22) | copy-start | bytes 100
  563.0 2.1 copy-start
  565.1 3.8 copy-start.1
  568.9 3.0 copy-start.2
  571.9 2.3 copy-start.3

commit v11 on v10

--- a/solution.py
+++ b/solution.py
@@ -361,7 +361,7 @@
     paired = cuts // 2 if n_ctx > 1 else 0
     tile = 512
     per_kind = width_here // tile
-    chunk = 32
+    chunk = 64
     n_tile = 3 * per_kind
     n_copy = (n_fsdp - 1) * n_ctx * (1 + 2 * cuts) + 2 * per * (n_ctx - 1) + 6 + per
     lag = 4
@@ -765,7 +765,7 @@
     wide, units = up_x.shape
     width_here = out_x.shape[0]
     tile = 512
-    chunk = 32
+    chunk = 128
     n_wide = width // tile
     n_swap = n_wide + 1
     sizes = [width // n_ctx, units // n_ctx, units // n_ctx]
@@ -837,9 +837,11 @@
             if g == 0:
                 down.prefetch()
             move(cot_ref.at[mover.z * per + g], cot_rows.at[g, 0], ("cot", g))
-        for g in range(per):
+
+        def load_rest(g):
             move(hat_ref.at[g], hat1.at[g], ("hat", g))
             move(slope_ref.at[g], slope.at[g], ("slope", g))
+
         mover.greet(tp=True)
         mover.begin(deals[0])
 
@@ -860,6 +862,7 @@
             part[g, :, width:] = dot(gelu[g], a_down_ref[...]).astype(BF16)
             swap_copy(0, g, n_wide, NR).start()
 
+        load_rest(0)
         for g in range(per):
             mover.relay(deals[g])
             if g + 1 < per:
@@ -885,6 +888,8 @@
                 wide_v[g, rows, :width] = low
                 wide_v[g, rows, width:] = (dot_nt(low, b_down_ref[...]) * pick).astype(BF16)
 
+            if g + 1 < per:
+                load_rest(g + 1)
             by_rows(second_norm)
             move(part.at[g, :, pl.ds(0, width)], acts_out.at[g], ("part", g))
             own = part.at[g, pl.ds(0, piece), pl.ds(0, width)]
@@ -1108,18 +1113,24 @@
                 copy = pltpu.make_async_copy(
                     source.at[:, g], kv_room.at[g, k], load.at[g * n_ctx + k]
                 )
-                copy.start()
+                if g == 0:
+                    copy.start()
                 loads[g].append(copy)
+        mover.greet(tp=True)
+        for copy in loads[0]:
+            copy.wait()
         staging = [move(ref, room) for ref, room in zip(early_refs, staged)]
         staging.append(move(grads_ref, early_part.at[:, :, pl.ds(0, before)]))
+        for group in loads[1:]:
+            for copy in group:
+                copy.start()
         load_foot = move(w_ref.at[pl.ds(width, foot)], foot_room)
         ring.prefetch()
         load_dy1 = move(dy1_ref, dy1_room)
-        mover.greet(tp=True)
 
         def compute(u):
             g, c = units[u]
-            if c == 0:
+            if c == 0 and g:
                 for copy in loads[g]:
                     copy.wait()
 
@@ -1144,7 +1155,8 @@
                     own[u, k, 1, :, to] = dvalues[k]
                 return carry
 
-            lax.fori_loop(0, high, one, 0)
+            for h in range(high):
+                one(h, 0)
 
         def hand(u, level):
             half = 2**level
@@ -1269,7 +1281,7 @@
             if g == 0:
                 load_dy1.wait()
             if g + 1 < per:
-                for t in range(n_wide // 2):
+                for t in range(n_wide - 1):
                     finish_tile(g, t)
                     done.add((g, t))
         for n in range(per):

time: 580 us -> 562 us (0.969)
  Pallas kernels: 564 us -> 547 us
    pallas_call x1, Pallas kernels: 134 us -> 122 us  [finish(): pl.pallas_call(kernel, in_specs=[vmem] * 8 + [anywhere] * (3 + n_ctx + n_...]
where the time goes in v11:
time: 562 us; the launch traced here: 558 us
  Pallas kernels  547 us (97%)
  local copies, waits for them, and re-layouts  8.72 us (2%)
    pallas_call x1, Pallas kernels, forward_and_gather(): pl.pallas_call(kernel, in_specs=[vmem] * 7 + [anywhere] * 8, out_specs=[s...  206 us
    pallas_call x1, Pallas kernels, finish(): pl.pallas_call(kernel, in_specs=[vmem] * 8 + [anywhere] * (3 + n_ctx + n_...  122 us
    pallas_call x1, Pallas kernels, middle(): pl.pallas_call(kernel, in_specs=[vmem] * 10 + [anywhere] * 7, out_specs=[...  111 us
    pallas_call x1, Pallas kernels, move(): pl.pallas_call(kernel, in_specs=spaces, out_specs=[pl.BlockSpec(memory_sp...  101 us

profile of v11, /device:TPU:0, one launch (start us, length us, event | category | flops | bytes accessed | tf_op | source)
XLA Modules:
  0.0 558.5 jit_solution(12827258050969216881)
XLA Ops:
  0.6 0.7 dynamic_slice.7
  1.4 0.7 fusion.2
  2.0 0.1 add_multiply_fusion
  2.1 0.1 iota_add_fusion
  2.2 0.1 add.83
  2.3 0.1 compare_select_fusion
  2.4 1.3 broadcast_in_dim.12.refs_0_.refs_1_
  3.7 0.7 dynamic_slice.6
  4.4 0.6 compare_convert_fusion.refs_2_.refs_0_.refs_7_
  5.0 101.4 %shard_map.258 = (bf16[2,4,64,2048]{3,2,1,0:T(8,128)(2,1)}, bf16[2432,3072]{1,0:T(8,128)(2,1)}) custom-call(bf16[8,64,2048]{2,1,0:T(8,128)(2,1)} %refs_0_.1, bf16[3,512,1024]{2,1,0:T(8,128)(2,1)} %refs_1_.3, bf16[3,128,1024]{2,1,0:T(8,128)(2,1)} %refs_2_.2), custom_call_target="tpu_custom_call" | custom-call | tf_op jit(solution)/shard_map/pallas_call | solution.py:331
  106.4 205.7 %shard_map.259 = (bf16[2,2,256,1024]{3,2,1,0:T(8,128)(2,1)}, bf16[2,2,256,1024]{3,2,1,0:T(8,128)(2,1)}, bf16[2,2,256,1024]{3,2,1,0:T(8,128)(2,1)}, bf16[2,256,10...) custom-call(f32[2,1024,128]{2,1,0:T(8,128)} %broadcast_in_dim.12.ref, ...), custom_call_target="tpu_custom_call" | custom-call | tf_op jit(solution)/shard_map/pallas_call | solution.py:625
  312.1 111.5 %shard_map.260 = (bf16[2,256,2048]{2,1,0:T(8,128)(2,1)}, f32[2,256,2048]{2,1,0:T(8,128)}, bf16[2,256,2176]{2,1,0:T(8,128)(2,1)}, bf16[2,4,64,2048]{3,2,1,0:T(8,1...) custom-call(f32[2,1,128]{2,1,0:T(1,128)} %compare_convert_fusion.ref, ...), custom_call_target="tpu_custom_call" | custom-call | tf_op jit(solution)/shard_map/pallas_call | solution.py:978
  423.6 0.0 copy-start.4
  423.6 121.7 %shard_map.261 = (bf16[8,64,2048]{2,1,0:T(8,128)(2,1)}, bf16[4,4,32,3840]{3,2,1,0:T(8,128)(2,1)}, bf16[4,4,32,2304]{3,2,1,0:T(8,128)(2,1)}) custom-call(bf16[2,256,1024]{2,1,0:T(8,128)(2,1)} %get-tuple-element.58.refs_0_, f32[2,1024,128]{2,1,0:T(8,128)} %broadcast_in_dim.12.refs_0_.refs_1_, bf16[2,256,1024]{2,1,0:T(8,128)(2,1)} %get-tuple-element.59.refs_2_, ...), custom_call_target="tpu_custom_call" | custom-call | tf_op jit(solution)/shard_map/pallas_call | solution.py:1345
  545.4 0.1 iota_add_fusion.1
  545.4 0.1 add.87
  545.5 0.1 fusion.chosen_ref
  545.6 0.0 copy-start
  545.6 2.1 copy-done
  547.7 3.8 shard_map.263
  551.6 3.0 shard_map.262
  554.6 1.3 copy.31
  555.9 1.0 copy-done.3
  556.9 1.3 copy.32
  (8 shorter events, 0.0 us)
Async XLA Ops:
  423.6 121.8 %copy-start.4 = (s32[8]{0:T(128)S(1)}, s32[8]{0:T(128)}, u32[]{:S(2)}) copy-start(s32[8]{0:T(128)} %param.22) | copy-start | bytes 100
  545.6 2.1 copy-start
  547.7 3.8 copy-start.1
  551.6 3.0 copy-start.2
  554.6 2.3 copy-start.3

commit v12 on v11

--- a/solution.py
+++ b/solution.py
@@ -552,7 +552,7 @@
         ring.prefetch()
         loads = [move(x_ref.at[g], x_room.at[rows[g], pl.ds(0, width)]) for g in range(per)]
         mover.greet(tp=True)
-        ahead = 3
+        ahead = 2
         for item in items[:ahead]:
             mover.begin(item)
         sibling = {"ctx": flip(mover.ct, 1)}

time: 562 us -> 566 us (level)
  no operation moved by 1% of the time
where the time goes in v12:
time: 566 us; the launch traced here: 562 us
  Pallas kernels  551 us (97%)
  local copies, waits for them, and re-layouts  8.72 us (2%)
    pallas_call x1, Pallas kernels, forward_and_gather(): pl.pallas_call(kernel, in_specs=[vmem] * 7 + [anywhere] * 8, out_specs=[s...  211 us
    pallas_call x1, Pallas kernels, finish(): pl.pallas_call(kernel, in_specs=[vmem] * 8 + [anywhere] * (3 + n_ctx + n_...  122 us
    pallas_call x1, Pallas kernels, middle(): pl.pallas_call(kernel, in_specs=[vmem] * 10 + [anywhere] * 7, out_specs=[...  110 us
    pallas_call x1, Pallas kernels, move(): pl.pallas_call(kernel, in_specs=spaces, out_specs=[pl.BlockSpec(memory_sp...  101 us

profile of v12, /device:TPU:0, one launch (start us, length us, event | category | flops | bytes accessed | tf_op | source)
XLA Modules:
  0.0 562.1 jit_solution(5932205683862281326)
XLA Ops:
  0.6 0.7 dynamic_slice.7
  1.4 0.7 fusion.2
  2.0 0.1 add_multiply_fusion
  2.1 0.1 iota_add_fusion
  2.2 0.1 add.83
  2.3 0.1 compare_select_fusion
  2.4 1.3 broadcast_in_dim.12.refs_0_.refs_1_
  3.7 0.7 dynamic_slice.6
  4.4 0.6 compare_convert_fusion.refs_2_.refs_0_.refs_7_
  5.0 101.4 %shard_map.258 = (bf16[2,4,64,2048]{3,2,1,0:T(8,128)(2,1)}, bf16[2432,3072]{1,0:T(8,128)(2,1)}) custom-call(bf16[8,64,2048]{2,1,0:T(8,128)(2,1)} %refs_0_.1, bf16[3,512,1024]{2,1,0:T(8,128)(2,1)} %refs_1_.3, bf16[3,128,1024]{2,1,0:T(8,128)(2,1)} %refs_2_.2), custom_call_target="tpu_custom_call" | custom-call | tf_op jit(solution)/shard_map/pallas_call | solution.py:331
  106.4 210.9 %shard_map.259 = (bf16[2,2,256,1024]{3,2,1,0:T(8,128)(2,1)}, bf16[2,2,256,1024]{3,2,1,0:T(8,128)(2,1)}, bf16[2,2,256,1024]{3,2,1,0:T(8,128)(2,1)}, bf16[2,256,10...) custom-call(f32[2,1024,128]{2,1,0:T(8,128)} %broadcast_in_dim.12.ref, ...), custom_call_target="tpu_custom_call" | custom-call | tf_op jit(solution)/shard_map/pallas_call | solution.py:625
  317.4 110.1 %shard_map.260 = (bf16[2,256,2048]{2,1,0:T(8,128)(2,1)}, f32[2,256,2048]{2,1,0:T(8,128)}, bf16[2,256,2176]{2,1,0:T(8,128)(2,1)}, bf16[2,4,64,2048]{3,2,1,0:T(8,1...) custom-call(f32[2,1,128]{2,1,0:T(1,128)} %compare_convert_fusion.ref, ...), custom_call_target="tpu_custom_call" | custom-call | tf_op jit(solution)/shard_map/pallas_call | solution.py:978
  427.5 0.0 copy-start.4
  427.5 121.5 %shard_map.261 = (bf16[8,64,2048]{2,1,0:T(8,128)(2,1)}, bf16[4,4,32,3840]{3,2,1,0:T(8,128)(2,1)}, bf16[4,4,32,2304]{3,2,1,0:T(8,128)(2,1)}) custom-call(bf16[2,256,1024]{2,1,0:T(8,128)(2,1)} %get-tuple-element.58.refs_0_, f32[2,1024,128]{2,1,0:T(8,128)} %broadcast_in_dim.12.refs_0_.refs_1_, bf16[2,256,1024]{2,1,0:T(8,128)(2,1)} %get-tuple-element.59.refs_2_, ...), custom_call_target="tpu_custom_call" | custom-call | tf_op jit(solution)/shard_map/pallas_call | solution.py:1345
  549.0 0.1 iota_add_fusion.1
  549.1 0.1 add.87
  549.2 0.1 fusion.chosen_ref
  549.3 0.0 copy-start
  549.3 2.1 copy-done
  551.4 3.8 shard_map.263
  555.2 3.0 shard_map.262
  558.2 1.3 copy.31
  559.5 1.0 copy-done.3
  560.6 1.3 copy.32
  (8 shorter events, 0.0 us)
Async XLA Ops:
  427.5 121.5 %copy-start.4 = (s32[8]{0:T(128)S(1)}, s32[8]{0:T(128)}, u32[]{:S(2)}) copy-start(s32[8]{0:T(128)} %param.22) | copy-start | bytes 100
  549.3 2.1 copy-start
  551.4 3.8 copy-start.1
  555.2 3.0 copy-start.2
  558.2 2.3 copy-start.3
